TPU v7x, 32 devices: a whole 2x2x4 slice. The times are simulated.
32 devices in a mesh: rep: 8 (over z, y), shard: 4 (over x, core).
Axes of the slice: x: 2, y: 2, z: 4, core: 2. Of those that a mesh axis runs over, the one named last changes fastest.
Arguments:
- tokens: bfloat16 [8, 1024, 2304], P('rep', 'shard'), may hold values from -6 to 6
- cotangent: bfloat16 [8, 1024, 2304], P('rep', 'shard'), may hold values from -6 to 6
- sequence_adapter_index: int32 [8], P('rep'), may hold values from 0 to 7
- image_span_start: int32 [8, 2], P('rep'), may hold values from 0 to 768, as said below
- attention_norm_gain: bfloat16 [2304], replicated, may hold values from 0.099609375 to 1.8984375
- feedforward_norm_gain: bfloat16 [2304], replicated, may hold values from 0.099609375 to 1.8984375
- query_key_value_weight: bfloat16 [3, 2304, 2304], P(None, 'shard'), may hold values from -0.125 to 0.125
- attention_output_weight: bfloat16 [2304, 2304], P('shard'), may hold values from -2 to 2
- gate_up_projection_weight: bfloat16 [2, 2304, 5760], P(None, 'shard'), may hold values from -0.125 to 0.125
- down_projection_weight: bfloat16 [5760, 2304], P('shard'), may hold values from -0.625 to 0.625
- adapter_model_input_maps: bfloat16 [6, 8, 16, 2304], P(None, 'shard'), may hold values from -0.125 to 0.125
- adapter_model_output_maps: bfloat16 [5, 8, 16, 2304], P(None, 'shard'), may hold values from -1.5 to 1.5
- adapter_hidden_input_map: bfloat16 [8, 16, 5760], P('shard'), may hold values from -0.078125 to 0.078125
- adapter_hidden_output_maps: bfloat16 [2, 8, 16, 5760], P(None, 'shard'), may hold values from -1.5 to 1.5
Outputs:
- output: bfloat16 [8, 1024, 2304], P('rep', 'shard')
- input_grad: float32 [8, 1024, 2304], P('rep', 'shard')
- grad_a_model: float32 [6, 8, 16, 2304], P(None, 'shard')
- grad_b_model: float32 [5, 8, 16, 2304], P(None, 'shard')
- grad_a_hidden: float32 [8, 16, 5760], P('shard')
- grad_b_hidden: float32 [2, 8, 16, 5760], P(None, 'shard')
Inputs may be any that keep to these rules, and one draw needn't show every extreme that they name: `image_span_start`: in each sequence the first span starts in 0 to 256 and the second in 512 to 768; some sequence's first span starts at 0 and some sequence's second span ends at the sequence's end.
All inputs are finite; a program needn't handle non-finite values.
Results may differ from a plain program's by a relative error of at most 0.023.
Values may be sent and summed in bfloat16 or wider, within the bound.
No kernel may reach another device: no remote copies, remote signals or barrier semaphores. Data moves between devices by JAX's collectives and lax.ppermute only.
A program may use at most 512 MiB of HBM per device.

v0:
```python
import math

import jax
import jax.numpy as jnp
from jax import lax
from jax.sharding import PartitionSpec as P

HDIM = 64
SPAN = 256


EPS = 1e-05
THETA = 10000.0
BRANCH = 1.4 / math.sqrt(40.0)


def norm_rows(values, gain):
    return values * lax.rsqrt(jnp.mean(values * values, axis=-1, keepdims=True) + EPS) * gain


def rotate(values, positions):
    rows = values.shape[0]
    heads = values.shape[1] // HDIM
    half = HDIM // 2
    exponent = jnp.arange(half, dtype=jnp.float32) * (-2.0 / HDIM)
    frequency = jnp.exp(exponent * math.log(THETA))
    angle = positions.astype(jnp.float32)[:, None] * frequency[None, :]
    cosine = jnp.concatenate([jnp.cos(angle), jnp.cos(angle)], axis=1)[:, None, :]
    sine = jnp.concatenate([jnp.sin(angle), jnp.sin(angle)], axis=1)[:, None, :]
    split = values.reshape(rows, heads, HDIM)
    turned = jnp.concatenate([-split[..., half:], split[..., :half]], axis=-1)
    return (split * cosine + turned * sine).reshape(rows, heads * HDIM)


def span_label(positions, starts):
    label = jnp.full(positions.shape, -1, jnp.int32)
    for number in range(starts.shape[0]):
        inside = (positions >= starts[number]) & (positions < starts[number] + SPAN)
        label = jnp.where(inside, jnp.int32(number), label)
    return label


def visible_pairs(rows, columns, starts):
    row_label = span_label(rows, starts)[:, None]
    column_label = span_label(columns, starts)[None, :]
    causal = columns[None, :] <= rows[:, None]
    return causal | (row_label == column_label) & (row_label >= 0)


def rounded_amount(values):
    return lax.optimization_barrier(values.astype(jnp.bfloat16)).astype(jnp.float32)


def heads_of(values):
    return values.reshape(values.shape[0], values.shape[1] // HDIM, HDIM)


def attention_scores(queries, keys, visible):
    raw = jnp.einsum(
        "qhd,khd->hqk", heads_of(queries), heads_of(keys), preferred_element_type=jnp.float32
    )
    return jnp.where(visible[None], raw * (1.0 / math.sqrt(HDIM)), -1e30)


def shards(
    tokens,
    cotangent,
    sequence_adapter_index,
    image_span_start,
    attention_norm_gain,
    feedforward_norm_gain,
    query_key_value_weight,
    attention_output_weight,
    gate_up_projection_weight,
    down_projection_weight,
    adapter_model_input_maps,
    adapter_model_output_maps,
    adapter_hidden_input_map,
    adapter_hidden_output_maps,
):
    local_rows = tokens.shape[1]
    width = tokens.shape[2]
    group = lax.axis_size("shard")
    place = lax.axis_index("shard")
    pick = sequence_adapter_index[0]
    starts = image_span_start[0]
    positions_local = place * local_rows + jnp.arange(local_rows, dtype=jnp.int32)
    positions_all = jnp.arange(local_rows * group, dtype=jnp.int32)
    visible = visible_pairs(positions_local, positions_all, starts)
    residual_in = tokens[0].astype(jnp.float32)
    gain_one = attention_norm_gain.astype(jnp.float32)
    gain_two = feedforward_norm_gain.astype(jnp.float32)
    a_model_all, b_model_all, a_hidden_all, b_hidden_all = (
        lax.all_gather(adapter_model_input_maps, "shard", axis=1, tiled=True),
        lax.all_gather(adapter_model_output_maps, "shard", axis=1, tiled=True),
        lax.all_gather(adapter_hidden_input_map[None], "shard", axis=1, tiled=True),
        lax.all_gather(adapter_hidden_output_maps, "shard", axis=1, tiled=True),
    )
    a_one = lax.dynamic_index_in_dim(a_model_all, pick, 1, keepdims=False)
    b_one = lax.dynamic_index_in_dim(b_model_all, pick, 1, keepdims=False)
    single_hidden_input_map = lax.dynamic_index_in_dim(a_hidden_all, pick, 1, keepdims=False)[0]
    b_hidden_one = lax.dynamic_index_in_dim(b_hidden_all, pick, 1, keepdims=False)
    normed = norm_rows(residual_in, gain_one).astype(jnp.bfloat16)
    empty = jnp.zeros((local_rows, width), jnp.float32)
    pieces = lax.all_gather(query_key_value_weight, "shard", axis=1, tiled=True)
    columns = normed
    base_query, base_key, base_value = tuple(
        (jnp.dot(columns, pieces[slot], preferred_element_type=jnp.float32) for slot in range(3))
    )
    narrow_first = jnp.einsum(
        "td,srd->str", normed, a_one[0:3], preferred_element_type=jnp.float32
    ).astype(jnp.bfloat16)
    lifted_first = jnp.einsum(
        "str,srd->std", narrow_first, b_one[0:3], preferred_element_type=jnp.float32
    )
    query = base_query + lifted_first[0]
    key_pre = base_key + lifted_first[1]
    value_low = (base_value + lifted_first[2]).astype(jnp.bfloat16)
    query_turned = rotate(query, positions_local).astype(jnp.bfloat16)
    key_turned = rotate(key_pre, positions_local).astype(jnp.bfloat16)
    keys_all, values_all = (
        lax.all_gather(key_turned, "shard", axis=0, tiled=True),
        lax.all_gather(value_low, "shard", axis=0, tiled=True),
    )
    scores = attention_scores(query_turned, keys_all, visible)
    top = jnp.max(scores, axis=-1, keepdims=True)
    weights = jnp.exp(scores - top)
    total = jnp.sum(weights, axis=-1, keepdims=True)
    log_total = top + jnp.log(total)
    probs = weights / total
    mixed = jnp.einsum(
        "hqk,khd->qhd",
        probs.astype(jnp.bfloat16),
        heads_of(values_all),
        preferred_element_type=jnp.float32,
    )
    mixed_low = mixed.reshape(local_rows, width).astype(jnp.bfloat16)
    columns = mixed_low
    base_out = jnp.dot(
        columns,
        lax.all_gather(attention_output_weight, "shard", axis=0, tiled=True),
        preferred_element_type=jnp.float32,
    )
    narrow_out = jnp.einsum(
        "td,rd->tr", mixed_low, a_one[3], preferred_element_type=jnp.float32
    ).astype(jnp.bfloat16)
    branch = base_out + jnp.dot(narrow_out, b_one[3], preferred_element_type=jnp.float32)
    middle = residual_in + BRANCH * branch
    normed_second = norm_rows(middle, gain_two).astype(jnp.bfloat16)
    narrow_mlp = jnp.einsum(
        "td,srd->str", normed_second, a_one[4:6], preferred_element_type=jnp.float32
    ).astype(jnp.bfloat16)
    lifted_mlp = jnp.einsum(
        "str,srf->stf", narrow_mlp, b_hidden_one, preferred_element_type=jnp.float32
    )
    columns = normed_second
    base_gate_up = jnp.einsum(
        "tr,srf->stf",
        columns,
        lax.all_gather(gate_up_projection_weight, "shard", axis=1, tiled=True),
        preferred_element_type=jnp.float32,
    )
    gate = base_gate_up[0] + lifted_mlp[0]
    up = base_gate_up[1] + lifted_mlp[1]
    hidden_low = (jax.nn.silu(gate) * up).astype(jnp.bfloat16)
    narrow_down = jnp.einsum(
        "tf,rf->tr", hidden_low, single_hidden_input_map, preferred_element_type=jnp.float32
    ).astype(jnp.bfloat16)
    columns = hidden_low
    base_down = jnp.dot(
        columns,
        lax.all_gather(down_projection_weight, "shard", axis=0, tiled=True),
        preferred_element_type=jnp.float32,
    )
    feed = base_down + jnp.dot(narrow_down, b_one[4], preferred_element_type=jnp.float32)
    output = (middle + BRANCH * feed).astype(jnp.bfloat16)
    grad_out = cotangent[0].astype(jnp.float32)
    grad_feed = (BRANCH * grad_out).astype(jnp.bfloat16)
    grad_b_down = jnp.einsum(
        "tr,td->rd", narrow_down, grad_feed, preferred_element_type=jnp.float32
    )
    down_lowrank_gradient = jnp.einsum(
        "td,rd->tr", grad_feed, b_one[4], preferred_element_type=jnp.float32
    ).astype(jnp.bfloat16)
    grad_a_down = jnp.einsum(
        "tr,tf->rf", down_lowrank_gradient, hidden_low, preferred_element_type=jnp.float32
    )
    adapter_hidden_output = jnp.dot(
        down_lowrank_gradient, single_hidden_input_map, preferred_element_type=jnp.float32
    )
    frozen_hidden_output = jnp.einsum(
        "td,rd->tr",
        grad_feed,
        lax.all_gather(down_projection_weight, "shard", axis=0, tiled=True),
        preferred_element_type=jnp.float32,
    )
    hidden_gradient = rounded_amount(frozen_hidden_output + adapter_hidden_output)
    _, silu_back = jax.vjp(lambda gate_in, up_in: jax.nn.silu(gate_in) * up_in, gate, up)
    grad_gate, grad_up = silu_back(hidden_gradient)
    stacked_mlp = jnp.stack([grad_gate.astype(jnp.bfloat16), grad_up.astype(jnp.bfloat16)])
    grad_b_mlp = jnp.einsum(
        "str,stf->srf", narrow_mlp, stacked_mlp, preferred_element_type=jnp.float32
    )
    grad_narrow_mlp = jnp.einsum(
        "stf,srf->str", stacked_mlp, b_hidden_one, preferred_element_type=jnp.float32
    ).astype(jnp.bfloat16)
    grad_a_mlp = jnp.einsum(
        "str,td->srd", grad_narrow_mlp, normed_second, preferred_element_type=jnp.float32
    )
    adapter_second_output = jnp.einsum(
        "str,srd->td", grad_narrow_mlp, a_one[4:6], preferred_element_type=jnp.float32
    )
    frozen_second_output = jnp.einsum(
        "stf,srf->tr",
        stacked_mlp,
        lax.all_gather(gate_up_projection_weight, "shard", axis=1, tiled=True),
        preferred_element_type=jnp.float32,
    )
    second_normed_gradient = frozen_second_output + adapter_second_output
    _, norm_back_second = jax.vjp(lambda values: norm_rows(values, gain_two), middle)
    grad_middle = grad_out + norm_back_second(second_normed_gradient)[0]
    grad_branch = (BRANCH * grad_middle).astype(jnp.bfloat16)
    grad_b_out = jnp.einsum(
        "tr,td->rd", narrow_out, grad_branch, preferred_element_type=jnp.float32
    )
    grad_narrow_out = jnp.einsum(
        "td,rd->tr", grad_branch, b_one[3], preferred_element_type=jnp.float32
    ).astype(jnp.bfloat16)
    grad_a_out = jnp.einsum(
        "tr,td->rd", grad_narrow_out, mixed_low, preferred_element_type=jnp.float32
    )
    base_mixed = jnp.einsum(
        "td,rd->tr",
        grad_branch,
        lax.all_gather(attention_output_weight, "shard", axis=0, tiled=True),
        preferred_element_type=jnp.float32,
    )
    grad_mixed = (
        base_mixed + jnp.dot(grad_narrow_out, a_one[3], preferred_element_type=jnp.float32)
    ).astype(jnp.bfloat16)
    probs_again = jnp.exp(attention_scores(query_turned, keys_all, visible) - log_total)
    grad_mixed_heads = heads_of(grad_mixed)
    grad_probs = jnp.einsum(
        "qhd,khd->hqk", grad_mixed_heads, heads_of(values_all), preferred_element_type=jnp.float32
    )
    inner = jnp.sum(grad_probs * probs_again, axis=-1, keepdims=True)
    grad_scores = (probs_again * (grad_probs - inner)).astype(jnp.bfloat16)
    scale = 1.0 / math.sqrt(HDIM)
    grad_query_turned = (
        jnp.einsum(
            "hqk,khd->qhd", grad_scores, heads_of(keys_all), preferred_element_type=jnp.float32
        ).reshape(local_rows, width)
        * scale
    )
    key_terms = (
        jnp.einsum(
            "hqk,qhd->khd", grad_scores, heads_of(query_turned), preferred_element_type=jnp.float32
        ).reshape(keys_all.shape[0], width)
        * scale
    )
    value_terms = jnp.einsum(
        "hqk,qhd->khd",
        probs_again.astype(jnp.bfloat16),
        grad_mixed_heads,
        preferred_element_type=jnp.float32,
    ).reshape(keys_all.shape[0], width)
    grad_key_turned, grad_value = (
        lax.psum_scatter(
            key_terms.astype(jnp.bfloat16), "shard", scatter_dimension=0, tiled=True
        ).astype(jnp.float32),
        lax.psum_scatter(
            value_terms.astype(jnp.bfloat16), "shard", scatter_dimension=0, tiled=True
        ).astype(jnp.float32),
    )
    _, turn_back = jax.vjp(lambda values: rotate(values, positions_local), empty)
    stacked_first = jnp.stack(
        [
            turn_back(grad_query_turned)[0].astype(jnp.bfloat16),
            turn_back(grad_key_turned)[0].astype(jnp.bfloat16),
            grad_value.astype(jnp.bfloat16),
        ]
    )
    grad_b_first = jnp.einsum(
        "str,std->srd", narrow_first, stacked_first, preferred_element_type=jnp.float32
    )
    grad_narrow_first = jnp.einsum(
        "std,srd->str", stacked_first, b_one[0:3], preferred_element_type=jnp.float32
    ).astype(jnp.bfloat16)
    grad_a_first = jnp.einsum(
        "str,td->srd", grad_narrow_first, normed, preferred_element_type=jnp.float32
    )
    base_normed = jnp.einsum(
        "std,srd->tr",
        stacked_first,
        lax.all_gather(query_key_value_weight, "shard", axis=1, tiled=True),
        preferred_element_type=jnp.float32,
    )
    grad_normed = base_normed + jnp.einsum(
        "str,srd->td", grad_narrow_first, a_one[0:3], preferred_element_type=jnp.float32
    )
    _, norm_back_first = jax.vjp(lambda values: norm_rows(values, gain_one), residual_in)
    input_grad = grad_middle + norm_back_first(grad_normed)[0]
    grad_a_model_one = jnp.concatenate([grad_a_first, grad_a_out[None], grad_a_mlp], axis=0)
    grad_b_model_one = jnp.concatenate([grad_b_first, grad_b_out[None], grad_b_down[None]], axis=0)
    per_processor_share = adapter_model_input_maps.shape[1]
    adapters_total = per_processor_share * group
    chosen = (jnp.arange(adapters_total, dtype=jnp.int32) == pick).astype(jnp.float32)[
        None, :, None, None
    ]
    spread_a_model = grad_a_model_one[:, None] * chosen
    spread_b_model = grad_b_model_one[:, None] * chosen
    spread_a_hidden = grad_a_down[None, None] * chosen
    spread_b_hidden = grad_b_mlp[:, None] * chosen
    owned = (
        lax.psum_scatter(
            spread_a_model.astype(jnp.bfloat16), "shard", scatter_dimension=1, tiled=True
        ).astype(jnp.float32),
        lax.psum_scatter(
            spread_b_model.astype(jnp.bfloat16), "shard", scatter_dimension=1, tiled=True
        ).astype(jnp.float32),
        lax.psum_scatter(
            spread_a_hidden.astype(jnp.bfloat16), "shard", scatter_dimension=1, tiled=True
        ).astype(jnp.float32),
        lax.psum_scatter(
            spread_b_hidden.astype(jnp.bfloat16), "shard", scatter_dimension=1, tiled=True
        ).astype(jnp.float32),
    )
    summed = (
        lax.psum(owned[0].astype(jnp.bfloat16), "rep").astype(jnp.float32),
        lax.psum(owned[1].astype(jnp.bfloat16), "rep").astype(jnp.float32),
        lax.psum(owned[2].astype(jnp.bfloat16), "rep").astype(jnp.float32),
        lax.psum(owned[3].astype(jnp.bfloat16), "rep").astype(jnp.float32),
    )
    return (output[None], input_grad[None], summed[0], summed[1], summed[2][0], summed[3])


def solution(mesh):
    in_specs = (
        P("rep", "shard", None),
        P("rep", "shard", None),
        P("rep"),
        P("rep", None),
        P(),
        P(),
        P(None, "shard", None),
        P("shard", None),
        P(None, "shard", None),
        P("shard", None),
        P(None, "shard", None, None),
        P(None, "shard", None, None),
        P("shard", None, None),
        P(None, "shard", None, None),
    )
    out_specs = (
        P("rep", "shard", None),
        P("rep", "shard", None),
        P(None, "shard", None, None),
        P(None, "shard", None, None),
        P("shard", None, None),
        P(None, "shard", None, None),
    )
    return jax.shard_map(shards, mesh=mesh, in_specs=in_specs, out_specs=out_specs, check_vma=False)
```

profile of v0, /device:TPU:0, one launch (start us, length us, event | category | flops | bytes accessed | tf_op | source)
XLA Modules:
  0.0 1554.7 jit_solution(16283073855144799213)
XLA Ops:
  14.0 29.6 %all-gather.14.cloned.1.call-done = bf16[6,8,16,2304]{3,2,0,1:T(8,128)(2,1)} async-done(((bf16[6,2,16,2304]{3,2,0,1:T(8,128)(2,1)}), bf16[6,8,16,2304]{3,2,0,1:T(8,128)(2,1)}) %all-gather.14.cloned.1.call-update) | async-done | bytes 3538960 | tf_op jit(solution)/shard_map/all_gather | solution.py:94
  45.1 28.1 %all-gather.16.cloned.1.call-done = bf16[5,8,16,2304]{3,2,0,1:T(8,128)(2,1)} async-done(((bf16[5,2,16,2304]{3,2,0,1:T(8,128)(2,1)}), bf16[5,8,16,2304]{3,2,0,1:T(8,128)(2,1)}) %all-gather.16.cloned.1.call-update) | async-done | bytes 2949136 | tf_op jit(solution)/shard_map/all_gather | solution.py:95
  73.2 4.9 fusion.100
  78.2 188.6 %all-gather.12.cloned.1.call-done = bf16[3,2304,2304]{2,1,0:T(8,128)(2,1)} async-done(((bf16[3,576,2304]{2,1,0:T(8,128)(2,1)}), bf16[3,2304,2304]{2,1,0:T(8,128)(2,1)}) %all-gather.12.cloned.1.call-update) | async-done | bytes 31850512 | tf_op jit(solution)/shard_map/all_gather | solution.py:105
  266.8 8.7 fusion.30
  281.0 11.8 fusion.24
  292.8 3.2 copy.54
  295.9 9.0 fusion.25
  305.0 3.2 copy.58
  308.2 3.0 slice_negate_fusion.2
  313.9 3.1 copy.59
  317.0 3.0 copy.55
  320.0 6.1 add_convert_fusion
  334.8 95.9 %all-gather.28.cloned.1.call-done = bf16[5760,2304]{1,0:T(8,128)(2,1)} async-done(((bf16[1440,2304]{1,0:T(8,128)(2,1)}), bf16[5760,2304]{1,0:T(8,128)(2,1)}) %all-gather.28.cloned.1.call-update) | async-done | bytes 26542096 | tf_op jit(solution)/shard_map/all_gather | solution.py:172
  430.7 15.2 fusion.93
  445.9 5.3 all-gather.30.cloned.1.call-done
  451.2 5.3 fusion.10
  457.2 33.5 %all-gather.18.cloned.1.call-done = bf16[1024,2304]{1,0:T(8,128)(2,1)} async-done(((bf16[256,2304]{1,0:T(8,128)(2,1)}), bf16[1024,2304]{1,0:T(8,128)(2,1)}) %all-gather.18.cloned.1.call-update) | async-done | bytes 4718608 | tf_op jit(solution)/shard_map/all_gather | solution.py:123
  490.7 6.6 copy.52
  497.3 33.0 %all-gather.20.cloned.1.call-done = bf16[1024,2304]{1,0:T(8,128)(2,1)} async-done(((bf16[256,2304]{1,0:T(8,128)(2,1)}), bf16[1024,2304]{1,0:T(8,128)(2,1)}) %all-gather.20.cloned.1.call-update) | async-done | bytes 4718608 | tf_op jit(solution)/shard_map/all_gather | solution.py:122
  530.3 6.6 copy.60
  536.9 19.5 %fusion.6 = (f32[36,256]{1,0:T(8,128)S(1)}, f32[36,256,1024]{2,1,0:T(8,128)}) fusion(pred[256,1024]{1,0:T(8,128)(4,1)S(1)} %fusion.91, bf16[256,36,64]{0,2,1:T(8,128)(2,1)S(1)} %bitcast.303, bf16[1024,36,64]{0,2,1:T(8,128)(2,1)} %bitcast.298), kind=kOutput, calls=%fused_computation.11 | convolution fusion | flops 1236261888 | bytes 43945984 | tf_op jit(solution)/shard_map/qhd,khd->hqk/dot_general | solution.py:59
  556.4 17.6 %fusion = f32[36,256]{1,0:T(8,128)S(1)} fusion(f32[36,256]{1,0:T(8,128)S(1)} %get-tuple-element.39, f32[36,256,1024]{2,1,0:T(8,128)} %get-tuple-element.40, pred[256,1024]{1,0:T(8,128)(4,1)S(1)} %fusion.91), kind=kLoop, calls=%fused_computation.6 | loop fusion | flops 37739520 | bytes 38084608 | tf_op jit(solution)/shard_map/reduce_sum | solution.py:128
  574.0 15.9 %fusion.65 = bf16[36,64,256]{2,1,0:T(8,128)(2,1)S(1)} fusion(bf16[1024,36,64]{0,2,1:T(8,128)(2,1)S(1)} %bitcast.301, f32[36,256]{1,0:T(8,128)S(1)} %fusion, f32[36,256]{1,0:T(8,128)S(1)} %get-tuple-element.39, f32[36,256,1024]{2,1,0:T(8,128)} %get-tuple-element.40, pred[256,1024]{1,0:T(8,128)(4,1)S(1)} %fusion.91), kind=kOutput, calls=%fused_computation.121 | convolution fusion | flops 1255735296 | bytes 43982848 | tf_op jit(solution)/shard_map/hqk,khd->qhd/dot_general | solution.py:131
  591.8 11.1 all-gather.22.cloned.1.call-done
  602.9 6.2 fusion.146
  614.0 17.9 %all-gather.26.cloned.1.call-done = bf16[2,8,16,5760]{3,2,1,0:T(8,128)(2,1)} async-done(((bf16[2,2,16,5760]{3,2,1,0:T(8,128)(2,1)}), bf16[2,8,16,5760]{3,2,1,0:T(8,128)(2,1)}) %all-gather.26.cloned.1.call-update) | async-done | bytes 2949136 | tf_op jit(solution)/shard_map/all_gather | solution.py:97
  631.9 7.1 fusion.96
  638.9 308.1 %all-gather.24.cloned.1.call-done = bf16[2,2304,5760]{2,1,0:T(8,128)(2,1)} async-done(((bf16[2,576,5760]{2,1,0:T(8,128)(2,1)}), bf16[2,2304,5760]{2,1,0:T(8,128)(2,1)}) %all-gather.24.cloned.1.call-update) | async-done | bytes 53084176 | tf_op jit(solution)/shard_map/all_gather | solution.py:160
  947.0 26.5 %convolution_bitcast_fusion = f32[2,256,5760]{2,1,0:T(8,128)} fusion(bf16[256,2304,1]{1,0,2:T(8,128)(2,1)S(1)} %fusion.66, bf16[2,2304,5760]{2,1,0:T(8,128)(2,1)} %all-gather.24.cloned.1.call-done), kind=kOutput, calls=%fused_computation.18 | convolution fusion | flops 13589544960 | bytes 66060288 | tf_op jit(solution)/shard_map/tr,srf->stf/dot_general | solution.py:157
  973.5 13.2 fusion.43
  987.9 7.3 fusion.34
  995.1 24.2 %convolution_bitcast_fusion.2 = f32[256,2304]{1,0:T(8,128)} fusion(bf16[2,2304,5760]{2,1,0:T(8,128)(2,1)} %all-gather.24.cloned.1.call-done, bf16[1,256,5760]{2,1,0:T(8,128)(2,1)} %get-tuple-element.17, bf16[1,256,5760]{2,1,0:T(8,128)(2,1)} %get-tuple-element.13), kind=kOutput, calls=%fused_computation.55 | convolution fusion | flops 13592494080 | bytes 61341696 | tf_op jit(solution)/shard_map/stf,srf->tr/dot_general | solution.py:213
  1019.4 3.7 fusion.84
  1027.2 3.0 fusion.137
  1033.6 29.5 %multiply_reduce_fusion = (f32[36,256]{1,0:T(8,128)S(1)}, f32[36,256,1024]{2,1,0:T(8,128)}) fusion(f32[36,256]{1,0:T(8,128)S(1)} %copy-done.34, f32[36,256,1024]{2,1,0:T(8,128)} %get-tuple-element.40, pred[256,1024]{1,0:T(8,128)(4,1)S(1)} %copy-done.18, bf16[256,36,64]{0,2,1:T(8,128)(2,1)S(1)} %bitcast.315, bf16[1024,36,64]{0,2,1:T(8,128)(2,1)} %bitcast.300), kind=kOutput, calls=%fused_computation.1 | convolution fusion | flops 1255136256 | bytes 81731584 | tf_op jit(solution)/shard_map/qhd,khd->hqk/dot_general | solution.py:243
  1063.0 31.4 %multiply_convert_fusion = bf16[36,256,1024]{2,1,0:T(8,128)(2,1)} fusion(f32[36,256,1024]{2,1,0:T(8,128)} %get-tuple-element.46, f32[36,256]{1,0:T(8,128)S(1)} %get-tuple-element.45, f32[36,256]{1,0:T(8,128)S(1)} %copy-done.34, f32[36,256,1024]{2,1,0:T(8,128)} %get-tuple-element.40, pred[256,1024]{1,0:T(8,128)(4,1)S(1)} %copy-done.18), kind=kLoop, calls=%fused_computation | loop fusion | flops 56623104 | bytes 94707712 | tf_op jit(solution)/shard_map/convert_element_type | solution.py:247
  1094.4 12.0 multiply_convert_fusion.1
  1106.5 21.0 %fusion.44 = bf16[36,64,1024]{2,1,0:T(8,128)(2,1)} fusion(bf16[256,36,64]{0,2,1:T(8,128)(2,1)S(1)} %bitcast.316, f32[36,256]{1,0:T(8,128)S(1)} %copy-done.34, f32[36,256,1024]{2,1,0:T(8,128)} %get-tuple-element.40, pred[256,1024]{1,0:T(8,128)(4,1)S(1)} %copy-done.18), kind=kOutput, calls=%fused_computation.89 | convolution fusion | flops 1248067584 | bytes 43945984 | tf_op jit(solution)/shard_map/hqk,qhd->khd/dot_general | solution.py:261
  1127.5 6.7 copy.62
  1135.0 11.1 bitcast_multiply_fusion.3
  1150.0 7.9 fusion.88
  1168.8 36.0 %reduce-scatter.15.cloned.1.call-done = bf16[256,2304]{1,0:T(8,128)(2,1)} async-done(((bf16[1024,2304]{1,0:T(8,128)(2,1)}), bf16[256,2304]{1,0:T(8,128)(2,1)}) %reduce-scatter.15.cloned.1.call-update) | async-done | bytes 1179664 | tf_op jit(solution)/shard_map/reduce_scatter | solution.py:271
  1220.5 13.7 fusion.147
  1236.7 148.9 %all-reduce.14.cloned.1.call-done = (bf16[6,8,16,2304]{3,2,1,0:T(8,128)(2,1)}, bf16[5,8,16,2304]{3,2,1,0:T(8,128)(2,1)}, bf16[2,8,16,5760]{3,2,1,0:T(8,128)(2,1)}) async-done(((bf16[6,8,16,2304]{3,2,1,0:T(8,128)(2,1)}, bf16[5,8,16,2304]{3,2,1,0:T(8,128)(2,1)}, bf16[2,8,16,5760]{3,2,1,0:T(8,128)(2,1)}), (bf16[6,8,16,2304]{3,2,1,0:T(8,128)(2,1)}, bf16[5,8,16,2304]{3,2,1,0:T(8,128)(2,1)}, ...) | async-done | bytes 9437200
  1391.9 24.4 %reduce-scatter.17.cloned.1.call-done = bf16[1,2,16,5760]{3,2,1,0:T(8,128)(2,1)} async-done(((bf16[1,8,16,5760]{3,2,1,0:T(8,128)(2,1)}), bf16[1,2,16,5760]{3,2,1,0:T(8,128)(2,1)}) %reduce-scatter.17.cloned.1.call-update) | async-done | bytes 368656 | tf_op jit(solution)/shard_map/reduce_scatter | solution.py:321
  1416.4 15.4 convolution_bitcast_fusion.1
  1435.6 105.1 %all-reduce.12.cloned.1.call-done = (bf16[6,2,16,2304]{3,2,1,0:T(8,128)(2,1)}, bf16[5,2,16,2304]{3,2,1,0:T(8,128)(2,1)}, bf16[2,16,5760]{2,1,0:T(8,128)(2,1)}, bf16[2,2,16,5760]{3,2,1,0:T(8,128)(2,1)}) async-done(((bf16[6,2,16,2304]{3,2,1,0:T(8,128)(2,1)}, bf16[5,2,16,2304]{3,2,1,0:T(8,128)(2,1)}, bf16[2,16,5760]{2,1,0:T(8,128)(2,1)}, bf16[2,2,16,5760]{3,2,1,0:T(8,128)(2,1)}), ...) | async-done | bytes 2727952 | tf_op jit(solution)/shard_map/psum | solution.py:329
  (254 shorter events, 88.8 us)
Async XLA Ops:
  7.2 36.5 %all-gather.14.cloned.1.call-start = ((), (), s32[]{:S(2)}) async-start(), calls=%async_computation.4 | async-start | bytes 4423680 | tf_op jit(solution)/shard_map/all_gather | solution.py:94
  9.4 63.8 %all-gather.16.cloned.1.call-start = ((), (), s32[]{:S(2)}) async-start(), calls=%async_computation.5 | async-start | bytes 3686400 | tf_op jit(solution)/shard_map/all_gather | solution.py:95
  10.4 256.3 %all-gather.12.cloned.1.call-start = ((), (), s32[]{:S(2)}) async-start(), calls=%async_computation.3 | async-start | bytes 39813120 | tf_op jit(solution)/shard_map/all_gather | solution.py:105
  11.2 419.5 %all-gather.28.cloned.1.call-start = ((), (), s32[]{:S(2)}) async-start(), calls=%async_computation.11 | async-start | bytes 33177600 | tf_op jit(solution)/shard_map/all_gather | solution.py:172
  11.8 439.4 %all-gather.30.cloned.1.call-start = ((), (), s32[]{:S(2)}) async-start(), calls=%async_computation.15 | async-start | bytes 1843200 | tf_op jit(solution)/shard_map/all_gather | solution.py:96
  12.4 478.3 %all-gather.18.cloned.1.call-start = ((), (), s32[]{:S(2)}) async-start(), calls=%async_computation.6 | async-start | bytes 5898240 | tf_op jit(solution)/shard_map/all_gather | solution.py:123
  13.1 282.9 %copy-start.53 = (f32[2304]{0:T(1024)}, f32[2304]{0:T(1024)S(1)}, u32[]{:S(2)}) copy-start(f32[2304]{0:T(1024)S(1)} %convert_element_type.235) | copy-start | bytes 27652
  14.0 281.9 %copy-start.68 = (f32[256]{0:T(256)}, f32[256]{0:T(256)S(1)}, u32[]{:S(2)}) copy-start(f32[256]{0:T(256)S(1)} %fusion.123) | copy-start | bytes 3076
  45.1 33.1 %copy-start.61 = (bf16[3,16,256]{2,1,0:T(8,128)(2,1)}, bf16[3,16,256]{2,1,0:T(8,128)(2,1)S(1)}, u32[]{:S(2)}) copy-start(bf16[3,16,256]{2,1,0:T(8,128)(2,1)S(1)} %fusion.81) | copy-start | bytes 73732
  275.5 254.9 %all-gather.20.cloned.1.call-start = ((), (), s32[]{:S(2)}) async-start(), calls=%async_computation.7 | async-start | bytes 5898240 | tf_op jit(solution)/shard_map/all_gather | solution.py:122
  326.1 276.7 %all-gather.22.cloned.1.call-start = ((), (), s32[]{:S(2)}) async-start(), calls=%async_computation.8 | async-start | bytes 13271040 | tf_op jit(solution)/shard_map/all_gather | solution.py:141
  326.9 305.0 %all-gather.26.cloned.1.call-start = ((), (), s32[]{:S(2)}) async-start(), calls=%async_computation.10 | async-start | bytes 3686400 | tf_op jit(solution)/shard_map/all_gather | solution.py:97
  327.7 5.7 copy-start.19
  327.7 619.3 %all-gather.24.cloned.1.call-start = ((), (), s32[]{:S(2)}) async-start(), calls=%async_computation.9 | async-start | bytes 66355200 | tf_op jit(solution)/shard_map/all_gather | solution.py:160
  328.3 836.1 %reduce-scatter.13.cloned.1.call-start = ((), (), s32[]{:S(2)}) async-start(), calls=%async_computation.12 | async-start | bytes 5898240 | tf_op jit(solution)/shard_map/reduce_scatter | solution.py:268
  333.4 240.6 %copy-start.17 = (pred[256,1024]{1,0:T(8,128)(4,1)}, pred[256,1024]{1,0:T(8,128)(4,1)S(1)}, u32[]{:S(2)}) copy-start(pred[256,1024]{1,0:T(8,128)(4,1)S(1)} %fusion.91) | copy-start | bytes 786436
  334.8 116.4 %copy-start.55 = (bf16[256,16]{0,1:T(8,128)(2,1)}, bf16[256,16]{0,1:T(8,128)(2,1)S(1)}, u32[]{:S(2)}) copy-start(bf16[256,16]{0,1:T(8,128)(2,1)S(1)} %fusion.85) | copy-start | bytes 24580
  445.9 10.7 copy-start.22
  457.2 79.8 %copy-start.8 = (bf16[256,2304]{0,1:T(8,128)(2,1)}, bf16[256,2304]{0,1:T(8,128)(2,1)S(1)}, u32[]{:S(2)}) copy-start(bf16[256,2304]{0,1:T(8,128)(2,1)S(1)} %copy.56) | copy-start | bytes 3538948
  556.4 17.6 %copy-start.43 = (f32[36,256]{1,0:T(8,128)}, f32[36,256]{1,0:T(8,128)S(1)}, u32[]{:S(2)}) copy-start(f32[36,256]{1,0:T(8,128)S(1)} %get-tuple-element.39) | copy-start | bytes 110596
  556.4 17.6 %copy-start.6 = (bf16[1024,2304]{0,1:T(8,128)(2,1)S(1)}, bf16[1024,2304]{0,1:T(8,128)(2,1)}, u32[]{:S(2)}) copy-start(bf16[1024,2304]{0,1:T(8,128)(2,1)} %copy.52) | copy-start | bytes 14155780
  574.0 15.9 %copy-start.46 = (f32[36,256]{1,0:T(8,128)}, f32[36,256]{1,0:T(8,128)S(1)}, u32[]{:S(2)}) copy-start(f32[36,256]{1,0:T(8,128)S(1)} %fusion) | copy-start | bytes 110596
  589.9 12.9 copy-start.15
  591.8 17.3 %copy-start.11 = (bf16[1,256,2304]{2,1,0:T(8,128)(2,1)S(1)}, bf16[1,256,2304]{2,1,0:T(8,128)(2,1)}, u32[]{:S(2)}) copy-start(bf16[1,256,2304]{2,1,0:T(8,128)(2,1)} %param.14) | copy-start | bytes 3538948
  602.9 6.2 copy-start.48
  610.7 414.8 %copy-start.1 = (f32[256,2304]{1,0:T(8,128)}, f32[256,2304]{1,0:T(8,128)S(1)}, u32[]{:S(2)}) copy-start(f32[256,2304]{1,0:T(8,128)S(1)} %get-tuple-element.42) | copy-start | bytes 7077892
  611.8 335.2 %copy-start.13 = (bf16[256,2304,1]{1,0,2:T(8,128)(2,1)}, bf16[256,2304,1]{1,0,2:T(8,128)(2,1)S(1)}, u32[]{:S(2)}) copy-start(bf16[256,2304,1]{1,0,2:T(8,128)(2,1)S(1)} %fusion.66) | copy-start | bytes 3538948
  947.0 26.5 %copy-start.7 = (bf16[256,5760]{1,0:T(8,128)(2,1)S(1)}, bf16[256,5760]{1,0:T(8,128)(2,1)}, u32[]{:S(2)}) copy-start(bf16[256,5760]{1,0:T(8,128)(2,1)} %fusion.10) | copy-start | bytes 8847364
  973.5 14.3 copy-start
  995.1 24.2 %copy-start.24 = (bf16[1,256,5760]{2,1,0:T(8,128)(2,1)S(1)}, bf16[1,256,5760]{2,1,0:T(8,128)(2,1)}, u32[]{:S(2)}) copy-start(bf16[1,256,5760]{2,1,0:T(8,128)(2,1)} %get-tuple-element.17) | copy-start | bytes 8847364
  1019.3 6.8 slice-start
  1019.3 6.8 slice-start.1
  1063.0 31.4 %copy-start.9 = (bf16[256,2304]{0,1:T(8,128)(2,1)S(1)}, bf16[256,2304]{0,1:T(8,128)(2,1)}, u32[]{:S(2)}) copy-start(bf16[256,2304]{0,1:T(8,128)(2,1)} %copy-done.8) | copy-start | bytes 3538948
  1106.4 98.4 %reduce-scatter.15.cloned.1.call-start = ((), (), s32[]{:S(2)}) async-start(), calls=%async_computation.13 | async-start | bytes 5898240 | tf_op jit(solution)/shard_map/reduce_scatter | solution.py:271
  1134.2 251.4 %all-reduce.14.cloned.1.call-start = ((), (), s32[]{:S(2)}) async-start(), calls=%async_computation.17 | async-start | bytes 18874368
  1148.9 56.0 %copy-start.27 = (bf16[1,256,2304]{2,1,0:T(8,128)(2,1)}, bf16[1,256,2304]{2,1,0:T(8,128)(2,1)S(1)}, u32[]{:S(2)}) copy-start(bf16[1,256,2304]{2,1,0:T(8,128)(2,1)S(1)} %copy.63) | copy-start | bytes 3538948
  1150.0 8.0 copy-start.21
  1150.0 9.0 copy-start.4
  1150.0 9.0 copy-start.49
  1150.0 10.0 copy-start.52
  1150.0 11.0 copy-start.26
  1168.8 38.1 %copy-start.29 = (bf16[1,256,2304]{2,1,0:T(8,128)(2,1)}, bf16[1,256,2304]{2,1,0:T(8,128)(2,1)S(1)}, u32[]{:S(2)}) copy-start(bf16[1,256,2304]{2,1,0:T(8,128)(2,1)S(1)} %copy.64) | copy-start | bytes 3538948
  1214.9 201.5 %reduce-scatter.17.cloned.1.call-start = ((), (), s32[]{:S(2)}) async-start(), calls=%async_computation.14 | async-start | bytes 1843200 | tf_op jit(solution)/shard_map/reduce_scatter | solution.py:321
  1220.5 13.8 copy-start.2
  1220.5 320.3 %all-reduce.12.cloned.1.call-start = ((), (), s32[]{:S(2)}) async-start(), calls=%async_computation.16 | async-start | bytes 5455872 | tf_op jit(solution)/shard_map/psum | solution.py:329
  1220.5 13.8 copy-start.58
  1389.8 26.6 %copy-start.28 = (bf16[1,256,2304]{2,1,0:T(8,128)(2,1)S(1)}, bf16[1,256,2304]{2,1,0:T(8,128)(2,1)}, u32[]{:S(2)}) copy-start(bf16[1,256,2304]{2,1,0:T(8,128)(2,1)} %copy-done.27) | copy-start | bytes 3538948
  1416.4 15.4 copy-start.60
  (44 other events, 93.9 us)
Sparse Core Ops, SparseCore 0:
  10.1 33.4 all-gather.13
  45.8 27.4 all-gather.15
  74.8 191.9 all-gather.11
  268.2 162.4 all-gather.27
  432.1 19.0 all-gather.29
  453.2 37.4 all-gather.17
  492.8 37.4 all-gather.19
  531.9 70.9 all-gather.21
  604.4 27.4 all-gather.25
  633.3 313.6 all-gather.23
  1106.6 47.8 reduce-scatter.12
  1157.0 47.8 reduce-scatter.14
  1215.0 170.5 all-reduce.13
  1388.6 27.6 reduce-scatter.16
  1421.2 119.4 all-reduce.11
where the time goes:
time: 1560 us; the launch traced here: 1550 us
  waiting for transfers between devices  1070 us (69%)
  matrix products  302 us (19%)
  other arithmetic  108 us (7%)
  local copies, waits for them, and re-layouts  56.9 us (4%)
  between operations  18 us (1%)
    all_gather x1, waiting for transfers between devices, shards(): lax.all_gather(gate_up_projection_weight, 'shard', axis=1, tiled=True)  308 us
    all_gather x1, waiting for transfers between devices, shards(): pieces = lax.all_gather(query_key_value_weight, 'shard', axis=1, tiled=True)  189 us
    unnamed x16, waiting for transfers between devices  153 us
    psum x1, waiting for transfers between devices, shards(): lax.psum(owned[0].astype(jnp.bfloat16), 'rep').astype(jnp.float32)  105 us
    all_gather x1, waiting for transfers between devices, shards(): lax.all_gather(down_projection_weight, 'shard', axis=0, tiled=True)  95.9 us
    reduce_scatter x1, waiting for transfers between devices, shards(): lax.psum_scatter(value_terms.astype(jnp.bfloat16), 'shard', scatter_dimen...  36 us
    all_gather x1, waiting for transfers between devices, shards(): lax.all_gather(value_low, 'shard', axis=0, tiled=True)  33.5 us
    all_gather x1, waiting for transfers between devices, shards(): lax.all_gather(key_turned, 'shard', axis=0, tiled=True)  33 us
  transfers between devices with their start and end apart: 15, of which 14 were waited for; matrix products, arithmetic and copies ran while one was open for 18% of the time, Pallas kernels for 0%

commit v1 on v0

v1 whole, which is shorter than its diff:
```python
import functools
import math

import jax
import jax.numpy as jnp
from jax import lax
from jax.experimental import pallas as pl
from jax.experimental.pallas import tpu as pltpu
from jax.sharding import PartitionSpec as P

HDIM = 64
SPAN = 256
EPS = 1e-05
THETA = 10000.0
BRANCH = 1.4 / math.sqrt(40.0)
EXTRA = 128
F32 = jnp.float32
BF16 = jnp.bfloat16
LOG2E = math.log2(math.e)
VMEM_LIMIT = 56 << 20


def hop(values, axis, bit):
    size = lax.axis_size(axis)
    return lax.ppermute(values, axis, [(i, i ^ bit) for i in range(size)])


def core(values):
    return hop(values, "shard", 1)


def across(values):
    return hop(values, "shard", 2)


def gather_tokens(own):
    far = across(own)
    near = core(own)
    return own, near, far, core(far)


def scatter_tokens(blocks):
    chip_sum = (blocks[2].astype(F32) + core(blocks[3]).astype(F32)).astype(BF16)
    far = across(chip_sum)
    near = core(blocks[1])
    return blocks[0].astype(F32) + near.astype(F32) + far.astype(F32)


def sum_group(values):
    other = rows_of(core(values), 4)
    other = jnp.concatenate([other[1], other[0], other[3], other[2]])
    values = (values.astype(F32) + other.astype(F32)).astype(BF16)
    far = rows_of(across(values), 2)
    return (values.astype(F32) + jnp.concatenate([far[1], far[0]]).astype(F32)).astype(BF16)


def rows_of(values, count):
    size = values.shape[0] // count
    return tuple(values[i * size : (i + 1) * size] for i in range(count))


def norm_rows(values, gain):
    return values * lax.rsqrt(jnp.mean(values * values, axis=-1, keepdims=True) + EPS) * gain


def norm_back(values, gain, grad):
    width = values.shape[-1]
    scale = lax.rsqrt(jnp.mean(values * values, axis=-1, keepdims=True) + EPS)
    moved = grad * gain
    inner = jnp.sum(values * moved, axis=-1, keepdims=True) / width
    return scale * moved - values * (scale * scale * scale) * inner


def dot(left, right):
    return jnp.dot(left, right, preferred_element_type=F32)


def dot_t(left, right):
    return lax.dot_general(left, right, (((1,), (1,)), ((), ())), preferred_element_type=F32)


def t_dot(left, right):
    return lax.dot_general(left, right, (((0,), (0,)), ((), ())), preferred_element_type=F32)


def picked(bank, pick, place):
    per = bank.shape[1]
    rank = bank.shape[2]
    owner = pick // per
    mine = lax.dynamic_index_in_dim(bank, pick % per, 1, keepdims=False)
    mine = jnp.where(owner == place, mine, jnp.zeros_like(mine))
    chip = mine + core(mine)
    inside = place % 2
    part = lax.dynamic_slice_in_dim(chip, inside * (rank // 2), rank // 2, 1)
    far = across(part)
    other = core(far)
    low = jnp.where(inside == 0, far, other)
    high = jnp.where(inside == 0, other, far)
    return chip + jnp.concatenate([low, high], axis=1)


def pad_columns(pieces, width):
    used = sum(piece.shape[1] for piece in pieces)
    rest = jnp.zeros((pieces[0].shape[0], width - used), pieces[0].dtype)
    return jnp.concatenate(list(pieces) + [rest], axis=1)


def gather_reps(values, rep_place):
    size = lax.axis_size("rep")
    buffer = jnp.zeros((size,) + values.shape, values.dtype)
    buffer = lax.dynamic_update_slice_in_dim(buffer, values[None], rep_place, 0)
    bit = 1
    while bit < size:
        base = (rep_place // bit) * bit
        have = lax.dynamic_slice_in_dim(buffer, base, bit, 0)
        got = hop(have, "rep", bit)
        buffer = lax.dynamic_update_slice_in_dim(buffer, got, base ^ bit, 0)
        bit *= 2
    return buffer


def owned_sums(values, chosen, place, rep_place):
    group = lax.axis_size("shard")
    everyone = gather_reps(values.astype(BF16), rep_place)
    adapters = chosen.shape[1]
    per = adapters // group

    def sums_for(owner):
        marks = lax.dynamic_slice_in_dim(chosen, owner * per, per, 1)
        return jnp.sum(
            marks[:, :, None, None] * everyone[:, None].astype(F32), axis=0
        ).astype(BF16)

    got = jnp.zeros((group, per) + values.shape, BF16)
    got = lax.dynamic_update_slice_in_dim(got, sums_for(place)[None], place, 0)
    for j in range(1, group):
        arrived = hop(sums_for(place ^ j), "shard", j)
        got = lax.dynamic_update_slice_in_dim(got, arrived[None], place ^ j, 0)
    return jnp.concatenate([got[i] for i in range(group)], axis=-1).astype(F32)


def exchange(weight, size, place, rep_place):
    rows = weight.shape[1]
    quarter = rows // 4
    part = rep_place % 4

    def columns(owner):
        return lax.dynamic_slice_in_dim(weight, owner * size, size, 2)

    pieces = [(place * rows, columns(place)), ((place ^ 1) * rows, core(columns(place ^ 1)))]
    for j in (2, 3):
        mine = lax.dynamic_slice(
            weight, (0, part * quarter, (place ^ j) * size), (weight.shape[0], quarter, size)
        )
        first = hop(mine, "shard", j)
        near, late = (2, 1) if j == 2 else (1, 2)
        second = hop(first, "rep", near)
        third = hop(first, "rep", late)
        fourth = hop(second, "rep", late)
        for bits, piece in ((0, first), (near, second), (late, third), (near ^ late, fourth)):
            pieces.append(((place ^ j) * rows + (part ^ bits) * quarter, piece))
    offsets = jnp.stack([row.astype(jnp.int32) for row, _ in pieces])
    return offsets, [piece for _, piece in pieces]


def load_pieces(offsets, pieces, whole, sems):
    copies = []
    for number, piece in enumerate(pieces):
        start = pl.multiple_of(offsets[number], 16)
        target = whole.at[:, pl.ds(start, piece.shape[1]), :]
        copy = pltpu.make_async_copy(piece, target, sems.at[number])
        copy.start()
        copies.append(copy)
    return copies


def vmem():
    return pl.BlockSpec(memory_space=pltpu.VMEM)


def smem():
    return pl.BlockSpec(memory_space=pltpu.SMEM)


def anywhere():
    return pl.BlockSpec(memory_space=pl.ANY)


def call(kernel, outs, in_specs, out_specs, scratch, flops, moved, name, **more):
    return pl.pallas_call(
        kernel,
        out_shape=outs,
        in_specs=in_specs,
        out_specs=out_specs,
        scratch_shapes=scratch,
        compiler_params=pltpu.CompilerParams(vmem_limit_bytes=VMEM_LIMIT),
        cost_estimate=pl.CostEstimate(flops=flops, bytes_accessed=moved, transcendentals=0),
        name=name,
        **more,
    )


def turn(values, cosine, sine):
    half = HDIM // 2
    turned = jnp.concatenate([-values[:, half:], values[:, :half]], axis=1)
    return values * cosine + turned * sine


def project(blocks, place, offsets, pieces, a_first, b_first, cosine, sine):
    rows, width = blocks[0].shape
    count = len(blocks)
    size = pieces[0].shape[2]
    heads = size // HDIM
    rank = b_first.shape[1]
    n = len(pieces)

    def kernel(place_ref, offsets_ref, *refs):
        x_refs, refs = refs[:count], refs[count:]
        piece_refs, refs = refs[:n], refs[n:]
        a_ref, b_ref, cos_ref, sin_ref, q_ref, k_ref, v_ref, narrow_ref, whole, sems = refs
        copies = load_pieces(offsets_ref, piece_refs, whole, sems)
        for block in range(count):
            narrow = dot_t(x_refs[block][...], a_ref[...]).astype(BF16)
            narrow_ref[pl.ds(block * rows, rows), :] = narrow
        for copy in copies:
            copy.wait()
        for block in range(count):
            start = pl.multiple_of((place_ref[0] ^ block) * rows, rows)
            x = x_refs[block][...]
            narrow = narrow_ref[pl.ds(block * rows, rows), :]
            cosine_here = cos_ref[pl.ds(start, rows), :]
            sine_here = sin_ref[pl.ds(start, rows), :]
            for number, out in enumerate((q_ref, k_ref, v_ref)):
                pre = dot(x, whole[number]) + dot(
                    narrow[:, number * rank : (number + 1) * rank], b_ref[number]
                )
                for head in range(heads):
                    part = pre[:, head * HDIM : (head + 1) * HDIM]
                    if number < 2:
                        part = turn(part, cosine_here, sine_here)
                    out[head, pl.ds(start, rows), :] = part.astype(BF16)

    by_heads = jax.ShapeDtypeStruct((heads, rows * count, HDIM), BF16)
    return call(
        kernel,
        [by_heads] * 3 + [jax.ShapeDtypeStruct((rows * count, 3 * rank), BF16)],
        [smem(), smem()] + [vmem()] * count + [anywhere()] * n + [vmem()] * 4,
        [vmem()] * 4,
        [pltpu.VMEM((3, width, size), BF16), pltpu.SemaphoreType.DMA((n,))],
        2 * rows * count * width * 3 * size,
        2 * (rows * count * width + 3 * width * size + 6 * rows * count * size),
        "project",
    )(place[None], offsets, *blocks, *pieces, a_first, b_first, cosine, sine)


def label_of(positions, starts_ref):
    label = jnp.full(positions.shape, -1, jnp.int32)
    for number in range(starts_ref.shape[0]):
        inside = (positions >= starts_ref[number]) & (positions < starts_ref[number] + SPAN)
        label = jnp.where(inside, jnp.int32(number), label)
    return label


def hidden_bias(query_at, key_at, starts_ref):
    query_label = label_of(query_at, starts_ref)
    key_label = label_of(key_at, starts_ref)
    visible = (key_at <= query_at) | (query_label == key_label) & (query_label >= 0)
    return jnp.where(visible, 0.0, -1e30)


def crosses(starts_ref, edge, rows):
    hit = None
    for number in range(starts_ref.shape[0]):
        start = starts_ref[number]
        here = (start < edge) & (start + SPAN > edge)
        hit = here if hit is None else hit | here
    return hit


def attend(starts, query, key, value, rows):
    heads, length, _ = query.shape
    count = length // rows
    factor = LOG2E / math.sqrt(HDIM)

    def kernel(starts_ref, q_ref, k_ref, v_ref, o_ref, bias):
        @pl.when(pl.program_id(0) == 0)
        def _():
            for block in range(count):
                shape = (rows, 2 * rows)
                query_at = block * rows + lax.broadcasted_iota(jnp.int32, shape, 0)
                key_at = block * rows + lax.broadcasted_iota(jnp.int32, shape, 1)
                bias[block] = hidden_bias(query_at, key_at, starts_ref)

        def one(block, extra):
            low, high = block * rows, (block + 1 + extra) * rows
            q = q_ref[0, low : low + rows, :]
            edge = dot_t(q, k_ref[0, low:high, :]) + bias[block, :, : high - low]
            top = jnp.max(edge, axis=1, keepdims=True)
            if block:
                before = dot_t(q, k_ref[0, :low, :])
                top = jnp.maximum(top, jnp.max(before, axis=1, keepdims=True))
            shift = top * factor
            weight = jnp.exp2(edge * factor - shift)
            total = jnp.sum(weight, axis=1, keepdims=True)
            out = dot(weight.astype(BF16), v_ref[0, low:high, :])
            if block:
                weight = jnp.exp2(before * factor - shift)
                total = total + jnp.sum(weight, axis=1, keepdims=True)
                out = out + dot(weight.astype(BF16), v_ref[0, :low, :])
            o_ref[0, low : low + rows, :] = (out / total).astype(BF16)

        for block in range(count):
            if block == count - 1:
                one(block, 0)
                continue
            wide = crosses(starts_ref, (block + 1) * rows, rows)
            pl.when(wide)(functools.partial(one, block, 1))
            pl.when(jnp.logical_not(wide))(functools.partial(one, block, 0))

    spec = pl.BlockSpec((1, length, HDIM), lambda h: (h, 0, 0))
    return call(
        kernel,
        jax.ShapeDtypeStruct(query.shape, BF16),
        [smem(), spec, spec, spec],
        spec,
        [pltpu.VMEM((count, rows, 2 * rows), F32)],
        4 * heads * length * length * HDIM * 4,
        16 * heads * length * HDIM,
        "attend",
        grid=(heads,),
    )(starts, query, key, value)


def attend_back(starts, query, key, value, grad, cosine, sine, rows):
    heads, length, _ = query.shape
    count = length // rows
    scale = 1.0 / math.sqrt(HDIM)
    factor = LOG2E * scale

    def kernel(
        starts_ref, q_ref, k_ref, v_ref, g_ref, cos_ref, sin_ref, dq_ref, dk_ref, dv_ref,
        bias, key_sum, value_sum, key_turned,
    ):
        @pl.when(pl.program_id(0) == 0)
        def _():
            for block in range(count):
                shape = (2 * rows, rows)
                query_at = block * rows + lax.broadcasted_iota(jnp.int32, shape, 1)
                key_at = block * rows + lax.broadcasted_iota(jnp.int32, shape, 0)
                bias[block] = hidden_bias(query_at, key_at, starts_ref)

        key_sum[...] = jnp.zeros_like(key_sum)
        value_sum[...] = jnp.zeros_like(value_sum)
        key_turned[...] = k_ref[0].astype(F32).T.astype(BF16)

        def one(block, extra):
            low, high = block * rows, (block + 1 + extra) * rows
            q = q_ref[0, low : low + rows, :]
            g = g_ref[0, low : low + rows, :]
            raw = dot_t(k_ref[0, low:high, :], q) + bias[block, : high - low, :]
            if block:
                raw = jnp.concatenate([dot_t(k_ref[0, :low, :], q), raw], axis=0)
            top = jnp.max(raw, axis=0, keepdims=True)
            weight = jnp.exp2(raw * factor - top * factor)
            probs = weight * (1.0 / jnp.sum(weight, axis=0, keepdims=True))
            grad_probs = dot_t(v_ref[0, :high, :], g)
            inner = jnp.sum(grad_probs * probs, axis=0, keepdims=True)
            grad_scores = (probs * (grad_probs - inner)).astype(BF16)
            value_sum[:high, :] += dot(probs.astype(BF16), g)
            key_sum[:high, :] += dot(grad_scores, q)
            turned = dot(key_turned[:, :high], grad_scores)
            back = turned.T * scale
            dq_ref[0, low : low + rows, :] = turn(
                back, cos_ref[low : low + rows, :], -sin_ref[low : low + rows, :]
            ).astype(BF16)

        for block in range(count):
            if block == count - 1:
                one(block, 0)
                continue
            wide = crosses(starts_ref, (block + 1) * rows, rows)
            pl.when(wide)(functools.partial(one, block, 1))
            pl.when(jnp.logical_not(wide))(functools.partial(one, block, 0))
        dk_ref[0] = turn(key_sum[...] * scale, cos_ref[...], -sin_ref[...]).astype(BF16)
        dv_ref[0] = value_sum[...].astype(BF16)

    spec = pl.BlockSpec((1, length, HDIM), lambda h: (h, 0, 0))
    table = pl.BlockSpec((length, HDIM), lambda h: (0, 0))
    return call(
        kernel,
        [jax.ShapeDtypeStruct(query.shape, BF16)] * 3,
        [smem(), spec, spec, spec, spec, table, table],
        [spec] * 3,
        [
            pltpu.VMEM((count, 2 * rows, rows), F32),
            pltpu.VMEM((length, HDIM), F32),
            pltpu.VMEM((length, HDIM), F32),
            pltpu.VMEM((HDIM, length), BF16),
        ],
        10 * heads * length * length * HDIM * 4,
        32 * heads * length * HDIM,
        "attend_back",
        grid=(heads,),
    )(starts, query, key, value, grad, cosine, sine)


def rows_by_heads(ref, start, rows):
    return jnp.concatenate([ref[head, pl.ds(start, rows), :] for head in range(ref.shape[0])], axis=1)


def close_attention(mixed, place, weight, a_out, wanted, rows):
    size, width = weight.shape
    rank = a_out.shape[0]

    def kernel(place_ref, m_ref, w_ref, a_ref, *outs):
        for block, out in zip(wanted, outs):
            start = pl.multiple_of((place_ref[0] ^ block) * rows, rows)
            here = rows_by_heads(m_ref, start, rows)
            out[:, :width] = dot(here, w_ref[...]).astype(BF16)
            narrow = dot_t(here, a_ref[...]).astype(BF16)
            out[:, width:] = jnp.concatenate(
                [narrow, jnp.zeros((rows, EXTRA - rank), BF16)], axis=1
            )

    return call(
        kernel,
        [jax.ShapeDtypeStruct((rows, width + EXTRA), BF16)] * len(wanted),
        [smem()] + [vmem()] * 3,
        [vmem()] * len(wanted),
        [],
        2 * rows * len(wanted) * size * width,
        2 * size * width + 2 * rows * len(wanted) * (width + size),
        "close_attention",
    )(place[None], mixed, weight, a_out)


def open_attention(blocks, place, mixed, weight, a_out, b_out):
    rows, width_ext = blocks[0].shape
    size, width = weight.shape
    rank = a_out.shape[0]
    count = len(blocks)
    heads = size // HDIM

    def kernel(place_ref, *refs):
        g_refs, refs = refs[:count], refs[count:]
        m_ref, w_ref, a_ref, b_ref, out, sum_ref = refs
        total = jnp.zeros((rank, size), F32)
        for block in range(count):
            start = pl.multiple_of((place_ref[0] ^ block) * rows, rows)
            grad = g_refs[block][:, :width]
            narrow = dot_t(grad, b_ref[...]).astype(BF16)
            back = dot_t(grad, w_ref[...]) + dot(narrow, a_ref[...])
            for head in range(heads):
                out[head, pl.ds(start, rows), :] = back[:, head * HDIM : (head + 1) * HDIM].astype(BF16)
            total = total + t_dot(narrow, rows_by_heads(m_ref, start, rows))
        sum_ref[...] = total

    return call(
        kernel,
        [
            jax.ShapeDtypeStruct(mixed.shape, BF16),
            jax.ShapeDtypeStruct((rank, size), F32),
        ],
        [smem()] + [vmem()] * (count + 4),
        [vmem()] * 2,
        [],
        2 * rows * count * size * width,
        2 * size * width + 2 * rows * count * (width + 2 * size),
        "open_attention",
    )(place[None], *blocks, mixed, weight, a_out, b_out)


def feed_forward(blocks, grads, offsets, pieces, down, a_mlp, b_down, a_hidden, b_hidden):
    rows, width = blocks[0].shape
    count = len(blocks)
    size = down.shape[0]
    rank = b_down.shape[0]
    n = len(pieces)

    def kernel(offsets_ref, *refs):
        x_refs, refs = refs[:count], refs[count:]
        g_refs, refs = refs[:count], refs[count:]
        piece_refs, refs = refs[:n], refs[n:]
        down_hbm, am_ref, bd_ref, ah_ref, bh_ref = refs[:5]
        refs = refs[5:]
        feed_refs, refs = refs[:count], refs[count:]
        back_refs, refs = refs[:count], refs[count:]
        a_sum, b_sum, whole, down_ref, sems, down_sem = refs
        copies = load_pieces(offsets_ref, piece_refs, whole, sems)
        down_copy = pltpu.make_async_copy(down_hbm, down_ref, down_sem)
        down_copy.start()
        for copy in copies:
            copy.wait()
        pad = jnp.zeros((rows, EXTRA - rank), BF16)
        for block in range(count):
            x = x_refs[block][...]
            narrow = dot_t(x, am_ref[...]).astype(BF16)
            gate = dot(x, whole[0]) + dot(narrow[:, :rank], bh_ref[0])
            up = dot(x, whole[1]) + dot(narrow[:, rank:], bh_ref[1])
            sigmoid = 1.0 / (1.0 + jnp.exp(-gate))
            silu = gate * sigmoid
            hidden = (silu * up).astype(BF16)
            if block == 0:
                down_copy.wait()
            feed_refs[block][:, :width] = dot(hidden, down_ref[...]).astype(BF16)
            feed_refs[block][:, width:] = jnp.concatenate(
                [dot_t(hidden, ah_ref[...]).astype(BF16), pad], axis=1
            )
            grad = g_refs[block][...]
            grad_narrow = dot_t(grad, bd_ref[...]).astype(BF16)
            grad_hidden = dot_t(grad, down_ref[...]) + dot(grad_narrow, ah_ref[...])
            grad_hidden = grad_hidden.astype(BF16).astype(F32)
            grad_up = (grad_hidden * silu).astype(BF16)
            grad_gate = (grad_hidden * up * (sigmoid * (1.0 + gate * (1.0 - sigmoid)))).astype(BF16)
            back = dot_t(grad_gate, whole[0]) + dot_t(grad_up, whole[1])
            back_refs[block][:, :width] = back.astype(BF16)
            back_refs[block][:, width:] = jnp.concatenate(
                [
                    dot_t(grad_gate, bh_ref[0]).astype(BF16),
                    dot_t(grad_up, bh_ref[1]).astype(BF16),
                    pad[:, rank:],
                ],
                axis=1,
            )
            terms = (
                t_dot(grad_narrow, hidden),
                t_dot(narrow[:, :rank], grad_gate),
                t_dot(narrow[:, rank:], grad_up),
            )
            if block == 0:
                a_sum[...] = terms[0]
                b_sum[0] = terms[1]
                b_sum[1] = terms[2]
            else:
                a_sum[...] += terms[0]
                b_sum[0] += terms[1]
                b_sum[1] += terms[2]

    out = jax.ShapeDtypeStruct((rows, width + EXTRA), BF16)
    return call(
        kernel,
        [out] * (2 * count)
        + [jax.ShapeDtypeStruct((rank, size), F32), jax.ShapeDtypeStruct((2, rank, size), F32)],
        [smem()] + [vmem()] * (2 * count) + [anywhere()] * (n + 1) + [vmem()] * 4,
        [vmem()] * (2 * count + 2),
        [
            pltpu.VMEM((2, width, size), BF16),
            pltpu.VMEM((size, width), BF16),
            pltpu.SemaphoreType.DMA((n,)),
            pltpu.SemaphoreType.DMA,
        ],
        12 * rows * count * width * size,
        6 * width * size + 8 * rows * count * width,
        "feed_forward",
    )(offsets, *blocks, *grads, *pieces, down, a_mlp, b_down, a_hidden, b_hidden)


def project_back(grads, place, offsets, pieces, narrow_first, b_first, wanted, rows):
    heads = grads[0].shape[0]
    maps, _, size = pieces[0].shape
    width = 4 * pieces[0].shape[1]
    rank = b_first.shape[1]
    n = len(pieces)
    count = len(wanted)

    def kernel(place_ref, offsets_ref, *refs):
        g_refs, refs = refs[:maps], refs[maps:]
        piece_refs, refs = refs[:n], refs[n:]
        narrow_ref, b_ref = refs[:2]
        back_refs, refs = refs[2 : 2 + count], refs[2 + count :]
        thin_ref, sum_ref, whole, sems = refs
        copies = load_pieces(offsets_ref, piece_refs, whole, sems)
        waiting = True
        for index, block in enumerate(wanted):
            start = pl.multiple_of((place_ref[0] ^ block) * rows, rows)
            parts = [rows_by_heads(g_refs[number], start, rows) for number in range(maps)]
            narrow = narrow_ref[block * rows : (block + 1) * rows, :]
            thin = [dot_t(parts[number], b_ref[number]) for number in range(maps)]
            thin_ref[index * rows : (index + 1) * rows, :] = jnp.concatenate(thin, axis=1).astype(BF16)
            for number in range(maps):
                term = t_dot(narrow[:, number * rank : (number + 1) * rank], parts[number])
                if index == 0:
                    sum_ref[number] = term
                else:
                    sum_ref[number] += term
            if waiting:
                for copy in copies:
                    copy.wait()
                waiting = False
            back = dot_t(parts[0], whole[0])
            for number in range(1, maps):
                back = back + dot_t(parts[number], whole[number])
            back_refs[index][...] = back.astype(BF16)

    return call(
        kernel,
        [jax.ShapeDtypeStruct((rows, width), BF16)] * count
        + [
            jax.ShapeDtypeStruct((rows * count, maps * rank), BF16),
            jax.ShapeDtypeStruct((maps, rank, size), F32),
        ],
        [smem(), smem()] + [vmem()] * maps + [anywhere()] * n + [vmem()] * 2,
        [vmem()] * (count + 2),
        [pltpu.VMEM((maps, width, size), BF16), pltpu.SemaphoreType.DMA((n,))],
        2 * rows * count * width * maps * size,
        2 * (rows * count * (width + maps * size) + maps * width * size),
        "project_back",
    )(place[None], offsets, *grads, *pieces, narrow_first, b_first)


def shards(
    tokens,
    cotangent,
    sequence_adapter_index,
    image_span_start,
    attention_norm_gain,
    feedforward_norm_gain,
    query_key_value_weight,
    attention_output_weight,
    gate_up_projection_weight,
    down_projection_weight,
    adapter_model_input_maps,
    adapter_model_output_maps,
    adapter_hidden_input_map,
    adapter_hidden_output_maps,
):
    rows = tokens.shape[1]
    width = tokens.shape[2]
    rank = adapter_model_input_maps.shape[2]
    group = lax.axis_size("shard")
    place = lax.axis_index("shard").astype(jnp.int32)
    rep_place = lax.axis_index("rep").astype(jnp.int32)
    pick = sequence_adapter_index[0]
    starts = image_span_start[0]
    head_cols = width // group
    ff_cols = down_projection_weight.shape[0]

    gain_one = attention_norm_gain.astype(F32)
    gain_two = feedforward_norm_gain.astype(F32)
    residual_in = tokens[0].astype(F32)
    grad_out = cotangent[0].astype(F32)

    normed = norm_rows(residual_in, gain_one).astype(BF16)
    grad_feed = (BRANCH * grad_out).astype(BF16)
    first_offsets, first_pieces = exchange(query_key_value_weight, head_cols, place, rep_place)
    first_blocks = gather_tokens(normed)
    model_one = picked(
        jnp.concatenate([adapter_model_input_maps, adapter_model_output_maps]), pick, place
    )
    hidden_one = picked(
        jnp.concatenate([adapter_hidden_input_map[None], adapter_hidden_output_maps]), pick, place
    )
    a_one, b_one = model_one[:6], model_one[6:]

    def own_columns(values, size):
        return lax.dynamic_slice_in_dim(values, place * size, size, values.ndim - 1)

    a_first = a_one[0:3].reshape(3 * rank, width)
    b_first = own_columns(b_one[0:3], head_cols)
    a_out = own_columns(a_one[3], head_cols)
    b_out = b_one[3]
    a_mlp = a_one[4:6].reshape(2 * rank, width)
    b_down = b_one[4]
    hidden_cols = own_columns(hidden_one, ff_cols)
    a_hidden, b_hidden = hidden_cols[0], hidden_cols[1:]

    picks = lax.all_gather(sequence_adapter_index, "rep", axis=0, tiled=True)
    adapters = adapter_model_input_maps.shape[1] * group
    chosen = (picks[:, None] == jnp.arange(adapters, dtype=jnp.int32)[None, :]).astype(F32)

    half = HDIM // 2
    frequency = jnp.exp(jnp.arange(half, dtype=F32) * (-2.0 / HDIM) * math.log(THETA))
    angle = jnp.arange(rows * group, dtype=jnp.int32).astype(F32)[:, None] * frequency[None, :]
    cosine = jnp.concatenate([jnp.cos(angle), jnp.cos(angle)], axis=1)
    sine = jnp.concatenate([jnp.sin(angle), jnp.sin(angle)], axis=1)

    query, key, value, narrow_first = project(
        first_blocks, place, first_offsets, first_pieces, a_first, b_first, cosine, sine
    )
    mlp_offsets, mlp_pieces = exchange(gate_up_projection_weight, ff_cols, place, rep_place)
    feed_blocks = gather_tokens(grad_feed)
    mixed = attend(starts, query, key, value, rows)

    far_out = close_attention(mixed, place, attention_output_weight, a_out, (2, 3), rows)
    near_out = close_attention(mixed, place, attention_output_weight, a_out, (0, 1), rows)
    branch_own = scatter_tokens((*near_out, *far_out))
    narrow_out = branch_own[:, width : width + rank].astype(BF16)
    branch = branch_own[:, :width] + dot(narrow_out, b_out)
    middle = residual_in + BRANCH * branch
    normed_second = norm_rows(middle, gain_two).astype(BF16)
    second_blocks = gather_tokens(normed_second)

    *parts, a_near, b_near = feed_forward(
        second_blocks[:2], feed_blocks[:2], mlp_offsets, mlp_pieces, down_projection_weight,
        a_mlp, b_down, a_hidden, b_hidden,
    )
    feed_near, back_near = parts[:2], parts[2:]
    *parts, a_far, b_far = feed_forward(
        second_blocks[2:], feed_blocks[2:], mlp_offsets, mlp_pieces, down_projection_weight,
        a_mlp, b_down, a_hidden, b_hidden,
    )
    feed_far, back_far = parts[:2], parts[2:]
    second_own = scatter_tokens((*back_near, *back_far))
    grad_narrow_mlp = second_own[:, width : width + 2 * rank].astype(BF16)
    grad_normed_second = second_own[:, :width] + dot(grad_narrow_mlp, a_mlp)
    grad_middle = grad_out + norm_back(middle, gain_two, grad_normed_second)
    grad_branch = (BRANCH * grad_middle).astype(BF16)
    branch_blocks = gather_tokens(
        pad_columns([grad_branch, narrow_out, grad_narrow_mlp], width + EXTRA)
    )

    feed_own = scatter_tokens((*feed_near, *feed_far))
    narrow_down = feed_own[:, width : width + rank].astype(BF16)
    feed = feed_own[:, :width] + dot(narrow_down, b_down)
    output = (middle + BRANCH * feed).astype(BF16)
    narrow_down_blocks = gather_tokens(narrow_down)

    grad_mixed, grad_a_out = open_attention(
        branch_blocks, place, mixed, attention_output_weight, a_out, b_out
    )
    first_grads = attend_back(starts, query, key, value, grad_mixed, cosine, sine, rows)
    *far_back, thin_far, b_first_far = project_back(
        first_grads, place, first_offsets, first_pieces, narrow_first, b_first, (2, 3), rows
    )
    *near_back, thin_near, b_first_near = project_back(
        first_grads, place, first_offsets, first_pieces, narrow_first, b_first, (0, 1), rows
    )
    grad_narrow_first = sum_group(jnp.concatenate([thin_near, thin_far]))
    grad_normed = scatter_tokens((*near_back, *far_back)) + dot(grad_narrow_first[:rows], a_first)
    input_grad = grad_middle + norm_back(residual_in, gain_one, grad_normed)

    def columns_product(thin, wide):
        total = sum(t_dot(left, right) for left, right in zip(thin, wide))
        return own_columns(total, head_cols)

    wide_branch = [block[:, :width] for block in branch_blocks]
    thin_out = [block[:, width : width + rank] for block in branch_blocks]
    thin_mlp = [block[:, width + rank : width + 3 * rank] for block in branch_blocks]
    early_model = jnp.concatenate(
        [
            grad_a_out,
            columns_product(thin_mlp, second_blocks),
            columns_product(thin_out, wide_branch),
            columns_product(narrow_down_blocks, feed_blocks),
        ]
    )
    early_hidden = jnp.concatenate(
        [a_near + a_far, (b_near + b_far).reshape(2 * rank, ff_cols)]
    )
    late_model = jnp.concatenate(
        [
            columns_product(rows_of(grad_narrow_first, group), first_blocks),
            (b_first_near + b_first_far).reshape(3 * rank, head_cols),
        ]
    )
    early_model = owned_sums(early_model, chosen, place, rep_place)
    early_hidden = owned_sums(early_hidden, chosen, place, rep_place)
    late_model = owned_sums(late_model, chosen, place, rep_place)

    def maps_first(values):
        per, count, n = values.shape
        return values.reshape(per, count // rank, rank, n).transpose(1, 0, 2, 3)

    early_model, early_hidden, late_model = map(maps_first, (early_model, early_hidden, late_model))
    grad_a_model = jnp.concatenate([late_model[0:3], early_model[0:3]])
    grad_b_model = jnp.concatenate([late_model[3:6], early_model[3:5]])
    return (
        output[None], input_grad[None], grad_a_model, grad_b_model, early_hidden[0], early_hidden[1:3],
    )


def solution(mesh):
    in_specs = (
        P("rep", "shard", None),
        P("rep", "shard", None),
        P("rep"),
        P("rep", None),
        P(),
        P(),
        P(None, "shard", None),
        P("shard", None),
        P(None, "shard", None),
        P("shard", None),
        P(None, "shard", None, None),
        P(None, "shard", None, None),
        P("shard", None, None),
        P(None, "shard", None, None),
    )
    out_specs = (
        P("rep", "shard", None),
        P("rep", "shard", None),
        P(None, "shard", None, None),
        P(None, "shard", None, None),
        P("shard", None, None),
        P(None, "shard", None, None),
    )
    return jax.shard_map(shards, mesh=mesh, in_specs=in_specs, out_specs=out_specs, check_vma=False)
```

time: 1560 us -> 834 us (0.53)
  waiting for transfers between devices: 1070 us -> 337 us
  matrix products: 302 us -> 29.9 us
  Pallas kernels: 0 us -> 247 us
  other arithmetic: 108 us -> 49.3 us
  starting transfers between devices: 0.77 us -> 55.4 us
  blocking collectives: 0 us -> 22.8 us
  local copies, waits for them, and re-layouts: 56.9 us -> 79.2 us
    all_gather x10 -> x0, waiting for transfers between devices: 751 us -> none  [the longest x1 308 us: shards(): lax.all_gather(gate_up_projection_weight, 'shard', axis=1, tiled=True)]
    ppermute x0 -> x71, waiting for transfers between devices: none -> 337 us  [hop(): return lax.ppermute(values, axis, [(i, i ^ bit) for i in range(size)])]
    dot_general x40 -> x20, matrix products: 302 us -> 29.9 us  [the longest x16 21.9 us: t_dot(): lax.dot_general(left, right, (((0,), (0,)), ((), ())), preferred_element_...]
    pallas_call x0 -> x10, Pallas kernels: none -> 247 us  [the longest x2 99 us: feed_forward(): call(kernel, [out] * (2 * count) + [jax.ShapeDtypeStruct((rank, size), F3...]
    unnamed x16 -> x0, waiting for transfers between devices: 153 us -> none
    psum x1 -> x0, waiting for transfers between devices: 105 us -> none  [shards(): lax.psum(owned[0].astype(jnp.bfloat16), 'rep').astype(jnp.float32)]
    reduce_scatter x3 -> x0, waiting for transfers between devices: 60.4 us -> none  [the longest x1 36 us: shards(): lax.psum_scatter(value_terms.astype(jnp.bfloat16), 'shard', scatter_dimen...]
    ppermute x0 -> x71, starting transfers between devices: none -> 55.4 us  [hop(): return lax.ppermute(values, axis, [(i, i ^ bit) for i in range(size)])]
  transfers between devices with their start and end apart: 15 -> 71, of which waited for: 14 -> 31; matrix products, arithmetic and copies ran while one was open for 18% -> 15% of each run, Pallas kernels for 0% -> 13%
where the time goes in v1:
time: 834 us; the launch traced here: 824 us
  waiting for transfers between devices  337 us (40%)
  Pallas kernels  247 us (30%)
  local copies, waits for them, and re-layouts  79.2 us (9%)
  starting transfers between devices  55.4 us (7%)
  other arithmetic  49.3 us (6%)
  matrix products  29.9 us (4%)
  blocking collectives  22.8 us (3%)
    ppermute x71, waiting for transfers between devices, hop(): return lax.ppermute(values, axis, [(i, i ^ bit) for i in range(size)])  337 us
    pallas_call x2, Pallas kernels, feed_forward(): call(kernel, [out] * (2 * count) + [jax.ShapeDtypeStruct((rank, size), F3...  99 us
    ppermute x71, starting transfers between devices, hop(): return lax.ppermute(values, axis, [(i, i ^ bit) for i in range(size)])  55.4 us
    pallas_call x1, Pallas kernels, attend_back(): call(kernel, [jax.ShapeDtypeStruct(query.shape, BF16)] * 3, [smem(), spec...  51.1 us
    pallas_call x2, Pallas kernels, project_back(): call(kernel, [jax.ShapeDtypeStruct((rows, width), BF16)] * count + [jax.S...  29.6 us
    pallas_call x1, Pallas kernels, attend(): call(kernel, jax.ShapeDtypeStruct(query.shape, BF16), [smem(), spec, spec...  23 us
    unnamed x1, blocking collectives  22.8 us
    dot_general x16, matrix products, t_dot(): lax.dot_general(left, right, (((0,), (0,)), ((), ())), preferred_element_...  21.9 us
  transfers between devices with their start and end apart: 71, of which 31 were waited for; matrix products, arithmetic and copies ran while one was open for 15% of the time, Pallas kernels for 13%

profile of v1, /device:TPU:0, one launch (start us, length us, event | category | flops | bytes accessed | tf_op | source)
XLA Modules:
  0.0 824.0 jit_solution(90822567280720583)
XLA Ops:
  8.5 7.2 constant_dynamic-slice_fusion.22
  15.9 2.9 constant_dynamic-slice_fusion.20
  23.9 43.9 %collective-permute-done.13 = bf16[11,8,2304]{2,1,0:T(8,128)(2,1)} collective-permute-done((bf16[11,8,2304]{2,1,0:T(8,128)(2,1)S(1)}, bf16[11,8,2304]{2,1,0:T(8,128)(2,1)}, u32[]{:S(2)}, u32[]{:S(2)}) %collective-permute-start.13) | collective-permute-done | bytes 405536 | tf_op jit(solution)/shard_map/ppermute | solution.py:25
  76.5 10.5 %collective-permute-done.5.refs_7_.refs_6_ = bf16[3,144,576]{2,1,0:T(8,128)(2,1)S(1)} collective-permute-done((bf16[3,144,576]{2,1,0:T(8,128)(2,1)}, bf16[3,144,576]{2,1,0:T(8,128)(2,1)S(1)}, u32[]{:S(2)}, u32[]{:S(2)}) %collective-permute-start.5) | collective-permute-done | bytes 497696 | tf_op jit(solution)/shard_map/ppermute | solution.py:25
  91.0 10.4 %collective-permute-done.9.refs_11_.refs_10_ = bf16[3,144,576]{2,1,0:T(8,128)(2,1)S(1)} collective-permute-done((bf16[3,144,576]{2,1,0:T(8,128)(2,1)}, bf16[3,144,576]{2,1,0:T(8,128)(2,1)S(1)}, u32[]{:S(2)}, u32[]{:S(2)}) %collective-permute-start.9) | collective-permute-done | bytes 497696 | tf_op jit(solution)/shard_map/ppermute | solution.py:25
  108.2 6.6 collective-permute-done.7.refs_9_.refs_8_
  117.3 20.9 %project.1 = (bf16[9,1024,64]{2,1,0:T(8,128)(2,1)}, bf16[9,1024,64]{2,1,0:T(8,128)(2,1)}, bf16[9,1024,64]{2,1,0:T(8,128)(2,1)}, bf16[1024,48]{1,0:T(8,128)(2,1)}) custom-call(s32[1]{0:T(128)} %bitcast.1.place_ref, s32[10]{0:T(128)} %stack.54.offsets_ref, bf16[256,2304]{1,0:T(8,128)(2,1)} %fusion.3.refs_0_, bf16[256,2304]{1,0:T(8,128)(2,1)} %copy-done.33, ...), custom_call_target="tpu_custom_call" | custom-call | flops 8153726976 | bytes 19759104 | tf_op jit(solution)/shard_map/project/pallas_call | solution.py:244
  138.2 23.0 %attend.1.m_ref.refs_4_ = bf16[9,1024,64]{2,1,0:T(8,128)(2,1)} custom-call(s32[2]{0:T(128)} %bitcast.159, bf16[9,1024,64]{2,1,0:T(8,128)(2,1)} %get-tuple-element.39.q_ref, bf16[9,1024,64]{2,1,0:T(8,128)(2,1)} %get-tuple-element.40.k_ref, bf16[9,1024,64]{2,1,0:T(8,128)(2,1)} %get-tuple-element.41.v_ref), custom_call_target="tpu_custom_call" | custom-call | flops 9663676416 | bytes 9437184 | tf_op jit(solution)/shard_map/attend/pallas_call | solution.py:321
  161.3 5.8 close_attention.3
  167.8 5.8 close_attention.2
  177.8 3.6 constant_dynamic-slice_fusion.14
  181.4 9.0 %constant_dynamic-slice_fusion.16 = (bf16[2,576,1440]{2,1,0:T(8,128)(2,1)S(1)}, bf16[2,576,1440]{2,1,0:T(8,128)(2,1)}) fusion(bf16[2,576,5760]{2,1,0:T(8,128)(2,1)} %param.22, s32[]{:T(128)S(6)} %select_n.223, s32[]{:T(128)S(6)} %select_n.222), kind=kLoop, calls=%fused_computation.179 | loop fusion | bytes 13271048 | tf_op jit(solution)/shard_map/dynamic_slice | solution.py:148
  192.3 14.5 %collective-permute-done.17 = bf16[256,2432]{1,0:T(8,128)(2,1)} collective-permute-done((bf16[256,2432]{1,0:T(8,128)(2,1)}, bf16[256,2432]{1,0:T(8,128)(2,1)}, u32[]{:S(2)}, u32[]{:S(2)}) %collective-permute-start.17) | collective-permute-done | bytes 1245216 | tf_op jit(solution)/shard_map/ppermute | solution.py:25
  210.2 15.5 %collective-permute-done.21.refs_6_ = bf16[2,144,1440]{2,1,0:T(8,128)(2,1)S(1)} collective-permute-done((bf16[2,144,1440]{2,1,0:T(8,128)(2,1)S(1)}, bf16[2,144,1440]{2,1,0:T(8,128)(2,1)S(1)}, u32[]{:S(2)}, u32[]{:S(2)}) %collective-permute-start.21) | collective-permute-done | bytes 829472 | tf_op jit(solution)/shard_map/ppermute | solution.py:25
  225.6 24.5 %collective-permute-done.30 = bf16[3,8,5760]{2,1,0:T(8,128)(2,1)S(1)} collective-permute-done((bf16[3,8,5760]{2,1,0:T(8,128)(2,1)S(1)}, bf16[3,8,5760]{2,1,0:T(8,128)(2,1)S(1)}, u32[]{:S(2)}, u32[]{:S(2)}) %collective-permute-start.30) | collective-permute-done | bytes 276512 | tf_op jit(solution)/shard_map/ppermute | solution.py:25
  257.1 17.2 %collective-permute-done.22.refs_7_ = bf16[2,144,1440]{2,1,0:T(8,128)(2,1)S(1)} collective-permute-done((bf16[2,144,1440]{2,1,0:T(8,128)(2,1)S(1)}, bf16[2,144,1440]{2,1,0:T(8,128)(2,1)S(1)}, u32[]{:S(2)}, u32[]{:S(2)}) %collective-permute-start.22) | collective-permute-done | bytes 829472 | tf_op jit(solution)/shard_map/ppermute | solution.py:25
  275.2 19.7 %collective-permute-done.26.refs_11_ = bf16[2,144,1440]{2,1,0:T(8,128)(2,1)S(1)} collective-permute-done((bf16[2,144,1440]{2,1,0:T(8,128)(2,1)S(1)}, bf16[2,144,1440]{2,1,0:T(8,128)(2,1)S(1)}, u32[]{:S(2)}, u32[]{:S(2)}) %collective-permute-start.26) | collective-permute-done | bytes 829472 | tf_op jit(solution)/shard_map/ppermute | solution.py:25
  300.0 13.1 %collective-permute-done.24.refs_9_ = bf16[2,144,1440]{2,1,0:T(8,128)(2,1)S(1)} collective-permute-done((bf16[2,144,1440]{2,1,0:T(8,128)(2,1)S(1)}, bf16[2,144,1440]{2,1,0:T(8,128)(2,1)S(1)}, u32[]{:S(2)}, u32[]{:S(2)}) %collective-permute-start.24) | collective-permute-done | bytes 829472 | tf_op jit(solution)/shard_map/ppermute | solution.py:25
  313.1 8.6 %collective-permute-done.33.refs_0_ = bf16[256,2304]{1,0:T(8,128)(2,1)} collective-permute-done((bf16[256,2304]{1,0:T(8,128)(2,1)S(1)}, bf16[256,2304]{1,0:T(8,128)(2,1)}, u32[]{:S(2)}, u32[]{:S(2)}) %collective-permute-start.33) | collective-permute-done | bytes 1179680 | tf_op jit(solution)/shard_map/ppermute | solution.py:25
  324.2 49.3 %feed_forward.2 = (bf16[256,2432]{1,0:T(8,128)(2,1)}, bf16[256,2432]{1,0:T(8,128)(2,1)}, bf16[256,2432]{1,0:T(8,128)(2,1)}, bf16[256,2432]{1,0:T(8,128)(2,1)}, f...) custom-call(s32[10]{0:T(128)} %stack.54.offsets_ref, bf16[256,2304]{1,0:T(8,128)(2,1)} %copy-done.14, ...), custom_call_target="tpu_custom_call" | custom-call | flops 20384317440 | bytes 29343744 | tf_op jit(solution)/shard_map/feed_forward/pallas_call | solution.py:540
  373.6 49.6 %feed_forward.3 = (bf16[256,2432]{1,0:T(8,128)(2,1)}, bf16[256,2432]{1,0:T(8,128)(2,1)}, bf16[256,2432]{1,0:T(8,128)(2,1)}, bf16[256,2432]{1,0:T(8,128)(2,1)}, f...) custom-call(s32[10]{0:T(128)} %stack.54.offsets_ref, bf16[256,2304]{1,0:T(8,128)(2,1)} %collective-permute-done.33.refs_0_, ...), custom_call_target="tpu_custom_call" | custom-call | flops 20384317440 | bytes 29343744 | tf_op jit(solution)/shard_map/feed_forward/pallas_call | solution.py:540
  427.9 5.7 collective-permute-done.65
  438.4 7.4 collective-permute-done.66
  454.7 22.8 %all-reduce = s32[8]{0:T(128)S(1)} all-reduce(s32[8]{0:T(128)} %dynamic-update-slice), channel_id=1, replica_groups=mesh['rep'=8,'shard'=4] {'rep'}, use_global_device_ids=true, to_apply=%add | all-reduce | flops 8 | bytes 64
  489.4 7.5 collective-permute-done.69
  497.4 8.8 %collective-permute-done.70 = bf16[2,48,1440]{2,1,0:T(8,128)(2,1)S(1)} collective-permute-done((bf16[2,48,1440]{2,1,0:T(8,128)(2,1)S(1)}, bf16[2,48,1440]{2,1,0:T(8,128)(2,1)S(1)}, u32[]{:S(2)}, u32[]{:S(2)}) %collective-permute-start.70) | collective-permute-done | bytes 276512 | tf_op jit(solution)/shard_map/ppermute | solution.py:25
  507.2 3.7 concatenate.158
  521.9 22.6 %collective-permute-done.41 = bf16[256,2432]{1,0:T(8,128)(2,1)S(1)} collective-permute-done((bf16[256,2432]{1,0:T(8,128)(2,1)S(1)}, bf16[256,2432]{1,0:T(8,128)(2,1)S(1)}, u32[]{:S(2)}, u32[]{:S(2)}) %collective-permute-start.41) | collective-permute-done | bytes 1245216 | tf_op jit(solution)/shard_map/ppermute | solution.py:25
  552.0 3.2 concatenate.127.refs_0_
  556.3 15.0 %collective-permute-done.38 = bf16[256,2432]{1,0:T(8,128)(2,1)} collective-permute-done((bf16[256,2432]{1,0:T(8,128)(2,1)}, bf16[256,2432]{1,0:T(8,128)(2,1)}, u32[]{:S(2)}, u32[]{:S(2)}) %collective-permute-start.38) | collective-permute-done | bytes 1245216 | tf_op jit(solution)/shard_map/ppermute | solution.py:25
  579.3 19.1 %collective-permute-done.57 = bf16[256,16]{1,0:T(8,128)(2,1)S(1)} collective-permute-done((bf16[256,16]{1,0:T(8,128)(2,1)S(1)}, bf16[256,16]{1,0:T(8,128)(2,1)S(1)}, u32[]{:S(2)}, u32[]{:S(2)}) %collective-permute-start.57) | collective-permute-done | bytes 8224 | tf_op jit(solution)/shard_map/ppermute | solution.py:25
  611.1 12.1 %open_attention.1 = (bf16[9,1024,64]{2,1,0:T(8,128)(2,1)}, f32[16,576]{1,0:T(8,128)}) custom-call(s32[1]{0:T(128)} %bitcast.1.place_ref, bf16[256,2432]{1,0:T(8,128)(2,1)} %concatenate.127.refs_0_, bf16[256,2432]{1,0:T(8,128)(2,1)} %copy-done.12, bf16[256,2432]{1,0:T(8,128)(2,1)} %copy-done.13, bf16[256,2432]{1,0:T(8,128)(2,1)} %copy-done.11, ...), custom_call_target="tpu_custom_call" | custom-call | flops 2717908992 | bytes 9732096 | tf_op jit(solution)/shard_map/open_attention/pallas_call | solution.py:458
  623.2 51.1 %attend_back.1 = (bf16[9,1024,64]{2,1,0:T(8,128)(2,1)}, bf16[9,1024,64]{2,1,0:T(8,128)(2,1)}, bf16[9,1024,64]{2,1,0:T(8,128)(2,1)}) custom-call(s32[2]{0:T(128)} %bitcast.160, bf16[9,1024,64]{2,1,0:T(8,128)(2,1)} %get-tuple-element.39.q_ref, bf16[9,1024,64]{2,1,0:T(8,128)(2,1)} %get-tuple-element.40.k_ref, bf16[9,1024,64]{2,1,0:T(8,128)(2,1)} %get-tuple-element.41.v_ref, ...), custom_call_target="tpu_custom_call" | custom-call | flops 24159191040 | bytes 18874368 | tf_op jit(solution)/shard_map/attend_back/pallas_call | solution.py:389
  674.3 14.8 %project_back.3 = (bf16[256,2304]{1,0:T(8,128)(2,1)}, bf16[256,2304]{1,0:T(8,128)(2,1)}, bf16[512,48]{1,0:T(8,128)(2,1)}, f32[3,16,576]{2,1,0:T(8,128)}) custom-call(s32[1]{0:T(128)} %bitcast.1.place_ref, s32[10]{0:T(128)} %stack.54.offsets_ref, bf16[9,1024,64]{2,1,0:T(8,128)(2,1)} %get-tuple-element.55.refs_0_, ...), custom_call_target="tpu_custom_call" | custom-call | flops 4076863488 | bytes 12091392 | tf_op jit(solution)/shard_map/project_back/pallas_call | solution.py:595
  690.7 14.8 %project_back.2 = (bf16[256,2304]{1,0:T(8,128)(2,1)}, bf16[256,2304]{1,0:T(8,128)(2,1)}, bf16[512,48]{1,0:T(8,128)(2,1)}, f32[3,16,576]{2,1,0:T(8,128)}) custom-call(s32[1]{0:T(128)} %bitcast.1.place_ref, s32[10]{0:T(128)} %stack.54.offsets_ref, bf16[9,1024,64]{2,1,0:T(8,128)(2,1)} %get-tuple-element.55.refs_0_, ...), custom_call_target="tpu_custom_call" | custom-call | flops 4076863488 | bytes 12091392 | tf_op jit(solution)/shard_map/project_back/pallas_call | solution.py:595
  715.9 3.9 collective-permute-done.59
  720.9 3.7 collective-permute-done.49
  730.3 3.8 collective-permute-done.50
  734.5 3.2 fusion.14
  738.3 4.3 collective-permute-done.51
  744.5 6.3 collective-permute-start.52
  750.8 9.7 %collective-permute-done.61 = bf16[4,80,576]{2,1,0:T(8,128)(2,1)S(1)} collective-permute-done((bf16[4,80,576]{2,1,0:T(8,128)(2,1)S(1)}, bf16[4,80,576]{2,1,0:T(8,128)(2,1)S(1)}, u32[]{:S(2)}, u32[]{:S(2)}) %collective-permute-start.61) | collective-permute-done | bytes 368672 | tf_op jit(solution)/shard_map/ppermute | solution.py:25
  764.0 5.9 collective-permute-done.63
  769.9 3.5 collective-permute-done.64
  783.6 4.0 collective-permute-done.54
  787.6 3.8 collective-permute-done.55
  798.0 19.5 %collective-permute-done.47 = bf16[256,2304]{1,0:T(8,128)(2,1)S(1)} collective-permute-done((bf16[256,2304]{1,0:T(8,128)(2,1)}, bf16[256,2304]{1,0:T(8,128)(2,1)S(1)}, u32[]{:S(2)}, u32[]{:S(2)}) %collective-permute-start.47) | collective-permute-done | bytes 1179680 | tf_op jit(solution)/shard_map/ppermute | solution.py:25
  820.0 3.8 fusion.7
  (419 shorter events, 175.3 us)
Async XLA Ops:
  2.7 17.8 %collective-permute-start.12 = (bf16[11,16,2304]{2,1,0:T(8,128)(2,1)S(1)}, bf16[11,16,2304]{2,1,0:T(8,128)(2,1)}, u32[]{:S(2)}, u32[]{:S(2)}) collective-permute-start(bf16[11,16,2304]{2,1,0:T(8,128)(2,1)S(1)} %fusion.24), channel_id=1, source_target_pairs={{0,1},{1,0},{2,3},{3,2},{4,5},{5,4},{6,7},{7,6},{8,9},{9,8},{10,11... | collective-permute-start | bytes 2433032 | tf_op jit(solution)/shard_map/ppermute | solution.py:25
  6.0 84.3 %collective-permute-start.1 = (bf16[256,2304]{1,0:T(8,128)(2,1)}, bf16[256,2304]{1,0:T(8,128)(2,1)}, u32[]{:S(2)}, u32[]{:S(2)}) collective-permute-start(bf16[256,2304]{1,0:T(8,128)(2,1)} %fusion.3.refs_0_), channel_id=1, source_target_pairs={{0,2},{1,3},{2,0},{3,1},{4,6},{5,7},{6,4},{7,5},{8,10},{9,11},{10,... | collective-permute-start | bytes 3538952 | tf_op jit(solution)/shard_map/ppermute | solution.py:25
  15.7 100.4 %collective-permute-start.3 = (bf16[3,576,576]{2,1,0:T(8,128)(2,1)}, bf16[3,576,576]{2,1,0:T(8,128)(2,1)}, u32[]{:S(2)}, u32[]{:S(2)}) collective-permute-start(bf16[3,576,576]{2,1,0:T(8,128)(2,1)} %get-tuple-element.110), channel_id=1, source_target_pairs={{0,1},{1,0},{2,3},{3,2},{4,5},{5,4},{6,7},{7,6},{8,9},{9,8},{10,11... | collective-permute-start | bytes 5971976 | tf_op jit(solution)/shard_map/ppermute | solution.py:25
  18.8 53.0 %collective-permute-start.4 = (bf16[3,144,576]{2,1,0:T(8,128)(2,1)}, bf16[3,144,576]{2,1,0:T(8,128)(2,1)}, u32[]{:S(2)}, u32[]{:S(2)}) collective-permute-start(bf16[3,144,576]{2,1,0:T(8,128)(2,1)} %get-tuple-element.109), channel_id=1, source_target_pairs={{0,2},{1,3},{2,0},{3,1},{4,6},{5,7},{6,4},{7,5},{8,10},{9,11},{10,... | collective-permute-start | bytes 1493000 | tf_op jit(solution)/shard_map/ppermute | solution.py:25
  19.1 57.3 %collective-permute-start.8 = (bf16[3,144,576]{2,1,0:T(8,128)(2,1)}, bf16[3,144,576]{2,1,0:T(8,128)(2,1)}, u32[]{:S(2)}, u32[]{:S(2)}) collective-permute-start(bf16[3,144,576]{2,1,0:T(8,128)(2,1)} %get-tuple-element.108), channel_id=1, source_target_pairs={{0,3},{1,2},{2,1},{3,0},{4,7},{5,6},{6,5},{7,4},{8,11},{9,10},{10,... | collective-permute-start | bytes 1493000 | tf_op jit(solution)/shard_map/ppermute | solution.py:25
  22.1 45.7 %collective-permute-start.13 = (bf16[11,8,2304]{2,1,0:T(8,128)(2,1)S(1)}, bf16[11,8,2304]{2,1,0:T(8,128)(2,1)}, u32[]{:S(2)}, u32[]{:S(2)}) collective-permute-start(bf16[11,8,2304]{2,1,0:T(8,128)(2,1)S(1)} %constant_dynamic-slice_fusion.19), channel_id=1, source_target_pairs={{0,2},{1,3},{2,0},{3,1},{4,6},{5,7},{6,4},{7,5},{8,10},{9,11},{10,... | collective-permute-start | bytes 1216520 | tf_op jit(solution)/shard_map/ppermute | solution.py:25
  71.8 15.2 %collective-permute-start.5 = (bf16[3,144,576]{2,1,0:T(8,128)(2,1)}, bf16[3,144,576]{2,1,0:T(8,128)(2,1)S(1)}, u32[]{:S(2)}, u32[]{:S(2)}) collective-permute-start(bf16[3,144,576]{2,1,0:T(8,128)(2,1)} %collective-permute-done.4.refs_6_.refs_5_), channel_id=1, source_target_pairs={{0,8},{4,12},{8,0},{12,4},{16,24},{20,28},{24,16},{28,20},{1,9},{5... | collective-permute-start | bytes 1493000 | tf_op jit(solution)/shard_map/ppermute | solution.py:25
  73.6 15.1 %collective-permute-start.6 = (bf16[3,144,576]{2,1,0:T(8,128)(2,1)}, bf16[3,144,576]{2,1,0:T(8,128)(2,1)S(1)}, u32[]{:S(2)}, u32[]{:S(2)}) collective-permute-start(bf16[3,144,576]{2,1,0:T(8,128)(2,1)} %collective-permute-done.4.refs_6_.refs_5_), channel_id=1, source_target_pairs={{0,4},{4,0},{8,12},{12,8},{16,20},{20,16},{24,28},{28,24},{1,5},{5... | collective-permute-start | bytes 1493000 | tf_op jit(solution)/shard_map/ppermute | solution.py:25
  76.5 30.3 %collective-permute-start = (bf16[256,2304]{1,0:T(8,128)(2,1)}, bf16[256,2304]{1,0:T(8,128)(2,1)S(1)}, u32[]{:S(2)}, u32[]{:S(2)}) collective-permute-start(bf16[256,2304]{1,0:T(8,128)(2,1)} %fusion.3.refs_0_), channel_id=1, source_target_pairs={{0,1},{1,0},{2,3},{3,2},{4,5},{5,4},{6,7},{7,6},{8,9},{9,8},{10,11... | collective-permute-start | bytes 3538952 | tf_op jit(solution)/shard_map/ppermute | solution.py:25
  87.0 14.5 %collective-permute-start.9 = (bf16[3,144,576]{2,1,0:T(8,128)(2,1)}, bf16[3,144,576]{2,1,0:T(8,128)(2,1)S(1)}, u32[]{:S(2)}, u32[]{:S(2)}) collective-permute-start(bf16[3,144,576]{2,1,0:T(8,128)(2,1)} %collective-permute-done.8.refs_10_.refs_9_), channel_id=1, source_target_pairs={{0,4},{4,0},{8,12},{12,8},{16,20},{20,16},{24,28},{28,24},{1,5},{5... | collective-permute-start | bytes 1493000 | tf_op jit(solution)/shard_map/ppermute | solution.py:25
  88.7 14.4 %collective-permute-start.10 = (bf16[3,144,576]{2,1,0:T(8,128)(2,1)}, bf16[3,144,576]{2,1,0:T(8,128)(2,1)S(1)}, u32[]{:S(2)}, u32[]{:S(2)}) collective-permute-start(bf16[3,144,576]{2,1,0:T(8,128)(2,1)} %collective-permute-done.8.refs_10_.refs_9_), channel_id=1, source_target_pairs={{0,8},{4,12},{8,0},{12,4},{16,24},{20,28},{24,16},{28,20},{1,9},{5... | collective-permute-start | bytes 1493000 | tf_op jit(solution)/shard_map/ppermute | solution.py:25
  90.3 25.8 %collective-permute-start.2 = (bf16[256,2304]{1,0:T(8,128)(2,1)}, bf16[256,2304]{1,0:T(8,128)(2,1)S(1)}, u32[]{:S(2)}, u32[]{:S(2)}) collective-permute-start(bf16[256,2304]{1,0:T(8,128)(2,1)} %collective-permute-done.1.refs_2_), channel_id=1, source_target_pairs={{0,1},{1,0},{2,3},{3,2},{4,5},{5,4},{6,7},{7,6},{8,9},{9,8},{10,11... | collective-permute-start | bytes 3538952 | tf_op jit(solution)/shard_map/ppermute | solution.py:25
  101.5 13.4 %collective-permute-start.7 = (bf16[3,144,576]{2,1,0:T(8,128)(2,1)S(1)}, bf16[3,144,576]{2,1,0:T(8,128)(2,1)S(1)}, u32[]{:S(2)}, u32[]{:S(2)}) collective-permute-start(bf16[3,144,576]{2,1,0:T(8,128)(2,1)S(1)} %collective-permute-done.5.refs_7_.refs_6_), channel_id=1, source_target_pairs={{0,4},{4,0},{8,12},{12,8},{16,20},{20,16},{24,28},{28,24},{1,5},{5... | collective-permute-start | bytes 1493000 | tf_op jit(solution)/shard_map/ppermute | solution.py:25
  106.7 147.2 %collective-permute-start.35 = (bf16[256,2304]{1,0:T(8,128)(2,1)}, bf16[256,2304]{1,0:T(8,128)(2,1)}, u32[]{:S(2)}, u32[]{:S(2)}) collective-permute-start(bf16[256,2304]{1,0:T(8,128)(2,1)} %fusion.refs_2_), channel_id=1, source_target_pairs={{0,2},{1,3},{2,0},{3,1},{4,6},{5,7},{6,4},{7,5},{8,10},{9,11},{10,... | collective-permute-start | bytes 3538952 | tf_op jit(solution)/shard_map/ppermute | solution.py:25
  114.9 140.6 %collective-permute-start.19 = (bf16[256,2304]{1,0:T(8,128)(2,1)}, bf16[256,2304]{1,0:T(8,128)(2,1)}, u32[]{:S(2)}, u32[]{:S(2)}) collective-permute-start(bf16[256,2304]{1,0:T(8,128)(2,1)} %fusion.refs_2_), channel_id=1, source_target_pairs={{0,1},{1,0},{2,3},{3,2},{4,5},{5,4},{6,7},{7,6},{8,9},{9,8},{10,11... | collective-permute-start | bytes 3538952 | tf_op jit(solution)/shard_map/ppermute | solution.py:25
  167.2 23.2 %collective-permute-start.29 = (bf16[3,16,5760]{2,1,0:T(8,128)(2,1)S(1)}, bf16[3,16,5760]{2,1,0:T(8,128)(2,1)S(1)}, u32[]{:S(2)}, u32[]{:S(2)}) collective-permute-start(bf16[3,16,5760]{2,1,0:T(8,128)(2,1)S(1)} %fusion.27), channel_id=1, source_target_pairs={{0,1},{1,0},{2,3},{3,2},{4,5},{5,4},{6,7},{7,6},{8,9},{9,8},{10,11... | collective-permute-start | bytes 1658888 | tf_op jit(solution)/shard_map/ppermute | solution.py:25
  173.6 17.5 %collective-permute-start.15 = (bf16[256,2432]{1,0:T(8,128)(2,1)}, bf16[256,2432]{1,0:T(8,128)(2,1)S(1)}, u32[]{:S(2)}, u32[]{:S(2)}) collective-permute-start(bf16[256,2432]{1,0:T(8,128)(2,1)} %get-tuple-element.43), channel_id=1, source_target_pairs={{0,1},{1,0},{2,3},{3,2},{4,5},{5,4},{6,7},{7,6},{8,9},{9,8},{10,11... | collective-permute-start | bytes 3735560 | tf_op jit(solution)/shard_map/ppermute | solution.py:25
  176.3 30.5 %collective-permute-start.17 = (bf16[256,2432]{1,0:T(8,128)(2,1)}, bf16[256,2432]{1,0:T(8,128)(2,1)}, u32[]{:S(2)}, u32[]{:S(2)}) collective-permute-start(bf16[256,2432]{1,0:T(8,128)(2,1)} %add_convert_fusion.2), channel_id=1, source_target_pairs={{0,2},{1,3},{2,0},{3,1},{4,6},{5,7},{6,4},{7,5},{8,10},{9,11},{10,... | collective-permute-start | bytes 3735560 | tf_op jit(solution)/shard_map/ppermute | solution.py:25
  190.4 35.2 %collective-permute-start.21 = (bf16[2,144,1440]{2,1,0:T(8,128)(2,1)S(1)}, bf16[2,144,1440]{2,1,0:T(8,128)(2,1)S(1)}, u32[]{:S(2)}, u32[]{:S(2)}) collective-permute-start(bf16[2,144,1440]{2,1,0:T(8,128)(2,1)S(1)} %copy-done.40), channel_id=1, source_target_pairs={{0,2},{1,3},{2,0},{3,1},{4,6},{5,7},{6,4},{7,5},{8,10},{9,11},{10,... | collective-permute-start | bytes 2488328 | tf_op jit(solution)/shard_map/ppermute | solution.py:25
  191.6 60.2 %collective-permute-start.25 = (bf16[2,144,1440]{2,1,0:T(8,128)(2,1)S(1)}, bf16[2,144,1440]{2,1,0:T(8,128)(2,1)S(1)}, u32[]{:S(2)}, u32[]{:S(2)}) collective-permute-start(bf16[2,144,1440]{2,1,0:T(8,128)(2,1)S(1)} %copy-done.39), channel_id=1, source_target_pairs={{0,3},{1,2},{2,1},{3,0},{4,7},{5,6},{6,5},{7,4},{8,11},{9,10},{10,... | collective-permute-start | bytes 2488328 | tf_op jit(solution)/shard_map/ppermute | solution.py:25
  206.8 43.3 %collective-permute-start.30 = (bf16[3,8,5760]{2,1,0:T(8,128)(2,1)S(1)}, bf16[3,8,5760]{2,1,0:T(8,128)(2,1)S(1)}, u32[]{:S(2)}, u32[]{:S(2)}) collective-permute-start(bf16[3,8,5760]{2,1,0:T(8,128)(2,1)S(1)} %constant_dynamic-slice_fusion.13), channel_id=1, source_target_pairs={{0,2},{1,3},{2,0},{3,1},{4,6},{5,7},{6,4},{7,5},{8,10},{9,11},{10,... | collective-permute-start | bytes 829448 | tf_op jit(solution)/shard_map/ppermute | solution.py:25
  225.6 96.1 %collective-permute-start.20 = (bf16[2,576,1440]{2,1,0:T(8,128)(2,1)S(1)}, bf16[2,576,1440]{2,1,0:T(8,128)(2,1)S(1)}, u32[]{:S(2)}, u32[]{:S(2)}) collective-permute-start(bf16[2,576,1440]{2,1,0:T(8,128)(2,1)S(1)} %get-tuple-element.106), channel_id=1, source_target_pairs={{0,1},{1,0},{2,3},{3,2},{4,5},{5,4},{6,7},{7,6},{8,9},{9,8},{10,11... | collective-permute-start | bytes 9953288 | tf_op jit(solution)/shard_map/ppermute | solution.py:25
  251.8 22.5 %collective-permute-start.22 = (bf16[2,144,1440]{2,1,0:T(8,128)(2,1)S(1)}, bf16[2,144,1440]{2,1,0:T(8,128)(2,1)S(1)}, u32[]{:S(2)}, u32[]{:S(2)}) collective-permute-start(bf16[2,144,1440]{2,1,0:T(8,128)(2,1)S(1)} %collective-permute-done.21.refs_6_), channel_id=1, source_target_pairs={{0,8},{4,12},{8,0},{12,4},{16,24},{20,28},{24,16},{28,20},{1,9},{5... | collective-permute-start | bytes 2488328 | tf_op jit(solution)/shard_map/ppermute | solution.py:25
  253.4 41.9 %collective-permute-start.23 = (bf16[2,144,1440]{2,1,0:T(8,128)(2,1)S(1)}, bf16[2,144,1440]{2,1,0:T(8,128)(2,1)S(1)}, u32[]{:S(2)}, u32[]{:S(2)}) collective-permute-start(bf16[2,144,1440]{2,1,0:T(8,128)(2,1)S(1)} %collective-permute-done.21.refs_6_), channel_id=1, source_target_pairs={{0,4},{4,0},{8,12},{12,8},{16,20},{20,16},{24,28},{28,24},{1,5},{5... | collective-permute-start | bytes 2488328 | tf_op jit(solution)/shard_map/ppermute | solution.py:25
  253.9 40.9 %collective-permute-start.26 = (bf16[2,144,1440]{2,1,0:T(8,128)(2,1)S(1)}, bf16[2,144,1440]{2,1,0:T(8,128)(2,1)S(1)}, u32[]{:S(2)}, u32[]{:S(2)}) collective-permute-start(bf16[2,144,1440]{2,1,0:T(8,128)(2,1)S(1)} %collective-permute-done.25.refs_10_), channel_id=1, source_target_pairs={{0,4},{4,0},{8,12},{12,8},{16,20},{20,16},{24,28},{28,24},{1,5},{5... | collective-permute-start | bytes 2488328 | tf_op jit(solution)/shard_map/ppermute | solution.py:25
  255.4 41.4 %collective-permute-start.27 = (bf16[2,144,1440]{2,1,0:T(8,128)(2,1)S(1)}, bf16[2,144,1440]{2,1,0:T(8,128)(2,1)S(1)}, u32[]{:S(2)}, u32[]{:S(2)}) collective-permute-start(bf16[2,144,1440]{2,1,0:T(8,128)(2,1)S(1)} %collective-permute-done.25.refs_10_), channel_id=1, source_target_pairs={{0,8},{4,12},{8,0},{12,4},{16,24},{20,28},{24,16},{28,20},{1,9},{5... | collective-permute-start | bytes 2488328 | tf_op jit(solution)/shard_map/ppermute | solution.py:25
  274.3 38.8 %collective-permute-start.24 = (bf16[2,144,1440]{2,1,0:T(8,128)(2,1)S(1)}, bf16[2,144,1440]{2,1,0:T(8,128)(2,1)S(1)}, u32[]{:S(2)}, u32[]{:S(2)}) collective-permute-start(bf16[2,144,1440]{2,1,0:T(8,128)(2,1)S(1)} %collective-permute-done.22.refs_7_), channel_id=1, source_target_pairs={{0,4},{4,0},{8,12},{12,8},{16,20},{20,16},{24,28},{28,24},{1,5},{5... | collective-permute-start | bytes 2488328 | tf_op jit(solution)/shard_map/ppermute | solution.py:25
  294.9 26.9 %collective-permute-start.28 = (bf16[2,144,1440]{2,1,0:T(8,128)(2,1)S(1)}, bf16[2,144,1440]{2,1,0:T(8,128)(2,1)S(1)}, u32[]{:S(2)}, u32[]{:S(2)}) collective-permute-start(bf16[2,144,1440]{2,1,0:T(8,128)(2,1)S(1)} %collective-permute-done.26.refs_11_), channel_id=1, source_target_pairs={{0,8},{4,12},{8,0},{12,4},{16,24},{20,28},{24,16},{28,20},{1,9},{5... | collective-permute-start | bytes 2488328 | tf_op jit(solution)/shard_map/ppermute | solution.py:25
  295.3 26.4 %collective-permute-start.33 = (bf16[256,2304]{1,0:T(8,128)(2,1)S(1)}, bf16[256,2304]{1,0:T(8,128)(2,1)}, u32[]{:S(2)}, u32[]{:S(2)}) collective-permute-start(bf16[256,2304]{1,0:T(8,128)(2,1)S(1)} %multiply_convert_fusion.1.refs_0_), channel_id=1, source_target_pairs={{0,2},{1,3},{2,0},{3,1},{4,6},{5,7},{6,4},{7,5},{8,10},{9,11},{10,... | collective-permute-start | bytes 3538952 | tf_op jit(solution)/shard_map/ppermute | solution.py:25
  296.8 24.9 %collective-permute-start.18 = (bf16[256,2304]{1,0:T(8,128)(2,1)S(1)}, bf16[256,2304]{1,0:T(8,128)(2,1)S(1)}, u32[]{:S(2)}, u32[]{:S(2)}) collective-permute-start(bf16[256,2304]{1,0:T(8,128)(2,1)S(1)} %multiply_convert_fusion.1.refs_0_), channel_id=1, source_target_pairs={{0,1},{1,0},{2,3},{3,2},{4,5},{5,4},{6,7},{7,6},{8,9},{9,8},{10,11... | collective-permute-start | bytes 3538952 | tf_op jit(solution)/shard_map/ppermute | solution.py:25
  313.1 60.5 %collective-permute-start.36 = (bf16[256,2304]{1,0:T(8,128)(2,1)}, bf16[256,2304]{1,0:T(8,128)(2,1)}, u32[]{:S(2)}, u32[]{:S(2)}) collective-permute-start(bf16[256,2304]{1,0:T(8,128)(2,1)} %collective-permute-done.35.refs_2_), channel_id=1, source_target_pairs={{0,1},{1,0},{2,3},{3,2},{4,5},{5,4},{6,7},{7,6},{8,9},{9,8},{10,11... | collective-permute-start | bytes 3538952 | tf_op jit(solution)/shard_map/ppermute | solution.py:25
  321.7 51.9 %collective-permute-start.34 = (bf16[256,2304]{1,0:T(8,128)(2,1)}, bf16[256,2304]{1,0:T(8,128)(2,1)}, u32[]{:S(2)}, u32[]{:S(2)}) collective-permute-start(bf16[256,2304]{1,0:T(8,128)(2,1)} %collective-permute-done.33.refs_0_), channel_id=1, source_target_pairs={{0,1},{1,0},{2,3},{3,2},{4,5},{5,4},{6,7},{7,6},{8,9},{9,8},{10,11... | collective-permute-start | bytes 3538952 | tf_op jit(solution)/shard_map/ppermute | solution.py:25
  449.4 30.8 %collective-permute-start.67 = (bf16[4,48,1440]{2,1,0:T(8,128)(2,1)}, bf16[4,48,1440]{2,1,0:T(8,128)(2,1)}, u32[]{:S(2)}, u32[]{:S(2)}) collective-permute-start(bf16[4,48,1440]{2,1,0:T(8,128)(2,1)} %constant_dynamic-slice_fusion), channel_id=1, source_target_pairs={{0,16},{4,20},{8,24},{12,28},{16,0},{20,4},{24,8},{28,12},{1,17},{... | collective-permute-start | bytes 1658888 | tf_op jit(solution)/shard_map/ppermute | solution.py:25
  479.2 77.2 %collective-permute-start.32 = (bf16[256,2432]{1,0:T(8,128)(2,1)}, bf16[256,2432]{1,0:T(8,128)(2,1)}, u32[]{:S(2)}, u32[]{:S(2)}) collective-permute-start(bf16[256,2432]{1,0:T(8,128)(2,1)} %get-tuple-element.47), channel_id=1, source_target_pairs={{0,1},{1,0},{2,3},{3,2},{4,5},{5,4},{6,7},{7,6},{8,9},{9,8},{10,11... | collective-permute-start | bytes 3735560 | tf_op jit(solution)/shard_map/ppermute | solution.py:25
  479.2 42.7 %collective-permute-start.39 = (bf16[256,2432]{1,0:T(8,128)(2,1)}, bf16[256,2432]{1,0:T(8,128)(2,1)}, u32[]{:S(2)}, u32[]{:S(2)}) collective-permute-start(bf16[256,2432]{1,0:T(8,128)(2,1)} %get-tuple-element.51), channel_id=1, source_target_pairs={{0,1},{1,0},{2,3},{3,2},{4,5},{5,4},{6,7},{7,6},{8,9},{9,8},{10,11... | collective-permute-start | bytes 3735560 | tf_op jit(solution)/shard_map/ppermute | solution.py:25
  479.7 37.9 %collective-permute-start.37 = (bf16[256,2432]{1,0:T(8,128)(2,1)}, bf16[256,2432]{1,0:T(8,128)(2,1)}, u32[]{:S(2)}, u32[]{:S(2)}) collective-permute-start(bf16[256,2432]{1,0:T(8,128)(2,1)} %get-tuple-element.49), channel_id=1, source_target_pairs={{0,1},{1,0},{2,3},{3,2},{4,5},{5,4},{6,7},{7,6},{8,9},{9,8},{10,11... | collective-permute-start | bytes 3735560 | tf_op jit(solution)/shard_map/ppermute | solution.py:25
  479.7 32.8 %collective-permute-start.40 = (bf16[256,2432]{1,0:T(8,128)(2,1)}, bf16[256,2432]{1,0:T(8,128)(2,1)}, u32[]{:S(2)}, u32[]{:S(2)}) collective-permute-start(bf16[256,2432]{1,0:T(8,128)(2,1)} %get-tuple-element.53), channel_id=1, source_target_pairs={{0,1},{1,0},{2,3},{3,2},{4,5},{5,4},{6,7},{7,6},{8,9},{9,8},{10,11... | collective-permute-start | bytes 3735560 | tf_op jit(solution)/shard_map/ppermute | solution.py:25
  514.2 30.3 %collective-permute-start.41 = (bf16[256,2432]{1,0:T(8,128)(2,1)S(1)}, bf16[256,2432]{1,0:T(8,128)(2,1)S(1)}, u32[]{:S(2)}, u32[]{:S(2)}) collective-permute-start(bf16[256,2432]{1,0:T(8,128)(2,1)S(1)} %add_convert_fusion), channel_id=1, source_target_pairs={{0,2},{1,3},{2,0},{3,1},{4,6},{5,7},{6,4},{7,5},{8,10},{9,11},{10,... | collective-permute-start | bytes 3735560 | tf_op jit(solution)/shard_map/ppermute | solution.py:25
  520.9 50.3 %collective-permute-start.38 = (bf16[256,2432]{1,0:T(8,128)(2,1)}, bf16[256,2432]{1,0:T(8,128)(2,1)}, u32[]{:S(2)}, u32[]{:S(2)}) collective-permute-start(bf16[256,2432]{1,0:T(8,128)(2,1)} %add_convert_fusion.1), channel_id=1, source_target_pairs={{0,2},{1,3},{2,0},{3,1},{4,6},{5,7},{6,4},{7,5},{8,10},{9,11},{10,... | collective-permute-start | bytes 3735560 | tf_op jit(solution)/shard_map/ppermute | solution.py:25
  555.2 50.2 %collective-permute-start.42 = (bf16[256,2432]{1,0:T(8,128)(2,1)}, bf16[256,2432]{1,0:T(8,128)(2,1)S(1)}, u32[]{:S(2)}, u32[]{:S(2)}) collective-permute-start(bf16[256,2432]{1,0:T(8,128)(2,1)} %concatenate.127.refs_0_), channel_id=1, source_target_pairs={{0,1},{1,0},{2,3},{3,2},{4,5},{5,4},{6,7},{7,6},{8,9},{9,8},{10,11... | collective-permute-start | bytes 3735560 | tf_op jit(solution)/shard_map/ppermute | solution.py:25
  555.2 46.4 %collective-permute-start.43 = (bf16[256,2432]{1,0:T(8,128)(2,1)}, bf16[256,2432]{1,0:T(8,128)(2,1)S(1)}, u32[]{:S(2)}, u32[]{:S(2)}) collective-permute-start(bf16[256,2432]{1,0:T(8,128)(2,1)} %concatenate.127.refs_0_), channel_id=1, source_target_pairs={{0,2},{1,3},{2,0},{3,1},{4,6},{5,7},{6,4},{7,5},{8,10},{9,11},{10,... | collective-permute-start | bytes 3735560 | tf_op jit(solution)/shard_map/ppermute | solution.py:25
  573.9 24.5 %collective-permute-start.57 = (bf16[256,16]{1,0:T(8,128)(2,1)S(1)}, bf16[256,16]{1,0:T(8,128)(2,1)S(1)}, u32[]{:S(2)}, u32[]{:S(2)}) collective-permute-start(bf16[256,16]{1,0:T(8,128)(2,1)S(1)} %slice.330), channel_id=1, source_target_pairs={{0,2},{1,3},{2,0},{3,1},{4,6},{5,7},{6,4},{7,5},{8,10},{9,11},{10,... | collective-permute-start | bytes 24584 | tf_op jit(solution)/shard_map/ppermute | solution.py:25
  575.1 24.9 %collective-permute-start.56 = (bf16[256,16]{1,0:T(8,128)(2,1)S(1)}, bf16[256,16]{1,0:T(8,128)(2,1)S(1)}, u32[]{:S(2)}, u32[]{:S(2)}) collective-permute-start(bf16[256,16]{1,0:T(8,128)(2,1)S(1)} %slice.330), channel_id=1, source_target_pairs={{0,1},{1,0},{2,3},{3,2},{4,5},{5,4},{6,7},{7,6},{8,9},{9,8},{10,11... | collective-permute-start | bytes 24584 | tf_op jit(solution)/shard_map/ppermute | solution.py:25
  730.2 30.3 %collective-permute-start.61 = (bf16[4,80,576]{2,1,0:T(8,128)(2,1)S(1)}, bf16[4,80,576]{2,1,0:T(8,128)(2,1)S(1)}, u32[]{:S(2)}, u32[]{:S(2)}) collective-permute-start(bf16[4,80,576]{2,1,0:T(8,128)(2,1)S(1)} %constant_dynamic-slice_fusion.3), channel_id=1, source_target_pairs={{0,16},{4,20},{8,24},{12,28},{16,0},{20,4},{24,8},{28,12},{1,17},{... | collective-permute-start | bytes 1105928 | tf_op jit(solution)/shard_map/ppermute | solution.py:25
  737.8 42.7 %collective-permute-start.46 = (bf16[256,2304]{1,0:T(8,128)(2,1)}, bf16[256,2304]{1,0:T(8,128)(2,1)}, u32[]{:S(2)}, u32[]{:S(2)}) collective-permute-start(bf16[256,2304]{1,0:T(8,128)(2,1)} %get-tuple-element.62), channel_id=1, source_target_pairs={{0,1},{1,0},{2,3},{3,2},{4,5},{5,4},{6,7},{7,6},{8,9},{9,8},{10,11... | collective-permute-start | bytes 3538952 | tf_op jit(solution)/shard_map/ppermute | solution.py:25
  737.8 60.2 %collective-permute-start.45 = (bf16[256,2304]{1,0:T(8,128)(2,1)}, bf16[256,2304]{1,0:T(8,128)(2,1)}, u32[]{:S(2)}, u32[]{:S(2)}) collective-permute-start(bf16[256,2304]{1,0:T(8,128)(2,1)} %get-tuple-element.60), channel_id=1, source_target_pairs={{0,1},{1,0},{2,3},{3,2},{4,5},{5,4},{6,7},{7,6},{8,9},{9,8},{10,11... | collective-permute-start | bytes 3538952 | tf_op jit(solution)/shard_map/ppermute | solution.py:25
  744.5 29.6 %collective-permute-start.52 = (bf16[4,96,576]{2,1,0:T(8,128)(2,1)}, bf16[4,96,576]{2,1,0:T(8,128)(2,1)}, u32[]{:S(2)}, u32[]{:S(2)}) collective-permute-start(bf16[4,96,576]{2,1,0:T(8,128)(2,1)} %constant_dynamic-slice_fusion.9), channel_id=1, source_target_pairs={{0,16},{4,20},{8,24},{12,28},{16,0},{20,4},{24,8},{28,12},{1,17},{... | collective-permute-start | bytes 1327112 | tf_op jit(solution)/shard_map/ppermute | solution.py:25
  783.1 34.3 %collective-permute-start.47 = (bf16[256,2304]{1,0:T(8,128)(2,1)}, bf16[256,2304]{1,0:T(8,128)(2,1)S(1)}, u32[]{:S(2)}, u32[]{:S(2)}) collective-permute-start(bf16[256,2304]{1,0:T(8,128)(2,1)} %add_convert_fusion.3), channel_id=1, source_target_pairs={{0,2},{1,3},{2,0},{3,1},{4,6},{5,7},{6,4},{7,5},{8,10},{9,11},{10,... | collective-permute-start | bytes 3538952 | tf_op jit(solution)/shard_map/ppermute | solution.py:25
  (104 other events, 1046.6 us)

commit v2 on v1

--- a/solution.py
+++ b/solution.py
@@ -33,27 +33,6 @@
     return hop(values, "shard", 2)
 
 
-def gather_tokens(own):
-    far = across(own)
-    near = core(own)
-    return own, near, far, core(far)
-
-
-def scatter_tokens(blocks):
-    chip_sum = (blocks[2].astype(F32) + core(blocks[3]).astype(F32)).astype(BF16)
-    far = across(chip_sum)
-    near = core(blocks[1])
-    return blocks[0].astype(F32) + near.astype(F32) + far.astype(F32)
-
-
-def sum_group(values):
-    other = rows_of(core(values), 4)
-    other = jnp.concatenate([other[1], other[0], other[3], other[2]])
-    values = (values.astype(F32) + other.astype(F32)).astype(BF16)
-    far = rows_of(across(values), 2)
-    return (values.astype(F32) + jnp.concatenate([far[1], far[0]]).astype(F32)).astype(BF16)
-
-
 def rows_of(values, count):
     size = values.shape[0] // count
     return tuple(values[i * size : (i + 1) * size] for i in range(count))
@@ -83,84 +62,102 @@
     return lax.dot_general(left, right, (((0,), (0,)), ((), ())), preferred_element_type=F32)
 
 
-def picked(bank, pick, place):
+def pad_columns(pieces, width):
+    used = sum(piece.shape[1] for piece in pieces)
+    rest = jnp.zeros((pieces[0].shape[0], width - used), pieces[0].dtype)
+    return jnp.concatenate(list(pieces) + [rest], axis=1)
+
+
+def start_reps(values, rep_place):
+    buffer = jnp.zeros((lax.axis_size("rep"),) + values.shape, values.dtype)
+    return lax.dynamic_update_slice_in_dim(buffer, values[None], rep_place, 0)
+
+
+def reps_step(buffer, rep_place, bit):
+    base = (rep_place // bit) * bit
+    have = lax.dynamic_slice_in_dim(buffer, base, bit, 0)
+    return lax.dynamic_update_slice_in_dim(buffer, hop(have, "rep", bit), base ^ bit, 0)
+
+
+def reps_rest(buffer, rep_place, bit):
+    while bit < lax.axis_size("rep"):
+        buffer = reps_step(buffer, rep_place, bit)
+        bit *= 2
+    return buffer
+
+
+def send_sums(everyone, chosen, place):
+    group = lax.axis_size("shard")
+    per = chosen.shape[1] // group
+    sent = []
+    for j in range(group):
+        marks = lax.dynamic_slice_in_dim(chosen, (place ^ j) * per, per, 1)
+        sums = jnp.sum(marks[:, :, None, None] * everyone[:, None].astype(F32), axis=0).astype(BF16)
+        sent.append(hop(sums, "shard", j) if j else sums)
+    return sent
+
+
+def arrange_sums(sent, place):
+    got = jnp.zeros((len(sent),) + sent[0].shape, BF16)
+    for j, piece in enumerate(sent):
+        got = lax.dynamic_update_slice_in_dim(got, piece[None], place ^ j, 0)
+    return got
+
+
+def add_relative(values, other, bit):
+    blocks = rows_of(other, 4)
+    other = jnp.concatenate([blocks[i ^ bit] for i in range(4)])
+    return (values.astype(F32) + other.astype(F32)).astype(BF16)
+
+
+def chip_picked(bank, pick, place):
     per = bank.shape[1]
     rank = bank.shape[2]
     owner = pick // per
     mine = lax.dynamic_index_in_dim(bank, pick % per, 1, keepdims=False)
     mine = jnp.where(owner == place, mine, jnp.zeros_like(mine))
     chip = mine + core(mine)
-    inside = place % 2
-    part = lax.dynamic_slice_in_dim(chip, inside * (rank // 2), rank // 2, 1)
-    far = across(part)
+    return chip, lax.dynamic_slice_in_dim(chip, (place % 2) * (rank // 2), rank // 2, 1)
+
+
+def whole_picked(chip, far, place):
     other = core(far)
-    low = jnp.where(inside == 0, far, other)
-    high = jnp.where(inside == 0, other, far)
+    low = jnp.where(place % 2 == 0, far, other)
+    high = jnp.where(place % 2 == 0, other, far)
     return chip + jnp.concatenate([low, high], axis=1)
 
 
-def pad_columns(pieces, width):
-    used = sum(piece.shape[1] for piece in pieces)
-    rest = jnp.zeros((pieces[0].shape[0], width - used), pieces[0].dtype)
-    return jnp.concatenate(list(pieces) + [rest], axis=1)
-
-
-def gather_reps(values, rep_place):
-    size = lax.axis_size("rep")
-    buffer = jnp.zeros((size,) + values.shape, values.dtype)
-    buffer = lax.dynamic_update_slice_in_dim(buffer, values[None], rep_place, 0)
-    bit = 1
-    while bit < size:
-        base = (rep_place // bit) * bit
-        have = lax.dynamic_slice_in_dim(buffer, base, bit, 0)
-        got = hop(have, "rep", bit)
-        buffer = lax.dynamic_update_slice_in_dim(buffer, got, base ^ bit, 0)
-        bit *= 2
-    return buffer
-
-
-def owned_sums(values, chosen, place, rep_place):
-    group = lax.axis_size("shard")
-    everyone = gather_reps(values.astype(BF16), rep_place)
-    adapters = chosen.shape[1]
-    per = adapters // group
-
-    def sums_for(owner):
-        marks = lax.dynamic_slice_in_dim(chosen, owner * per, per, 1)
-        return jnp.sum(
-            marks[:, :, None, None] * everyone[:, None].astype(F32), axis=0
-        ).astype(BF16)
-
-    got = jnp.zeros((group, per) + values.shape, BF16)
-    got = lax.dynamic_update_slice_in_dim(got, sums_for(place)[None], place, 0)
-    for j in range(1, group):
-        arrived = hop(sums_for(place ^ j), "shard", j)
-        got = lax.dynamic_update_slice_in_dim(got, arrived[None], place ^ j, 0)
-    return jnp.concatenate([got[i] for i in range(group)], axis=-1).astype(F32)
-
-
-def exchange(weight, size, place, rep_place):
+def after(value, *others):
+    return lax.optimization_barrier((value, others))[0]
+
+
+def leaving(weight, size, place, rep_place):
+    quarter = weight.shape[1] // 4
+    part = rep_place % 4
+    return [
+        lax.dynamic_slice(
+            weight, (0, part * quarter, (place ^ j) * size), (weight.shape[0], quarter, size)
+        )
+        for j in (2, 3)
+    ]
+
+
+def finish(weight, size, first, second, third, place, rep_place, near):
     rows = weight.shape[1]
     quarter = rows // 4
     part = rep_place % 4
-
-    def columns(owner):
-        return lax.dynamic_slice_in_dim(weight, owner * size, size, 2)
-
-    pieces = [(place * rows, columns(place)), ((place ^ 1) * rows, core(columns(place ^ 1)))]
-    for j in (2, 3):
-        mine = lax.dynamic_slice(
-            weight, (0, part * quarter, (place ^ j) * size), (weight.shape[0], quarter, size)
-        )
-        first = hop(mine, "shard", j)
-        near, late = (2, 1) if j == 2 else (1, 2)
-        second = hop(first, "rep", near)
-        third = hop(first, "rep", late)
-        fourth = hop(second, "rep", late)
-        for bits, piece in ((0, first), (near, second), (late, third), (near ^ late, fourth)):
+    own = lax.dynamic_slice_in_dim(weight, place * size, size, 2)
+    pieces = [(place * rows, own), ((place ^ 1) * rows, near)]
+    for number, (j, one, two) in enumerate(((2, 2, 1), (3, 1, 2))):
+        parts = (first[number], second[number], *third[number])
+        for bits, piece in zip((0, one, two, one ^ two), parts):
             pieces.append(((place ^ j) * rows + (part ^ bits) * quarter, piece))
     offsets = jnp.stack([row.astype(jnp.int32) for row, _ in pieces])
     return offsets, [piece for _, piece in pieces]
+
+
+def near_columns(weight, size, place):
+    return core(lax.dynamic_slice_in_dim(weight, (place ^ 1) * size, size, 2))
 
 
 def load_pieces(offsets, pieces, whole, sems):
@@ -331,14 +328,14 @@
     )(starts, query, key, value)
 
 
-def attend_back(starts, query, key, value, grad, cosine, sine, rows):
-    heads, length, _ = query.shape
+def attend_back(starts, place, query, key, value, near, far, cosine, sine, rows, first, heads):
+    length = query.shape[1]
     count = length // rows
     scale = 1.0 / math.sqrt(HDIM)
     factor = LOG2E * scale
 
     def kernel(
-        starts_ref, q_ref, k_ref, v_ref, g_ref, cos_ref, sin_ref, dq_ref, dk_ref, dv_ref,
+        starts_ref, place_ref, q_ref, k_ref, v_ref, near_ref, far_ref, cos_ref, sin_ref, dq_ref, dk_ref, dv_ref,
         bias, key_sum, value_sum, key_turned,
     ):
         @pl.when(pl.program_id(0) == 0)
@@ -356,7 +353,9 @@
         def one(block, extra):
             low, high = block * rows, (block + 1 + extra) * rows
             q = q_ref[0, low : low + rows, :]
-            g = g_ref[0, low : low + rows, :]
+            relative = place_ref[0] ^ block
+            at = pl.multiple_of((relative % 2) * rows, rows)
+            g = jnp.where(relative < 2, near_ref[0, pl.ds(at, rows), :], far_ref[0, pl.ds(at, rows), :])
             raw = dot_t(k_ref[0, low:high, :], q) + bias[block, : high - low, :]
             if block:
                 raw = jnp.concatenate([dot_t(k_ref[0, :low, :], q), raw], axis=0)
@@ -384,13 +383,15 @@
         dk_ref[0] = turn(key_sum[...] * scale, cos_ref[...], -sin_ref[...]).astype(BF16)
         dv_ref[0] = value_sum[...].astype(BF16)
 
-    spec = pl.BlockSpec((1, length, HDIM), lambda h: (h, 0, 0))
+    spec = pl.BlockSpec((1, length, HDIM), lambda h: (first + h, 0, 0))
+    half = pl.BlockSpec((1, length // 2, HDIM), lambda h: (first + h, 0, 0))
+    out = pl.BlockSpec((1, length, HDIM), lambda h: (h, 0, 0))
     table = pl.BlockSpec((length, HDIM), lambda h: (0, 0))
     return call(
         kernel,
-        [jax.ShapeDtypeStruct(query.shape, BF16)] * 3,
-        [smem(), spec, spec, spec, spec, table, table],
-        [spec] * 3,
+        [jax.ShapeDtypeStruct((heads, length, HDIM), BF16)] * 3,
+        [smem(), smem(), spec, spec, spec, half, half, table, table],
+        [out] * 3,
         [
             pltpu.VMEM((count, 2 * rows, rows), F32),
             pltpu.VMEM((length, HDIM), F32),
@@ -401,11 +402,13 @@
         32 * heads * length * HDIM,
         "attend_back",
         grid=(heads,),
-    )(starts, query, key, value, grad, cosine, sine)
-
-
-def rows_by_heads(ref, start, rows):
-    return jnp.concatenate([ref[head, pl.ds(start, rows), :] for head in range(ref.shape[0])], axis=1)
+    )(starts, place[None], query, key, value, near, far, cosine, sine)
+
+
+def rows_by_heads(refs, start, rows):
+    return jnp.concatenate(
+        [ref[head, pl.ds(start, rows), :] for ref in refs for head in range(ref.shape[0])], axis=1
+    )
 
 
 def close_attention(mixed, place, weight, a_out, wanted, rows):
@@ -415,7 +418,7 @@
     def kernel(place_ref, m_ref, w_ref, a_ref, *outs):
         for block, out in zip(wanted, outs):
             start = pl.multiple_of((place_ref[0] ^ block) * rows, rows)
-            here = rows_by_heads(m_ref, start, rows)
+            here = rows_by_heads([m_ref], start, rows)
             out[:, :width] = dot(here, w_ref[...]).astype(BF16)
             narrow = dot_t(here, a_ref[...]).astype(BF16)
             out[:, width:] = jnp.concatenate(
@@ -434,7 +437,7 @@
     )(place[None], mixed, weight, a_out)
 
 
-def open_attention(blocks, place, mixed, weight, a_out, b_out):
+def open_attention(blocks, wanted, place, mixed, weight, a_out, b_out):
     rows, width_ext = blocks[0].shape
     size, width = weight.shape
     rank = a_out.shape[0]
@@ -446,19 +449,20 @@
         m_ref, w_ref, a_ref, b_ref, out, sum_ref = refs
         total = jnp.zeros((rank, size), F32)
         for block in range(count):
-            start = pl.multiple_of((place_ref[0] ^ block) * rows, rows)
+            start = pl.multiple_of((place_ref[0] ^ wanted[block]) * rows, rows)
             grad = g_refs[block][:, :width]
             narrow = dot_t(grad, b_ref[...]).astype(BF16)
             back = dot_t(grad, w_ref[...]) + dot(narrow, a_ref[...])
             for head in range(heads):
-                out[head, pl.ds(start, rows), :] = back[:, head * HDIM : (head + 1) * HDIM].astype(BF16)
-            total = total + t_dot(narrow, rows_by_heads(m_ref, start, rows))
+                part = back[:, head * HDIM : (head + 1) * HDIM]
+                out[head, block * rows : (block + 1) * rows, :] = part.astype(BF16)
+            total = total + t_dot(narrow, rows_by_heads([m_ref], start, rows))
         sum_ref[...] = total
 
     return call(
         kernel,
         [
-            jax.ShapeDtypeStruct(mixed.shape, BF16),
+            jax.ShapeDtypeStruct((heads, rows * count, HDIM), BF16),
             jax.ShapeDtypeStruct((rank, size), F32),
         ],
         [smem()] + [vmem()] * (count + 4),
@@ -555,57 +559,80 @@
     )(offsets, *blocks, *grads, *pieces, down, a_mlp, b_down, a_hidden, b_hidden)
 
 
-def project_back(grads, place, offsets, pieces, narrow_first, b_first, wanted, rows):
-    heads = grads[0].shape[0]
-    maps, _, size = pieces[0].shape
-    width = 4 * pieces[0].shape[1]
-    rank = b_first.shape[1]
-    n = len(pieces)
-    count = len(wanted)
-
-    def kernel(place_ref, offsets_ref, *refs):
-        g_refs, refs = refs[:maps], refs[maps:]
-        piece_refs, refs = refs[:n], refs[n:]
-        narrow_ref, b_ref = refs[:2]
-        back_refs, refs = refs[2 : 2 + count], refs[2 + count :]
-        thin_ref, sum_ref, whole, sems = refs
-        copies = load_pieces(offsets_ref, piece_refs, whole, sems)
-        waiting = True
-        for index, block in enumerate(wanted):
+def thin_back(grads, place, narrow_first, b_first, rows):
+    maps, rank, size = b_first.shape
+    parts_each = len(grads) // maps
+    count = narrow_first.shape[0] // rows
+
+    def kernel(place_ref, *refs):
+        g_refs, refs = refs[: len(grads)], refs[len(grads) :]
+        narrow_ref, b_ref, thin_ref, sum_ref = refs
+        for block in range(count):
             start = pl.multiple_of((place_ref[0] ^ block) * rows, rows)
-            parts = [rows_by_heads(g_refs[number], start, rows) for number in range(maps)]
             narrow = narrow_ref[block * rows : (block + 1) * rows, :]
-            thin = [dot_t(parts[number], b_ref[number]) for number in range(maps)]
-            thin_ref[index * rows : (index + 1) * rows, :] = jnp.concatenate(thin, axis=1).astype(BF16)
+            thin = []
             for number in range(maps):
-                term = t_dot(narrow[:, number * rank : (number + 1) * rank], parts[number])
-                if index == 0:
+                part = rows_by_heads(
+                    g_refs[number * parts_each : (number + 1) * parts_each], start, rows
+                )
+                thin.append(dot_t(part, b_ref[number]))
+                term = t_dot(narrow[:, number * rank : (number + 1) * rank], part)
+                if block == 0:
                     sum_ref[number] = term
                 else:
                     sum_ref[number] += term
-            if waiting:
-                for copy in copies:
-                    copy.wait()
-                waiting = False
-            back = dot_t(parts[0], whole[0])
-            for number in range(1, maps):
-                back = back + dot_t(parts[number], whole[number])
-            back_refs[index][...] = back.astype(BF16)
+            thin_ref[block * rows : (block + 1) * rows, :] = jnp.concatenate(thin, axis=1).astype(BF16)
 
     return call(
         kernel,
-        [jax.ShapeDtypeStruct((rows, width), BF16)] * count
-        + [
+        [
             jax.ShapeDtypeStruct((rows * count, maps * rank), BF16),
             jax.ShapeDtypeStruct((maps, rank, size), F32),
         ],
-        [smem(), smem()] + [vmem()] * maps + [anywhere()] * n + [vmem()] * 2,
-        [vmem()] * (count + 2),
+        [smem()] + [vmem()] * (len(grads) + 2),
+        [vmem()] * 2,
+        [],
+        4 * rows * count * maps * size * 128,
+        4 * rows * count * maps * size,
+        "thin_back",
+    )(place[None], *grads, narrow_first, b_first)
+
+
+def project_back(grads, place, offsets, pieces, wanted, rows):
+    maps, _, size = pieces[0].shape
+    width = 4 * pieces[0].shape[1]
+    n = len(pieces)
+    count = len(wanted)
+    parts_each = len(grads) // maps
+
+    def kernel(place_ref, offsets_ref, *refs):
+        g_refs, refs = refs[: len(grads)], refs[len(grads) :]
+        piece_refs, refs = refs[:n], refs[n:]
+        back_refs, (whole, sems) = refs[:count], refs[count:]
+        copies = load_pieces(offsets_ref, piece_refs, whole, sems)
+        for copy in copies:
+            copy.wait()
+        for index, block in enumerate(wanted):
+            start = pl.multiple_of((place_ref[0] ^ block) * rows, rows)
+            back = None
+            for number in range(maps):
+                part = rows_by_heads(
+                    g_refs[number * parts_each : (number + 1) * parts_each], start, rows
+                )
+                term = dot_t(part, whole[number])
+                back = term if back is None else back + term
+            back_refs[index][...] = back.astype(BF16)
+
+    return call(
+        kernel,
+        [jax.ShapeDtypeStruct((rows, width), BF16)] * count,
+        [smem(), smem()] + [vmem()] * len(grads) + [anywhere()] * n,
+        [vmem()] * count,
         [pltpu.VMEM((maps, width, size), BF16), pltpu.SemaphoreType.DMA((n,))],
         2 * rows * count * width * maps * size,
         2 * (rows * count * (width + maps * size) + maps * width * size),
         "project_back",
-    )(place[None], offsets, *grads, *pieces, narrow_first, b_first)
+    )(place[None], offsets, *grads, *pieces)
 
 
 def shards(
@@ -640,132 +667,245 @@
     residual_in = tokens[0].astype(F32)
     grad_out = cotangent[0].astype(F32)
 
+    def own_columns(values, size):
+        return lax.dynamic_slice_in_dim(values, place * size, size, values.ndim - 1)
+
+    first_one = [hop(piece, "shard", j) for j, piece in zip(
+        (2, 3), leaving(query_key_value_weight, head_cols, place, rep_place))]
     normed = norm_rows(residual_in, gain_one).astype(BF16)
     grad_feed = (BRANCH * grad_out).astype(BF16)
-    first_offsets, first_pieces = exchange(query_key_value_weight, head_cols, place, rep_place)
-    first_blocks = gather_tokens(normed)
-    model_one = picked(
-        jnp.concatenate([adapter_model_input_maps, adapter_model_output_maps]), pick, place
-    )
-    hidden_one = picked(
-        jnp.concatenate([adapter_hidden_input_map[None], adapter_hidden_output_maps]), pick, place
-    )
-    a_one, b_one = model_one[:6], model_one[6:]
-
-    def own_columns(values, size):
-        return lax.dynamic_slice_in_dim(values, place * size, size, values.ndim - 1)
-
-    a_first = a_one[0:3].reshape(3 * rank, width)
-    b_first = own_columns(b_one[0:3], head_cols)
-    a_out = own_columns(a_one[3], head_cols)
-    b_out = b_one[3]
-    a_mlp = a_one[4:6].reshape(2 * rank, width)
-    b_down = b_one[4]
-    hidden_cols = own_columns(hidden_one, ff_cols)
-    a_hidden, b_hidden = hidden_cols[0], hidden_cols[1:]
-
-    picks = lax.all_gather(sequence_adapter_index, "rep", axis=0, tiled=True)
-    adapters = adapter_model_input_maps.shape[1] * group
-    chosen = (picks[:, None] == jnp.arange(adapters, dtype=jnp.int32)[None, :]).astype(F32)
-
+    normed_near = core(normed)
+    first_near = near_columns(query_key_value_weight, head_cols, place)
+    front_chip, front_part = chip_picked(
+        jnp.concatenate([adapter_model_input_maps[0:3], adapter_model_output_maps[0:3]]), pick, place
+    )
+    front_far = across(after(front_part, first_one))
+    first_two = [hop(first_one[0], "rep", 2), hop(first_one[1], "rep", 1)]
+    normed_far = across(after(normed, front_far, first_two))
+    front = whole_picked(front_chip, front_far, place)
+    a_first = front[:3].reshape(3 * rank, width)
+    b_first = own_columns(front[3:], head_cols)
+    first_three = [
+        [hop(first_one[0], "rep", 1), hop(first_two[0], "rep", 1)],
+        [hop(first_one[1], "rep", 2), hop(first_two[1], "rep", 2)],
+    ]
     half = HDIM // 2
     frequency = jnp.exp(jnp.arange(half, dtype=F32) * (-2.0 / HDIM) * math.log(THETA))
     angle = jnp.arange(rows * group, dtype=jnp.int32).astype(F32)[:, None] * frequency[None, :]
     cosine = jnp.concatenate([jnp.cos(angle), jnp.cos(angle)], axis=1)
     sine = jnp.concatenate([jnp.sin(angle), jnp.sin(angle)], axis=1)
-
+    mlp_leaving = leaving(gate_up_projection_weight, ff_cols, place, rep_place)
+    normed_far, front, mlp_leaving, first_three, cosine, sine = lax.optimization_barrier(
+        (normed_far, front, mlp_leaving, first_three, cosine, sine)
+    )
+    first_blocks = (normed, normed_near, normed_far, core(normed_far))
+    first_offsets, first_pieces = finish(
+        query_key_value_weight, head_cols, first_one, first_two, first_three, place, rep_place,
+        first_near,
+    )
+
+    mlp_one = [hop(piece, "shard", j) for j, piece in zip((2, 3), mlp_leaving)]
+    rest_chip, rest_part = chip_picked(
+        jnp.concatenate([adapter_model_input_maps[3:6], adapter_model_output_maps[3:5]]), pick, place
+    )
+    wide_chip, wide_part = chip_picked(
+        jnp.concatenate([adapter_hidden_input_map[None], adapter_hidden_output_maps]), pick, place
+    )
+    rest_far = across(after(rest_part, normed_far))
+    wide_far = across(after(wide_part, normed_far))
     query, key, value, narrow_first = project(
         first_blocks, place, first_offsets, first_pieces, a_first, b_first, cosine, sine
     )
-    mlp_offsets, mlp_pieces = exchange(gate_up_projection_weight, ff_cols, place, rep_place)
-    feed_blocks = gather_tokens(grad_feed)
+    query, mlp_one[0], rest_far = lax.optimization_barrier((query, mlp_one[0], rest_far))
+    mlp_two = [hop(mlp_one[0], "rep", 2), None]
+    rest = whole_picked(rest_chip, rest_far, place)
     mixed = attend(starts, query, key, value, rows)
+    mixed, mlp_one[1], mlp_two[0], wide_far, rest = lax.optimization_barrier(
+        (mixed, mlp_one[1], mlp_two[0], wide_far, rest)
+    )
+    a_out = own_columns(rest[0], head_cols)
+    a_mlp = rest[1:3].reshape(2 * rank, width)
+    b_out, b_down = rest[3], rest[4]
+    mlp_two[1] = hop(mlp_one[1], "rep", 1)
+    feed_far_in = across(after(grad_feed, mixed))
+    feed_near_in = core(grad_feed)
+    hidden_one = whole_picked(wide_chip, wide_far, place)
+    hidden_cols = own_columns(hidden_one, ff_cols)
+    a_hidden, b_hidden = hidden_cols[0], hidden_cols[1:]
+    mlp_near = near_columns(gate_up_projection_weight, ff_cols, place)
 
     far_out = close_attention(mixed, place, attention_output_weight, a_out, (2, 3), rows)
-    near_out = close_attention(mixed, place, attention_output_weight, a_out, (0, 1), rows)
-    branch_own = scatter_tokens((*near_out, *far_out))
+    far_sum = (far_out[0].astype(F32) + core(far_out[1]).astype(F32)).astype(BF16)
+    far_sum, mixed_here, mlp_two[1] = lax.optimization_barrier((far_sum, mixed, mlp_two[1]))
+    branch_far = across(far_sum)
+    mlp_three = [
+        [hop(mlp_one[0], "rep", 1), hop(mlp_two[0], "rep", 1)],
+        [hop(mlp_one[1], "rep", 2), hop(mlp_two[1], "rep", 2)],
+    ]
+    near_out = close_attention(mixed_here, place, attention_output_weight, a_out, (0, 1), rows)
+    branch_own = near_out[0].astype(F32) + core(near_out[1]).astype(F32) + branch_far.astype(F32)
     narrow_out = branch_own[:, width : width + rank].astype(BF16)
     branch = branch_own[:, :width] + dot(narrow_out, b_out)
     middle = residual_in + BRANCH * branch
     normed_second = norm_rows(middle, gain_two).astype(BF16)
-    second_blocks = gather_tokens(normed_second)
-
+    second_far = across(normed_second)
+    second_near = core(normed_second)
+    second_near, mlp_three, feed_near_in, feed_far_in, hidden_cols = lax.optimization_barrier(
+        (second_near, mlp_three, feed_near_in, feed_far_in, hidden_cols)
+    )
+    a_hidden, b_hidden = hidden_cols[0], hidden_cols[1:]
+    mlp_offsets, mlp_pieces = finish(
+        gate_up_projection_weight, ff_cols, mlp_one, mlp_two, mlp_three, place, rep_place, mlp_near
+    )
+    feed_far_near = core(feed_far_in)
     *parts, a_near, b_near = feed_forward(
-        second_blocks[:2], feed_blocks[:2], mlp_offsets, mlp_pieces, down_projection_weight,
-        a_mlp, b_down, a_hidden, b_hidden,
+        (normed_second, second_near), (grad_feed, feed_near_in), mlp_offsets, mlp_pieces,
+        down_projection_weight, a_mlp, b_down, a_hidden, b_hidden,
     )
     feed_near, back_near = parts[:2], parts[2:]
+    second_far, feed_far_near, back_near = lax.optimization_barrier(
+        (second_far, feed_far_near, back_near)
+    )
+    second_blocks = (normed_second, second_near, second_far, core(second_far))
+    feed_blocks = (grad_feed, feed_near_in, feed_far_in, feed_far_near)
+    back_here = core(back_near[1])
     *parts, a_far, b_far = feed_forward(
         second_blocks[2:], feed_blocks[2:], mlp_offsets, mlp_pieces, down_projection_weight,
         a_mlp, b_down, a_hidden, b_hidden,
     )
     feed_far, back_far = parts[:2], parts[2:]
-    second_own = scatter_tokens((*back_near, *back_far))
+    back_sum = (back_far[0].astype(F32) + core(back_far[1]).astype(F32)).astype(BF16)
+    back_from_far = across(back_sum)
+    feed_near, feed_far, back_sum = lax.optimization_barrier((feed_near, feed_far, back_sum))
+    feed_here = feed_near[0].astype(F32) + core(feed_near[1]).astype(F32)
+    feed_sum = (feed_far[0].astype(F32) + core(feed_far[1]).astype(F32)).astype(BF16)
+    back_from_far, feed_here, feed_sum = lax.optimization_barrier((back_from_far, feed_here, feed_sum))
+    second_own = back_near[0].astype(F32) + back_here.astype(F32) + back_from_far.astype(F32)
     grad_narrow_mlp = second_own[:, width : width + 2 * rank].astype(BF16)
     grad_normed_second = second_own[:, :width] + dot(grad_narrow_mlp, a_mlp)
     grad_middle = grad_out + norm_back(middle, gain_two, grad_normed_second)
     grad_branch = (BRANCH * grad_middle).astype(BF16)
-    branch_blocks = gather_tokens(
-        pad_columns([grad_branch, narrow_out, grad_narrow_mlp], width + EXTRA)
-    )
-
-    feed_own = scatter_tokens((*feed_near, *feed_far))
+    branch_rows = pad_columns([grad_branch, narrow_out, grad_narrow_mlp], width + EXTRA)
+    branch_far_in = across(branch_rows)
+    branch_near_in = core(branch_rows)
+
+    mixed_near, grad_a_near = open_attention(
+        (branch_rows, branch_near_in), (0, 1), place, mixed, attention_output_weight, a_out, b_out
+    )
+    branch_far_in, mixed_near = lax.optimization_barrier((branch_far_in, mixed_near))
+    feed_from_far = across(after(feed_sum, branch_far_in))
+    branch_blocks = (branch_rows, branch_near_in, branch_far_in, core(branch_far_in))
+    mixed_far, grad_a_far = open_attention(
+        branch_blocks[2:], (2, 3), place, mixed, attention_output_weight, a_out, b_out
+    )
+
+    def columns_product(thin, wide):
+        total = sum(t_dot(left, right) for left, right in zip(thin, wide))
+        return own_columns(total, head_cols)
+
+    def attend_part(first, heads, starts):
+        return attend_back(
+            starts, place, query, key, value, mixed_near, mixed_far, cosine, sine, rows, first, heads
+        )
+
+    heads = query.shape[0]
+    third = heads // 3
+    part_one = attend_part(0, third, starts)
+    part_one, feed_from_far, starts_two = lax.optimization_barrier((part_one, feed_from_far, starts))
+
+    feed_own = feed_here + feed_from_far.astype(F32)
     narrow_down = feed_own[:, width : width + rank].astype(BF16)
     feed = feed_own[:, :width] + dot(narrow_down, b_down)
     output = (middle + BRANCH * feed).astype(BF16)
-    narrow_down_blocks = gather_tokens(narrow_down)
-
-    grad_mixed, grad_a_out = open_attention(
-        branch_blocks, place, mixed, attention_output_weight, a_out, b_out
-    )
-    first_grads = attend_back(starts, query, key, value, grad_mixed, cosine, sine, rows)
-    *far_back, thin_far, b_first_far = project_back(
-        first_grads, place, first_offsets, first_pieces, narrow_first, b_first, (2, 3), rows
-    )
-    *near_back, thin_near, b_first_near = project_back(
-        first_grads, place, first_offsets, first_pieces, narrow_first, b_first, (0, 1), rows
-    )
-    grad_narrow_first = sum_group(jnp.concatenate([thin_near, thin_far]))
-    grad_normed = scatter_tokens((*near_back, *far_back)) + dot(grad_narrow_first[:rows], a_first)
-    input_grad = grad_middle + norm_back(residual_in, gain_one, grad_normed)
-
-    def columns_product(thin, wide):
-        total = sum(t_dot(left, right) for left, right in zip(thin, wide))
-        return own_columns(total, head_cols)
-
+    down_far = across(narrow_down)
+    down_near = core(narrow_down)
     wide_branch = [block[:, :width] for block in branch_blocks]
     thin_out = [block[:, width : width + rank] for block in branch_blocks]
     thin_mlp = [block[:, width + rank : width + 3 * rank] for block in branch_blocks]
-    early_model = jnp.concatenate(
+    early_ready = jnp.concatenate(
         [
-            grad_a_out,
+            grad_a_near + grad_a_far,
             columns_product(thin_mlp, second_blocks),
             columns_product(thin_out, wide_branch),
+        ]
+    )
+    output, down_far, down_near, early_ready, starts_two = lax.optimization_barrier(
+        (output, down_far, down_near, early_ready, starts_two)
+    )
+    narrow_down_blocks = (narrow_down, down_near, down_far, core(down_far))
+    mark = jnp.full((rank, head_cols), pick.astype(F32))
+    early = jnp.concatenate(
+        [
+            early_ready,
             columns_product(narrow_down_blocks, feed_blocks),
+            (a_near + a_far).reshape(-1, head_cols),
+            (b_near + b_far).reshape(-1, head_cols),
+            mark,
         ]
-    )
-    early_hidden = jnp.concatenate(
-        [a_near + a_far, (b_near + b_far).reshape(2 * rank, ff_cols)]
-    )
-    late_model = jnp.concatenate(
+    ).astype(BF16)
+    early_all = start_reps(early, rep_place)
+    early_one = reps_step(early_all, rep_place, 1)
+    early_two = reps_step(early_one, rep_place, 2)
+    early_two, starts_two = lax.optimization_barrier((early_two, starts_two))
+    early_rest = reps_rest(early_two, rep_place, 4)
+    part_two = attend_part(third, third, starts_two)
+    early_rest, part_two, starts_three = lax.optimization_barrier((early_rest, part_two, starts_two))
+    picks = early_rest[:, -1, :1].astype(F32)
+    adapters = adapter_model_input_maps.shape[1] * group
+    chosen = (picks == jnp.arange(adapters, dtype=jnp.int32).astype(F32)[None, :]).astype(F32)
+    early_sent = send_sums(early_rest[:, :-rank], chosen, place)
+    part_three = attend_part(2 * third, heads - 2 * third, starts_three)
+    early_sent, part_three = lax.optimization_barrier((early_sent, part_three))
+    early_got = arrange_sums(early_sent, place)
+    first_grads = [part[number] for number in range(3) for part in (part_one, part_two, part_three)]
+
+    thin, grad_b_first = thin_back(first_grads, place, narrow_first, b_first, rows)
+    first_grads, thin = lax.optimization_barrier((first_grads, thin))
+    thin_one = add_relative(thin, core(thin), 1)
+    back_rows_far = project_back(first_grads, place, first_offsets, first_pieces, (2, 3), rows)
+    sum_far = (back_rows_far[0].astype(F32) + core(back_rows_far[1]).astype(F32)).astype(BF16)
+    thin_one, sum_far, grads_here = lax.optimization_barrier((thin_one, sum_far, first_grads))
+    thin_far = across(thin_one)
+    back_far_in = across(sum_far)
+    back_rows_near = project_back(grads_here, place, first_offsets, first_pieces, (0, 1), rows)
+    thin_far, back_rows_near = lax.optimization_barrier((thin_far, back_rows_near))
+    grad_narrow_first = add_relative(thin_one, thin_far, 2)
+    back_here = back_rows_near[0].astype(F32) + core(back_rows_near[1]).astype(F32)
+
+    late = jnp.concatenate(
         [
             columns_product(rows_of(grad_narrow_first, group), first_blocks),
-            (b_first_near + b_first_far).reshape(3 * rank, head_cols),
+            grad_b_first.reshape(3 * rank, head_cols),
         ]
-    )
-    early_model = owned_sums(early_model, chosen, place, rep_place)
-    early_hidden = owned_sums(early_hidden, chosen, place, rep_place)
-    late_model = owned_sums(late_model, chosen, place, rep_place)
-
-    def maps_first(values):
-        per, count, n = values.shape
-        return values.reshape(per, count // rank, rank, n).transpose(1, 0, 2, 3)
-
-    early_model, early_hidden, late_model = map(maps_first, (early_model, early_hidden, late_model))
-    grad_a_model = jnp.concatenate([late_model[0:3], early_model[0:3]])
-    grad_b_model = jnp.concatenate([late_model[3:6], early_model[3:5]])
+    ).astype(BF16)
+    late_all = reps_rest(start_reps(late, rep_place), rep_place, 1)
+    late_sent = send_sums(late_all, chosen, place)
+    late_sent, back_far_in = lax.optimization_barrier((late_sent, back_far_in))
+    late_got = arrange_sums(late_sent, place)
+    grad_normed = back_here + back_far_in.astype(F32) + dot(grad_narrow_first[:rows], a_first)
+    input_grad = grad_middle + norm_back(residual_in, gain_one, grad_normed)
+
+    def whole_maps(got, low, high, n):
+        group_size, per = got.shape[:2]
+        part = got[:, :, low:high].reshape(group_size, per, -1, rank, n)
+        part = jnp.concatenate([part[i] for i in range(group_size)], axis=-1)
+        return part.transpose(1, 0, 2, 3).astype(F32)
+
+    split = 5 * rank
+    hidden_rows = rank * ff_cols // head_cols
+    grad_a_model = jnp.concatenate(
+        [whole_maps(late_got, 0, 3 * rank, head_cols), whole_maps(early_got, 0, 3 * rank, head_cols)]
+    )
+    grad_b_model = jnp.concatenate(
+        [
+            whole_maps(late_got, 3 * rank, 6 * rank, head_cols),
+            whole_maps(early_got, 3 * rank, split, head_cols),
+        ]
+    )
+    grad_hidden_maps = whole_maps(early_got, split, split + 3 * hidden_rows, ff_cols)
     return (
-        output[None], input_grad[None], grad_a_model, grad_b_model, early_hidden[0], early_hidden[1:3],
+        output[None], input_grad[None], grad_a_model, grad_b_model, grad_hidden_maps[0],
+        grad_hidden_maps[1:3],
     )
 
 

time: 834 us -> 720 us (0.86)
  waiting for transfers between devices: 337 us -> 240 us
  blocking collectives: 22.8 us -> 0 us
  Pallas kernels: 247 us -> 261 us
  local copies, waits for them, and re-layouts: 79.2 us -> 92.9 us
  starting transfers between devices: 55.4 us -> 44.3 us
    ppermute x71 -> x68, waiting for transfers between devices: 337 us -> 240 us  [hop(): return lax.ppermute(values, axis, [(i, i ^ bit) for i in range(size)])]
    unnamed x1 -> x0, blocking collectives: 22.8 us -> none
    pallas_call x4 -> x8, Pallas kernels: 92.8 us -> 107 us  [the longest x3 57.7 us: attend_back(): call(kernel, [jax.ShapeDtypeStruct((heads, length, HDIM), BF16)] * 3, [sm...]
    ppermute x71 -> x68, starting transfers between devices: 55.4 us -> 44.3 us  [hop(): return lax.ppermute(values, axis, [(i, i ^ bit) for i in range(size)])]
    squeeze x2 -> x6, local copies, waits for them, and re-layouts: 1.58 us -> 10.4 us  [the longest x4 8.64 us: whole_maps(): part = jnp.concatenate([part[i] for i in range(group_size)], axis=-1)]
    unnamed x164 -> x152, local copies, waits for them, and re-layouts: 18.3 us -> 12.8 us
    dynamic_slice x16 -> x14, local copies, waits for them, and re-layouts: 28.1 us -> 30.8 us  [the longest x2 16.2 us: near_columns(): return core(lax.dynamic_slice_in_dim(weight, (place ^ 1) * size, size, 2))]
  transfers between devices with their start and end apart: 71 -> 68, of which waited for: 31 -> 29; matrix products, arithmetic and copies ran while one was open for 15% -> 16% of each run, Pallas kernels for 13% -> 25%
where the time goes in v2:
time: 720 us; the launch traced here: 715 us
  Pallas kernels  261 us (36%)
  waiting for transfers between devices  240 us (33%)
  local copies, waits for them, and re-layouts  92.9 us (13%)
  other arithmetic  48.7 us (7%)
  starting transfers between devices  44.3 us (6%)
  matrix products  25.1 us (3%)
    ppermute x68, waiting for transfers between devices, hop(): return lax.ppermute(values, axis, [(i, i ^ bit) for i in range(size)])  240 us
    pallas_call x2, Pallas kernels, feed_forward(): call(kernel, [out] * (2 * count) + [jax.ShapeDtypeStruct((rank, size), F3...  98.8 us
    pallas_call x3, Pallas kernels, attend_back(): call(kernel, [jax.ShapeDtypeStruct((heads, length, HDIM), BF16)] * 3, [sm...  57.7 us
    ppermute x68, starting transfers between devices, hop(): return lax.ppermute(values, axis, [(i, i ^ bit) for i in range(size)])  44.3 us
    pallas_call x2, Pallas kernels, project_back(): call(kernel, [jax.ShapeDtypeStruct((rows, width), BF16)] * count, [smem()...  26.9 us
    pallas_call x1, Pallas kernels, attend(): call(kernel, jax.ShapeDtypeStruct(query.shape, BF16), [smem(), spec, spec...  23 us
    pallas_call x1, Pallas kernels, project(): call(kernel, [by_heads] * 3 + [jax.ShapeDtypeStruct((rows * count, 3 * ra...  21 us
    dot_general x16, matrix products, t_dot(): lax.dot_general(left, right, (((0,), (0,)), ((), ())), preferred_element_...  17.5 us
  transfers between devices with their start and end apart: 68, of which 29 were waited for; matrix products, arithmetic and copies ran while one was open for 16% of the time, Pallas kernels for 25%

profile of v2, /device:TPU:0, one launch (start us, length us, event | category | flops | bytes accessed | tf_op | source)
XLA Modules:
  0.0 714.6 jit_solution(8038802749065744852)
XLA Ops:
  3.2 2.9 constant_dynamic-slice_fusion.19
  6.2 2.7 collective-permute-start.2
  13.4 4.1 constant_dynamic-slice_fusion.17
  17.5 3.4 multiply_sine_fusion
  22.7 11.0 %collective-permute-done.3.refs_10_.refs_15_ = bf16[3,144,576]{2,1,0:T(8,128)(2,1)} collective-permute-done((bf16[3,144,576]{2,1,0:T(8,128)(2,1)}, bf16[3,144,576]{2,1,0:T(8,128)(2,1)}, u32[]{:S(2)}, u32[]{:S(2)}) %collective-permute-start.3) | collective-permute-done | bytes 497696 | tf_op jit(solution)/shard_map/ppermute | solution.py:25
  38.3 7.2 %constant_dynamic-slice_fusion.15 = (bf16[3,576,576]{2,1,0:T(8,128)(2,1)}, bf16[3,576,576]{2,1,0:T(8,128)(2,1)}) fusion(bf16[3,576,2304]{2,1,0:T(8,128)(2,1)} %param.20, s32[]{:T(128)S(6)} %select_n.252, s32[]{:T(128)S(6)} %select_n.251), kind=kLoop, calls=%fused_computation.169 | loop fusion | bytes 7962632 | tf_op jit(solution)/shard_map/dynamic_slice | solution.py:160
  46.2 2.9 pad_maximum_fusion
  56.9 9.3 %collective-permute-done.11.refs_12_.refs_17_ = bf16[3,144,576]{2,1,0:T(8,128)(2,1)S(1)} collective-permute-done((bf16[3,144,576]{2,1,0:T(8,128)(2,1)}, bf16[3,144,576]{2,1,0:T(8,128)(2,1)S(1)}, u32[]{:S(2)}, u32[]{:S(2)}) %collective-permute-start.11) | collective-permute-done | bytes 497696 | tf_op jit(solution)/shard_map/ppermute | solution.py:25
  68.8 10.6 %collective-permute-done.10.refs_9_.refs_14_ = bf16[3,144,576]{2,1,0:T(8,128)(2,1)S(1)} collective-permute-done((bf16[3,144,576]{2,1,0:T(8,128)(2,1)}, bf16[3,144,576]{2,1,0:T(8,128)(2,1)S(1)}, u32[]{:S(2)}, u32[]{:S(2)}) %collective-permute-start.10) | collective-permute-done | bytes 497696 | tf_op jit(solution)/shard_map/ppermute | solution.py:25
  87.9 21.0 %project.1 = (bf16[9,1024,64]{2,1,0:T(8,128)(2,1)}, bf16[9,1024,64]{2,1,0:T(8,128)(2,1)}, bf16[9,1024,64]{2,1,0:T(8,128)(2,1)}, bf16[1024,48]{1,0:T(8,128)(2,1)}) custom-call(s32[1]{0:T(128)} %bitcast.1.place_ref, s32[10]{0:T(128)} %stack.54.offsets_ref, bf16[256,2304]{1,0:T(8,128)(2,1)} %copy-done.15, bf16[256,2304]{1,0:T(8,128)(2,1)} %copy-done.36, ...), custom_call_target="tpu_custom_call" | custom-call | flops 8153726976 | bytes 19759104 | tf_op jit(solution)/shard_map/project/pallas_call | solution.py:241
  111.5 23.0 %attend.1.m_ref.refs_2_ = bf16[9,1024,64]{2,1,0:T(8,128)(2,1)} custom-call(s32[2]{0:T(128)} %bitcast.173, bf16[9,1024,64]{2,1,0:T(8,128)(2,1)} %get-tuple-element.157.q_ref, bf16[9,1024,64]{2,1,0:T(8,128)(2,1)} %get-tuple-element.158.k_ref, bf16[9,1024,64]{2,1,0:T(8,128)(2,1)} %get-tuple-element.159.v_ref), custom_call_target="tpu_custom_call" | custom-call | flops 9663676416 | bytes 9437184 | tf_op jit(solution)/shard_map/attend/pallas_call | solution.py:318
  136.2 5.7 close_attention.2
  146.8 17.5 %collective-permute-done.24.refs_11_ = bf16[2,144,1440]{2,1,0:T(8,128)(2,1)S(1)} collective-permute-done((bf16[2,144,1440]{2,1,0:T(8,128)(2,1)}, bf16[2,144,1440]{2,1,0:T(8,128)(2,1)S(1)}, u32[]{:S(2)}, u32[]{:S(2)}) %collective-permute-start.24) | collective-permute-done | bytes 829472 | tf_op jit(solution)/shard_map/ppermute | solution.py:25
  164.2 6.0 close_attention.3
  172.4 9.0 %constant_dynamic-slice_fusion.10 = (bf16[2,576,1440]{2,1,0:T(8,128)(2,1)S(1)}, bf16[2,576,1440]{2,1,0:T(8,128)(2,1)}) fusion(bf16[2,576,5760]{2,1,0:T(8,128)(2,1)} %param.22, s32[]{:T(128)S(6)} %select_n.266, s32[]{:T(128)S(6)} %select_n.265), kind=kLoop, calls=%fused_computation.164 | loop fusion | bytes 13271048 | tf_op jit(solution)/shard_map/dynamic_slice | solution.py:160
  183.9 16.3 %collective-permute-done.26 = bf16[256,2432]{1,0:T(8,128)(2,1)} collective-permute-done((bf16[256,2432]{1,0:T(8,128)(2,1)S(1)}, bf16[256,2432]{1,0:T(8,128)(2,1)}, u32[]{:S(2)}, u32[]{:S(2)}) %collective-permute-start.26) | collective-permute-done | bytes 1245216 | tf_op jit(solution)/shard_map/ppermute | solution.py:25
  208.6 14.1 %collective-permute-done.30.refs_9_ = bf16[2,144,1440]{2,1,0:T(8,128)(2,1)S(1)} collective-permute-done((bf16[2,144,1440]{2,1,0:T(8,128)(2,1)S(1)}, bf16[2,144,1440]{2,1,0:T(8,128)(2,1)S(1)}, u32[]{:S(2)}, u32[]{:S(2)}) %collective-permute-start.30) | collective-permute-done | bytes 829472 | tf_op jit(solution)/shard_map/ppermute | solution.py:25
  224.0 4.7 collective-permute-done.31.refs_12_
  229.3 6.0 collective-permute-done.34.refs_2_
  235.3 10.7 %collective-permute-done.32.refs_13_ = bf16[2,144,1440]{2,1,0:T(8,128)(2,1)S(1)} collective-permute-done((bf16[2,144,1440]{2,1,0:T(8,128)(2,1)S(1)}, bf16[2,144,1440]{2,1,0:T(8,128)(2,1)S(1)}, u32[]{:S(2)}, u32[]{:S(2)}) %collective-permute-start.32) | collective-permute-done | bytes 829472 | tf_op jit(solution)/shard_map/ppermute | solution.py:25
  249.2 49.5 %feed_forward.2 = (bf16[256,2432]{1,0:T(8,128)(2,1)}, bf16[256,2432]{1,0:T(8,128)(2,1)}, bf16[256,2432]{1,0:T(8,128)(2,1)}, bf16[256,2432]{1,0:T(8,128)(2,1)}, f...) custom-call(s32[10]{0:T(128)} %stack.54.offsets_ref, bf16[256,2304]{1,0:T(8,128)(2,1)} %copy-done.14, ...), custom_call_target="tpu_custom_call" | custom-call | flops 20384317440 | bytes 29343744 | tf_op jit(solution)/shard_map/feed_forward/pallas_call | solution.py:544
  299.3 2.7 collective-permute-done.38.refs_1_
  303.0 49.3 %feed_forward.3 = (bf16[256,2432]{1,0:T(8,128)(2,1)}, bf16[256,2432]{1,0:T(8,128)(2,1)}, bf16[256,2432]{1,0:T(8,128)(2,1)}, bf16[256,2432]{1,0:T(8,128)(2,1)}, f...) custom-call(s32[10]{0:T(128)} %stack.54.offsets_ref, bf16[256,2304]{1,0:T(8,128)(2,1)} %collective-permute-done.27.refs_0_, ...), custom_call_target="tpu_custom_call" | custom-call | flops 20384317440 | bytes 29343744 | tf_op jit(solution)/shard_map/feed_forward/pallas_call | solution.py:544
  352.8 2.8 collective-permute-done.39
  363.9 25.3 %collective-permute-done.40 = bf16[256,2432]{1,0:T(8,128)(2,1)S(1)} collective-permute-done((bf16[256,2432]{1,0:T(8,128)(2,1)S(1)}, bf16[256,2432]{1,0:T(8,128)(2,1)S(1)}, u32[]{:S(2)}, u32[]{:S(2)}) %collective-permute-start.40) | collective-permute-done | bytes 1245216 | tf_op jit(solution)/shard_map/ppermute | solution.py:25
  391.7 2.9 multiply_convert_fusion
  395.3 3.6 concatenate.106.refs_0_
  407.8 8.1 %open_attention.2 = (bf16[9,512,64]{2,1,0:T(8,128)(2,1)}, f32[16,576]{1,0:T(8,128)}) custom-call(s32[1]{0:T(128)} %bitcast.1.place_ref, bf16[256,2432]{1,0:T(8,128)(2,1)} %concatenate.106.refs_0_, bf16[256,2432]{1,0:T(8,128)(2,1)} %collective-permute-done.45.refs_1_, bf16[9,1024,64]{2,1,0:T(8,128)(2,1)} %attend.1.m_ref.refs_2_, bf16[576,2304]{1,0:T(8,128)(2,1)} %refs_3_.3, ...), custom_call_target="tpu_custom_call" | custom-call | flops 1358954496 | bytes 6193152 | tf_op jit(solution)/shard_map/open_attention/pallas_call | solution.py:462
  415.8 13.2 %collective-permute-done.44.refs_0_ = bf16[256,2432]{1,0:T(8,128)(2,1)} collective-permute-done((bf16[256,2432]{1,0:T(8,128)(2,1)}, bf16[256,2432]{1,0:T(8,128)(2,1)}, u32[]{:S(2)}, u32[]{:S(2)}) %collective-permute-start.44) | collective-permute-done | bytes 1245216 | tf_op jit(solution)/shard_map/ppermute | solution.py:25
  439.5 7.9 %open_attention.3 = (bf16[9,512,64]{2,1,0:T(8,128)(2,1)}, f32[16,576]{1,0:T(8,128)}) custom-call(s32[1]{0:T(128)} %bitcast.1.place_ref, bf16[256,2432]{1,0:T(8,128)(2,1)} %collective-permute-done.44.refs_0_, bf16[256,2432]{1,0:T(8,128)(2,1)} %copy-done.12, bf16[9,1024,64]{2,1,0:T(8,128)(2,1)} %attend.1.m_ref.refs_2_, bf16[576,2304]{1,0:T(8,128)(2,1)} %refs_3_.3, ...), custom_call_target="tpu_custom_call" | custom-call | flops 1358954496 | bytes 6193152 | tf_op jit(solution)/shard_map/open_attention/pallas_call | solution.py:462
  447.4 19.1 %attend_back.3 = (bf16[3,1024,64]{2,1,0:T(8,128)(2,1)}, bf16[3,1024,64]{2,1,0:T(8,128)(2,1)}, bf16[3,1024,64]{2,1,0:T(8,128)(2,1)}) custom-call(s32[2]{0:T(128)} %bitcast.174, s32[1]{0:T(128)} %bitcast.1.place_ref, bf16[9,1024,64]{2,1,0:T(8,128)(2,1)} %get-tuple-element.157.q_ref, bf16[9,1024,64]{2,1,0:T(8,128)(2,1)} %get-tuple-element.158.k_ref, ...), custom_call_target="tpu_custom_call" | custom-call | flops 8053063680 | bytes 6291456 | tf_op jit(solution)/shard_map/attend_back/pallas_call | solution.py:390
  468.1 2.5 fusion.11
  481.4 8.8 %collective-permute-done.51 = bf16[1,216,576]{2,1,0:T(8,128)(2,1)} collective-permute-done((bf16[1,216,576]{2,1,0:T(8,128)(2,1)}, bf16[1,216,576]{2,1,0:T(8,128)(2,1)}, u32[]{:S(2)}, u32[]{:S(2)}) %collective-permute-start.51) | collective-permute-done | bytes 248864 | tf_op jit(solution)/shard_map/ppermute | solution.py:25
  492.4 14.2 %collective-permute-done.52 = bf16[2,216,576]{2,1,0:T(8,128)(2,1)} collective-permute-done((bf16[2,216,576]{2,1,0:T(8,128)(2,1)}, bf16[2,216,576]{2,1,0:T(8,128)(2,1)}, u32[]{:S(2)}, u32[]{:S(2)}) %collective-permute-start.52) | collective-permute-done | bytes 497696 | tf_op jit(solution)/shard_map/ppermute | solution.py:25
  511.0 19.1 %attend_back.4 = (bf16[3,1024,64]{2,1,0:T(8,128)(2,1)}, bf16[3,1024,64]{2,1,0:T(8,128)(2,1)}, bf16[3,1024,64]{2,1,0:T(8,128)(2,1)}) custom-call(s32[2]{0:T(128)} %bitcast.175, s32[1]{0:T(128)} %bitcast.1.place_ref, bf16[9,1024,64]{2,1,0:T(8,128)(2,1)} %get-tuple-element.157.q_ref, bf16[9,1024,64]{2,1,0:T(8,128)(2,1)} %get-tuple-element.158.k_ref, ...), custom_call_target="tpu_custom_call" | custom-call | flops 8053063680 | bytes 6291456 | tf_op jit(solution)/shard_map/attend_back/pallas_call | solution.py:390
  530.2 28.4 %collective-permute-done.53 = bf16[4,216,576]{2,1,0:T(8,128)(2,1)} collective-permute-done((bf16[4,216,576]{2,1,0:T(8,128)(2,1)}, bf16[4,216,576]{2,1,0:T(8,128)(2,1)}, u32[]{:S(2)}, u32[]{:S(2)}) %collective-permute-start.53) | collective-permute-done | bytes 995360 | tf_op jit(solution)/shard_map/ppermute | solution.py:25
  560.6 3.6 multiply_reduce_fusion
  566.2 19.4 %attend_back.5 = (bf16[3,1024,64]{2,1,0:T(8,128)(2,1)}, bf16[3,1024,64]{2,1,0:T(8,128)(2,1)}, bf16[3,1024,64]{2,1,0:T(8,128)(2,1)}) custom-call(s32[2]{0:T(128)} %bitcast.176, s32[1]{0:T(128)} %bitcast.1.place_ref, bf16[9,1024,64]{2,1,0:T(8,128)(2,1)} %get-tuple-element.157.q_ref, bf16[9,1024,64]{2,1,0:T(8,128)(2,1)} %get-tuple-element.158.k_ref, ...), custom_call_target="tpu_custom_call" | custom-call | flops 8053063680 | bytes 6291456 | tf_op jit(solution)/shard_map/attend_back/pallas_call | solution.py:390
  585.6 3.3 collective-permute-done.56
  588.9 6.0 thin_back.1
  594.9 13.3 %project_back.2 = (bf16[256,2304]{1,0:T(8,128)(2,1)}, bf16[256,2304]{1,0:T(8,128)(2,1)}) custom-call(s32[1]{0:T(128)} %bitcast.1.place_ref, s32[10]{0:T(128)} %stack.54.offsets_ref, bf16[3,1024,64]{2,1,0:T(8,128)(2,1)} %get-tuple-element.259.refs_0_, bf16[3,1024,64]{2,1,0:T(8,128)(2,1)} %get-tuple-element.260.refs_1_, ...), custom_call_target="tpu_custom_call" | custom-call | flops 4076863488 | bytes 12091392 | tf_op jit(solution)/shard_map/project_back/pallas_call | solution.py:626
  614.4 13.5 %project_back.3 = (bf16[256,2304]{1,0:T(8,128)(2,1)}, bf16[256,2304]{1,0:T(8,128)(2,1)}) custom-call(s32[1]{0:T(128)} %bitcast.1.place_ref, s32[10]{0:T(128)} %stack.54.offsets_ref, bf16[3,1024,64]{2,1,0:T(8,128)(2,1)} %get-tuple-element.259.refs_0_, bf16[3,1024,64]{2,1,0:T(8,128)(2,1)} %get-tuple-element.260.refs_1_, ...), custom_call_target="tpu_custom_call" | custom-call | flops 4076863488 | bytes 12091392 | tf_op jit(solution)/shard_map/project_back/pallas_call | solution.py:626
  642.5 3.5 concatenate.126
  650.9 5.5 collective-permute-done.62
  663.5 17.5 %collective-permute-done.63 = bf16[4,96,576]{2,1,0:T(8,128)(2,1)} collective-permute-done((bf16[4,96,576]{2,1,0:T(8,128)(2,1)}, bf16[4,96,576]{2,1,0:T(8,128)(2,1)}, u32[]{:S(2)}, u32[]{:S(2)}) %collective-permute-start.63) | collective-permute-done | bytes 442400 | tf_op jit(solution)/shard_map/ppermute | solution.py:25
  690.9 4.8 collective-permute-done.65
  695.7 4.5 collective-permute-done.66
  709.6 2.7 fusion.8
  (403 shorter events, 168.6 us)
Async XLA Ops:
  2.7 18.2 %collective-permute-start.1 = (bf16[6,16,2304]{2,1,0:T(8,128)(2,1)S(1)}, bf16[6,16,2304]{2,1,0:T(8,128)(2,1)}, u32[]{:S(2)}, u32[]{:S(2)}) collective-permute-start(bf16[6,16,2304]{2,1,0:T(8,128)(2,1)S(1)} %fusion.26), channel_id=1, source_target_pairs={{0,1},{1,0},{2,3},{3,2},{4,5},{5,4},{6,7},{7,6},{8,9},{9,8},{10,11... | collective-permute-start | bytes 1327112 | tf_op jit(solution)/shard_map/ppermute | solution.py:25
  6.2 16.6 %collective-permute-start.2 = (bf16[3,144,576]{2,1,0:T(8,128)(2,1)}, bf16[3,144,576]{2,1,0:T(8,128)(2,1)S(1)}, u32[]{:S(2)}, u32[]{:S(2)}) collective-permute-start(bf16[3,144,576]{2,1,0:T(8,128)(2,1)} %get-tuple-element.325), channel_id=1, source_target_pairs={{0,2},{1,3},{2,0},{3,1},{4,6},{5,7},{6,4},{7,5},{8,10},{9,11},{10,... | collective-permute-start | bytes 1493000 | tf_op jit(solution)/shard_map/ppermute | solution.py:25
  8.9 24.9 %collective-permute-start.3 = (bf16[3,144,576]{2,1,0:T(8,128)(2,1)}, bf16[3,144,576]{2,1,0:T(8,128)(2,1)}, u32[]{:S(2)}, u32[]{:S(2)}) collective-permute-start(bf16[3,144,576]{2,1,0:T(8,128)(2,1)} %get-tuple-element.324), channel_id=1, source_target_pairs={{0,3},{1,2},{2,1},{3,0},{4,7},{5,6},{6,5},{7,4},{8,11},{9,10},{10,... | collective-permute-start | bytes 1493000 | tf_op jit(solution)/shard_map/ppermute | solution.py:25
  9.7 39.3 %collective-permute-start.16 = (bf16[5,16,2304]{2,1,0:T(8,128)(2,1)}, bf16[5,16,2304]{2,1,0:T(8,128)(2,1)}, u32[]{:S(2)}, u32[]{:S(2)}) collective-permute-start(bf16[5,16,2304]{2,1,0:T(8,128)(2,1)} %fusion.30), channel_id=1, source_target_pairs={{0,1},{1,0},{2,3},{3,2},{4,5},{5,4},{6,7},{7,6},{8,9},{9,8},{10,11... | collective-permute-start | bytes 1105928 | tf_op jit(solution)/shard_map/ppermute | solution.py:25
  11.7 39.7 %collective-permute-start.20 = (bf16[3,16,5760]{2,1,0:T(8,128)(2,1)}, bf16[3,16,5760]{2,1,0:T(8,128)(2,1)}, u32[]{:S(2)}, u32[]{:S(2)}) collective-permute-start(bf16[3,16,5760]{2,1,0:T(8,128)(2,1)} %fusion.22), channel_id=1, source_target_pairs={{0,1},{1,0},{2,3},{3,2},{4,5},{5,4},{6,7},{7,6},{8,9},{9,8},{10,11... | collective-permute-start | bytes 1658888 | tf_op jit(solution)/shard_map/ppermute | solution.py:25
  33.8 16.4 %collective-permute-start.4 = (bf16[6,8,2304]{2,1,0:T(8,128)(2,1)}, bf16[6,8,2304]{2,1,0:T(8,128)(2,1)}, u32[]{:S(2)}, u32[]{:S(2)}) collective-permute-start(bf16[6,8,2304]{2,1,0:T(8,128)(2,1)} %constant_dynamic-slice_fusion.21), channel_id=1, source_target_pairs={{0,2},{1,3},{2,0},{3,1},{4,6},{5,7},{6,4},{7,5},{8,10},{9,11},{10,... | collective-permute-start | bytes 663560 | tf_op jit(solution)/shard_map/ppermute | solution.py:25
  35.2 18.1 %collective-permute-start.5 = (bf16[3,144,576]{2,1,0:T(8,128)(2,1)S(1)}, bf16[3,144,576]{2,1,0:T(8,128)(2,1)}, u32[]{:S(2)}, u32[]{:S(2)}) collective-permute-start(bf16[3,144,576]{2,1,0:T(8,128)(2,1)S(1)} %collective-permute-done.2.refs_6_.refs_11_), channel_id=1, source_target_pairs={{0,8},{4,12},{8,0},{12,4},{16,24},{20,28},{24,16},{28,20},{1,9},{5... | collective-permute-start | bytes 1493000 | tf_op jit(solution)/shard_map/ppermute | solution.py:25
  36.8 17.1 %collective-permute-start.6 = (bf16[3,144,576]{2,1,0:T(8,128)(2,1)}, bf16[3,144,576]{2,1,0:T(8,128)(2,1)}, u32[]{:S(2)}, u32[]{:S(2)}) collective-permute-start(bf16[3,144,576]{2,1,0:T(8,128)(2,1)} %collective-permute-done.3.refs_10_.refs_15_), channel_id=1, source_target_pairs={{0,4},{4,0},{8,12},{12,8},{16,20},{20,16},{24,28},{28,24},{1,5},{5... | collective-permute-start | bytes 1493000 | tf_op jit(solution)/shard_map/ppermute | solution.py:25
  49.0 37.0 %collective-permute-start.14 = (bf16[3,576,576]{2,1,0:T(8,128)(2,1)}, bf16[3,576,576]{2,1,0:T(8,128)(2,1)S(1)}, u32[]{:S(2)}, u32[]{:S(2)}) collective-permute-start(bf16[3,576,576]{2,1,0:T(8,128)(2,1)} %get-tuple-element.322), channel_id=1, source_target_pairs={{0,1},{1,0},{2,3},{3,2},{4,5},{5,4},{6,7},{7,6},{8,9},{9,8},{10,11... | collective-permute-start | bytes 5971976 | tf_op jit(solution)/shard_map/ppermute | solution.py:25
  51.5 14.7 %collective-permute-start.11 = (bf16[3,144,576]{2,1,0:T(8,128)(2,1)}, bf16[3,144,576]{2,1,0:T(8,128)(2,1)S(1)}, u32[]{:S(2)}, u32[]{:S(2)}) collective-permute-start(bf16[3,144,576]{2,1,0:T(8,128)(2,1)} %collective-permute-done.3.refs_10_.refs_15_), channel_id=1, source_target_pairs={{0,8},{4,12},{8,0},{12,4},{16,24},{20,28},{24,16},{28,20},{1,9},{5... | collective-permute-start | bytes 1493000 | tf_op jit(solution)/shard_map/ppermute | solution.py:25
  53.3 15.5 %collective-permute-start.9 = (bf16[3,144,576]{2,1,0:T(8,128)(2,1)S(1)}, bf16[3,144,576]{2,1,0:T(8,128)(2,1)S(1)}, u32[]{:S(2)}, u32[]{:S(2)}) collective-permute-start(bf16[3,144,576]{2,1,0:T(8,128)(2,1)S(1)} %collective-permute-done.2.refs_6_.refs_11_), channel_id=1, source_target_pairs={{0,4},{4,0},{8,12},{12,8},{16,20},{20,16},{24,28},{28,24},{1,5},{5... | collective-permute-start | bytes 1493000 | tf_op jit(solution)/shard_map/ppermute | solution.py:25
  53.9 27.3 %collective-permute-start.7 = (bf16[256,2304]{1,0:T(8,128)(2,1)S(1)}, bf16[256,2304]{1,0:T(8,128)(2,1)S(1)}, u32[]{:S(2)}, u32[]{:S(2)}) collective-permute-start(bf16[256,2304]{1,0:T(8,128)(2,1)S(1)} %fusion.3.refs_0_), channel_id=1, source_target_pairs={{0,2},{1,3},{2,0},{3,1},{4,6},{5,7},{6,4},{7,5},{8,10},{9,11},{10,... | collective-permute-start | bytes 3538952 | tf_op jit(solution)/shard_map/ppermute | solution.py:25
  55.4 24.0 %collective-permute-start.10 = (bf16[3,144,576]{2,1,0:T(8,128)(2,1)}, bf16[3,144,576]{2,1,0:T(8,128)(2,1)S(1)}, u32[]{:S(2)}, u32[]{:S(2)}) collective-permute-start(bf16[3,144,576]{2,1,0:T(8,128)(2,1)} %collective-permute-done.5.refs_7_.refs_12_), channel_id=1, source_target_pairs={{0,4},{4,0},{8,12},{12,8},{16,20},{20,16},{24,28},{28,24},{1,5},{5... | collective-permute-start | bytes 1493000 | tf_op jit(solution)/shard_map/ppermute | solution.py:25
  66.2 13.8 %collective-permute-start.12 = (bf16[3,144,576]{2,1,0:T(8,128)(2,1)}, bf16[3,144,576]{2,1,0:T(8,128)(2,1)S(1)}, u32[]{:S(2)}, u32[]{:S(2)}) collective-permute-start(bf16[3,144,576]{2,1,0:T(8,128)(2,1)} %collective-permute-done.6.refs_11_.refs_16_), channel_id=1, source_target_pairs={{0,8},{4,12},{8,0},{12,4},{16,24},{20,28},{24,16},{28,20},{1,9},{5... | collective-permute-start | bytes 1493000 | tf_op jit(solution)/shard_map/ppermute | solution.py:25
  68.8 16.6 %collective-permute-start = (bf16[256,2304]{1,0:T(8,128)(2,1)S(1)}, bf16[256,2304]{1,0:T(8,128)(2,1)S(1)}, u32[]{:S(2)}, u32[]{:S(2)}) collective-permute-start(bf16[256,2304]{1,0:T(8,128)(2,1)S(1)} %fusion.3.refs_0_), channel_id=1, source_target_pairs={{0,1},{1,0},{2,3},{3,2},{4,5},{5,4},{6,7},{7,6},{8,9},{9,8},{10,11... | collective-permute-start | bytes 3538952 | tf_op jit(solution)/shard_map/ppermute | solution.py:25
  82.7 26.6 %collective-permute-start.15 = (bf16[2,144,1440]{2,1,0:T(8,128)(2,1)}, bf16[2,144,1440]{2,1,0:T(8,128)(2,1)}, u32[]{:S(2)}, u32[]{:S(2)}) collective-permute-start(bf16[2,144,1440]{2,1,0:T(8,128)(2,1)} %get-tuple-element.155), channel_id=1, source_target_pairs={{0,2},{1,3},{2,0},{3,1},{4,6},{5,7},{6,4},{7,5},{8,10},{9,11},{10,... | collective-permute-start | bytes 2488328 | tf_op jit(solution)/shard_map/ppermute | solution.py:25
  84.0 25.3 %collective-permute-start.17 = (bf16[5,8,2304]{2,1,0:T(8,128)(2,1)}, bf16[5,8,2304]{2,1,0:T(8,128)(2,1)S(1)}, u32[]{:S(2)}, u32[]{:S(2)}) collective-permute-start(bf16[5,8,2304]{2,1,0:T(8,128)(2,1)} %constant_dynamic-slice_fusion.13), channel_id=1, source_target_pairs={{0,2},{1,3},{2,0},{3,1},{4,6},{5,7},{6,4},{7,5},{8,10},{9,11},{10,... | collective-permute-start | bytes 552968 | tf_op jit(solution)/shard_map/ppermute | solution.py:25
  85.5 49.2 %collective-permute-start.21 = (bf16[3,8,5760]{2,1,0:T(8,128)(2,1)}, bf16[3,8,5760]{2,1,0:T(8,128)(2,1)S(1)}, u32[]{:S(2)}, u32[]{:S(2)}) collective-permute-start(bf16[3,8,5760]{2,1,0:T(8,128)(2,1)} %constant_dynamic-slice_fusion.12), channel_id=1, source_target_pairs={{0,2},{1,3},{2,0},{3,1},{4,6},{5,7},{6,4},{7,5},{8,10},{9,11},{10,... | collective-permute-start | bytes 829448 | tf_op jit(solution)/shard_map/ppermute | solution.py:25
  86.1 48.7 %collective-permute-start.18 = (bf16[2,144,1440]{2,1,0:T(8,128)(2,1)}, bf16[2,144,1440]{2,1,0:T(8,128)(2,1)}, u32[]{:S(2)}, u32[]{:S(2)}) collective-permute-start(bf16[2,144,1440]{2,1,0:T(8,128)(2,1)} %get-tuple-element.160), channel_id=1, source_target_pairs={{0,3},{1,2},{2,1},{3,0},{4,7},{5,6},{6,5},{7,4},{8,11},{9,10},{10,... | collective-permute-start | bytes 2488328 | tf_op jit(solution)/shard_map/ppermute | solution.py:25
  109.3 25.2 %collective-permute-start.22 = (bf16[5,8,2304]{2,1,0:T(8,128)(2,1)S(1)}, bf16[5,8,2304]{2,1,0:T(8,128)(2,1)S(1)}, u32[]{:S(2)}, u32[]{:S(2)}) collective-permute-start(bf16[5,8,2304]{2,1,0:T(8,128)(2,1)S(1)} %collective-permute-done.17), channel_id=1, source_target_pairs={{0,1},{1,0},{2,3},{3,2},{4,5},{5,4},{6,7},{7,6},{8,9},{9,8},{10,11... | collective-permute-start | bytes 552968 | tf_op jit(solution)/shard_map/ppermute | solution.py:25
  109.9 24.9 %collective-permute-start.19 = (bf16[2,144,1440]{2,1,0:T(8,128)(2,1)}, bf16[2,144,1440]{2,1,0:T(8,128)(2,1)S(1)}, u32[]{:S(2)}, u32[]{:S(2)}) collective-permute-start(bf16[2,144,1440]{2,1,0:T(8,128)(2,1)} %collective-permute-done.15.refs_6_), channel_id=1, source_target_pairs={{0,8},{4,12},{8,0},{12,4},{16,24},{20,28},{24,16},{28,20},{1,9},{5... | collective-permute-start | bytes 2488328 | tf_op jit(solution)/shard_map/ppermute | solution.py:25
  142.0 22.3 %collective-permute-start.24 = (bf16[2,144,1440]{2,1,0:T(8,128)(2,1)}, bf16[2,144,1440]{2,1,0:T(8,128)(2,1)S(1)}, u32[]{:S(2)}, u32[]{:S(2)}) collective-permute-start(bf16[2,144,1440]{2,1,0:T(8,128)(2,1)} %collective-permute-done.18.refs_10_), channel_id=1, source_target_pairs={{0,4},{4,0},{8,12},{12,8},{16,20},{20,16},{24,28},{28,24},{1,5},{5... | collective-permute-start | bytes 2488328 | tf_op jit(solution)/shard_map/ppermute | solution.py:25
  170.3 29.9 %collective-permute-start.26 = (bf16[256,2432]{1,0:T(8,128)(2,1)S(1)}, bf16[256,2432]{1,0:T(8,128)(2,1)}, u32[]{:S(2)}, u32[]{:S(2)}) collective-permute-start(bf16[256,2432]{1,0:T(8,128)(2,1)S(1)} %add_convert_fusion.2), channel_id=1, source_target_pairs={{0,2},{1,3},{2,0},{3,1},{4,6},{5,7},{6,4},{7,5},{8,10},{9,11},{10,... | collective-permute-start | bytes 3735560 | tf_op jit(solution)/shard_map/ppermute | solution.py:25
  172.1 33.7 %collective-permute-start.33 = (bf16[256,2304]{1,0:T(8,128)(2,1)}, bf16[256,2304]{1,0:T(8,128)(2,1)}, u32[]{:S(2)}, u32[]{:S(2)}) collective-permute-start(bf16[256,2304]{1,0:T(8,128)(2,1)} %fusion.refs_2_), channel_id=1, source_target_pairs={{0,1},{1,0},{2,3},{3,2},{4,5},{5,4},{6,7},{7,6},{8,9},{9,8},{10,11... | collective-permute-start | bytes 3538952 | tf_op jit(solution)/shard_map/ppermute | solution.py:25
  181.4 66.0 %collective-permute-start.37 = (bf16[2,576,1440]{2,1,0:T(8,128)(2,1)S(1)}, bf16[2,576,1440]{2,1,0:T(8,128)(2,1)S(1)}, u32[]{:S(2)}, u32[]{:S(2)}) collective-permute-start(bf16[2,576,1440]{2,1,0:T(8,128)(2,1)S(1)} %get-tuple-element.318), channel_id=1, source_target_pairs={{0,1},{1,0},{2,3},{3,2},{4,5},{5,4},{6,7},{7,6},{8,9},{9,8},{10,11... | collective-permute-start | bytes 9953288 | tf_op jit(solution)/shard_map/ppermute | solution.py:25
  181.7 24.4 %collective-permute-start.29 = (bf16[2,144,1440]{2,1,0:T(8,128)(2,1)}, bf16[2,144,1440]{2,1,0:T(8,128)(2,1)S(1)}, u32[]{:S(2)}, u32[]{:S(2)}) collective-permute-start(bf16[2,144,1440]{2,1,0:T(8,128)(2,1)} %collective-permute-done.15.refs_6_), channel_id=1, source_target_pairs={{0,4},{4,0},{8,12},{12,8},{16,20},{20,16},{24,28},{28,24},{1,5},{5... | collective-permute-start | bytes 2488328 | tf_op jit(solution)/shard_map/ppermute | solution.py:25
  183.9 22.8 %collective-permute-start.35 = (bf16[3,8,5760]{2,1,0:T(8,128)(2,1)S(1)}, bf16[3,8,5760]{2,1,0:T(8,128)(2,1)S(1)}, u32[]{:S(2)}, u32[]{:S(2)}) collective-permute-start(bf16[3,8,5760]{2,1,0:T(8,128)(2,1)S(1)} %copy-done.49), channel_id=1, source_target_pairs={{0,1},{1,0},{2,3},{3,2},{4,5},{5,4},{6,7},{7,6},{8,9},{9,8},{10,11... | collective-permute-start | bytes 829448 | tf_op jit(solution)/shard_map/ppermute | solution.py:25
  200.2 22.5 %collective-permute-start.30 = (bf16[2,144,1440]{2,1,0:T(8,128)(2,1)S(1)}, bf16[2,144,1440]{2,1,0:T(8,128)(2,1)S(1)}, u32[]{:S(2)}, u32[]{:S(2)}) collective-permute-start(bf16[2,144,1440]{2,1,0:T(8,128)(2,1)S(1)} %copy-done.66), channel_id=1, source_target_pairs={{0,4},{4,0},{8,12},{12,8},{16,20},{20,16},{24,28},{28,24},{1,5},{5... | collective-permute-start | bytes 2488328 | tf_op jit(solution)/shard_map/ppermute | solution.py:25
  205.8 22.9 %collective-permute-start.31 = (bf16[2,144,1440]{2,1,0:T(8,128)(2,1)}, bf16[2,144,1440]{2,1,0:T(8,128)(2,1)S(1)}, u32[]{:S(2)}, u32[]{:S(2)}) collective-permute-start(bf16[2,144,1440]{2,1,0:T(8,128)(2,1)} %collective-permute-done.18.refs_10_), channel_id=1, source_target_pairs={{0,8},{4,12},{8,0},{12,4},{16,24},{20,28},{24,16},{28,20},{1,9},{5... | collective-permute-start | bytes 2488328 | tf_op jit(solution)/shard_map/ppermute | solution.py:25
  206.1 29.2 %collective-permute-start.34 = (bf16[256,2304]{1,0:T(8,128)(2,1)}, bf16[256,2304]{1,0:T(8,128)(2,1)}, u32[]{:S(2)}, u32[]{:S(2)}) collective-permute-start(bf16[256,2304]{1,0:T(8,128)(2,1)} %fusion.refs_2_), channel_id=1, source_target_pairs={{0,2},{1,3},{2,0},{3,1},{4,6},{5,7},{6,4},{7,5},{8,10},{9,11},{10,... | collective-permute-start | bytes 3538952 | tf_op jit(solution)/shard_map/ppermute | solution.py:25
  206.7 39.4 %collective-permute-start.32 = (bf16[2,144,1440]{2,1,0:T(8,128)(2,1)S(1)}, bf16[2,144,1440]{2,1,0:T(8,128)(2,1)S(1)}, u32[]{:S(2)}, u32[]{:S(2)}) collective-permute-start(bf16[2,144,1440]{2,1,0:T(8,128)(2,1)S(1)} %copy-done.68), channel_id=1, source_target_pairs={{0,8},{4,12},{8,0},{12,4},{16,24},{20,28},{24,16},{28,20},{1,9},{5... | collective-permute-start | bytes 2488328 | tf_op jit(solution)/shard_map/ppermute | solution.py:25
  222.6 23.4 %collective-permute-start.28 = (bf16[256,2304]{1,0:T(8,128)(2,1)S(1)}, bf16[256,2304]{1,0:T(8,128)(2,1)S(1)}, u32[]{:S(2)}, u32[]{:S(2)}) collective-permute-start(bf16[256,2304]{1,0:T(8,128)(2,1)S(1)} %multiply_convert_fusion.1.refs_0_), channel_id=1, source_target_pairs={{0,1},{1,0},{2,3},{3,2},{4,5},{5,4},{6,7},{7,6},{8,9},{9,8},{10,11... | collective-permute-start | bytes 3538952 | tf_op jit(solution)/shard_map/ppermute | solution.py:25
  228.7 70.1 %collective-permute-start.27 = (bf16[256,2304]{1,0:T(8,128)(2,1)S(1)}, bf16[256,2304]{1,0:T(8,128)(2,1)}, u32[]{:S(2)}, u32[]{:S(2)}) collective-permute-start(bf16[256,2304]{1,0:T(8,128)(2,1)S(1)} %multiply_convert_fusion.1.refs_0_), channel_id=1, source_target_pairs={{0,2},{1,3},{2,0},{3,1},{4,6},{5,7},{6,4},{7,5},{8,10},{9,11},{10,... | collective-permute-start | bytes 3538952 | tf_op jit(solution)/shard_map/ppermute | solution.py:25
  246.8 52.0 %collective-permute-start.36 = (bf16[256,2304]{1,0:T(8,128)(2,1)}, bf16[256,2304]{1,0:T(8,128)(2,1)}, u32[]{:S(2)}, u32[]{:S(2)}) collective-permute-start(bf16[256,2304]{1,0:T(8,128)(2,1)} %collective-permute-done.34.refs_2_), channel_id=1, source_target_pairs={{0,1},{1,0},{2,3},{3,2},{4,5},{5,4},{6,7},{7,6},{8,9},{9,8},{10,11... | collective-permute-start | bytes 3538952 | tf_op jit(solution)/shard_map/ppermute | solution.py:25
  359.3 29.8 %collective-permute-start.43 = (bf16[256,2432]{1,0:T(8,128)(2,1)S(1)}, bf16[256,2432]{1,0:T(8,128)(2,1)S(1)}, u32[]{:S(2)}, u32[]{:S(2)}) collective-permute-start(bf16[256,2432]{1,0:T(8,128)(2,1)S(1)} %copy-done.63), channel_id=1, source_target_pairs={{0,1},{1,0},{2,3},{3,2},{4,5},{5,4},{6,7},{7,6},{8,9},{9,8},{10,11... | collective-permute-start | bytes 3735560 | tf_op jit(solution)/shard_map/ppermute | solution.py:25
  359.7 29.4 %collective-permute-start.40 = (bf16[256,2432]{1,0:T(8,128)(2,1)S(1)}, bf16[256,2432]{1,0:T(8,128)(2,1)S(1)}, u32[]{:S(2)}, u32[]{:S(2)}) collective-permute-start(bf16[256,2432]{1,0:T(8,128)(2,1)S(1)} %add_convert_fusion.1), channel_id=1, source_target_pairs={{0,2},{1,3},{2,0},{3,1},{4,6},{5,7},{6,4},{7,5},{8,10},{9,11},{10,... | collective-permute-start | bytes 3735560 | tf_op jit(solution)/shard_map/ppermute | solution.py:25
  398.9 30.1 %collective-permute-start.44 = (bf16[256,2432]{1,0:T(8,128)(2,1)}, bf16[256,2432]{1,0:T(8,128)(2,1)}, u32[]{:S(2)}, u32[]{:S(2)}) collective-permute-start(bf16[256,2432]{1,0:T(8,128)(2,1)} %concatenate.106.refs_0_), channel_id=1, source_target_pairs={{0,2},{1,3},{2,0},{3,1},{4,6},{5,7},{6,4},{7,5},{8,10},{9,11},{10,... | collective-permute-start | bytes 3735560 | tf_op jit(solution)/shard_map/ppermute | solution.py:25
  430.2 36.3 %collective-permute-start.47 = (bf16[256,2432]{1,0:T(8,128)(2,1)}, bf16[256,2432]{1,0:T(8,128)(2,1)}, u32[]{:S(2)}, u32[]{:S(2)}) collective-permute-start(bf16[256,2432]{1,0:T(8,128)(2,1)} %add_convert_fusion), channel_id=1, source_target_pairs={{0,2},{1,3},{2,0},{3,1},{4,6},{5,7},{6,4},{7,5},{8,10},{9,11},{10,... | collective-permute-start | bytes 3735560 | tf_op jit(solution)/shard_map/ppermute | solution.py:25
  492.1 14.5 %collective-permute-start.52 = (bf16[2,216,576]{2,1,0:T(8,128)(2,1)}, bf16[2,216,576]{2,1,0:T(8,128)(2,1)}, u32[]{:S(2)}, u32[]{:S(2)}) collective-permute-start(bf16[2,216,576]{2,1,0:T(8,128)(2,1)} %constant_dynamic-slice_fusion.8), channel_id=1, source_target_pairs={{0,8},{4,12},{8,0},{12,4},{16,24},{20,28},{24,16},{28,20},{1,9},{5... | collective-permute-start | bytes 1493000 | tf_op jit(solution)/shard_map/ppermute | solution.py:25
  508.8 49.9 %collective-permute-start.53 = (bf16[4,216,576]{2,1,0:T(8,128)(2,1)}, bf16[4,216,576]{2,1,0:T(8,128)(2,1)}, u32[]{:S(2)}, u32[]{:S(2)}) collective-permute-start(bf16[4,216,576]{2,1,0:T(8,128)(2,1)} %constant_dynamic-slice_fusion.7), channel_id=1, source_target_pairs={{0,16},{4,20},{8,24},{12,28},{16,0},{20,4},{24,8},{28,12},{1,17},{... | collective-permute-start | bytes 2985992 | tf_op jit(solution)/shard_map/ppermute | solution.py:25
  564.2 21.3 %collective-permute-start.54 = (bf16[2,200,576]{2,1,0:T(8,128)(2,1)S(1)}, bf16[2,200,576]{2,1,0:T(8,128)(2,1)S(1)}, u32[]{:S(2)}, u32[]{:S(2)}) collective-permute-start(bf16[2,200,576]{2,1,0:T(8,128)(2,1)S(1)} %get-tuple-element.309), channel_id=1, source_target_pairs={{0,1},{1,0},{2,3},{3,2},{4,5},{5,4},{6,7},{7,6},{8,9},{9,8},{10,11... | collective-permute-start | bytes 1382408 | tf_op jit(solution)/shard_map/ppermute | solution.py:25
  564.3 21.3 %collective-permute-start.55 = (bf16[2,200,576]{2,1,0:T(8,128)(2,1)S(1)}, bf16[2,200,576]{2,1,0:T(8,128)(2,1)S(1)}, u32[]{:S(2)}, u32[]{:S(2)}) collective-permute-start(bf16[2,200,576]{2,1,0:T(8,128)(2,1)S(1)} %get-tuple-element.310), channel_id=1, source_target_pairs={{0,2},{1,3},{2,0},{3,1},{4,6},{5,7},{6,4},{7,5},{8,10},{9,11},{10,... | collective-permute-start | bytes 1382408 | tf_op jit(solution)/shard_map/ppermute | solution.py:25
  565.7 23.2 %collective-permute-start.56 = (bf16[2,200,576]{2,1,0:T(8,128)(2,1)S(1)}, bf16[2,200,576]{2,1,0:T(8,128)(2,1)S(1)}, u32[]{:S(2)}, u32[]{:S(2)}) collective-permute-start(bf16[2,200,576]{2,1,0:T(8,128)(2,1)S(1)} %get-tuple-element.308), channel_id=1, source_target_pairs={{0,3},{1,2},{2,1},{3,0},{4,7},{5,6},{6,5},{7,4},{8,11},{9,10},{10,... | collective-permute-start | bytes 1382408 | tf_op jit(solution)/shard_map/ppermute | solution.py:25
  613.0 14.9 %collective-permute-start.59 = (bf16[1024,48]{1,0:T(8,128)(2,1)S(1)}, bf16[1024,48]{1,0:T(8,128)(2,1)S(1)}, u32[]{:S(2)}, u32[]{:S(2)}) collective-permute-start(bf16[1024,48]{1,0:T(8,128)(2,1)S(1)} %add_convert_fusion.5), channel_id=1, source_target_pairs={{0,2},{1,3},{2,0},{3,1},{4,6},{5,7},{6,4},{7,5},{8,10},{9,11},{10,... | collective-permute-start | bytes 294920 | tf_op jit(solution)/shard_map/ppermute | solution.py:25
  632.2 13.9 %collective-permute-start.61 = (bf16[1,96,576]{2,1,0:T(8,128)(2,1)}, bf16[1,96,576]{2,1,0:T(8,128)(2,1)}, u32[]{:S(2)}, u32[]{:S(2)}) collective-permute-start(bf16[1,96,576]{2,1,0:T(8,128)(2,1)} %constant_dynamic-slice_fusion.2), channel_id=1, source_target_pairs={{0,4},{4,0},{8,12},{12,8},{16,20},{20,16},{24,28},{28,24},{1,5},{5... | collective-permute-start | bytes 331784 | tf_op jit(solution)/shard_map/ppermute | solution.py:25
  650.2 49.9 %collective-permute-start.67 = (bf16[256,2304]{1,0:T(8,128)(2,1)}, bf16[256,2304]{1,0:T(8,128)(2,1)}, u32[]{:S(2)}, u32[]{:S(2)}) collective-permute-start(bf16[256,2304]{1,0:T(8,128)(2,1)} %add_convert_fusion.3), channel_id=1, source_target_pairs={{0,2},{1,3},{2,0},{3,1},{4,6},{5,7},{6,4},{7,5},{8,10},{9,11},{10,... | collective-permute-start | bytes 3538952 | tf_op jit(solution)/shard_map/ppermute | solution.py:25
  657.3 23.7 %collective-permute-start.63 = (bf16[4,96,576]{2,1,0:T(8,128)(2,1)}, bf16[4,96,576]{2,1,0:T(8,128)(2,1)}, u32[]{:S(2)}, u32[]{:S(2)}) collective-permute-start(bf16[4,96,576]{2,1,0:T(8,128)(2,1)} %constant_dynamic-slice_fusion), channel_id=1, source_target_pairs={{0,16},{4,20},{8,24},{12,28},{16,0},{20,4},{24,8},{28,12},{1,17},{... | collective-permute-start | bytes 1327112 | tf_op jit(solution)/shard_map/ppermute | solution.py:25
  690.5 18.6 %collective-permute-start.60 = (bf16[256,2304]{1,0:T(8,128)(2,1)}, bf16[256,2304]{1,0:T(8,128)(2,1)}, u32[]{:S(2)}, u32[]{:S(2)}) collective-permute-start(bf16[256,2304]{1,0:T(8,128)(2,1)} %get-tuple-element.271), channel_id=1, source_target_pairs={{0,1},{1,0},{2,3},{3,2},{4,5},{5,4},{6,7},{7,6},{8,9},{9,8},{10,11... | collective-permute-start | bytes 3538952 | tf_op jit(solution)/shard_map/ppermute | solution.py:25
  (95 other events, 903.3 us)

commit v3 on v2

v3 whole, which is shorter than its diff:
```python
import functools
import math

import jax
import jax.numpy as jnp
from jax import lax
from jax.experimental import pallas as pl
from jax.experimental.pallas import tpu as pltpu
from jax.sharding import PartitionSpec as P

HDIM = 64
SPAN = 256
EPS = 1e-05
THETA = 10000.0
BRANCH = 1.4 / math.sqrt(40.0)
EXTRA = 128
F32 = jnp.float32
BF16 = jnp.bfloat16
LOG2E = math.log2(math.e)


def hop(values, axis, bit):
    size = lax.axis_size(axis)
    return lax.ppermute(values, axis, [(i, i ^ bit) for i in range(size)])


def core(values):
    return hop(values, "shard", 1)


def across(values):
    return hop(values, "shard", 2)


def rows_of(values, count):
    size = values.shape[0] // count
    return tuple(values[i * size : (i + 1) * size] for i in range(count))


def norm_rows(values, gain):
    return values * lax.rsqrt(jnp.mean(values * values, axis=-1, keepdims=True) + EPS) * gain


def norm_back(values, gain, grad):
    width = values.shape[-1]
    scale = lax.rsqrt(jnp.mean(values * values, axis=-1, keepdims=True) + EPS)
    moved = grad * gain
    inner = jnp.sum(values * moved, axis=-1, keepdims=True) / width
    return scale * moved - values * (scale * scale * scale) * inner


def dot(left, right):
    return jnp.dot(left, right, preferred_element_type=F32)


def dot_t(left, right):
    return lax.dot_general(left, right, (((1,), (1,)), ((), ())), preferred_element_type=F32)


def t_dot(left, right):
    return lax.dot_general(left, right, (((0,), (0,)), ((), ())), preferred_element_type=F32)


def pad_columns(pieces, width):
    used = sum(piece.shape[1] for piece in pieces)
    rest = jnp.zeros((pieces[0].shape[0], width - used), pieces[0].dtype)
    return jnp.concatenate(list(pieces) + [rest], axis=1)


def reps_bits():
    bits = []
    bit = 2
    while bit < lax.axis_size("rep"):
        bits.append(bit)
        bit *= 2
    return bits + [1]


def both(held, arrived, rep_place, bit):
    low = jnp.concatenate([held, arrived])
    high = jnp.concatenate([arrived, held])
    return jnp.where((rep_place // bit) % 2 == 0, low, high)


def send_sums(everyone, chosen, place):
    group = lax.axis_size("shard")
    per = chosen.shape[1] // group
    sent = []
    for j in range(group):
        marks = lax.dynamic_slice_in_dim(chosen, (place ^ j) * per, per, 1)
        sums = jnp.sum(marks[:, :, None, None] * everyone[:, None].astype(F32), axis=0).astype(BF16)
        sent.append(hop(sums, "shard", j) if j else sums)
    return sent


def chip_picked(bank, pick, place):
    per = bank.shape[1]
    rank = bank.shape[2]
    owner = pick // per
    mine = lax.dynamic_index_in_dim(bank, pick % per, 1, keepdims=False)
    mine = jnp.where(owner == place, mine, jnp.zeros_like(mine))
    chip = mine + core(mine)
    return chip, lax.dynamic_slice_in_dim(chip, (place % 2) * (rank // 2), rank // 2, 1)


def whole_picked(chip, far, place):
    other = core(far)
    low = jnp.where(place % 2 == 0, far, other)
    high = jnp.where(place % 2 == 0, other, far)
    return chip + jnp.concatenate([low, high], axis=1)


def after(value, *others):
    return lax.optimization_barrier((value, others))[0]


def side(weight, row, count, owner, size):
    return lax.dynamic_slice(weight, (0, row, owner * size), (weight.shape[0], count, size))


def sides(weight, row, count, place, size, wanted, name):
    maps, _, columns = weight.shape

    def kernel(where_ref, w_ref, *refs):
        outs, (held, sem) = refs[:-2], refs[-2:]
        start = pl.multiple_of(where_ref[1], 16)
        copy = pltpu.make_async_copy(w_ref.at[:, pl.ds(start, count), :], held, sem)
        copy.start()
        copy.wait()

        def write(out, owner):
            out[...] = jnp.concatenate(
                [held[i, :, owner * size : (owner + 1) * size] for i in range(maps)], axis=1
            )

        for j, out in zip(wanted, outs):
            for owner in range(columns // size):
                pl.when((where_ref[0] ^ j) == owner)(functools.partial(write, out, owner))

    return call(
        kernel,
        [jax.ShapeDtypeStruct((count, maps * size), BF16)] * len(wanted),
        [smem(), anywhere()],
        [vmem()] * len(wanted),
        [pltpu.VMEM((maps, count, columns), BF16), pltpu.SemaphoreType.DMA],
        0,
        2 * maps * count * (columns + size * len(wanted)),
        name,
        limit=58,
    )(jnp.stack([place, jnp.asarray(row, jnp.int32)]), weight)


def arrange(rows, own, near, ways, place, rep_place):
    quarter = rows // 4
    part = rep_place % 4
    pieces = [(place * rows, own), ((place ^ 1) * rows, near)]
    for j, one, two, parts in zip((2, 3), (2, 1), (1, 2), ways):
        for bits, piece in zip((0, one, two, one ^ two), parts):
            pieces.append(((place ^ j) * rows + (part ^ bits) * quarter, piece))
    offsets = jnp.stack([row.astype(jnp.int32) for row, _ in pieces])
    return offsets, [piece for _, piece in pieces]


def fence(*values):
    return lax.optimization_barrier(values)


def load_pieces(offsets, pieces, whole, sems):
    copies = []
    for number, piece in enumerate(pieces):
        start = pl.multiple_of(offsets[number], 16)
        here = pl.ds(start, piece.shape[-2])
        target = whole.at[here, :] if len(piece.shape) == 2 else whole.at[:, here, :]
        copy = pltpu.make_async_copy(piece, target, sems.at[number])
        copy.start()
        copies.append(copy)
    return copies


def vmem():
    return pl.BlockSpec(memory_space=pltpu.VMEM)


def smem():
    return pl.BlockSpec(memory_space=pltpu.SMEM)


def anywhere():
    return pl.BlockSpec(memory_space=pl.ANY)


def call(kernel, outs, in_specs, out_specs, scratch, flops, moved, name, limit=56, **more):
    return pl.pallas_call(
        kernel,
        out_shape=outs,
        in_specs=in_specs,
        out_specs=out_specs,
        scratch_shapes=scratch,
        compiler_params=pltpu.CompilerParams(vmem_limit_bytes=limit << 20),
        cost_estimate=pl.CostEstimate(flops=flops, bytes_accessed=moved, transcendentals=0),
        name=name,
        **more,
    )


def turn(values, cosine, sine):
    half = HDIM // 2
    turned = jnp.concatenate([-values[:, half:], values[:, :half]], axis=1)
    return values * cosine + turned * sine


def project(blocks, place, offsets, pieces, a_first, b_first, cosine, sine):
    rows, width = blocks[0].shape
    count = len(blocks)
    size = pieces[0].shape[1]
    heads = size // (3 * HDIM)
    thin = a_first.shape[0]
    n = len(pieces)

    def kernel(place_ref, offsets_ref, *refs):
        x_refs, refs = refs[:count], refs[count:]
        piece_refs, refs = refs[:n], refs[n:]
        a_ref, b_ref, cos_ref, sin_ref, q_ref, k_ref, v_ref, narrow_ref, whole, sems = refs
        copies = load_pieces(offsets_ref, piece_refs, whole, sems)
        starts = [pl.multiple_of((place_ref[0] ^ block) * rows, rows) for block in range(count)]
        for block in range(count):
            narrow_ref[:, pl.ds(starts[block], rows)] = dot_t(a_ref[...], x_refs[block][...]).astype(BF16)
        for copy in copies:
            copy.wait()
        for block in range(count):
            start = starts[block]
            narrow = narrow_ref[:, pl.ds(start, rows)]
            pre = dot(x_refs[block][...], whole[...]) + t_dot(narrow, b_ref[...])
            cosine_here = cos_ref[pl.ds(start, rows), :]
            sine_here = sin_ref[pl.ds(start, rows), :]
            for number, out in enumerate((q_ref, k_ref, v_ref)):
                for head in range(heads):
                    at = (number * heads + head) * HDIM
                    part = pre[:, at : at + HDIM]
                    if number < 2:
                        part = turn(part, cosine_here, sine_here)
                    out[head, pl.ds(start, rows), :] = part.astype(BF16)

    by_heads = jax.ShapeDtypeStruct((heads, rows * count, HDIM), BF16)
    return call(
        kernel,
        [by_heads] * 3 + [jax.ShapeDtypeStruct((thin, rows * count), BF16)],
        [smem(), smem()] + [vmem()] * count + [anywhere()] * n + [vmem()] * 4,
        [vmem()] * 4,
        [pltpu.VMEM((width, size), BF16), pltpu.SemaphoreType.DMA((n,))],
        2 * rows * count * width * size,
        2 * (rows * count * width + width * size + 2 * rows * count * size),
        "project",
        limit=44,
    )(place[None], offsets, *blocks, *pieces, a_first, b_first, cosine, sine)


def label_of(positions, starts_ref):
    label = jnp.full(positions.shape, -1, jnp.int32)
    for number in range(starts_ref.shape[0]):
        inside = (positions >= starts_ref[number]) & (positions < starts_ref[number] + SPAN)
        label = jnp.where(inside, jnp.int32(number), label)
    return label


def hidden_bias(query_at, key_at, starts_ref):
    query_label = label_of(query_at, starts_ref)
    key_label = label_of(key_at, starts_ref)
    visible = (key_at <= query_at) | (query_label == key_label) & (query_label >= 0)
    return jnp.where(visible, 0.0, -1e30)


def crosses(starts_ref, edge, rows):
    hit = None
    for number in range(starts_ref.shape[0]):
        start = starts_ref[number]
        here = (start < edge) & (start + SPAN > edge)
        hit = here if hit is None else hit | here
    return hit


def attend(starts, query, key, value, rows):
    heads, length, _ = query.shape
    count = length // rows
    factor = LOG2E / math.sqrt(HDIM)

    def kernel(starts_ref, q_ref, k_ref, v_ref, o_ref, bias):
        @pl.when(pl.program_id(0) == 0)
        def _():
            for block in range(count):
                shape = (rows, 2 * rows)
                query_at = block * rows + lax.broadcasted_iota(jnp.int32, shape, 0)
                key_at = block * rows + lax.broadcasted_iota(jnp.int32, shape, 1)
                bias[block] = hidden_bias(query_at, key_at, starts_ref)

        def one(block, extra):
            low, high = block * rows, (block + 1 + extra) * rows
            q = q_ref[0, low : low + rows, :]
            edge = dot_t(q, k_ref[0, low:high, :]) + bias[block, :, : high - low]
            top = jnp.max(edge, axis=1, keepdims=True)
            if block:
                before = dot_t(q, k_ref[0, :low, :])
                top = jnp.maximum(top, jnp.max(before, axis=1, keepdims=True))
            shift = top * factor
            weight = jnp.exp2(edge * factor - shift)
            total = jnp.sum(weight, axis=1, keepdims=True)
            out = dot(weight.astype(BF16), v_ref[0, low:high, :])
            if block:
                weight = jnp.exp2(before * factor - shift)
                total = total + jnp.sum(weight, axis=1, keepdims=True)
                out = out + dot(weight.astype(BF16), v_ref[0, :low, :])
            o_ref[0, low : low + rows, :] = (out / total).astype(BF16)

        for block in range(count):
            if block == count - 1:
                one(block, 0)
                continue
            wide = crosses(starts_ref, (block + 1) * rows, rows)
            pl.when(wide)(functools.partial(one, block, 1))
            pl.when(jnp.logical_not(wide))(functools.partial(one, block, 0))

    spec = pl.BlockSpec((1, length, HDIM), lambda h: (h, 0, 0))
    return call(
        kernel,
        jax.ShapeDtypeStruct(query.shape, BF16),
        [smem(), spec, spec, spec],
        spec,
        [pltpu.VMEM((count, rows, 2 * rows), F32)],
        4 * heads * length * length * HDIM * 4,
        16 * heads * length * HDIM,
        "attend",
        limit=20,
        grid=(heads,),
    )(starts, query, key, value)


def attend_back(
    starts, place, query, key, value, near, far, cosine, sine, narrow, b_heads, rows, first, heads
):
    length = query.shape[1]
    thin = narrow.shape[0]
    rank = thin // 3
    count = length // rows
    scale = 1.0 / math.sqrt(HDIM)
    factor = LOG2E * scale

    def kernel(
        starts_ref, place_ref, q_ref, k_ref, v_ref, near_ref, far_ref, cos_ref, sin_ref,
        narrow_ref, b_ref, dq_ref, dk_ref, dv_ref, thin_ref, out_ref, bias, key_sum, value_sum, key_turned,
    ):
        @pl.when(pl.program_id(0) == 0)
        def _():
            for block in range(count):
                shape = (2 * rows, rows)
                query_at = block * rows + lax.broadcasted_iota(jnp.int32, shape, 1)
                key_at = block * rows + lax.broadcasted_iota(jnp.int32, shape, 0)
                bias[block] = hidden_bias(query_at, key_at, starts_ref)

            thin_ref[...] = jnp.zeros_like(thin_ref)

        key_sum[...] = jnp.zeros_like(key_sum)
        value_sum[...] = jnp.zeros_like(value_sum)
        key_turned[...] = k_ref[0].astype(F32).T.astype(BF16)

        def one(block, extra):
            low, high = block * rows, (block + 1 + extra) * rows
            q = q_ref[0, low : low + rows, :]
            relative = place_ref[0] ^ block
            at = pl.multiple_of((relative % 2) * rows, rows)
            g = jnp.where(relative < 2, near_ref[0, pl.ds(at, rows), :], far_ref[0, pl.ds(at, rows), :])
            raw = dot_t(k_ref[0, low:high, :], q) + bias[block, : high - low, :]
            if block:
                raw = jnp.concatenate([dot_t(k_ref[0, :low, :], q), raw], axis=0)
            top = jnp.max(raw, axis=0, keepdims=True)
            weight = jnp.exp2(raw * factor - top * factor)
            probs = weight * (1.0 / jnp.sum(weight, axis=0, keepdims=True))
            grad_probs = dot_t(v_ref[0, :high, :], g)
            inner = jnp.sum(grad_probs * probs, axis=0, keepdims=True)
            grad_scores = (probs * (grad_probs - inner)).astype(BF16)
            value_sum[:high, :] += dot(probs.astype(BF16), g)
            key_sum[:high, :] += dot(grad_scores, q)
            turned = dot(key_turned[:, :high], grad_scores)
            back = turned.T * scale
            dq_ref[0, low : low + rows, :] = turn(
                back, cos_ref[low : low + rows, :], -sin_ref[low : low + rows, :]
            ).astype(BF16)

        for block in range(count):
            if block == count - 1:
                one(block, 0)
                continue
            wide = crosses(starts_ref, (block + 1) * rows, rows)
            pl.when(wide)(functools.partial(one, block, 1))
            pl.when(jnp.logical_not(wide))(functools.partial(one, block, 0))
        dk_ref[0] = turn(key_sum[...] * scale, cos_ref[...], -sin_ref[...]).astype(BF16)
        dv_ref[0] = value_sum[...].astype(BF16)
        for number, ref in enumerate((dq_ref, dk_ref, dv_ref)):
            here = slice(number * rank, (number + 1) * rank)
            thin_ref[here, :] += dot_t(b_ref[0, here, :], ref[0])
            out_ref[0, here, :] = dot(narrow_ref[here, :], ref[0])

    spec = pl.BlockSpec((1, length, HDIM), lambda h: (first + h, 0, 0))
    half = pl.BlockSpec((1, length // 2, HDIM), lambda h: (first + h, 0, 0))
    out = pl.BlockSpec((1, length, HDIM), lambda h: (h, 0, 0))
    table = pl.BlockSpec((length, HDIM), lambda h: (0, 0))
    return call(
        kernel,
        [jax.ShapeDtypeStruct((heads, length, HDIM), BF16)] * 3
        + [
            jax.ShapeDtypeStruct((thin, length), F32),
            jax.ShapeDtypeStruct((heads, thin, HDIM), F32),
        ],
        [smem(), smem(), spec, spec, spec, half, half, table, table]
        + [
            pl.BlockSpec((thin, length), lambda h: (0, 0)),
            pl.BlockSpec((1, thin, HDIM), lambda h: (first + h, 0, 0)),
        ],
        [out] * 3
        + [
            pl.BlockSpec((thin, length), lambda h: (0, 0)),
            pl.BlockSpec((1, thin, HDIM), lambda h: (h, 0, 0)),
        ],
        [
            pltpu.VMEM((count, 2 * rows, rows), F32),
            pltpu.VMEM((length, HDIM), F32),
            pltpu.VMEM((length, HDIM), F32),
            pltpu.VMEM((HDIM, length), BF16),
        ],
        10 * heads * length * length * HDIM * 4,
        32 * heads * length * HDIM,
        "attend_back",
        limit=24,
        grid=(heads,),
    )(starts, place[None], query, key, value, near, far, cosine, sine, narrow, b_heads)


def rows_by_heads(refs, start, rows):
    return jnp.concatenate(
        [ref[head, pl.ds(start, rows), :] for ref in refs for head in range(ref.shape[0])], axis=1
    )


def close_attention(mixed, place, weight, a_out, wanted, rows):
    size, width = weight.shape
    rank = a_out.shape[0]

    def kernel(place_ref, m_ref, w_ref, a_ref, *outs):
        for block, out in zip(wanted, outs):
            start = pl.multiple_of((place_ref[0] ^ block) * rows, rows)
            here = rows_by_heads([m_ref], start, rows)
            out[:, :width] = dot(here, w_ref[...]).astype(BF16)
            narrow = dot_t(here, a_ref[...]).astype(BF16)
            out[:, width:] = jnp.concatenate(
                [narrow, jnp.zeros((rows, EXTRA - rank), BF16)], axis=1
            )

    return call(
        kernel,
        [jax.ShapeDtypeStruct((rows, width + EXTRA), BF16)] * len(wanted),
        [smem()] + [vmem()] * 3,
        [vmem()] * len(wanted),
        [],
        2 * rows * len(wanted) * size * width,
        2 * size * width + 2 * rows * len(wanted) * (width + size),
        "close_attention",
        limit=28,
    )(place[None], mixed, weight, a_out)


def open_attention(blocks, seconds, wanted, place, mixed, weight, a_out, b_out):
    rows, width_ext = blocks[0].shape
    size, width = weight.shape
    rank = a_out.shape[0]
    count = len(blocks)
    heads = size // HDIM

    def kernel(place_ref, *refs):
        g_refs, refs = refs[:count], refs[count:]
        s_refs, refs = refs[:count], refs[count:]
        m_ref, w_ref, a_ref, b_ref, out, sum_ref, wide_ref = refs
        total, branch, second = None, None, None
        for block in range(count):
            start = pl.multiple_of((place_ref[0] ^ wanted[block]) * rows, rows)
            grad = g_refs[block][:, :width]
            thin = g_refs[block][:, width:]
            narrow = dot_t(grad, b_ref[...]).astype(BF16)
            back = dot_t(grad, w_ref[...]) + dot(narrow, a_ref[...])
            for head in range(heads):
                part = back[:, head * HDIM : (head + 1) * HDIM]
                out[head, block * rows : (block + 1) * rows, :] = part.astype(BF16)
            terms = (
                t_dot(narrow, rows_by_heads([m_ref], start, rows)),
                t_dot(thin, grad)[:rank],
                t_dot(thin, s_refs[block][...])[rank : 3 * rank],
            )
            if block == 0:
                total, branch, second = terms
            else:
                total, branch, second = total + terms[0], branch + terms[1], second + terms[2]
        sum_ref[...] = total
        wide_ref[:rank, :] = branch
        wide_ref[rank:, :] = second

    return call(
        kernel,
        [
            jax.ShapeDtypeStruct((heads, rows * count, HDIM), BF16),
            jax.ShapeDtypeStruct((rank, size), F32),
            jax.ShapeDtypeStruct((3 * rank, width), F32),
        ],
        [smem()] + [vmem()] * (2 * count + 4),
        [vmem()] * 3,
        [],
        2 * rows * count * size * width,
        2 * size * width + 2 * rows * count * (2 * width + 2 * size),
        "open_attention",
        limit=32,
    )(place[None], *blocks, *seconds, mixed, weight, a_out, b_out)


def feed_forward(blocks, grads, offsets, pieces, down, a_mlp, b_down, a_hidden, b_hidden):
    rows, width = blocks[0].shape
    count = len(blocks)
    size = down.shape[0]
    rank = b_down.shape[0]
    n = len(pieces)

    def kernel(offsets_ref, *refs):
        x_refs, refs = refs[:count], refs[count:]
        g_refs, refs = refs[:count], refs[count:]
        piece_refs, refs = refs[:n], refs[n:]
        down_hbm, am_ref, bd_ref, ah_ref, bh_ref = refs[:5]
        refs = refs[5:]
        feed_refs, refs = refs[:count], refs[count:]
        back_refs, refs = refs[:count], refs[count:]
        sum_ref, whole, down_ref, grad_ref, sems, down_sem = refs
        down_copy = pltpu.make_async_copy(down_hbm, down_ref, down_sem)
        down_copy.start()
        copies = load_pieces(offsets_ref, piece_refs, whole, sems)
        narrows = [dot_t(x_refs[block][...], am_ref[...]).astype(BF16) for block in range(count)]
        thins = [dot_t(g_refs[block][...], bd_ref[...]).astype(BF16) for block in range(count)]
        down_copy.wait()
        for block in range(count):
            grad_ref[block] = (
                dot_t(g_refs[block][...], down_ref[...]) + dot(thins[block], ah_ref[...])
            ).astype(BF16)
        for copy in copies:
            copy.wait()
        pad = jnp.zeros((rows, EXTRA - rank), BF16)
        for block in range(count):
            x = x_refs[block][...]
            narrow = narrows[block]
            gate = dot(x, whole[0]) + dot(narrow[:, :rank], bh_ref[0])
            up = dot(x, whole[1]) + dot(narrow[:, rank:], bh_ref[1])
            sigmoid = 0.5 + 0.5 * jnp.tanh(0.5 * gate)
            silu = gate * sigmoid
            hidden = (silu * up).astype(BF16)
            grad_hidden = grad_ref[block].astype(F32)
            grad_up = (grad_hidden * silu).astype(BF16)
            grad_gate = (grad_hidden * up * (sigmoid + silu * (1.0 - sigmoid))).astype(BF16)
            feed_refs[block][:, :width] = dot(hidden, down_ref[...]).astype(BF16)
            feed_refs[block][:, width:] = jnp.concatenate(
                [dot_t(hidden, ah_ref[...]).astype(BF16), pad], axis=1
            )
            back = dot_t(grad_gate, whole[0]) + dot_t(grad_up, whole[1])
            back_refs[block][:, :width] = back.astype(BF16)
            back_refs[block][:, width:] = jnp.concatenate(
                [
                    dot_t(grad_gate, bh_ref[0]).astype(BF16),
                    dot_t(grad_up, bh_ref[1]).astype(BF16),
                    pad[:, rank:],
                ],
                axis=1,
            )
            terms = (
                t_dot(thins[block], hidden),
                t_dot(narrow[:, :rank], grad_gate),
                t_dot(narrow[:, rank:], grad_up),
            )
            for number, term in enumerate(terms):
                here = slice(number * rank, (number + 1) * rank)
                if block == 0:
                    sum_ref[here, :] = term
                else:
                    sum_ref[here, :] += term

    out = jax.ShapeDtypeStruct((rows, width + EXTRA), BF16)
    return call(
        kernel,
        [out] * (2 * count)
        + [jax.ShapeDtypeStruct((3 * rank, size), F32)],
        [smem()] + [vmem()] * (2 * count) + [anywhere()] * (n + 1) + [vmem()] * 4,
        [vmem()] * (2 * count + 1),
        [
            pltpu.VMEM((2, width, size), BF16),
            pltpu.VMEM((size, width), BF16),
            pltpu.VMEM((count, rows, size), BF16),
            pltpu.SemaphoreType.DMA((n,)),
            pltpu.SemaphoreType.DMA,
        ],
        12 * rows * count * width * size,
        6 * width * size + 8 * rows * count * width,
        "feed_forward",
    )(offsets, *blocks, *grads, *pieces, down, a_mlp, b_down, a_hidden, b_hidden)


def project_back(grads, place, offsets, pieces, wanted, rows):
    size = pieces[0].shape[1]
    width = 4 * pieces[0].shape[0]
    n = len(pieces)
    count = len(wanted)

    def kernel(place_ref, offsets_ref, *refs):
        g_refs, refs = refs[: len(grads)], refs[len(grads) :]
        piece_refs, refs = refs[:n], refs[n:]
        back_refs, (whole, sems) = refs[:count], refs[count:]
        copies = load_pieces(offsets_ref, piece_refs, whole, sems)
        starts = [pl.multiple_of((place_ref[0] ^ block) * rows, rows) for block in wanted]
        parts = [rows_by_heads(g_refs, start, rows) for start in starts]
        for copy in copies:
            copy.wait()
        for part, back in zip(parts, back_refs):
            back[...] = dot_t(part, whole[...]).astype(BF16)

    return call(
        kernel,
        [jax.ShapeDtypeStruct((rows, width), BF16)] * count,
        [smem(), smem()] + [vmem()] * len(grads) + [anywhere()] * n,
        [vmem()] * count,
        [pltpu.VMEM((width, size), BF16), pltpu.SemaphoreType.DMA((n,))],
        2 * rows * count * width * size,
        2 * (rows * count * (width + size) + width * size),
        "project_back",
        limit=56,
    )(place[None], offsets, *grads, *pieces)


def thin_product(thin, place, blocks):
    rows, width = blocks[0].shape
    count = len(blocks)

    def kernel(place_ref, thin_ref, *refs):
        total = None
        for block in range(count):
            start = pl.multiple_of((place_ref[0] ^ block) * rows, rows)
            term = dot(thin_ref[:, pl.ds(start, rows)], refs[block][...])
            total = term if total is None else total + term
        refs[count][...] = total

    return call(
        kernel,
        jax.ShapeDtypeStruct((thin.shape[0], width), F32),
        [smem()] + [vmem()] * (count + 1),
        vmem(),
        [],
        2 * 128 * rows * count * width,
        2 * rows * count * width,
        "thin_product",
        limit=24,
    )(place[None], thin, *blocks)


def shards(
    tokens,
    cotangent,
    sequence_adapter_index,
    image_span_start,
    attention_norm_gain,
    feedforward_norm_gain,
    query_key_value_weight,
    attention_output_weight,
    gate_up_projection_weight,
    down_projection_weight,
    adapter_model_input_maps,
    adapter_model_output_maps,
    adapter_hidden_input_map,
    adapter_hidden_output_maps,
):
    rows = tokens.shape[1]
    width = tokens.shape[2]
    rank = adapter_model_input_maps.shape[2]
    group = lax.axis_size("shard")
    place = lax.axis_index("shard").astype(jnp.int32)
    rep_place = lax.axis_index("rep").astype(jnp.int32)
    pick = sequence_adapter_index[0]
    starts = image_span_start[0]
    head_cols = width // group
    ff_cols = down_projection_weight.shape[0]
    k_rows = query_key_value_weight.shape[1]

    gain_one = attention_norm_gain.astype(F32)
    gain_two = feedforward_norm_gain.astype(F32)
    residual_in = tokens[0].astype(F32)
    grad_out = cotangent[0].astype(F32)

    def own_columns(values, size):
        return lax.dynamic_slice_in_dim(values, place * size, size, values.ndim - 1)

    quarter = k_rows // 4
    quarter_one, quarter_two = sides(
        query_key_value_weight, rep_place % 4 * quarter, quarter, place, head_cols, (2, 3), "sides_far"
    )
    first_a = hop(quarter_one, "shard", 2)
    first_b = hop(quarter_two, "shard", 3)
    normed = norm_rows(residual_in, gain_one).astype(BF16)
    normed_near = core(normed)
    front_chip, front_part = chip_picked(
        jnp.concatenate([adapter_model_input_maps[0:3], adapter_model_output_maps[0:3]]), pick, place
    )
    first_own, near_out = sides(
        query_key_value_weight, 0, k_rows, place, head_cols, (0, 1), "sides_near"
    )
    first_near = core(near_out)
    first_a, front_part, normed, first_own = fence(first_a, front_part, normed, first_own)
    first_a_two, first_a_three = hop(first_a, "rep", 2), hop(first_a, "rep", 1)
    front_far = across(front_part)
    first_b, first_a_two, first_a_three, normed = fence(first_b, first_a_two, first_a_three, normed)
    first_b_two, first_b_three = hop(first_b, "rep", 1), hop(first_b, "rep", 2)
    normed_far = across(normed)
    first_b_two, first_b_three, front_far, gate_up, grad_out, front_chip = fence(
        first_b_two, first_b_three, front_far, gate_up_projection_weight, grad_out, front_chip
    )
    first_a_four, first_b_four = hop(first_a_two, "rep", 1), hop(first_b_two, "rep", 2)
    mlp_leaving = [side(gate_up, rep_place % 4 * quarter, quarter, place ^ j, ff_cols) for j in (2, 3)]
    grad_feed = (BRANCH * grad_out).astype(BF16)
    half = HDIM // 2
    frequency = jnp.exp(jnp.arange(half, dtype=F32) * (-2.0 / HDIM) * math.log(THETA))
    angle = jnp.arange(rows * group, dtype=jnp.int32).astype(F32)[:, None] * frequency[None, :]
    cosine = jnp.concatenate([jnp.cos(angle), jnp.cos(angle)], axis=1)
    sine = jnp.concatenate([jnp.sin(angle), jnp.sin(angle)], axis=1)
    front = whole_picked(front_chip, front_far, place)
    a_first = front[:3].reshape(3 * rank, width)
    b_first = own_columns(front[3:], head_cols)
    b_wide = jnp.concatenate(
        [jnp.pad(b_first[i], ((0, 0), (i * head_cols, (2 - i) * head_cols))) for i in range(3)]
    )
    normed_far, first_a_four, first_b_four, mlp_leaving, grad_feed, cosine, sine, b_wide, a_first = fence(
        normed_far, first_a_four, first_b_four, mlp_leaving, grad_feed, cosine, sine, b_wide, a_first
    )
    first_blocks = (normed, normed_near, normed_far, core(normed_far))
    first_offsets, first_pieces = arrange(
        k_rows, first_own, first_near,
        (
            (first_a, first_a_two, first_a_three, first_a_four),
            (first_b, first_b_two, first_b_three, first_b_four),
        ),
        place, rep_place,
    )

    mlp_a, mlp_b = hop(mlp_leaving[0], "shard", 2), hop(mlp_leaving[1], "shard", 3)
    query, key, value, narrow_first = project(
        first_blocks, place, first_offsets, first_pieces, a_first, b_wide, cosine, sine
    )
    query, mlp_a, rest_bank, wide_bank = fence(
        query, mlp_a,
        (adapter_model_input_maps[3:6], adapter_model_output_maps[3:5]),
        (adapter_hidden_input_map[None], adapter_hidden_output_maps),
    )
    mlp_a_two, mlp_a_three = hop(mlp_a, "rep", 2), hop(mlp_a, "rep", 1)
    rest_chip, rest_part = chip_picked(jnp.concatenate(rest_bank), pick, place)
    wide_chip, wide_part = chip_picked(jnp.concatenate(wide_bank), pick, place)
    rest_part, wide_part, query = fence(rest_part, wide_part, query)
    rest_far, wide_far = across(rest_part), across(wide_part)
    mixed = attend(starts, query, key, value, rows)
    mixed, mlp_b, mlp_a_two, mlp_a_three, rest_far = fence(
        mixed, mlp_b, mlp_a_two, mlp_a_three, rest_far
    )
    mlp_b_two, mlp_b_three = hop(mlp_b, "rep", 1), hop(mlp_b, "rep", 2)
    rest = whole_picked(rest_chip, rest_far, place)
    a_out = own_columns(rest[0], head_cols)
    a_mlp = rest[1:3].reshape(2 * rank, width)
    b_out, b_down = rest[3], rest[4]
    far_out = close_attention(mixed, place, attention_output_weight, a_out, (2, 3), rows)
    far_sum = (far_out[0].astype(F32) + core(far_out[1]).astype(F32)).astype(BF16)
    far_sum, mixed_here, grad_feed, wide_far = fence(far_sum, mixed, grad_feed, wide_far)
    branch_far = across(far_sum)
    feed_near_in = core(grad_feed)
    near_out = close_attention(mixed_here, place, attention_output_weight, a_out, (0, 1), rows)
    near_out, mlp_b_two, mlp_b_three, gate_up = fence(near_out, mlp_b_two, mlp_b_three, gate_up)
    mlp_a_four, mlp_b_four = hop(mlp_a_two, "rep", 1), hop(mlp_b_two, "rep", 2)
    near_here = core(near_out[1])
    mlp_near = core(side(gate_up, 0, k_rows, place ^ 1, ff_cols))
    mlp_own = side(gate_up, 0, k_rows, place, ff_cols)
    hidden_cols = own_columns(whole_picked(wide_chip, wide_far, place), ff_cols)
    near_here, branch_far, hidden_cols, mlp_own, mlp_a_four, mlp_b_four = fence(
        near_here, branch_far, hidden_cols, mlp_own, mlp_a_four, mlp_b_four
    )
    feed_far_in = across(after(grad_feed, branch_far))
    a_hidden, b_hidden = hidden_cols[0], hidden_cols[1:]
    branch_own = near_out[0].astype(F32) + near_here.astype(F32) + branch_far.astype(F32)
    narrow_out = branch_own[:, width : width + rank].astype(BF16)
    branch = branch_own[:, :width] + dot(narrow_out, b_out)
    middle = residual_in + BRANCH * branch
    normed_second = norm_rows(middle, gain_two).astype(BF16)
    second_far = across(normed_second)
    second_near = core(normed_second)
    second_near, feed_near_in, mlp_near = fence(second_near, feed_near_in, mlp_near)
    mlp_offsets, mlp_pieces = arrange(
        k_rows, mlp_own, mlp_near,
        (
            (mlp_a, mlp_a_two, mlp_a_three, mlp_a_four),
            (mlp_b, mlp_b_two, mlp_b_three, mlp_b_four),
        ),
        place, rep_place,
    )
    *parts, sum_near = feed_forward(
        (normed_second, second_near), (grad_feed, feed_near_in), mlp_offsets, mlp_pieces,
        down_projection_weight, a_mlp, b_down, a_hidden, b_hidden,
    )
    feed_near, back_near = parts[:2], parts[2:]
    second_far, feed_far_in, back_near, feed_near = fence(second_far, feed_far_in, back_near, feed_near)
    second_blocks = (normed_second, second_near, second_far, core(second_far))
    feed_blocks = (grad_feed, feed_near_in, feed_far_in, core(feed_far_in))
    *parts, sum_far = feed_forward(
        second_blocks[2:], feed_blocks[2:], mlp_offsets, mlp_pieces, down_projection_weight,
        a_mlp, b_down, a_hidden, b_hidden,
    )
    feed_far, back_far = parts[:2], parts[2:]
    back_sum = (back_far[0].astype(F32) + core(back_far[1]).astype(F32)).astype(BF16)
    back_sum, back_near, feed_near, feed_far, sum_near = fence(
        back_sum, back_near, feed_near, feed_far, sum_near
    )
    back_from_far = across(back_sum)

    bits = reps_bits()
    back_here = core(back_near[1])
    feed_here = core(feed_near[1])
    feed_mate = core(feed_far[1])
    mark = jnp.full((rank, ff_cols), pick.astype(F32))
    wide_all = jnp.concatenate([sum_near + sum_far, mark]).astype(BF16)[None]
    wide_hop = hop(wide_all, "rep", bits[0])
    feed_here = feed_near[0].astype(F32) + feed_here.astype(F32)
    feed_sum = (feed_far[0].astype(F32) + feed_mate.astype(F32)).astype(BF16)
    back_from_far, feed_here, feed_sum, back_here, wide_hop = fence(
        back_from_far, feed_here, feed_sum, back_here, wide_hop
    )
    second_own = back_near[0].astype(F32) + back_here.astype(F32) + back_from_far.astype(F32)
    grad_narrow_mlp = second_own[:, width : width + 2 * rank].astype(BF16)
    grad_normed_second = second_own[:, :width] + dot(grad_narrow_mlp, a_mlp)
    grad_middle = grad_out + norm_back(middle, gain_two, grad_normed_second)
    grad_branch = (BRANCH * grad_middle).astype(BF16)
    branch_rows = pad_columns([grad_branch, narrow_out, grad_narrow_mlp], width + EXTRA)
    branch_rows, wide_hop = fence(branch_rows, wide_hop)
    branch_far_in = across(branch_rows)
    branch_near_in = core(branch_rows)
    wide_all = both(wide_all, wide_hop, rep_place, bits[0])
    for bit in bits[1:-2]:
        wide_all = both(wide_all, hop(wide_all, "rep", bit), rep_place, bit)
    wide_hop = hop(wide_all, "rep", bits[-2])
    branch_near_in, wide_all = fence(branch_near_in, wide_all)
    mixed_near, grad_a_near, thin_near = open_attention(
        (branch_rows, branch_near_in), second_blocks[:2], (0, 1), place, mixed,
        attention_output_weight, a_out, b_out,
    )
    branch_far_in, mixed_near = fence(branch_far_in, mixed_near)
    feed_from_far = across(after(feed_sum, branch_far_in))
    mixed_far, grad_a_far, thin_far = open_attention(
        (branch_far_in, core(branch_far_in)), second_blocks[2:], (2, 3), place, mixed,
        attention_output_weight, a_out, b_out,
    )

    b_heads = b_first.reshape(3 * rank, head_cols // HDIM, HDIM).transpose(1, 0, 2)

    def attend_part(first, heads, starts):
        return attend_back(
            starts, place, query, key, value, mixed_near, mixed_far, cosine, sine, narrow_first, b_heads,
            rows, first, heads,
        )

    mixed_far, wide_hop = fence(mixed_far, wide_hop)
    wide_all = both(wide_all, wide_hop, rep_place, bits[-2])
    wide_hop = hop(wide_all, "rep", bits[-1])
    wide_all, starts_one = fence(wide_all, starts)
    heads = query.shape[0]
    third = heads // 3
    part_one = attend_part(0, third, starts_one)
    part_one, feed_from_far, wide_hop, starts_two = fence(part_one, feed_from_far, wide_hop, starts_one)
    wide_all = both(wide_all, wide_hop, rep_place, bits[-1])
    picks = wide_all[:, -1, :1].astype(F32)
    adapters = adapter_model_input_maps.shape[1] * group
    chosen = (picks == jnp.arange(adapters, dtype=jnp.int32).astype(F32)[None, :]).astype(F32)
    wide_sent = send_sums(wide_all[:, :-rank], chosen, place)
    early_all = jnp.concatenate(
        [grad_a_near + grad_a_far, own_columns(thin_near + thin_far, head_cols)]
    ).astype(BF16)[None]
    early_hop = hop(early_all, "rep", bits[0])
    feed_own = feed_here + feed_from_far.astype(F32)
    narrow_down = feed_own[:, width : width + rank].astype(BF16)
    down_far = across(narrow_down)
    down_near = core(narrow_down)
    starts_two, narrow_down, early_all = fence(starts_two, narrow_down, early_all)
    part_two = attend_part(third, third, starts_two)
    part_two, wide_sent, early_hop, down_far, down_near, starts_three = fence(
        part_two, wide_sent, early_hop, down_far, down_near, starts_two
    )
    early_all = both(early_all, early_hop, rep_place, bits[0])
    for bit in bits[1:-2]:
        early_all = both(early_all, hop(early_all, "rep", bit), rep_place, bit)
    early_hop = hop(early_all, "rep", bits[-2])
    down_far_near = core(down_far)
    early_all, starts_three = fence(early_all, starts_three)
    part_three = attend_part(2 * third, heads - 2 * third, starts_three)
    part_three, early_hop, down_far_near = fence(part_three, early_hop, down_far_near)
    parts = (part_one, part_two, part_three)
    first_grads = [part[number] for number in range(3) for part in parts]
    thin = (part_one[3] + part_two[3] + part_three[3]).astype(BF16)
    thin_hop = core(thin)
    early_all = both(early_all, early_hop, rep_place, bits[-2])
    early_hop = hop(early_all, "rep", bits[-1])
    early_all, first_grads = fence(early_all, first_grads)
    back_rows_far = project_back(first_grads, place, first_offsets, first_pieces, (2, 3), rows)
    back_rows_far, thin_hop, early_hop = fence(back_rows_far, thin_hop, early_hop)
    back_mate = core(back_rows_far[1])
    thin = (thin.astype(F32) + thin_hop.astype(F32)).astype(BF16)
    thin_hop = across(thin)
    back_sum = (back_rows_far[0].astype(F32) + back_mate.astype(F32)).astype(BF16)
    thin_hop, back_sum, grad_b_heads = fence(thin_hop, back_sum, [part[4] for part in parts])
    back_far_in = across(back_sum)
    grad_narrow = (thin.astype(F32) + thin_hop.astype(F32)).astype(BF16)
    grad_b_first = jnp.concatenate(grad_b_heads).transpose(1, 0, 2).reshape(3 * rank, head_cols)
    down_thin = (narrow_down, down_near, down_far, down_far_near)
    grad_b_down = sum(t_dot(left, right) for left, right in zip(down_thin, feed_blocks))
    late_all = jnp.concatenate(
        [
            own_columns(thin_product(grad_narrow, place, first_blocks), head_cols),
            grad_b_first,
            own_columns(grad_b_down, head_cols),
        ]
    ).astype(BF16)[None]
    late_all, grads_here = fence(late_all, first_grads)
    late_hop = hop(late_all, "rep", bits[0])
    back_rows_near = project_back(grads_here, place, first_offsets, first_pieces, (0, 1), rows)
    late_hop, back_rows_near = fence(late_hop, back_rows_near)
    back_rows_here = core(back_rows_near[1])
    late_all = both(late_all, late_hop, rep_place, bits[0])
    for bit in bits[1:-2]:
        late_all = both(late_all, hop(late_all, "rep", bit), rep_place, bit)
    late_hop = hop(late_all, "rep", bits[-2])
    late_all, early_hop, early_all = fence(late_all, early_hop, early_all)
    early_sent = send_sums(both(early_all, early_hop, rep_place, bits[-1]), chosen, place)

    def whole_maps(stacked, low, high, n):
        part = stacked[:, :, low:high].reshape(group, stacked.shape[1], -1, rank, n)
        pieces = [lax.dynamic_index_in_dim(part, place ^ i, 0, keepdims=False) for i in range(group)]
        return jnp.concatenate(pieces, axis=-1).transpose(1, 0, 2, 3).astype(F32)

    feed = feed_here[:, :width] + feed_from_far[:, :width].astype(F32) + dot(narrow_down, b_down)
    output = (middle + BRANCH * feed).astype(BF16)
    late_hop, output = fence(late_hop, output)
    late_all = both(late_all, late_hop, rep_place, bits[-2])
    late_hop = hop(late_all, "rep", bits[-1])
    hidden_maps = whole_maps(jnp.stack(wide_sent), 0, 3 * rank, ff_cols)
    late_hop, hidden_maps, back_far_in = fence(late_hop, hidden_maps, back_far_in)
    late_sent = send_sums(both(late_all, late_hop, rep_place, bits[-1]), chosen, place)
    narrow_own = lax.dynamic_slice_in_dim(grad_narrow, place * rows, rows, 1)
    grad_normed = (
        back_rows_near[0].astype(F32) + back_rows_here.astype(F32) + back_far_in.astype(F32)
        + t_dot(narrow_own, a_first)
    )
    input_grad = grad_middle + norm_back(residual_in, gain_one, grad_normed)
    early_got = jnp.stack(early_sent)
    late_sent, input_grad, early_got = fence(late_sent, input_grad, early_got)
    late_got = jnp.stack(late_sent)
    grad_a_model = jnp.concatenate(
        [
            whole_maps(late_got, 0, 3 * rank, head_cols),
            whole_maps(early_got, 0, rank, head_cols),
            whole_maps(early_got, 2 * rank, 4 * rank, head_cols),
        ]
    )
    grad_b_model = jnp.concatenate(
        [
            whole_maps(late_got, 3 * rank, 6 * rank, head_cols),
            whole_maps(early_got, rank, 2 * rank, head_cols),
            whole_maps(late_got, 6 * rank, 7 * rank, head_cols),
        ]
    )
    return (
        output[None], input_grad[None], grad_a_model, grad_b_model, hidden_maps[0], hidden_maps[1:3],
    )


def solution(mesh):
    in_specs = (
        P("rep", "shard", None),
        P("rep", "shard", None),
        P("rep"),
        P("rep", None),
        P(),
        P(),
        P(None, "shard", None),
        P("shard", None),
        P(None, "shard", None),
        P("shard", None),
        P(None, "shard", None, None),
        P(None, "shard", None, None),
        P("shard", None, None),
        P(None, "shard", None, None),
    )
    out_specs = (
        P("rep", "shard", None),
        P("rep", "shard", None),
        P(None, "shard", None, None),
        P(None, "shard", None, None),
        P("shard", None, None),
        P(None, "shard", None, None),
    )
    return jax.shard_map(shards, mesh=mesh, in_specs=in_specs, out_specs=out_specs, check_vma=False)
```

time: 720 us -> 596 us (0.83)
  waiting for transfers between devices: 240 us -> 163 us
  Pallas kernels: 261 us -> 225 us
  local copies, waits for them, and re-layouts: 92.9 us -> 72.3 us
  matrix products: 25.1 us -> 9.28 us
  starting transfers between devices: 44.3 us -> 55.6 us
  other arithmetic: 48.7 us -> 58.8 us
    ppermute x68 -> x74, waiting for transfers between devices: 240 us -> 163 us  [hop(): return lax.ppermute(values, axis, [(i, i ^ bit) for i in range(size)])]
    unnamed x152 -> x211, local copies, waits for them, and re-layouts: 12.8 us -> 35.9 us
    pallas_call x7 -> x9, Pallas kernels: 183 us -> 160 us  [the longest x2 72.3 us: feed_forward(): call(kernel, [out] * (2 * count) + [jax.ShapeDtypeStruct((3 * rank, size)...]
    dynamic_slice x10 -> x17, local copies, waits for them, and re-layouts: 28.5 us -> 12.8 us  [the longest x2 12.6 us: side(): lax.dynamic_slice(weight, (0, row, owner * size), (weight.shape[0], count...]
    dot_general x16 -> x5, matrix products: 17.5 us -> 6.24 us  [t_dot(): lax.dot_general(left, right, (((0,), (0,)), ((), ())), preferred_element_...]
    dynamic_update_slice x15 -> x0, local copies, waits for them, and re-layouts: 11.3 us -> none  [the longest x6 6.98 us: reps_step(): lax.dynamic_update_slice_in_dim(buffer, hop(have, 'rep', bit), base ^ bit...]
    ppermute x68 -> x74, starting transfers between devices: 44.3 us -> 55.6 us  [hop(): return lax.ppermute(values, axis, [(i, i ^ bit) for i in range(size)])]
    concatenate x8 -> x9, local copies, waits for them, and re-layouts: 11.3 us -> 2.32 us  [the longest x7 2.06 us: whole_maps(): return jnp.concatenate(pieces, axis=-1).transpose(1, 0, 2, 3).astype(F32)]
  transfers between devices with their start and end apart: 68 -> 74, of which waited for: 29 -> 27; matrix products, arithmetic and copies ran while one was open for 16% -> 15% of each run, Pallas kernels for 25% -> 31%
where the time goes in v3:
time: 596 us; the launch traced here: 588 us
  Pallas kernels  225 us (38%)
  waiting for transfers between devices  163 us (27%)
  local copies, waits for them, and re-layouts  72.3 us (12%)
  other arithmetic  58.8 us (10%)
  starting transfers between devices  55.6 us (9%)
  matrix products  9.28 us (2%)
    ppermute x74, waiting for transfers between devices, hop(): return lax.ppermute(values, axis, [(i, i ^ bit) for i in range(size)])  163 us
    pallas_call x2, Pallas kernels, feed_forward(): call(kernel, [out] * (2 * count) + [jax.ShapeDtypeStruct((3 * rank, size)...  72.3 us
    ppermute x74, starting transfers between devices, hop(): return lax.ppermute(values, axis, [(i, i ^ bit) for i in range(size)])  55.6 us
    pallas_call x3, Pallas kernels, attend_back(): call(kernel, [jax.ShapeDtypeStruct((heads, length, HDIM), BF16)] * 3 + [j...  54.4 us
    unnamed x211, local copies, waits for them, and re-layouts  35.9 us
    pallas_call x2, Pallas kernels, project_back(): call(kernel, [jax.ShapeDtypeStruct((rows, width), BF16)] * count, [smem()...  24.7 us
    pallas_call x1, Pallas kernels, attend(): call(kernel, jax.ShapeDtypeStruct(query.shape, BF16), [smem(), spec, spec...  21.6 us
    pallas_call x1, Pallas kernels, project(): call(kernel, [by_heads] * 3 + [jax.ShapeDtypeStruct((thin, rows * count),...  20.5 us
  transfers between devices with their start and end apart: 74, of which 27 were waited for; matrix products, arithmetic and copies ran while one was open for 15% of the time, Pallas kernels for 31%

profile of v3, /device:TPU:0, one launch (start us, length us, event | category | flops | bytes accessed | tf_op | source)
XLA Modules:
  0.0 587.6 jit_solution(14295659840614278172)
XLA Ops:
  4.5 3.6 sides_far.1
  8.2 2.7 collective-permute-start
  12.3 6.7 %sides_near.1 = (bf16[576,1728]{1,0:T(8,128)(2,1)}, bf16[576,1728]{1,0:T(8,128)(2,1)}) custom-call(s32[2]{0:T(128)} %get-tuple-element.527.where_ref, bf16[3,576,2304]{2,1,0:T(8,128)(2,1)} %w_ref.5), custom_call_target="tpu_custom_call" | custom-call | bytes 11943936 | tf_op jit(solution)/shard_map/sides_near/pallas_call | solution.py:140
  20.3 14.1 %collective-permute-done.1.refs_6_.refs_11_ = bf16[144,1728]{1,0:T(8,128)(2,1)S(1)} collective-permute-done((bf16[144,1728]{1,0:T(8,128)(2,1)}, bf16[144,1728]{1,0:T(8,128)(2,1)S(1)}, u32[]{:S(2)}, u32[]{:S(2)}) %collective-permute-start.1) | collective-permute-done | bytes 497696 | tf_op jit(solution)/shard_map/ppermute | solution.py:24
  39.3 8.7 %collective-permute-done.4.refs_8_.refs_13_ = bf16[144,1728]{1,0:T(8,128)(2,1)S(1)} collective-permute-done((bf16[144,1728]{1,0:T(8,128)(2,1)S(1)}, bf16[144,1728]{1,0:T(8,128)(2,1)S(1)}, u32[]{:S(2)}, u32[]{:S(2)}) %collective-permute-start.4) | collective-permute-done | bytes 497696 | tf_op jit(solution)/shard_map/ppermute | solution.py:24
  52.6 3.0 multiply_sine_fusion
  55.6 2.9 pad_maximum_fusion.3
  62.6 2.8 collective-permute-done.5.refs_11_.refs_16_
  65.4 2.9 multiply_convert_fusion.2.refs_2_
  68.2 3.7 constant_dynamic-slice_fusion.21
  75.3 11.1 %collective-permute-done.11.refs_13_.refs_18_ = bf16[144,1728]{1,0:T(8,128)(2,1)S(1)} collective-permute-done((bf16[144,1728]{1,0:T(8,128)(2,1)}, bf16[144,1728]{1,0:T(8,128)(2,1)S(1)}, u32[]{:S(2)}, u32[]{:S(2)}) %collective-permute-start.11) | collective-permute-done | bytes 497696 | tf_op jit(solution)/shard_map/ppermute | solution.py:24
  99.2 20.5 %project.1 = (bf16[9,1024,64]{2,1,0:T(8,128)(2,1)}, bf16[9,1024,64]{2,1,0:T(8,128)(2,1)}, bf16[9,1024,64]{2,1,0:T(8,128)(2,1)}, bf16[48,1024]{1,0:T(8,128)(2,1)S(1)}) custom-call(s32[1]{0:T(128)} %bitcast.place_ref, s32[10]{0:T(128)S(1)} %stack.111.offsets_ref, bf16[256,2304]{1,0:T(8,128)(2,1)S(1)} %fusion.4.refs_0_, ...), custom_call_target="tpu_custom_call" | custom-call | flops 8153726976 | bytes 19759104 | tf_op jit(solution)/shard_map/project/pallas_call | solution.py:245
  122.9 11.1 %add.341 = bf16[3,16,5760]{2,1,0:T(8,128)(2,1)S(1)} add(bf16[3,16,5760]{2,1,0:T(8,128)(2,1)S(1)} %fusion.13, bf16[3,16,5760]{2,1,0:T(8,128)(2,1)S(1)} %collective-permute-done.17) | non-fusion elementwise | flops 276480 | bytes 1658880 | tf_op jit(solution)/shard_map/add | solution.py:102
  138.0 21.6 %attend.1.m_ref.refs_4_ = bf16[9,1024,64]{2,1,0:T(8,128)(2,1)S(1)} custom-call(s32[2]{0:T(128)S(1)} %bitcast.192, bf16[9,1024,64]{2,1,0:T(8,128)(2,1)S(1)} %copy-done.44, bf16[9,1024,64]{2,1,0:T(8,128)(2,1)S(1)} %copy-done.46, bf16[9,1024,64]{2,1,0:T(8,128)(2,1)S(1)} %copy-done.48), custom_call_target="tpu_custom_call" | custom-call | flops 9663676416 | bytes 9437184 | tf_op jit(solution)/shard_map/attend/pallas_call | solution.py:323
  162.1 3.3 close_attention.2
  172.3 3.4 collective-permute-done.24
  176.2 2.2 close_attention.3
  178.5 10.5 %collective-permute-done.26.refs_12_ = bf16[2,144,1440]{2,1,0:T(8,128)(2,1)S(1)} collective-permute-done((bf16[2,144,1440]{2,1,0:T(8,128)(2,1)}, bf16[2,144,1440]{2,1,0:T(8,128)(2,1)S(1)}, u32[]{:S(2)}, u32[]{:S(2)}) %collective-permute-start.26) | collective-permute-done | bytes 829472 | tf_op jit(solution)/shard_map/ppermute | solution.py:24
  191.9 8.9 %constant_dynamic-slice_fusion.16 = (bf16[2,576,1440]{2,1,0:T(8,128)(2,1)S(1)}, bf16[2,576,1440]{2,1,0:T(8,128)(2,1)}) fusion(bf16[2,576,5760]{2,1,0:T(8,128)(2,1)} %param.22, s32[]{:T(128)S(6)} %select_n.373, s32[]{:T(128)S(6)} %select_n.372), kind=kLoop, calls=%fused_computation.186 | loop fusion | bytes 13271048 | tf_op jit(solution)/shard_map/dynamic_slice | solution.py:118
  201.9 6.9 %collective-permute-done.30.refs_9_ = bf16[2,144,1440]{2,1,0:T(8,128)(2,1)S(1)} collective-permute-done((bf16[2,144,1440]{2,1,0:T(8,128)(2,1)}, bf16[2,144,1440]{2,1,0:T(8,128)(2,1)S(1)}, u32[]{:S(2)}, u32[]{:S(2)}) %collective-permute-start.30) | collective-permute-done | bytes 829472 | tf_op jit(solution)/shard_map/ppermute | solution.py:24
  208.8 2.2 collective-permute-done.31.refs_13_
  211.1 6.4 %collective-permute-done.28 = bf16[256,2432]{1,0:T(8,128)(2,1)S(1)} collective-permute-done((bf16[256,2432]{1,0:T(8,128)(2,1)S(1)}, bf16[256,2432]{1,0:T(8,128)(2,1)S(1)}, u32[]{:S(2)}, u32[]{:S(2)}) %collective-permute-start.28) | collective-permute-done | bytes 1245216 | tf_op jit(solution)/shard_map/ppermute | solution.py:24
  227.6 36.1 %feed_forward.2 = (bf16[256,2432]{1,0:T(8,128)(2,1)}, bf16[256,2432]{1,0:T(8,128)(2,1)}, bf16[256,2432]{1,0:T(8,128)(2,1)}, bf16[256,2432]{1,0:T(8,128)(2,1)}, f32[48,1440]{1,0:T(8,128)}) custom-call(s32[10]{0:T(128)} %copy-done.40, bf16[256,2304]{1,0:T(8,128)(2,1)} %copy-done.6, bf16[256,2304]{1,0:T(8,128)(2,1)} %copy-done.32, ...), custom_call_target="tpu_custom_call" | custom-call | flops 20384317440 | bytes 29343744 | tf_op jit(solution)/shard_map/feed_forward/pallas_call | solution.py:588
  263.8 11.9 %collective-permute-done.33.refs_2_ = bf16[256,2304]{1,0:T(8,128)(2,1)S(1)} collective-permute-done((bf16[256,2304]{1,0:T(8,128)(2,1)}, bf16[256,2304]{1,0:T(8,128)(2,1)S(1)}, u32[]{:S(2)}, u32[]{:S(2)}) %collective-permute-start.33) | collective-permute-done | bytes 1179680 | tf_op jit(solution)/shard_map/ppermute | solution.py:24
  276.2 2.3 collective-permute-done.37.refs_1_.refs_3_
  281.2 36.1 %feed_forward.3 = (bf16[256,2432]{1,0:T(8,128)(2,1)}, bf16[256,2432]{1,0:T(8,128)(2,1)}, bf16[256,2432]{1,0:T(8,128)(2,1)}, bf16[256,2432]{1,0:T(8,128)(2,1)}, f32[48,1440]{1,0:T(8,128)}) custom-call(s32[10]{0:T(128)} %copy-done.40, bf16[256,2304]{1,0:T(8,128)(2,1)} %copy-done.28, bf16[256,2304]{1,0:T(8,128)(2,1)} %copy-done.30, ...), custom_call_target="tpu_custom_call" | custom-call | flops 20384317440 | bytes 29343744 | tf_op jit(solution)/shard_map/feed_forward/pallas_call | solution.py:588
  317.6 3.0 collective-permute-done.39
  320.6 2.7 add_convert_fusion.1
  328.3 3.4 convert_add_fusion.2
  333.1 23.3 %collective-permute-done.40 = bf16[256,2432]{1,0:T(8,128)(2,1)S(1)} collective-permute-done((bf16[256,2432]{1,0:T(8,128)(2,1)}, bf16[256,2432]{1,0:T(8,128)(2,1)S(1)}, u32[]{:S(2)}, u32[]{:S(2)}) %collective-permute-start.40) | collective-permute-done | bytes 1245216 | tf_op jit(solution)/shard_map/ppermute | solution.py:24
  358.6 2.5 multiply_convert_fusion
  361.6 3.1 concatenate.189.refs_0_
  373.6 6.1 %open_attention.2 = (bf16[9,512,64]{2,1,0:T(8,128)(2,1)S(1)}, f32[16,576]{1,0:T(8,128)S(1)}, f32[48,2304]{1,0:T(8,128)S(1)}) custom-call(s32[1]{0:T(128)} %bitcast.place_ref, bf16[256,2432]{1,0:T(8,128)(2,1)S(1)} %copy-done.5, bf16[256,2432]{1,0:T(8,128)(2,1)} %collective-permute-done.45.refs_1_, bf16[256,2304]{1,0:T(8,128)(2,1)S(1)} %copy-done.7, ...), custom_call_target="tpu_custom_call" | custom-call | flops 1358954496 | bytes 8552448 | tf_op jit(solution)/shard_map/open_attention/pallas_call | solution.py:504
  381.5 13.4 %collective-permute-done.46.refs_0_ = bf16[256,2432]{1,0:T(8,128)(2,1)} collective-permute-done((bf16[256,2432]{1,0:T(8,128)(2,1)}, bf16[256,2432]{1,0:T(8,128)(2,1)}, u32[]{:S(2)}, u32[]{:S(2)}) %collective-permute-start.46) | collective-permute-done | bytes 1245216 | tf_op jit(solution)/shard_map/ppermute | solution.py:24
  405.5 6.7 %open_attention.3 = (bf16[9,512,64]{2,1,0:T(8,128)(2,1)S(1)}, f32[16,576]{1,0:T(8,128)S(1)}, f32[48,2304]{1,0:T(8,128)S(1)}) custom-call(s32[1]{0:T(128)} %bitcast.place_ref, bf16[256,2432]{1,0:T(8,128)(2,1)} %collective-permute-done.46.refs_0_, bf16[256,2432]{1,0:T(8,128)(2,1)} %collective-permute-done.47.refs_1_, bf16[256,2304]{1,0:T(8,128)(2,1)S(1)} %copy-done.29, ...), custom_call_target="tpu_custom_call" | custom-call | flops 1358954496 | bytes 8552448 | tf_op jit(solution)/shard_map/open_attention/pallas_call | solution.py:504
  412.2 3.9 collective-permute-done.48
  420.1 18.1 %attend_back.3 = (bf16[3,1024,64]{2,1,0:T(8,128)(2,1)S(1)}, bf16[3,1024,64]{2,1,0:T(8,128)(2,1)S(1)}, bf16[3,1024,64]{2,1,0:T(8,128)(2,1)S(1)}, f32[48,1024]{1,0:T(8,128)S(1)}, f32[3,48,64]{2,1,0:T(8,128)S(1)}) custom-call(s32[2]{0:T(128)S(1)} %bitcast.193, s32[1]{0:T(128)} %bitcast.place_ref, bf16[9,1024,64]{2,1,0:T(8,128)(2,1)S(1)} %copy-done.45, ...), custom_call_target="tpu_custom_call" | custom-call | flops 8053063680 | bytes 6291456 | tf_op jit(solution)/shard_map/attend_back/pallas_call | solution.py:406
  446.3 18.3 %attend_back.4 = (bf16[3,1024,64]{2,1,0:T(8,128)(2,1)S(1)}, bf16[3,1024,64]{2,1,0:T(8,128)(2,1)S(1)}, bf16[3,1024,64]{2,1,0:T(8,128)(2,1)S(1)}, f32[48,1024]{1,0:T(8,128)S(1)}, f32[3,48,64]{2,1,0:T(8,128)S(1)}) custom-call(s32[2]{0:T(128)S(1)} %bitcast.194, s32[1]{0:T(128)} %bitcast.place_ref, bf16[9,1024,64]{2,1,0:T(8,128)(2,1)S(1)} %copy-done.45, ...), custom_call_target="tpu_custom_call" | custom-call | flops 8053063680 | bytes 6291456 | tf_op jit(solution)/shard_map/attend_back/pallas_call | solution.py:406
  471.0 18.1 %attend_back.5 = (bf16[3,1024,64]{2,1,0:T(8,128)(2,1)S(1)}, bf16[3,1024,64]{2,1,0:T(8,128)(2,1)S(1)}, bf16[3,1024,64]{2,1,0:T(8,128)(2,1)S(1)}, f32[48,1024]{1,0:T(8,128)S(1)}, f32[3,48,64]{2,1,0:T(8,128)S(1)}) custom-call(s32[2]{0:T(128)S(1)} %bitcast.195, s32[1]{0:T(128)} %bitcast.place_ref, bf16[9,1024,64]{2,1,0:T(8,128)(2,1)S(1)} %copy-done.45, ...), custom_call_target="tpu_custom_call" | custom-call | flops 8053063680 | bytes 6291456 | tf_op jit(solution)/shard_map/attend_back/pallas_call | solution.py:406
  494.9 12.4 %project_back.2 = (bf16[256,2304]{1,0:T(8,128)(2,1)}, bf16[256,2304]{1,0:T(8,128)(2,1)}) custom-call(s32[1]{0:T(128)} %bitcast.place_ref, s32[10]{0:T(128)} %copy-done.40, bf16[3,1024,64]{2,1,0:T(8,128)(2,1)} %copy-done.10, bf16[3,1024,64]{2,1,0:T(8,128)(2,1)} %copy-done.13, bf16[3,1024,64]{2,1,0:T(8,128)(2,1)} %copy-done.16, ...), custom_call_target="tpu_custom_call" | custom-call | flops 4076863488 | bytes 12091392 | tf_op jit(solution)/shard_map/project_back/pallas_call | solution.py:625
  515.2 2.7 collective-permute-done.61
  518.0 2.9 thin_product.1
  522.1 12.4 %project_back.3 = (bf16[256,2304]{1,0:T(8,128)(2,1)}, bf16[256,2304]{1,0:T(8,128)(2,1)}) custom-call(s32[1]{0:T(128)} %bitcast.place_ref, s32[10]{0:T(128)} %copy-done.40, bf16[3,1024,64]{2,1,0:T(8,128)(2,1)} %copy-done.10, bf16[3,1024,64]{2,1,0:T(8,128)(2,1)} %copy-done.13, bf16[3,1024,64]{2,1,0:T(8,128)(2,1)} %copy-done.16, ...), custom_call_target="tpu_custom_call" | custom-call | flops 4076863488 | bytes 12091392 | tf_op jit(solution)/shard_map/project_back/pallas_call | solution.py:625
  539.4 10.1 %collective-permute-done.64 = bf16[2,112,576]{2,1,0:T(8,128)(2,1)S(1)} collective-permute-done((bf16[2,112,576]{2,1,0:T(8,128)(2,1)S(1)}, bf16[2,112,576]{2,1,0:T(8,128)(2,1)S(1)}, u32[]{:S(2)}, u32[]{:S(2)}) %collective-permute-start.64) | collective-permute-done | bytes 258080 | tf_op jit(solution)/shard_map/ppermute | solution.py:24
  550.6 3.3 collective-permute-done.72
  554.3 9.1 %collective-permute-done.65 = bf16[4,112,576]{2,1,0:T(8,128)(2,1)S(1)} collective-permute-done((bf16[4,112,576]{2,1,0:T(8,128)(2,1)S(1)}, bf16[4,112,576]{2,1,0:T(8,128)(2,1)S(1)}, u32[]{:S(2)}, u32[]{:S(2)}) %collective-permute-start.65) | collective-permute-done | bytes 516128 | tf_op jit(solution)/shard_map/ppermute | solution.py:24
  571.5 2.5 fusion.7
  575.9 6.2 %collective-permute-done.68 = bf16[2,112,576]{2,1,0:T(8,128)(2,1)S(1)} collective-permute-done((bf16[2,112,576]{2,1,0:T(8,128)(2,1)S(1)}, bf16[2,112,576]{2,1,0:T(8,128)(2,1)S(1)}, u32[]{:S(2)}, u32[]{:S(2)}) %collective-permute-start.68) | collective-permute-done | bytes 258080 | tf_op jit(solution)/shard_map/ppermute | solution.py:24
  (473 shorter events, 154.5 us)
Async XLA Ops:
  3.4 16.1 %collective-permute-start.2 = (bf16[6,16,2304]{2,1,0:T(8,128)(2,1)S(1)}, bf16[6,16,2304]{2,1,0:T(8,128)(2,1)S(1)}, u32[]{:S(2)}, u32[]{:S(2)}) collective-permute-start(bf16[6,16,2304]{2,1,0:T(8,128)(2,1)S(1)} %fusion.17), channel_id=1, source_target_pairs={{0,1},{1,0},{2,3},{3,2},{4,5},{5,4},{6,7},{7,6},{8,9},{9,8},{10,11... | collective-permute-start | bytes 1327112 | tf_op jit(solution)/shard_map/ppermute | solution.py:24
  8.2 31.1 %collective-permute-start = (bf16[144,1728]{1,0:T(8,128)(2,1)}, bf16[144,1728]{1,0:T(8,128)(2,1)S(1)}, u32[]{:S(2)}, u32[]{:S(2)}) collective-permute-start(bf16[144,1728]{1,0:T(8,128)(2,1)} %get-tuple-element.219), channel_id=1, source_target_pairs={{0,3},{1,2},{2,1},{3,0},{4,7},{5,6},{6,5},{7,4},{8,11},{9,10},{10,... | collective-permute-start | bytes 1493000 | tf_op jit(solution)/shard_map/ppermute | solution.py:24
  10.8 23.6 %collective-permute-start.1 = (bf16[144,1728]{1,0:T(8,128)(2,1)}, bf16[144,1728]{1,0:T(8,128)(2,1)S(1)}, u32[]{:S(2)}, u32[]{:S(2)}) collective-permute-start(bf16[144,1728]{1,0:T(8,128)(2,1)} %get-tuple-element.220), channel_id=1, source_target_pairs={{0,2},{1,3},{2,0},{3,1},{4,6},{5,7},{6,4},{7,5},{8,10},{9,11},{10,... | collective-permute-start | bytes 1493000 | tf_op jit(solution)/shard_map/ppermute | solution.py:24
  12.1 81.9 %collective-permute-start.8 = (bf16[256,2304]{1,0:T(8,128)(2,1)S(1)}, bf16[256,2304]{1,0:T(8,128)(2,1)}, u32[]{:S(2)}, u32[]{:S(2)}) collective-permute-start(bf16[256,2304]{1,0:T(8,128)(2,1)S(1)} %fusion.4.refs_0_), channel_id=1, source_target_pairs={{0,1},{1,0},{2,3},{3,2},{4,5},{5,4},{6,7},{7,6},{8,9},{9,8},{10,11... | collective-permute-start | bytes 3538952 | tf_op jit(solution)/shard_map/ppermute | solution.py:24
  19.1 75.0 %collective-permute-start.14 = (bf16[576,1728]{1,0:T(8,128)(2,1)}, bf16[576,1728]{1,0:T(8,128)(2,1)}, u32[]{:S(2)}, u32[]{:S(2)}) collective-permute-start(bf16[576,1728]{1,0:T(8,128)(2,1)} %get-tuple-element.235), channel_id=1, source_target_pairs={{0,1},{1,0},{2,3},{3,2},{4,5},{5,4},{6,7},{7,6},{8,9},{9,8},{10,11... | collective-permute-start | bytes 5971976 | tf_op jit(solution)/shard_map/ppermute | solution.py:24
  34.4 13.5 %collective-permute-start.4 = (bf16[144,1728]{1,0:T(8,128)(2,1)S(1)}, bf16[144,1728]{1,0:T(8,128)(2,1)S(1)}, u32[]{:S(2)}, u32[]{:S(2)}) collective-permute-start(bf16[144,1728]{1,0:T(8,128)(2,1)S(1)} %collective-permute-done.1.refs_6_.refs_11_), channel_id=1, source_target_pairs={{0,4},{4,0},{8,12},{12,8},{16,20},{20,16},{24,28},{28,24},{1,5},{5... | collective-permute-start | bytes 1493000 | tf_op jit(solution)/shard_map/ppermute | solution.py:24
  50.6 14.8 %collective-permute-start.5 = (bf16[144,1728]{1,0:T(8,128)(2,1)S(1)}, bf16[144,1728]{1,0:T(8,128)(2,1)}, u32[]{:S(2)}, u32[]{:S(2)}) collective-permute-start(bf16[144,1728]{1,0:T(8,128)(2,1)S(1)} %collective-permute-done.refs_10_.refs_15_), channel_id=1, source_target_pairs={{0,4},{4,0},{8,12},{12,8},{16,20},{20,16},{24,28},{28,24},{1,5},{5... | collective-permute-start | bytes 1493000 | tf_op jit(solution)/shard_map/ppermute | solution.py:24
  58.5 16.0 %collective-permute-start.10 = (bf16[144,1728]{1,0:T(8,128)(2,1)S(1)}, bf16[144,1728]{1,0:T(8,128)(2,1)S(1)}, u32[]{:S(2)}, u32[]{:S(2)}) collective-permute-start(bf16[144,1728]{1,0:T(8,128)(2,1)S(1)} %collective-permute-done.3.refs_7_.refs_12_), channel_id=1, source_target_pairs={{0,4},{4,0},{8,12},{12,8},{16,20},{20,16},{24,28},{28,24},{1,5},{5... | collective-permute-start | bytes 1493000 | tf_op jit(solution)/shard_map/ppermute | solution.py:24
  61.1 26.1 %collective-permute-start.9 = (bf16[256,2304]{1,0:T(8,128)(2,1)S(1)}, bf16[256,2304]{1,0:T(8,128)(2,1)}, u32[]{:S(2)}, u32[]{:S(2)}) collective-permute-start(bf16[256,2304]{1,0:T(8,128)(2,1)S(1)} %fusion.4.refs_0_), channel_id=1, source_target_pairs={{0,2},{1,3},{2,0},{3,1},{4,6},{5,7},{6,4},{7,5},{8,10},{9,11},{10,... | collective-permute-start | bytes 3538952 | tf_op jit(solution)/shard_map/ppermute | solution.py:24
  71.9 14.4 %collective-permute-start.11 = (bf16[144,1728]{1,0:T(8,128)(2,1)}, bf16[144,1728]{1,0:T(8,128)(2,1)S(1)}, u32[]{:S(2)}, u32[]{:S(2)}) collective-permute-start(bf16[144,1728]{1,0:T(8,128)(2,1)} %collective-permute-done.5.refs_11_.refs_16_), channel_id=1, source_target_pairs={{0,8},{4,12},{8,0},{12,4},{16,24},{20,28},{24,16},{28,20},{1,9},{5... | collective-permute-start | bytes 1493000 | tf_op jit(solution)/shard_map/ppermute | solution.py:24
  87.2 32.5 %collective-permute-start.15 = (bf16[2,144,1440]{2,1,0:T(8,128)(2,1)}, bf16[2,144,1440]{2,1,0:T(8,128)(2,1)}, u32[]{:S(2)}, u32[]{:S(2)}) collective-permute-start(bf16[2,144,1440]{2,1,0:T(8,128)(2,1)} %get-tuple-element.245), channel_id=1, source_target_pairs={{0,2},{1,3},{2,0},{3,1},{4,6},{5,7},{6,4},{7,5},{8,10},{9,11},{10,... | collective-permute-start | bytes 2488328 | tf_op jit(solution)/shard_map/ppermute | solution.py:24
  120.9 38.7 %collective-permute-start.18 = (bf16[2,144,1440]{2,1,0:T(8,128)(2,1)S(1)}, bf16[2,144,1440]{2,1,0:T(8,128)(2,1)S(1)}, u32[]{:S(2)}, u32[]{:S(2)}) collective-permute-start(bf16[2,144,1440]{2,1,0:T(8,128)(2,1)S(1)} %copy-done.76), channel_id=1, source_target_pairs={{0,3},{1,2},{2,1},{3,0},{4,7},{5,6},{6,5},{7,4},{8,11},{9,10},{10,... | collective-permute-start | bytes 2488328 | tf_op jit(solution)/shard_map/ppermute | solution.py:24
  121.2 38.5 %collective-permute-start.20 = (bf16[2,144,1440]{2,1,0:T(8,128)(2,1)}, bf16[2,144,1440]{2,1,0:T(8,128)(2,1)S(1)}, u32[]{:S(2)}, u32[]{:S(2)}) collective-permute-start(bf16[2,144,1440]{2,1,0:T(8,128)(2,1)} %collective-permute-done.15.refs_6_), channel_id=1, source_target_pairs={{0,4},{4,0},{8,12},{12,8},{16,20},{20,16},{24,28},{28,24},{1,5},{5... | collective-permute-start | bytes 2488328 | tf_op jit(solution)/shard_map/ppermute | solution.py:24
  121.9 37.8 %collective-permute-start.19 = (bf16[2,144,1440]{2,1,0:T(8,128)(2,1)}, bf16[2,144,1440]{2,1,0:T(8,128)(2,1)S(1)}, u32[]{:S(2)}, u32[]{:S(2)}) collective-permute-start(bf16[2,144,1440]{2,1,0:T(8,128)(2,1)} %collective-permute-done.15.refs_6_), channel_id=1, source_target_pairs={{0,8},{4,12},{8,0},{12,4},{16,24},{20,28},{24,16},{28,20},{1,9},{5... | collective-permute-start | bytes 2488328 | tf_op jit(solution)/shard_map/ppermute | solution.py:24
  134.8 24.8 %collective-permute-start.21 = (bf16[5,8,2304]{2,1,0:T(8,128)(2,1)S(1)}, bf16[5,8,2304]{2,1,0:T(8,128)(2,1)S(1)}, u32[]{:S(2)}, u32[]{:S(2)}) collective-permute-start(bf16[5,8,2304]{2,1,0:T(8,128)(2,1)S(1)} %constant_dynamic-slice_fusion.19), channel_id=1, source_target_pairs={{0,2},{1,3},{2,0},{3,1},{4,6},{5,7},{6,4},{7,5},{8,10},{9,11},{10,... | collective-permute-start | bytes 552968 | tf_op jit(solution)/shard_map/ppermute | solution.py:24
  167.1 21.8 %collective-permute-start.26 = (bf16[2,144,1440]{2,1,0:T(8,128)(2,1)}, bf16[2,144,1440]{2,1,0:T(8,128)(2,1)S(1)}, u32[]{:S(2)}, u32[]{:S(2)}) collective-permute-start(bf16[2,144,1440]{2,1,0:T(8,128)(2,1)} %copy-done.98), channel_id=1, source_target_pairs={{0,8},{4,12},{8,0},{12,4},{16,24},{20,28},{24,16},{28,20},{1,9},{5... | collective-permute-start | bytes 2488328 | tf_op jit(solution)/shard_map/ppermute | solution.py:24
  168.3 22.8 %collective-permute-start.25 = (bf16[2,144,1440]{2,1,0:T(8,128)(2,1)}, bf16[2,144,1440]{2,1,0:T(8,128)(2,1)S(1)}, u32[]{:S(2)}, u32[]{:S(2)}) collective-permute-start(bf16[2,144,1440]{2,1,0:T(8,128)(2,1)} %copy-done.98), channel_id=1, source_target_pairs={{0,4},{4,0},{8,12},{12,8},{16,20},{20,16},{24,28},{28,24},{1,5},{5... | collective-permute-start | bytes 2488328 | tf_op jit(solution)/shard_map/ppermute | solution.py:24
  169.6 39.2 %collective-permute-start.30 = (bf16[2,144,1440]{2,1,0:T(8,128)(2,1)}, bf16[2,144,1440]{2,1,0:T(8,128)(2,1)S(1)}, u32[]{:S(2)}, u32[]{:S(2)}) collective-permute-start(bf16[2,144,1440]{2,1,0:T(8,128)(2,1)} %copy-done.100), channel_id=1, source_target_pairs={{0,4},{4,0},{8,12},{12,8},{16,20},{20,16},{24,28},{28,24},{1,5},{5... | collective-permute-start | bytes 2488328 | tf_op jit(solution)/shard_map/ppermute | solution.py:24
  175.7 25.1 %collective-permute-start.29 = (bf16[3,8,5760]{2,1,0:T(8,128)(2,1)S(1)}, bf16[3,8,5760]{2,1,0:T(8,128)(2,1)S(1)}, u32[]{:S(2)}, u32[]{:S(2)}) collective-permute-start(bf16[3,8,5760]{2,1,0:T(8,128)(2,1)S(1)} %collective-permute-done.24), channel_id=1, source_target_pairs={{0,1},{1,0},{2,3},{3,2},{4,5},{5,4},{6,7},{7,6},{8,9},{9,8},{10,11... | collective-permute-start | bytes 829448 | tf_op jit(solution)/shard_map/ppermute | solution.py:24
  175.7 49.7 %collective-permute-start.35 = (bf16[256,2304]{1,0:T(8,128)(2,1)}, bf16[256,2304]{1,0:T(8,128)(2,1)}, u32[]{:S(2)}, u32[]{:S(2)}) collective-permute-start(bf16[256,2304]{1,0:T(8,128)(2,1)} %multiply_convert_fusion.2.refs_2_), channel_id=1, source_target_pairs={{0,1},{1,0},{2,3},{3,2},{4,5},{5,4},{6,7},{7,6},{8,9},{9,8},{10,11... | collective-permute-start | bytes 3538952 | tf_op jit(solution)/shard_map/ppermute | solution.py:24
  189.0 28.5 %collective-permute-start.28 = (bf16[256,2432]{1,0:T(8,128)(2,1)S(1)}, bf16[256,2432]{1,0:T(8,128)(2,1)S(1)}, u32[]{:S(2)}, u32[]{:S(2)}) collective-permute-start(bf16[256,2432]{1,0:T(8,128)(2,1)S(1)} %add_convert_fusion.2), channel_id=1, source_target_pairs={{0,2},{1,3},{2,0},{3,1},{4,6},{5,7},{6,4},{7,5},{8,10},{9,11},{10,... | collective-permute-start | bytes 3735560 | tf_op jit(solution)/shard_map/ppermute | solution.py:24
  191.1 20.0 %collective-permute-start.31 = (bf16[2,144,1440]{2,1,0:T(8,128)(2,1)S(1)}, bf16[2,144,1440]{2,1,0:T(8,128)(2,1)S(1)}, u32[]{:S(2)}, u32[]{:S(2)}) collective-permute-start(bf16[2,144,1440]{2,1,0:T(8,128)(2,1)S(1)} %collective-permute-done.25.refs_11_), channel_id=1, source_target_pairs={{0,8},{4,12},{8,0},{12,4},{16,24},{20,28},{24,16},{28,20},{1,9},{5... | collective-permute-start | bytes 2488328 | tf_op jit(solution)/shard_map/ppermute | solution.py:24
  200.8 16.7 %collective-permute-start.27 = (bf16[256,2432]{1,0:T(8,128)(2,1)S(1)}, bf16[256,2432]{1,0:T(8,128)(2,1)S(1)}, u32[]{:S(2)}, u32[]{:S(2)}) collective-permute-start(bf16[256,2432]{1,0:T(8,128)(2,1)S(1)} %get-tuple-element.268), channel_id=1, source_target_pairs={{0,1},{1,0},{2,3},{3,2},{4,5},{5,4},{6,7},{7,6},{8,9},{9,8},{10,11... | collective-permute-start | bytes 3735560 | tf_op jit(solution)/shard_map/ppermute | solution.py:24
  208.8 16.6 %collective-permute-start.36 = (bf16[2,576,1440]{2,1,0:T(8,128)(2,1)S(1)}, bf16[2,576,1440]{2,1,0:T(8,128)(2,1)S(1)}, u32[]{:S(2)}, u32[]{:S(2)}) collective-permute-start(bf16[2,576,1440]{2,1,0:T(8,128)(2,1)S(1)} %get-tuple-element.458), channel_id=1, source_target_pairs={{0,1},{1,0},{2,3},{3,2},{4,5},{5,4},{6,7},{7,6},{8,9},{9,8},{10,11... | collective-permute-start | bytes 9953288 | tf_op jit(solution)/shard_map/ppermute | solution.py:24
  222.1 41.6 %collective-permute-start.32 = (bf16[256,2304]{1,0:T(8,128)(2,1)S(1)}, bf16[256,2304]{1,0:T(8,128)(2,1)S(1)}, u32[]{:S(2)}, u32[]{:S(2)}) collective-permute-start(bf16[256,2304]{1,0:T(8,128)(2,1)S(1)} %multiply_convert_fusion.1.refs_0_.refs_2_), channel_id=1, source_target_pairs={{0,2},{1,3},{2,0},{3,1},{4,6},{5,7},{6,4},{7,5},{8,10},{9,11},{10,... | collective-permute-start | bytes 3538952 | tf_op jit(solution)/shard_map/ppermute | solution.py:24
  224.3 51.3 %collective-permute-start.33 = (bf16[256,2304]{1,0:T(8,128)(2,1)}, bf16[256,2304]{1,0:T(8,128)(2,1)S(1)}, u32[]{:S(2)}, u32[]{:S(2)}) collective-permute-start(bf16[256,2304]{1,0:T(8,128)(2,1)} %multiply_convert_fusion.2.refs_2_), channel_id=1, source_target_pairs={{0,2},{1,3},{2,0},{3,1},{4,6},{5,7},{6,4},{7,5},{8,10},{9,11},{10,... | collective-permute-start | bytes 3538952 | tf_op jit(solution)/shard_map/ppermute | solution.py:24
  327.1 29.3 %collective-permute-start.40 = (bf16[256,2432]{1,0:T(8,128)(2,1)}, bf16[256,2432]{1,0:T(8,128)(2,1)S(1)}, u32[]{:S(2)}, u32[]{:S(2)}) collective-permute-start(bf16[256,2432]{1,0:T(8,128)(2,1)} %add_convert_fusion.1), channel_id=1, source_target_pairs={{0,2},{1,3},{2,0},{3,1},{4,6},{5,7},{6,4},{7,5},{8,10},{9,11},{10,... | collective-permute-start | bytes 3735560 | tf_op jit(solution)/shard_map/ppermute | solution.py:24
  328.3 28.1 %collective-permute-start.43 = (bf16[256,2432]{1,0:T(8,128)(2,1)}, bf16[256,2432]{1,0:T(8,128)(2,1)S(1)}, u32[]{:S(2)}, u32[]{:S(2)}) collective-permute-start(bf16[256,2432]{1,0:T(8,128)(2,1)} %get-tuple-element.308), channel_id=1, source_target_pairs={{0,1},{1,0},{2,3},{3,2},{4,5},{5,4},{6,7},{7,6},{8,9},{9,8},{10,11... | collective-permute-start | bytes 3735560 | tf_op jit(solution)/shard_map/ppermute | solution.py:24
  364.8 30.1 %collective-permute-start.46 = (bf16[256,2432]{1,0:T(8,128)(2,1)}, bf16[256,2432]{1,0:T(8,128)(2,1)}, u32[]{:S(2)}, u32[]{:S(2)}) collective-permute-start(bf16[256,2432]{1,0:T(8,128)(2,1)} %concatenate.189.refs_0_), channel_id=1, source_target_pairs={{0,2},{1,3},{2,0},{3,1},{4,6},{5,7},{6,4},{7,5},{8,10},{9,11},{10,... | collective-permute-start | bytes 3735560 | tf_op jit(solution)/shard_map/ppermute | solution.py:24
  394.9 21.2 %collective-permute-start.48 = (bf16[2,64,1440]{2,1,0:T(8,128)(2,1)}, bf16[2,64,1440]{2,1,0:T(8,128)(2,1)}, u32[]{:S(2)}, u32[]{:S(2)}) collective-permute-start(bf16[2,64,1440]{2,1,0:T(8,128)(2,1)} %maximum_select_fusion.5), channel_id=1, source_target_pairs={{0,16},{4,20},{8,24},{12,28},{16,0},{20,4},{24,8},{28,12},{1,17},{... | collective-permute-start | bytes 1105928 | tf_op jit(solution)/shard_map/ppermute | solution.py:24
  399.5 38.7 %collective-permute-start.49 = (bf16[256,2432]{1,0:T(8,128)(2,1)}, bf16[256,2432]{1,0:T(8,128)(2,1)S(1)}, u32[]{:S(2)}, u32[]{:S(2)}) collective-permute-start(bf16[256,2432]{1,0:T(8,128)(2,1)} %add_convert_fusion), channel_id=1, source_target_pairs={{0,2},{1,3},{2,0},{3,1},{4,6},{5,7},{6,4},{7,5},{8,10},{9,11},{10,... | collective-permute-start | bytes 3735560 | tf_op jit(solution)/shard_map/ppermute | solution.py:24
  417.5 20.7 %collective-permute-start.50 = (bf16[4,64,1440]{2,1,0:T(8,128)(2,1)S(1)}, bf16[4,64,1440]{2,1,0:T(8,128)(2,1)S(1)}, u32[]{:S(2)}, u32[]{:S(2)}) collective-permute-start(bf16[4,64,1440]{2,1,0:T(8,128)(2,1)S(1)} %maximum_select_fusion.2), channel_id=1, source_target_pairs={{0,4},{4,0},{8,12},{12,8},{16,20},{20,16},{24,28},{28,24},{1,5},{5... | collective-permute-start | bytes 2211848 | tf_op jit(solution)/shard_map/ppermute | solution.py:24
  420.0 46.5 %collective-permute-start.54 = (bf16[1,64,576]{2,1,0:T(8,128)(2,1)S(1)}, bf16[1,64,576]{2,1,0:T(8,128)(2,1)S(1)}, u32[]{:S(2)}, u32[]{:S(2)}) collective-permute-start(bf16[1,64,576]{2,1,0:T(8,128)(2,1)S(1)} %pad_maximum_fusion.7), channel_id=1, source_target_pairs={{0,8},{4,12},{8,0},{12,4},{16,24},{20,28},{24,16},{28,20},{1,9},{5... | collective-permute-start | bytes 221192 | tf_op jit(solution)/shard_map/ppermute | solution.py:24
  440.8 27.3 %collective-permute-start.55 = (bf16[256,16]{1,0:T(8,128)(2,1)S(1)}, bf16[256,16]{1,0:T(8,128)(2,1)S(1)}, u32[]{:S(2)}, u32[]{:S(2)}) collective-permute-start(bf16[256,16]{1,0:T(8,128)(2,1)S(1)} %fusion.29), channel_id=1, source_target_pairs={{0,2},{1,3},{2,0},{3,1},{4,6},{5,7},{6,4},{7,5},{8,10},{9,11},{10,... | collective-permute-start | bytes 24584 | tf_op jit(solution)/shard_map/ppermute | solution.py:24
  444.1 24.0 %collective-permute-start.53 = (bf16[2,48,1440]{2,1,0:T(8,128)(2,1)S(1)}, bf16[2,48,1440]{2,1,0:T(8,128)(2,1)S(1)}, u32[]{:S(2)}, u32[]{:S(2)}) collective-permute-start(bf16[2,48,1440]{2,1,0:T(8,128)(2,1)S(1)} %get-tuple-element.444), channel_id=1, source_target_pairs={{0,3},{1,2},{2,1},{3,0},{4,7},{5,6},{6,5},{7,4},{8,11},{9,10},{10,... | collective-permute-start | bytes 829448 | tf_op jit(solution)/shard_map/ppermute | solution.py:24
  444.2 23.9 %collective-permute-start.51 = (bf16[2,48,1440]{2,1,0:T(8,128)(2,1)S(1)}, bf16[2,48,1440]{2,1,0:T(8,128)(2,1)S(1)}, u32[]{:S(2)}, u32[]{:S(2)}) collective-permute-start(bf16[2,48,1440]{2,1,0:T(8,128)(2,1)S(1)} %get-tuple-element.445), channel_id=1, source_target_pairs={{0,1},{1,0},{2,3},{3,2},{4,5},{5,4},{6,7},{7,6},{8,9},{9,8},{10,11... | collective-permute-start | bytes 829448 | tf_op jit(solution)/shard_map/ppermute | solution.py:24
  444.8 23.3 %collective-permute-start.52 = (bf16[2,48,1440]{2,1,0:T(8,128)(2,1)S(1)}, bf16[2,48,1440]{2,1,0:T(8,128)(2,1)S(1)}, u32[]{:S(2)}, u32[]{:S(2)}) collective-permute-start(bf16[2,48,1440]{2,1,0:T(8,128)(2,1)S(1)} %get-tuple-element.446), channel_id=1, source_target_pairs={{0,2},{1,3},{2,0},{3,1},{4,6},{5,7},{6,4},{7,5},{8,10},{9,11},{10,... | collective-permute-start | bytes 829448 | tf_op jit(solution)/shard_map/ppermute | solution.py:24
  468.7 23.1 %collective-permute-start.58 = (bf16[256,16]{1,0:T(8,128)(2,1)S(1)}, bf16[256,16]{1,0:T(8,128)(2,1)S(1)}, u32[]{:S(2)}, u32[]{:S(2)}) collective-permute-start(bf16[256,16]{1,0:T(8,128)(2,1)S(1)} %collective-permute-done.55), channel_id=1, source_target_pairs={{0,1},{1,0},{2,3},{3,2},{4,5},{5,4},{6,7},{7,6},{8,9},{9,8},{10,11... | collective-permute-start | bytes 24584 | tf_op jit(solution)/shard_map/ppermute | solution.py:24
  469.3 22.6 %collective-permute-start.57 = (bf16[2,64,576]{2,1,0:T(8,128)(2,1)S(1)}, bf16[2,64,576]{2,1,0:T(8,128)(2,1)S(1)}, u32[]{:S(2)}, u32[]{:S(2)}) collective-permute-start(bf16[2,64,576]{2,1,0:T(8,128)(2,1)S(1)} %maximum_select_fusion.8), channel_id=1, source_target_pairs={{0,16},{4,20},{8,24},{12,28},{16,0},{20,4},{24,8},{28,12},{1,17},{... | collective-permute-start | bytes 442376 | tf_op jit(solution)/shard_map/ppermute | solution.py:24
  492.5 14.7 %collective-permute-start.59 = (bf16[48,1024]{1,0:T(8,128)(2,1)S(1)}, bf16[48,1024]{1,0:T(8,128)(2,1)S(1)}, u32[]{:S(2)}, u32[]{:S(2)}) collective-permute-start(bf16[48,1024]{1,0:T(8,128)(2,1)S(1)} %add_convert_fusion.8), channel_id=1, source_target_pairs={{0,1},{1,0},{2,3},{3,2},{4,5},{5,4},{6,7},{7,6},{8,9},{9,8},{10,11... | collective-permute-start | bytes 294920 | tf_op jit(solution)/shard_map/ppermute | solution.py:24
  492.7 14.6 %collective-permute-start.60 = (bf16[4,64,576]{2,1,0:T(8,128)(2,1)S(1)}, bf16[4,64,576]{2,1,0:T(8,128)(2,1)S(1)}, u32[]{:S(2)}, u32[]{:S(2)}) collective-permute-start(bf16[4,64,576]{2,1,0:T(8,128)(2,1)S(1)} %maximum_select_fusion.6), channel_id=1, source_target_pairs={{0,4},{4,0},{8,12},{12,8},{16,20},{20,16},{24,28},{28,24},{1,5},{5... | collective-permute-start | bytes 884744 | tf_op jit(solution)/shard_map/ppermute | solution.py:24
  521.5 42.0 %collective-permute-start.66 = (bf16[256,2304]{1,0:T(8,128)(2,1)S(1)}, bf16[256,2304]{1,0:T(8,128)(2,1)S(1)}, u32[]{:S(2)}, u32[]{:S(2)}) collective-permute-start(bf16[256,2304]{1,0:T(8,128)(2,1)S(1)} %add_convert_fusion.4), channel_id=1, source_target_pairs={{0,2},{1,3},{2,0},{3,1},{4,6},{5,7},{6,4},{7,5},{8,10},{9,11},{10,... | collective-permute-start | bytes 3538952 | tf_op jit(solution)/shard_map/ppermute | solution.py:24
  534.5 15.0 %collective-permute-start.64 = (bf16[2,112,576]{2,1,0:T(8,128)(2,1)S(1)}, bf16[2,112,576]{2,1,0:T(8,128)(2,1)S(1)}, u32[]{:S(2)}, u32[]{:S(2)}) collective-permute-start(bf16[2,112,576]{2,1,0:T(8,128)(2,1)S(1)} %maximum_select_fusion.7), channel_id=1, source_target_pairs={{0,16},{4,20},{8,24},{12,28},{16,0},{20,4},{24,8},{28,12},{1,17},{... | collective-permute-start | bytes 774152 | tf_op jit(solution)/shard_map/ppermute | solution.py:24
  537.6 16.4 %collective-permute-start.72 = (bf16[2,64,576]{2,1,0:T(8,128)(2,1)S(1)}, bf16[2,64,576]{2,1,0:T(8,128)(2,1)S(1)}, u32[]{:S(2)}, u32[]{:S(2)}) collective-permute-start(bf16[2,64,576]{2,1,0:T(8,128)(2,1)S(1)} %get-tuple-element.454), channel_id=1, source_target_pairs={{0,2},{1,3},{2,0},{3,1},{4,6},{5,7},{6,4},{7,5},{8,10},{9,11},{10,... | collective-permute-start | bytes 442376 | tf_op jit(solution)/shard_map/ppermute | solution.py:24
  538.9 15.3 %collective-permute-start.73 = (bf16[2,64,576]{2,1,0:T(8,128)(2,1)S(1)}, bf16[2,64,576]{2,1,0:T(8,128)(2,1)S(1)}, u32[]{:S(2)}, u32[]{:S(2)}) collective-permute-start(bf16[2,64,576]{2,1,0:T(8,128)(2,1)S(1)} %get-tuple-element.455), channel_id=1, source_target_pairs={{0,3},{1,2},{2,1},{3,0},{4,7},{5,6},{6,5},{7,4},{8,11},{9,10},{10,... | collective-permute-start | bytes 442376 | tf_op jit(solution)/shard_map/ppermute | solution.py:24
  549.6 13.8 %collective-permute-start.65 = (bf16[4,112,576]{2,1,0:T(8,128)(2,1)S(1)}, bf16[4,112,576]{2,1,0:T(8,128)(2,1)S(1)}, u32[]{:S(2)}, u32[]{:S(2)}) collective-permute-start(bf16[4,112,576]{2,1,0:T(8,128)(2,1)S(1)} %maximum_select_fusion.4), channel_id=1, source_target_pairs={{0,4},{4,0},{8,12},{12,8},{16,20},{20,16},{24,28},{28,24},{1,5},{5... | collective-permute-start | bytes 1548296 | tf_op jit(solution)/shard_map/ppermute | solution.py:24
  550.5 19.4 %collective-permute-start.70 = (bf16[256,2304]{1,0:T(8,128)(2,1)S(1)}, bf16[256,2304]{1,0:T(8,128)(2,1)S(1)}, u32[]{:S(2)}, u32[]{:S(2)}) collective-permute-start(bf16[256,2304]{1,0:T(8,128)(2,1)S(1)} %copy-done.97), channel_id=1, source_target_pairs={{0,1},{1,0},{2,3},{3,2},{4,5},{5,4},{6,7},{7,6},{8,9},{9,8},{10,11... | collective-permute-start | bytes 3538952 | tf_op jit(solution)/shard_map/ppermute | solution.py:24
  568.4 13.7 %collective-permute-start.68 = (bf16[2,112,576]{2,1,0:T(8,128)(2,1)S(1)}, bf16[2,112,576]{2,1,0:T(8,128)(2,1)S(1)}, u32[]{:S(2)}, u32[]{:S(2)}) collective-permute-start(bf16[2,112,576]{2,1,0:T(8,128)(2,1)S(1)} %get-tuple-element.450), channel_id=1, source_target_pairs={{0,2},{1,3},{2,0},{3,1},{4,6},{5,7},{6,4},{7,5},{8,10},{9,11},{10,... | collective-permute-start | bytes 774152 | tf_op jit(solution)/shard_map/ppermute | solution.py:24
  (133 other events, 1212.3 us)

commit v4 on v3

--- a/solution.py
+++ b/solution.py
@@ -209,7 +209,7 @@
     return values * cosine + turned * sine
 
 
-def project(blocks, place, offsets, pieces, a_first, b_first, cosine, sine):
+def project(blocks, place, offsets, pieces, a_first, b_first, cosine_pair, sine_pair):
     rows, width = blocks[0].shape
     count = len(blocks)
     size = pieces[0].shape[1]
@@ -227,19 +227,26 @@
             narrow_ref[:, pl.ds(starts[block], rows)] = dot_t(a_ref[...], x_refs[block][...]).astype(BF16)
         for copy in copies:
             copy.wait()
+        both = 2 * heads * HDIM
+        lane = lax.broadcasted_iota(jnp.int32, (rows, both), 1) % HDIM
+        lower = lane < HDIM // 2
         for block in range(count):
             start = starts[block]
             narrow = narrow_ref[:, pl.ds(start, rows)]
             pre = dot(x_refs[block][...], whole[...]) + t_dot(narrow, b_ref[...])
-            cosine_here = cos_ref[pl.ds(start, rows), :]
-            sine_here = sin_ref[pl.ds(start, rows), :]
+            flat = pre[:, :both]
+            cosine_here = jnp.tile(cos_ref[pl.ds(start, rows), :], (1, both // (2 * HDIM)))
+            sine_here = jnp.tile(sin_ref[pl.ds(start, rows), :], (1, both // (2 * HDIM)))
+            other = jnp.where(
+                lower, pltpu.roll(flat, both - HDIM // 2, 1), pltpu.roll(flat, HDIM // 2, 1)
+            )
+            turned = (flat * cosine_here + other * sine_here).astype(BF16)
+            straight = pre[:, both:].astype(BF16)
             for number, out in enumerate((q_ref, k_ref, v_ref)):
                 for head in range(heads):
-                    at = (number * heads + head) * HDIM
-                    part = pre[:, at : at + HDIM]
-                    if number < 2:
-                        part = turn(part, cosine_here, sine_here)
-                    out[head, pl.ds(start, rows), :] = part.astype(BF16)
+                    at = (number % 2 * heads + head) * HDIM
+                    source = turned if number < 2 else straight
+                    out[head, pl.ds(start, rows), :] = source[:, at : at + HDIM]
 
     by_heads = jax.ShapeDtypeStruct((heads, rows * count, HDIM), BF16)
     return call(
@@ -251,8 +258,8 @@
         2 * rows * count * width * size,
         2 * (rows * count * width + width * size + 2 * rows * count * size),
         "project",
-        limit=44,
-    )(place[None], offsets, *blocks, *pieces, a_first, b_first, cosine, sine)
+        limit=56,
+    )(place[None], offsets, *blocks, *pieces, a_first, b_first, cosine_pair, sine_pair)
 
 
 def label_of(positions, starts_ref):
@@ -270,7 +277,7 @@
     return jnp.where(visible, 0.0, -1e30)
 
 
-def crosses(starts_ref, edge, rows):
+def crosses(starts_ref, edge):
     hit = None
     for number in range(starts_ref.shape[0]):
         start = starts_ref[number]
@@ -279,12 +286,21 @@
     return hit
 
 
+def fill_bias(bias, starts_ref, rows):
+    for block in range(bias.shape[0]):
+        shape = (2 * rows, rows)
+        query_at = block * rows + lax.broadcasted_iota(jnp.int32, shape, 1)
+        key_at = block * rows + lax.broadcasted_iota(jnp.int32, shape, 0)
+        bias[block] = hidden_bias(query_at, key_at, starts_ref)
+
+
 def attend(starts, query, key, value, rows):
     heads, length, _ = query.shape
     count = length // rows
     factor = LOG2E / math.sqrt(HDIM)
-
-    def kernel(starts_ref, q_ref, k_ref, v_ref, o_ref, bias):
+    each = 3
+
+    def kernel(starts_ref, q_ref, k_ref, v_ref, o_ref, log_ref, bias):
         @pl.when(pl.program_id(0) == 0)
         def _():
             for block in range(count):
@@ -295,47 +311,54 @@
 
         def one(block, extra):
             low, high = block * rows, (block + 1 + extra) * rows
-            q = q_ref[0, low : low + rows, :]
-            edge = dot_t(q, k_ref[0, low:high, :]) + bias[block, :, : high - low]
-            top = jnp.max(edge, axis=1, keepdims=True)
-            if block:
-                before = dot_t(q, k_ref[0, :low, :])
-                top = jnp.maximum(top, jnp.max(before, axis=1, keepdims=True))
-            shift = top * factor
-            weight = jnp.exp2(edge * factor - shift)
-            total = jnp.sum(weight, axis=1, keepdims=True)
-            out = dot(weight.astype(BF16), v_ref[0, low:high, :])
-            if block:
-                weight = jnp.exp2(before * factor - shift)
-                total = total + jnp.sum(weight, axis=1, keepdims=True)
-                out = out + dot(weight.astype(BF16), v_ref[0, :low, :])
-            o_ref[0, low : low + rows, :] = (out / total).astype(BF16)
+            here = slice(low, low + rows)
+            states = []
+            for head in range(each):
+                q = q_ref[head, here, :]
+                edge = dot_t(q, k_ref[head, low:high, :]) + bias[block, :, : high - low]
+                before = dot_t(q, k_ref[head, :low, :]) if block else None
+                states.append((edge, before))
+            for head, (edge, before) in enumerate(states):
+                top = jnp.max(edge, axis=1, keepdims=True)
+                if block:
+                    top = jnp.maximum(top, jnp.max(before, axis=1, keepdims=True))
+                shift = top * factor
+                weight = jnp.exp2(edge * factor - shift)
+                total = jnp.sum(weight, axis=1, keepdims=True)
+                out = dot(weight.astype(BF16), v_ref[head, low:high, :])
+                if block:
+                    weight = jnp.exp2(before * factor - shift)
+                    total = total + jnp.sum(weight, axis=1, keepdims=True)
+                    out = out + dot(weight.astype(BF16), v_ref[head, :low, :])
+                o_ref[head, here, :] = (out * (1.0 / total)).astype(BF16)
+                logs = jnp.broadcast_to(shift + jnp.log2(total), (rows, 128))
+                log_ref[head, :, here] = logs.T[:1]
 
         for block in range(count):
             if block == count - 1:
                 one(block, 0)
                 continue
-            wide = crosses(starts_ref, (block + 1) * rows, rows)
+            wide = crosses(starts_ref, (block + 1) * rows)
             pl.when(wide)(functools.partial(one, block, 1))
             pl.when(jnp.logical_not(wide))(functools.partial(one, block, 0))
 
-    spec = pl.BlockSpec((1, length, HDIM), lambda h: (h, 0, 0))
+    spec = pl.BlockSpec((each, length, HDIM), lambda h: (h, 0, 0))
     return call(
         kernel,
-        jax.ShapeDtypeStruct(query.shape, BF16),
+        [jax.ShapeDtypeStruct(query.shape, BF16), jax.ShapeDtypeStruct((heads, 1, length), F32)],
         [smem(), spec, spec, spec],
-        spec,
+        [spec, pl.BlockSpec((each, 1, length), lambda h: (h, 0, 0))],
         [pltpu.VMEM((count, rows, 2 * rows), F32)],
         4 * heads * length * length * HDIM * 4,
         16 * heads * length * HDIM,
         "attend",
-        limit=20,
-        grid=(heads,),
+        limit=32,
+        grid=(heads // each,),
     )(starts, query, key, value)
 
 
 def attend_back(
-    starts, place, query, key, value, near, far, cosine, sine, narrow, b_heads, rows, first, heads
+    starts, place, query, key, value, mixed, logs, near, far, cosine, sine, narrow, b_heads, rows, first, heads
 ):
     length = query.shape[1]
     thin = narrow.shape[0]
@@ -345,64 +368,85 @@
     factor = LOG2E * scale
 
     def kernel(
-        starts_ref, place_ref, q_ref, k_ref, v_ref, near_ref, far_ref, cos_ref, sin_ref,
-        narrow_ref, b_ref, dq_ref, dk_ref, dv_ref, thin_ref, out_ref, bias, key_sum, value_sum, key_turned,
+        starts_ref, place_ref, q_ref, k_ref, v_ref, o_ref, log_ref, near_ref, far_ref, cos_ref, sin_ref,
+        narrow_ref, b_ref, dq_ref, dk_ref, dv_ref, thin_ref, out_ref,
+        bias, key_sum, value_sum, key_turned, query_sum,
     ):
-        @pl.when(pl.program_id(0) == 0)
-        def _():
-            for block in range(count):
-                shape = (2 * rows, rows)
-                query_at = block * rows + lax.broadcasted_iota(jnp.int32, shape, 1)
-                key_at = block * rows + lax.broadcasted_iota(jnp.int32, shape, 0)
-                bias[block] = hidden_bias(query_at, key_at, starts_ref)
-
-            thin_ref[...] = jnp.zeros_like(thin_ref)
-
-        key_sum[...] = jnp.zeros_like(key_sum)
-        value_sum[...] = jnp.zeros_like(value_sum)
-        key_turned[...] = k_ref[0].astype(F32).T.astype(BF16)
-
-        def one(block, extra):
-            low, high = block * rows, (block + 1 + extra) * rows
-            q = q_ref[0, low : low + rows, :]
+        fill_bias(bias, starts_ref, rows)
+        ones = jnp.ones((8, HDIM), BF16)
+        for head in range(heads):
+            key_turned[head] = k_ref[head].astype(F32).T.astype(BF16)
+
+        def pair(head, query, keys, mask, new):
+            q, g, logs, inner = query
+            here = slice(keys * rows, (keys + 1) * rows)
+            raw = dot_t(k_ref[head, here, :], q)
+            if mask is not None:
+                raw = raw + mask
+            probs = jnp.exp2(raw * factor - logs)
+            grad_probs = dot_t(v_ref[head, here, :], g)
+            grad_scores = (probs * (grad_probs - inner)).astype(BF16)
+            value_term = dot(probs.astype(BF16), g)
+            key_term = dot(grad_scores, q)
+            if new:
+                value_sum[head, here, :] = value_term
+                key_sum[head, here, :] = key_term
+            else:
+                value_sum[head, here, :] += value_term
+                key_sum[head, here, :] += key_term
+            return dot(key_turned[head, :, here], grad_scores)
+
+        for block in reversed(range(count)):
+            here = slice(block * rows, (block + 1) * rows)
             relative = place_ref[0] ^ block
             at = pl.multiple_of((relative % 2) * rows, rows)
-            g = jnp.where(relative < 2, near_ref[0, pl.ds(at, rows), :], far_ref[0, pl.ds(at, rows), :])
-            raw = dot_t(k_ref[0, low:high, :], q) + bias[block, : high - low, :]
-            if block:
-                raw = jnp.concatenate([dot_t(k_ref[0, :low, :], q), raw], axis=0)
-            top = jnp.max(raw, axis=0, keepdims=True)
-            weight = jnp.exp2(raw * factor - top * factor)
-            probs = weight * (1.0 / jnp.sum(weight, axis=0, keepdims=True))
-            grad_probs = dot_t(v_ref[0, :high, :], g)
-            inner = jnp.sum(grad_probs * probs, axis=0, keepdims=True)
-            grad_scores = (probs * (grad_probs - inner)).astype(BF16)
-            value_sum[:high, :] += dot(probs.astype(BF16), g)
-            key_sum[:high, :] += dot(grad_scores, q)
-            turned = dot(key_turned[:, :high], grad_scores)
-            back = turned.T * scale
-            dq_ref[0, low : low + rows, :] = turn(
-                back, cos_ref[low : low + rows, :], -sin_ref[low : low + rows, :]
-            ).astype(BF16)
-
-        for block in range(count):
-            if block == count - 1:
-                one(block, 0)
-                continue
-            wide = crosses(starts_ref, (block + 1) * rows, rows)
-            pl.when(wide)(functools.partial(one, block, 1))
-            pl.when(jnp.logical_not(wide))(functools.partial(one, block, 0))
-        dk_ref[0] = turn(key_sum[...] * scale, cos_ref[...], -sin_ref[...]).astype(BF16)
-        dv_ref[0] = value_sum[...].astype(BF16)
-        for number, ref in enumerate((dq_ref, dk_ref, dv_ref)):
-            here = slice(number * rank, (number + 1) * rank)
-            thin_ref[here, :] += dot_t(b_ref[0, here, :], ref[0])
-            out_ref[0, here, :] = dot(narrow_ref[here, :], ref[0])
-
-    spec = pl.BlockSpec((1, length, HDIM), lambda h: (first + h, 0, 0))
-    half = pl.BlockSpec((1, length // 2, HDIM), lambda h: (first + h, 0, 0))
-    out = pl.BlockSpec((1, length, HDIM), lambda h: (h, 0, 0))
+            queries = []
+            for head in range(heads):
+                g = jnp.where(
+                    relative < 2, near_ref[head, pl.ds(at, rows), :], far_ref[head, pl.ds(at, rows), :]
+                )
+                product = g.astype(F32) * o_ref[head, here, :].astype(F32)
+                high = product.astype(BF16)
+                low = (product - high.astype(F32)).astype(BF16)
+                inner = (dot_t(ones, high) + dot_t(ones, low))[:1]
+                queries.append((q_ref[head, here, :], g, log_ref[head, :, here], inner))
+            last = block == count - 1
+            totals = [pair(head, queries[head], block, bias[block, :rows, :], last) for head in range(heads)]
+            for keys in range(block):
+                for head in range(heads):
+                    totals[head] = totals[head] + pair(head, queries[head], keys, None, last)
+            if not last:
+                for head in range(heads):
+                    query_sum[head] = totals[head]
+
+                @pl.when(crosses(starts_ref, (block + 1) * rows))
+                def _():
+                    for head in range(heads):
+                        query_sum[head] += pair(head, queries[head], block + 1, bias[block, rows:, :], False)
+
+                totals = [query_sum[head] for head in range(heads)]
+            for head in range(heads):
+                dq_ref[head, here, :] = turn(
+                    totals[head].T * scale, cos_ref[here, :], -sin_ref[here, :]
+                ).astype(BF16)
+        thins = [None] * 3
+        for head in range(heads):
+            dk_ref[head] = turn(key_sum[head] * scale, cos_ref[...], -sin_ref[...]).astype(BF16)
+            dv_ref[head] = value_sum[head].astype(BF16)
+            for number, ref in enumerate((dq_ref, dk_ref, dv_ref)):
+                here = slice(number * rank, (number + 1) * rank)
+                term = dot_t(b_ref[head, here, :], ref[head])
+                thins[number] = term if head == 0 else thins[number] + term
+                out_ref[head, here, :] = dot(narrow_ref[here, :], ref[head])
+        for number in range(3):
+            thin_ref[number * rank : (number + 1) * rank, :] = thins[number]
+
+    step = first // heads
+    spec = pl.BlockSpec((heads, length, HDIM), lambda h: (step, 0, 0))
+    half = pl.BlockSpec((heads, length // 2, HDIM), lambda h: (step, 0, 0))
+    out = pl.BlockSpec((heads, length, HDIM), lambda h: (0, 0, 0))
     table = pl.BlockSpec((length, HDIM), lambda h: (0, 0))
+    thin_spec = pl.BlockSpec((thin, length), lambda h: (0, 0))
     return call(
         kernel,
         [jax.ShapeDtypeStruct((heads, length, HDIM), BF16)] * 3
@@ -410,28 +454,25 @@
             jax.ShapeDtypeStruct((thin, length), F32),
             jax.ShapeDtypeStruct((heads, thin, HDIM), F32),
         ],
-        [smem(), smem(), spec, spec, spec, half, half, table, table]
-        + [
-            pl.BlockSpec((thin, length), lambda h: (0, 0)),
-            pl.BlockSpec((1, thin, HDIM), lambda h: (first + h, 0, 0)),
-        ],
-        [out] * 3
-        + [
-            pl.BlockSpec((thin, length), lambda h: (0, 0)),
-            pl.BlockSpec((1, thin, HDIM), lambda h: (h, 0, 0)),
-        ],
+        [smem(), smem(), spec, spec, spec, spec]
+        + [pl.BlockSpec((heads, 1, length), lambda h: (step, 0, 0)), half, half, table, table, thin_spec]
+        + [pl.BlockSpec((heads, thin, HDIM), lambda h: (step, 0, 0))],
+        [out] * 3 + [thin_spec, pl.BlockSpec((heads, thin, HDIM), lambda h: (0, 0, 0))],
         [
             pltpu.VMEM((count, 2 * rows, rows), F32),
-            pltpu.VMEM((length, HDIM), F32),
-            pltpu.VMEM((length, HDIM), F32),
-            pltpu.VMEM((HDIM, length), BF16),
+            pltpu.VMEM((heads, length, HDIM), F32),
+            pltpu.VMEM((heads, length, HDIM), F32),
+            pltpu.VMEM((heads, HDIM, length), BF16),
+            pltpu.VMEM((heads, HDIM, rows), F32),
         ],
         10 * heads * length * length * HDIM * 4,
         32 * heads * length * HDIM,
         "attend_back",
-        limit=24,
-        grid=(heads,),
-    )(starts, place[None], query, key, value, near, far, cosine, sine, narrow, b_heads)
+        limit=32,
+        grid=(1,),
+    )(
+        starts, place[None], query, key, value, mixed, logs, near, far, cosine, sine, narrow, b_heads
+    )
 
 
 def rows_by_heads(refs, start, rows):
@@ -537,52 +578,41 @@
         down_copy = pltpu.make_async_copy(down_hbm, down_ref, down_sem)
         down_copy.start()
         copies = load_pieces(offsets_ref, piece_refs, whole, sems)
-        narrows = [dot_t(x_refs[block][...], am_ref[...]).astype(BF16) for block in range(count)]
-        thins = [dot_t(g_refs[block][...], bd_ref[...]).astype(BF16) for block in range(count)]
+        x = jnp.concatenate([ref[...] for ref in x_refs], axis=0)
+        grad = jnp.concatenate([ref[...] for ref in g_refs], axis=0)
+        narrow = dot_t(x, am_ref[...]).astype(BF16)
+        thin = dot_t(grad, bd_ref[...]).astype(BF16)
         down_copy.wait()
-        for block in range(count):
-            grad_ref[block] = (
-                dot_t(g_refs[block][...], down_ref[...]) + dot(thins[block], ah_ref[...])
-            ).astype(BF16)
+        grad_ref[...] = (dot_t(grad, down_ref[...]) + dot(thin, ah_ref[...])).astype(BF16)
         for copy in copies:
             copy.wait()
-        pad = jnp.zeros((rows, EXTRA - rank), BF16)
+        gate = dot(x, whole[0]) + dot(narrow[:, :rank], bh_ref[0])
+        up = dot(x, whole[1]) + dot(narrow[:, rank:], bh_ref[1])
+        sigmoid = 0.5 + 0.5 * jnp.tanh(0.5 * gate)
+        silu = gate * sigmoid
+        hidden = (silu * up).astype(BF16)
+        grad_hidden = grad_ref[...].astype(F32)
+        grad_up = (grad_hidden * silu).astype(BF16)
+        grad_gate = (grad_hidden * up * (sigmoid + silu * (1.0 - sigmoid))).astype(BF16)
+        feed = dot(hidden, down_ref[...]).astype(BF16)
+        feed_thin = dot_t(hidden, ah_ref[...]).astype(BF16)
+        back = (dot_t(grad_gate, whole[0]) + dot_t(grad_up, whole[1])).astype(BF16)
+        back_thin = jnp.concatenate(
+            [dot_t(grad_gate, bh_ref[0]).astype(BF16), dot_t(grad_up, bh_ref[1]).astype(BF16)], axis=1
+        )
         for block in range(count):
-            x = x_refs[block][...]
-            narrow = narrows[block]
-            gate = dot(x, whole[0]) + dot(narrow[:, :rank], bh_ref[0])
-            up = dot(x, whole[1]) + dot(narrow[:, rank:], bh_ref[1])
-            sigmoid = 0.5 + 0.5 * jnp.tanh(0.5 * gate)
-            silu = gate * sigmoid
-            hidden = (silu * up).astype(BF16)
-            grad_hidden = grad_ref[block].astype(F32)
-            grad_up = (grad_hidden * silu).astype(BF16)
-            grad_gate = (grad_hidden * up * (sigmoid + silu * (1.0 - sigmoid))).astype(BF16)
-            feed_refs[block][:, :width] = dot(hidden, down_ref[...]).astype(BF16)
+            here = slice(block * rows, (block + 1) * rows)
+            feed_refs[block][:, :width] = feed[here]
             feed_refs[block][:, width:] = jnp.concatenate(
-                [dot_t(hidden, ah_ref[...]).astype(BF16), pad], axis=1
+                [feed_thin[here], jnp.zeros((rows, EXTRA - rank), BF16)], axis=1
             )
-            back = dot_t(grad_gate, whole[0]) + dot_t(grad_up, whole[1])
-            back_refs[block][:, :width] = back.astype(BF16)
+            back_refs[block][:, :width] = back[here]
             back_refs[block][:, width:] = jnp.concatenate(
-                [
-                    dot_t(grad_gate, bh_ref[0]).astype(BF16),
-                    dot_t(grad_up, bh_ref[1]).astype(BF16),
-                    pad[:, rank:],
-                ],
-                axis=1,
+                [back_thin[here], jnp.zeros((rows, EXTRA - 2 * rank), BF16)], axis=1
             )
-            terms = (
-                t_dot(thins[block], hidden),
-                t_dot(narrow[:, :rank], grad_gate),
-                t_dot(narrow[:, rank:], grad_up),
-            )
-            for number, term in enumerate(terms):
-                here = slice(number * rank, (number + 1) * rank)
-                if block == 0:
-                    sum_ref[here, :] = term
-                else:
-                    sum_ref[here, :] += term
+        sum_ref[:rank, :] = t_dot(thin, hidden)
+        sum_ref[rank : 2 * rank, :] = t_dot(narrow[:, :rank], grad_gate)
+        sum_ref[2 * rank :, :] = t_dot(narrow[:, rank:], grad_up)
 
     out = jax.ShapeDtypeStruct((rows, width + EXTRA), BF16)
     return call(
@@ -594,7 +624,7 @@
         [
             pltpu.VMEM((2, width, size), BF16),
             pltpu.VMEM((size, width), BF16),
-            pltpu.VMEM((count, rows, size), BF16),
+            pltpu.VMEM((count * rows, size), BF16),
             pltpu.SemaphoreType.DMA((n,)),
             pltpu.SemaphoreType.DMA,
         ],
@@ -701,26 +731,34 @@
         query_key_value_weight, rep_place % 4 * quarter, quarter, place, head_cols, (2, 3), "sides_far"
     )
     first_a = hop(quarter_one, "shard", 2)
-    first_b = hop(quarter_two, "shard", 3)
     normed = norm_rows(residual_in, gain_one).astype(BF16)
-    normed_near = core(normed)
     front_chip, front_part = chip_picked(
         jnp.concatenate([adapter_model_input_maps[0:3], adapter_model_output_maps[0:3]]), pick, place
     )
-    first_own, near_out = sides(
-        query_key_value_weight, 0, k_rows, place, head_cols, (0, 1), "sides_near"
-    )
+    first_a, front_part, quarter_two, normed, qkv = fence(
+        first_a, front_part, quarter_two, normed, query_key_value_weight
+    )
+    first_b = hop(quarter_two, "shard", 3)
+    first_a_two, first_a_three = hop(first_a, "rep", 2), hop(first_a, "rep", 1)
+    first_own, near_out = sides(qkv, 0, k_rows, place, head_cols, (0, 1), "sides_near")
+    normed_near = core(normed)
+    first_b, front_part, near_out, rest_bank, wide_bank = fence(
+        first_b, front_part, near_out,
+        (adapter_model_input_maps[3:6], adapter_model_output_maps[3:5]),
+        (adapter_hidden_input_map[None], adapter_hidden_output_maps),
+    )
+    front_far = across(front_part)
+    first_b_two, first_b_three = hop(first_b, "rep", 1), hop(first_b, "rep", 2)
+    front_far, normed, first_a_two, first_a_three = fence(front_far, normed, first_a_two, first_a_three)
+    normed_far = across(normed)
+    first_a_four = hop(first_a_two, "rep", 1)
     first_near = core(near_out)
-    first_a, front_part, normed, first_own = fence(first_a, front_part, normed, first_own)
-    first_a_two, first_a_three = hop(first_a, "rep", 2), hop(first_a, "rep", 1)
-    front_far = across(front_part)
-    first_b, first_a_two, first_a_three, normed = fence(first_b, first_a_two, first_a_three, normed)
-    first_b_two, first_b_three = hop(first_b, "rep", 1), hop(first_b, "rep", 2)
-    normed_far = across(normed)
-    first_b_two, first_b_three, front_far, gate_up, grad_out, front_chip = fence(
-        first_b_two, first_b_three, front_far, gate_up_projection_weight, grad_out, front_chip
-    )
-    first_a_four, first_b_four = hop(first_a_two, "rep", 1), hop(first_b_two, "rep", 2)
+    rest_chip, rest_part = chip_picked(jnp.concatenate(rest_bank), pick, place)
+    wide_chip, wide_part = chip_picked(jnp.concatenate(wide_bank), pick, place)
+    first_b_two, first_b_three, gate_up, grad_out, front_chip = fence(
+        first_b_two, first_b_three, gate_up_projection_weight, grad_out, front_chip
+    )
+    first_b_four = hop(first_b_two, "rep", 2)
     mlp_leaving = [side(gate_up, rep_place % 4 * quarter, quarter, place ^ j, ff_cols) for j in (2, 3)]
     grad_feed = (BRANCH * grad_out).astype(BF16)
     half = HDIM // 2
@@ -728,15 +766,19 @@
     angle = jnp.arange(rows * group, dtype=jnp.int32).astype(F32)[:, None] * frequency[None, :]
     cosine = jnp.concatenate([jnp.cos(angle), jnp.cos(angle)], axis=1)
     sine = jnp.concatenate([jnp.sin(angle), jnp.sin(angle)], axis=1)
+    cosine_pair = jnp.concatenate([jnp.cos(angle)] * 4, axis=1)
+    sine_pair = jnp.concatenate([-jnp.sin(angle), jnp.sin(angle)] * 2, axis=1)
+    tables = (cosine, sine, cosine_pair, sine_pair)
     front = whole_picked(front_chip, front_far, place)
     a_first = front[:3].reshape(3 * rank, width)
     b_first = own_columns(front[3:], head_cols)
     b_wide = jnp.concatenate(
         [jnp.pad(b_first[i], ((0, 0), (i * head_cols, (2 - i) * head_cols))) for i in range(3)]
     )
-    normed_far, first_a_four, first_b_four, mlp_leaving, grad_feed, cosine, sine, b_wide, a_first = fence(
-        normed_far, first_a_four, first_b_four, mlp_leaving, grad_feed, cosine, sine, b_wide, a_first
-    )
+    normed_far, first_a_four, first_b_four, mlp_leaving, grad_feed, b_wide, a_first, rest_part, wide_part, tables = fence(
+        normed_far, first_a_four, first_b_four, mlp_leaving, grad_feed, b_wide, a_first, rest_part, wide_part, tables
+    )
+    cosine, sine, cosine_pair, sine_pair = tables
     first_blocks = (normed, normed_near, normed_far, core(normed_far))
     first_offsets, first_pieces = arrange(
         k_rows, first_own, first_near,
@@ -749,19 +791,12 @@
 
     mlp_a, mlp_b = hop(mlp_leaving[0], "shard", 2), hop(mlp_leaving[1], "shard", 3)
     query, key, value, narrow_first = project(
-        first_blocks, place, first_offsets, first_pieces, a_first, b_wide, cosine, sine
-    )
-    query, mlp_a, rest_bank, wide_bank = fence(
-        query, mlp_a,
-        (adapter_model_input_maps[3:6], adapter_model_output_maps[3:5]),
-        (adapter_hidden_input_map[None], adapter_hidden_output_maps),
-    )
+        first_blocks, place, first_offsets, first_pieces, a_first, b_wide, cosine_pair, sine_pair
+    )
+    query, mlp_a, rest_part, wide_part = fence(query, mlp_a, rest_part, wide_part)
     mlp_a_two, mlp_a_three = hop(mlp_a, "rep", 2), hop(mlp_a, "rep", 1)
-    rest_chip, rest_part = chip_picked(jnp.concatenate(rest_bank), pick, place)
-    wide_chip, wide_part = chip_picked(jnp.concatenate(wide_bank), pick, place)
-    rest_part, wide_part, query = fence(rest_part, wide_part, query)
     rest_far, wide_far = across(rest_part), across(wide_part)
-    mixed = attend(starts, query, key, value, rows)
+    mixed, logs = attend(starts, query, key, value, rows)
     mixed, mlp_b, mlp_a_two, mlp_a_three, rest_far = fence(
         mixed, mlp_b, mlp_a_two, mlp_a_three, rest_far
     )
@@ -772,15 +807,18 @@
     b_out, b_down = rest[3], rest[4]
     far_out = close_attention(mixed, place, attention_output_weight, a_out, (2, 3), rows)
     far_sum = (far_out[0].astype(F32) + core(far_out[1]).astype(F32)).astype(BF16)
-    far_sum, mixed_here, grad_feed, wide_far = fence(far_sum, mixed, grad_feed, wide_far)
+    far_sum, mixed_here, grad_feed, wide_far, gate_up = fence(far_sum, mixed, grad_feed, wide_far, gate_up)
     branch_far = across(far_sum)
+    mlp_near_out = side(gate_up, 0, k_rows, place ^ 1, ff_cols)
+    mlp_own = side(gate_up, 0, k_rows, place, ff_cols)
     feed_near_in = core(grad_feed)
     near_out = close_attention(mixed_here, place, attention_output_weight, a_out, (0, 1), rows)
-    near_out, mlp_b_two, mlp_b_three, gate_up = fence(near_out, mlp_b_two, mlp_b_three, gate_up)
+    near_out, mlp_b_two, mlp_b_three, mlp_near_out, mlp_own = fence(
+        near_out, mlp_b_two, mlp_b_three, mlp_near_out, mlp_own
+    )
     mlp_a_four, mlp_b_four = hop(mlp_a_two, "rep", 1), hop(mlp_b_two, "rep", 2)
     near_here = core(near_out[1])
-    mlp_near = core(side(gate_up, 0, k_rows, place ^ 1, ff_cols))
-    mlp_own = side(gate_up, 0, k_rows, place, ff_cols)
+    mlp_near = core(mlp_near_out)
     hidden_cols = own_columns(whole_picked(wide_chip, wide_far, place), ff_cols)
     near_here, branch_far, hidden_cols, mlp_own, mlp_a_four, mlp_b_four = fence(
         near_here, branch_far, hidden_cols, mlp_own, mlp_a_four, mlp_b_four
@@ -863,74 +901,76 @@
 
     def attend_part(first, heads, starts):
         return attend_back(
-            starts, place, query, key, value, mixed_near, mixed_far, cosine, sine, narrow_first, b_heads,
-            rows, first, heads,
+            starts, place, query, key, value, mixed, logs, mixed_near, mixed_far, cosine, sine,
+            narrow_first, b_heads, rows, first, heads,
         )
 
-    mixed_far, wide_hop = fence(mixed_far, wide_hop)
-    wide_all = both(wide_all, wide_hop, rep_place, bits[-2])
-    wide_hop = hop(wide_all, "rep", bits[-1])
-    wide_all, starts_one = fence(wide_all, starts)
+    mixed_far, starts_one = fence(mixed_far, starts)
     heads = query.shape[0]
     third = heads // 3
     part_one = attend_part(0, third, starts_one)
     part_one, feed_from_far, wide_hop, starts_two = fence(part_one, feed_from_far, wide_hop, starts_one)
+    wide_all = both(wide_all, wide_hop, rep_place, bits[-2])
+    wide_hop = hop(wide_all, "rep", bits[-1])
+    feed_own = feed_here + feed_from_far.astype(F32)
+    narrow_down = feed_own[:, width : width + rank].astype(BF16)
+    down_far = across(narrow_down)
+    down_near = core(narrow_down)
+    starts_two, narrow_down = fence(starts_two, narrow_down)
+    part_two = attend_part(third, third, starts_two)
+    part_two, wide_hop, down_far, down_near, starts_three = fence(
+        part_two, wide_hop, down_far, down_near, starts_two
+    )
+    down_thin = (narrow_down, down_near, down_far, core(down_far))
     wide_all = both(wide_all, wide_hop, rep_place, bits[-1])
     picks = wide_all[:, -1, :1].astype(F32)
     adapters = adapter_model_input_maps.shape[1] * group
     chosen = (picks == jnp.arange(adapters, dtype=jnp.int32).astype(F32)[None, :]).astype(F32)
     wide_sent = send_sums(wide_all[:, :-rank], chosen, place)
+    grad_b_down = sum(t_dot(left, right) for left, right in zip(down_thin, feed_blocks))
     early_all = jnp.concatenate(
-        [grad_a_near + grad_a_far, own_columns(thin_near + thin_far, head_cols)]
+        [
+            grad_a_near + grad_a_far,
+            own_columns(jnp.concatenate([thin_near + thin_far, grad_b_down]), head_cols),
+        ]
     ).astype(BF16)[None]
     early_hop = hop(early_all, "rep", bits[0])
-    feed_own = feed_here + feed_from_far.astype(F32)
-    narrow_down = feed_own[:, width : width + rank].astype(BF16)
-    down_far = across(narrow_down)
-    down_near = core(narrow_down)
-    starts_two, narrow_down, early_all = fence(starts_two, narrow_down, early_all)
-    part_two = attend_part(third, third, starts_two)
-    part_two, wide_sent, early_hop, down_far, down_near, starts_three = fence(
-        part_two, wide_sent, early_hop, down_far, down_near, starts_two
-    )
+    early_all, starts_three = fence(early_all, starts_three)
+    part_three = attend_part(2 * third, heads - 2 * third, starts_three)
+    part_three, early_hop, wide_sent = fence(part_three, early_hop, wide_sent)
+    parts = (part_one, part_two, part_three)
+    first_grads = [part[number] for number in range(3) for part in parts]
+    thin = (part_one[3] + part_two[3] + part_three[3]).astype(BF16)
+    thin_hop = core(thin)
     early_all = both(early_all, early_hop, rep_place, bits[0])
     for bit in bits[1:-2]:
         early_all = both(early_all, hop(early_all, "rep", bit), rep_place, bit)
     early_hop = hop(early_all, "rep", bits[-2])
-    down_far_near = core(down_far)
-    early_all, starts_three = fence(early_all, starts_three)
-    part_three = attend_part(2 * third, heads - 2 * third, starts_three)
-    part_three, early_hop, down_far_near = fence(part_three, early_hop, down_far_near)
-    parts = (part_one, part_two, part_three)
-    first_grads = [part[number] for number in range(3) for part in parts]
-    thin = (part_one[3] + part_two[3] + part_three[3]).astype(BF16)
-    thin_hop = core(thin)
-    early_all = both(early_all, early_hop, rep_place, bits[-2])
-    early_hop = hop(early_all, "rep", bits[-1])
-    early_all, first_grads = fence(early_all, first_grads)
+    thin = (thin.astype(F32) + thin_hop.astype(F32)).astype(BF16)
+    thin, first_grads, early_all = fence(thin, first_grads, early_all)
+    thin_hop = across(thin)
     back_rows_far = project_back(first_grads, place, first_offsets, first_pieces, (2, 3), rows)
     back_rows_far, thin_hop, early_hop = fence(back_rows_far, thin_hop, early_hop)
     back_mate = core(back_rows_far[1])
-    thin = (thin.astype(F32) + thin_hop.astype(F32)).astype(BF16)
-    thin_hop = across(thin)
-    back_sum = (back_rows_far[0].astype(F32) + back_mate.astype(F32)).astype(BF16)
-    thin_hop, back_sum, grad_b_heads = fence(thin_hop, back_sum, [part[4] for part in parts])
-    back_far_in = across(back_sum)
     grad_narrow = (thin.astype(F32) + thin_hop.astype(F32)).astype(BF16)
-    grad_b_first = jnp.concatenate(grad_b_heads).transpose(1, 0, 2).reshape(3 * rank, head_cols)
-    down_thin = (narrow_down, down_near, down_far, down_far_near)
-    grad_b_down = sum(t_dot(left, right) for left, right in zip(down_thin, feed_blocks))
+    grad_b_first = jnp.concatenate([part[4] for part in parts]).transpose(1, 0, 2)
     late_all = jnp.concatenate(
         [
             own_columns(thin_product(grad_narrow, place, first_blocks), head_cols),
-            grad_b_first,
-            own_columns(grad_b_down, head_cols),
+            grad_b_first.reshape(3 * rank, head_cols),
         ]
     ).astype(BF16)[None]
-    late_all, grads_here = fence(late_all, first_grads)
+    late_all, grad_narrow, back_mate, early_all, early_hop = fence(
+        late_all, grad_narrow, back_mate, early_all, early_hop
+    )
     late_hop = hop(late_all, "rep", bits[0])
+    back_sum = (back_rows_far[0].astype(F32) + back_mate.astype(F32)).astype(BF16)
+    early_all = both(early_all, early_hop, rep_place, bits[-2])
+    early_hop = hop(early_all, "rep", bits[-1])
+    back_sum, grads_here, early_all = fence(back_sum, first_grads, early_all)
+    back_far_in = across(back_sum)
     back_rows_near = project_back(grads_here, place, first_offsets, first_pieces, (0, 1), rows)
-    late_hop, back_rows_near = fence(late_hop, back_rows_near)
+    late_hop, back_rows_near, early_hop = fence(late_hop, back_rows_near, early_hop)
     back_rows_here = core(back_rows_near[1])
     late_all = both(late_all, late_hop, rep_place, bits[0])
     for bit in bits[1:-2]:
@@ -972,7 +1012,7 @@
         [
             whole_maps(late_got, 3 * rank, 6 * rank, head_cols),
             whole_maps(early_got, rank, 2 * rank, head_cols),
-            whole_maps(late_got, 6 * rank, 7 * rank, head_cols),
+            whole_maps(early_got, 4 * rank, 5 * rank, head_cols),
         ]
     )
     return (

time: 596 us -> 548 us (0.919)
  Pallas kernels: 225 us -> 201 us
  other arithmetic: 58.8 us -> 42.7 us
  waiting for transfers between devices: 163 us -> 149 us
    pallas_call x3, Pallas kernels: 54.4 us -> 38.3 us  [attend_back(): call(kernel, [jax.ShapeDtypeStruct((heads, length, HDIM), BF16)] * 3 + [j...]
    ppermute x74, waiting for transfers between devices: 163 us -> 149 us  [hop(): return lax.ppermute(values, axis, [(i, i ^ bit) for i in range(size)])]
    add x3, other arithmetic: 11.3 us -> 1.46 us  [chip_picked(): chip = mine + core(mine)]
    pallas_call x1, Pallas kernels: 21.6 us -> 14.3 us  [attend(): call(kernel, [jax.ShapeDtypeStruct(query.shape, BF16), jax.ShapeDtypeStru...]
    unnamed x211 -> x227, local copies, waits for them, and re-layouts: 35.9 us -> 37.8 us
  transfers between devices with their start and end apart: 74 -> 74, of which waited for: 27 -> 30; matrix products, arithmetic and copies ran while one was open for 15% -> 14% of each run, Pallas kernels for 31% -> 30%
where the time goes in v4:
time: 548 us; the launch traced here: 540 us
  Pallas kernels  201 us (37%)
  waiting for transfers between devices  149 us (27%)
  local copies, waits for them, and re-layouts  78.2 us (14%)
  starting transfers between devices  57.2 us (10%)
  other arithmetic  42.7 us (8%)
  matrix products  7.8 us (1%)
    ppermute x74, waiting for transfers between devices, hop(): return lax.ppermute(values, axis, [(i, i ^ bit) for i in range(size)])  149 us
    pallas_call x2, Pallas kernels, feed_forward(): call(kernel, [out] * (2 * count) + [jax.ShapeDtypeStruct((3 * rank, size)...  71.4 us
    ppermute x74, starting transfers between devices, hop(): return lax.ppermute(values, axis, [(i, i ^ bit) for i in range(size)])  57.2 us
    pallas_call x3, Pallas kernels, attend_back(): call(kernel, [jax.ShapeDtypeStruct((heads, length, HDIM), BF16)] * 3 + [j...  38.3 us
    unnamed x227, local copies, waits for them, and re-layouts  37.8 us
    pallas_call x2, Pallas kernels, project_back(): call(kernel, [jax.ShapeDtypeStruct((rows, width), BF16)] * count, [smem()...  24.7 us
    pallas_call x1, Pallas kernels, project(): call(kernel, [by_heads] * 3 + [jax.ShapeDtypeStruct((thin, rows * count),...  21 us
    pallas_call x1, Pallas kernels, attend(): call(kernel, [jax.ShapeDtypeStruct(query.shape, BF16), jax.ShapeDtypeStru...  14.3 us
  transfers between devices with their start and end apart: 74, of which 30 were waited for; matrix products, arithmetic and copies ran while one was open for 14% of the time, Pallas kernels for 30%

profile of v4, /device:TPU:0, one launch (start us, length us, event | category | flops | bytes accessed | tf_op | source)
XLA Modules:
  0.0 539.7 jit_solution(13983192134359280730)
XLA Ops:
  1.4 2.0 fusion.44
  5.2 3.6 sides_far.1
  8.9 2.6 collective-permute-start
  29.0 7.0 %sides_near.1 = (bf16[576,1728]{1,0:T(8,128)(2,1)}, bf16[576,1728]{1,0:T(8,128)(2,1)}) custom-call(s32[2]{0:T(128)} %get-tuple-element.547.where_ref, bf16[3,576,2304]{2,1,0:T(8,128)(2,1)} %w_ref.4), custom_call_target="tpu_custom_call" | custom-call | bytes 11943936 | tf_op jit(solution)/shard_map/sides_near/pallas_call | solution.py:140
  36.0 3.3 collective-permute-done.2.refs_10_.refs_15_
  49.6 7.1 %collective-permute-done.4.refs_12_.refs_17_ = bf16[144,1728]{1,0:T(8,128)(2,1)S(1)} collective-permute-done((bf16[144,1728]{1,0:T(8,128)(2,1)}, bf16[144,1728]{1,0:T(8,128)(2,1)S(1)}, u32[]{:S(2)}, u32[]{:S(2)}) %collective-permute-start.4) | collective-permute-done | bytes 497696 | tf_op jit(solution)/shard_map/ppermute | solution.py:24
  61.8 3.6 constant_dynamic-slice_fusion.9
  70.2 8.6 %collective-permute-done.11.refs_13_.refs_18_ = bf16[144,1728]{1,0:T(8,128)(2,1)S(1)} collective-permute-done((bf16[144,1728]{1,0:T(8,128)(2,1)S(1)}, bf16[144,1728]{1,0:T(8,128)(2,1)S(1)}, u32[]{:S(2)}, u32[]{:S(2)}) %collective-permute-start.11) | collective-permute-done | bytes 497696 | tf_op jit(solution)/shard_map/ppermute | solution.py:24
  78.8 6.5 %collective-permute-done.9.refs_2_ = bf16[256,2304]{1,0:T(8,128)(2,1)S(1)} collective-permute-done((bf16[256,2304]{1,0:T(8,128)(2,1)S(1)}, bf16[256,2304]{1,0:T(8,128)(2,1)S(1)}, u32[]{:S(2)}, u32[]{:S(2)}) %collective-permute-start.9) | collective-permute-done | bytes 1179680 | tf_op jit(solution)/shard_map/ppermute | solution.py:24
  88.9 21.0 %project.1 = (bf16[9,1024,64]{2,1,0:T(8,128)(2,1)}, bf16[9,1024,64]{2,1,0:T(8,128)(2,1)}, bf16[9,1024,64]{2,1,0:T(8,128)(2,1)}, bf16[48,1024]{1,0:T(8,128)(2,1)}) custom-call(s32[1]{0:T(128)} %bitcast.place_ref, s32[10]{0:T(128)} %stack.111.offsets_ref, bf16[256,2304]{1,0:T(8,128)(2,1)} %copy-done.9, bf16[256,2304]{1,0:T(8,128)(2,1)} %copy-done.21, ...), custom_call_target="tpu_custom_call" | custom-call | flops 8153726976 | bytes 19759104 | tf_op jit(solution)/shard_map/project/pallas_call | solution.py:252
  118.5 14.3 %attend.1 = (bf16[9,1024,64]{2,1,0:T(8,128)(2,1)S(1)}, f32[9,1,1024]{2,1,0:T(1,128)S(1)}) custom-call(s32[2]{0:T(128)S(1)} %bitcast.176, bf16[9,1024,64]{2,1,0:T(8,128)(2,1)S(1)} %copy-done.36, bf16[9,1024,64]{2,1,0:T(8,128)(2,1)S(1)} %copy-done.38, bf16[9,1024,64]{2,1,0:T(8,128)(2,1)S(1)} %copy-done.40), custom_call_target="tpu_custom_call" | custom-call | flops 9663676416 | bytes 9437184 | tf_op jit(solution)/shard_map/attend/pallas_call | solution.py:346
  136.3 3.3 close_attention.2
  146.5 3.2 collective-permute-done.24
  150.2 8.9 %constant_dynamic-slice_fusion.4 = (bf16[2,576,1440]{2,1,0:T(8,128)(2,1)}, bf16[2,576,1440]{2,1,0:T(8,128)(2,1)S(1)}) fusion(bf16[2,576,5760]{2,1,0:T(8,128)(2,1)} %param.22, s32[]{:T(128)S(6)} %select_n.366, s32[]{:T(128)S(6)} %select_n.365), kind=kLoop, calls=%fused_computation.176 | loop fusion | bytes 13271048 | tf_op jit(solution)/shard_map/dynamic_slice | solution.py:118
  159.1 2.2 close_attention.3
  161.3 2.0 collective-permute-done.26.refs_12_
  167.4 15.6 %collective-permute-done.30.refs_9_ = bf16[2,144,1440]{2,1,0:T(8,128)(2,1)S(1)} collective-permute-done((bf16[2,144,1440]{2,1,0:T(8,128)(2,1)}, bf16[2,144,1440]{2,1,0:T(8,128)(2,1)S(1)}, u32[]{:S(2)}, u32[]{:S(2)}) %collective-permute-start.30) | collective-permute-done | bytes 829472 | tf_op jit(solution)/shard_map/ppermute | solution.py:24
  183.0 2.2 collective-permute-done.31.refs_13_
  185.2 6.6 %collective-permute-done.28 = bf16[256,2432]{1,0:T(8,128)(2,1)S(1)} collective-permute-done((bf16[256,2432]{1,0:T(8,128)(2,1)S(1)}, bf16[256,2432]{1,0:T(8,128)(2,1)S(1)}, u32[]{:S(2)}, u32[]{:S(2)}) %collective-permute-start.28) | collective-permute-done | bytes 1245216 | tf_op jit(solution)/shard_map/ppermute | solution.py:24
  201.8 35.9 %feed_forward.2 = (bf16[256,2432]{1,0:T(8,128)(2,1)}, bf16[256,2432]{1,0:T(8,128)(2,1)}, bf16[256,2432]{1,0:T(8,128)(2,1)}, bf16[256,2432]{1,0:T(8,128)(2,1)}, f32[48,1440]{1,0:T(8,128)}) custom-call(s32[10]{0:T(128)} %stack.111.offsets_ref, bf16[256,2304]{1,0:T(8,128)(2,1)} %copy-done.7, bf16[256,2304]{1,0:T(8,128)(2,1)} %copy-done.29, ...), custom_call_target="tpu_custom_call" | custom-call | flops 20384317440 | bytes 29343744 | tf_op jit(solution)/shard_map/feed_forward/pallas_call | solution.py:618
  237.7 11.4 %collective-permute-done.33.refs_2_ = bf16[256,2304]{1,0:T(8,128)(2,1)S(1)} collective-permute-done((bf16[256,2304]{1,0:T(8,128)(2,1)}, bf16[256,2304]{1,0:T(8,128)(2,1)S(1)}, u32[]{:S(2)}, u32[]{:S(2)}) %collective-permute-start.33) | collective-permute-done | bytes 1179680 | tf_op jit(solution)/shard_map/ppermute | solution.py:24
  249.7 2.3 collective-permute-done.37.refs_1_.refs_3_
  254.8 35.5 %feed_forward.3 = (bf16[256,2432]{1,0:T(8,128)(2,1)}, bf16[256,2432]{1,0:T(8,128)(2,1)}, bf16[256,2432]{1,0:T(8,128)(2,1)}, bf16[256,2432]{1,0:T(8,128)(2,1)}, f32[48,1440]{1,0:T(8,128)}) custom-call(s32[10]{0:T(128)} %stack.111.offsets_ref, bf16[256,2304]{1,0:T(8,128)(2,1)} %copy-done.25, bf16[256,2304]{1,0:T(8,128)(2,1)} %copy-done.27, ...), custom_call_target="tpu_custom_call" | custom-call | flops 20384317440 | bytes 29343744 | tf_op jit(solution)/shard_map/feed_forward/pallas_call | solution.py:618
  290.5 3.0 collective-permute-done.39
  293.5 2.7 add_convert_fusion.1
  300.3 3.4 convert_add_fusion.2
  305.1 23.1 %collective-permute-done.40 = bf16[256,2432]{1,0:T(8,128)(2,1)S(1)} collective-permute-done((bf16[256,2432]{1,0:T(8,128)(2,1)}, bf16[256,2432]{1,0:T(8,128)(2,1)S(1)}, u32[]{:S(2)}, u32[]{:S(2)}) %collective-permute-start.40) | collective-permute-done | bytes 1245216 | tf_op jit(solution)/shard_map/ppermute | solution.py:24
  330.3 2.5 multiply_convert_fusion
  332.8 3.5 concatenate.198.refs_0_
  345.1 6.1 %open_attention.2 = (bf16[9,512,64]{2,1,0:T(8,128)(2,1)S(1)}, f32[16,576]{1,0:T(8,128)S(1)}, f32[48,2304]{1,0:T(8,128)S(1)}) custom-call(s32[1]{0:T(128)} %bitcast.place_ref, bf16[256,2432]{1,0:T(8,128)(2,1)S(1)} %copy-done.6, bf16[256,2432]{1,0:T(8,128)(2,1)} %collective-permute-done.46.refs_1_, bf16[256,2304]{1,0:T(8,128)(2,1)S(1)} %copy-done.8, ...), custom_call_target="tpu_custom_call" | custom-call | flops 1358954496 | bytes 8552448 | tf_op jit(solution)/shard_map/open_attention/pallas_call | solution.py:545
  352.3 14.2 %collective-permute-done.45.refs_0_ = bf16[256,2432]{1,0:T(8,128)(2,1)} collective-permute-done((bf16[256,2432]{1,0:T(8,128)(2,1)}, bf16[256,2432]{1,0:T(8,128)(2,1)}, u32[]{:S(2)}, u32[]{:S(2)}) %collective-permute-start.45) | collective-permute-done | bytes 1245216 | tf_op jit(solution)/shard_map/ppermute | solution.py:24
  369.1 2.0 collective-permute-start.49
  375.4 6.7 %open_attention.3 = (bf16[9,512,64]{2,1,0:T(8,128)(2,1)S(1)}, f32[16,576]{1,0:T(8,128)S(1)}, f32[48,2304]{1,0:T(8,128)S(1)}) custom-call(s32[1]{0:T(128)} %bitcast.place_ref, bf16[256,2432]{1,0:T(8,128)(2,1)} %collective-permute-done.45.refs_0_, bf16[256,2432]{1,0:T(8,128)(2,1)} %collective-permute-done.47.refs_1_, bf16[256,2304]{1,0:T(8,128)(2,1)S(1)} %copy-done.26, ...), custom_call_target="tpu_custom_call" | custom-call | flops 1358954496 | bytes 8552448 | tf_op jit(solution)/shard_map/open_attention/pallas_call | solution.py:545
  383.8 12.7 %attend_back.3 = (bf16[3,1024,64]{2,1,0:T(8,128)(2,1)S(1)}, bf16[3,1024,64]{2,1,0:T(8,128)(2,1)S(1)}, bf16[3,1024,64]{2,1,0:T(8,128)(2,1)S(1)}, f32[48,1024]{1,0:T(8,128)S(1)}, f32[3,48,64]{2,1,0:T(8,128)S(1)}) custom-call(s32[2]{0:T(128)S(1)} %bitcast.177, s32[1]{0:T(128)} %bitcast.place_ref, bf16[9,1024,64]{2,1,0:T(8,128)(2,1)S(1)} %copy-done.37, ...), custom_call_target="tpu_custom_call" | custom-call | flops 8053063680 | bytes 6291456 | tf_op jit(solution)/shard_map/attend_back/pallas_call | solution.py:450
  403.0 12.9 %attend_back.4 = (bf16[3,1024,64]{2,1,0:T(8,128)(2,1)S(1)}, bf16[3,1024,64]{2,1,0:T(8,128)(2,1)S(1)}, bf16[3,1024,64]{2,1,0:T(8,128)(2,1)S(1)}, f32[48,1024]{1,0:T(8,128)S(1)}, f32[3,48,64]{2,1,0:T(8,128)S(1)}) custom-call(s32[2]{0:T(128)S(1)} %bitcast.178, s32[1]{0:T(128)} %bitcast.place_ref, bf16[9,1024,64]{2,1,0:T(8,128)(2,1)S(1)} %copy-done.37, ...), custom_call_target="tpu_custom_call" | custom-call | flops 8053063680 | bytes 6291456 | tf_op jit(solution)/shard_map/attend_back/pallas_call | solution.py:450
  416.0 5.4 collective-permute-done.50
  429.8 12.7 %attend_back.5 = (bf16[3,1024,64]{2,1,0:T(8,128)(2,1)S(1)}, bf16[3,1024,64]{2,1,0:T(8,128)(2,1)S(1)}, bf16[3,1024,64]{2,1,0:T(8,128)(2,1)S(1)}, f32[48,1024]{1,0:T(8,128)S(1)}, f32[3,48,64]{2,1,0:T(8,128)S(1)}) custom-call(s32[2]{0:T(128)S(1)} %bitcast.179, s32[1]{0:T(128)} %bitcast.place_ref, bf16[9,1024,64]{2,1,0:T(8,128)(2,1)S(1)} %copy-done.37, ...), custom_call_target="tpu_custom_call" | custom-call | flops 8053063680 | bytes 6291456 | tf_op jit(solution)/shard_map/attend_back/pallas_call | solution.py:450
  448.9 12.4 %project_back.2 = (bf16[256,2304]{1,0:T(8,128)(2,1)}, bf16[256,2304]{1,0:T(8,128)(2,1)}) custom-call(s32[1]{0:T(128)} %bitcast.place_ref, s32[10]{0:T(128)} %stack.111.offsets_ref, bf16[3,1024,64]{2,1,0:T(8,128)(2,1)} %copy-done.11, bf16[3,1024,64]{2,1,0:T(8,128)(2,1)} %copy-done.14, bf16[3,1024,64]{2,1,0:T(8,128)(2,1)} %copy-done.17, ...), custom_call_target="tpu_custom_call" | custom-call | flops 4076863488 | bytes 12091392 | tf_op jit(solution)/shard_map/project_back/pallas_call | solution.py:655
  461.4 3.0 add_convert_fusion.3
  467.6 4.2 concatenate.221
  472.8 2.3 thin_product.1
  480.2 12.4 %project_back.3 = (bf16[256,2304]{1,0:T(8,128)(2,1)}, bf16[256,2304]{1,0:T(8,128)(2,1)}) custom-call(s32[1]{0:T(128)} %bitcast.place_ref, s32[10]{0:T(128)} %stack.111.offsets_ref, bf16[3,1024,64]{2,1,0:T(8,128)(2,1)} %copy-done.11, bf16[3,1024,64]{2,1,0:T(8,128)(2,1)} %copy-done.14, bf16[3,1024,64]{2,1,0:T(8,128)(2,1)} %copy-done.17, ...), custom_call_target="tpu_custom_call" | custom-call | flops 4076863488 | bytes 12091392 | tf_op jit(solution)/shard_map/project_back/pallas_call | solution.py:655
  497.8 8.6 %collective-permute-done.64 = bf16[2,96,576]{2,1,0:T(8,128)(2,1)S(1)} collective-permute-done((bf16[2,96,576]{2,1,0:T(8,128)(2,1)S(1)}, bf16[2,96,576]{2,1,0:T(8,128)(2,1)S(1)}, u32[]{:S(2)}, u32[]{:S(2)}) %collective-permute-start.64) | collective-permute-done | bytes 221216 | tf_op jit(solution)/shard_map/ppermute | solution.py:24
  507.3 5.1 collective-permute-done.72
  512.4 2.3 collective-permute-done.73
  514.9 4.2 collective-permute-done.65
  526.9 2.5 fusion.9
  530.4 4.0 collective-permute-done.68
  (477 shorter events, 156.0 us)
Async XLA Ops:
  4.2 19.1 %collective-permute-start.1 = (bf16[6,16,2304]{2,1,0:T(8,128)(2,1)}, bf16[6,16,2304]{2,1,0:T(8,128)(2,1)}, u32[]{:S(2)}, u32[]{:S(2)}) collective-permute-start(bf16[6,16,2304]{2,1,0:T(8,128)(2,1)} %fusion.19), channel_id=1, source_target_pairs={{0,1},{1,0},{2,3},{3,2},{4,5},{5,4},{6,7},{7,6},{8,9},{9,8},{10,11... | collective-permute-start | bytes 1327112 | tf_op jit(solution)/shard_map/ppermute | solution.py:24
  8.9 15.7 %collective-permute-start = (bf16[144,1728]{1,0:T(8,128)(2,1)}, bf16[144,1728]{1,0:T(8,128)(2,1)S(1)}, u32[]{:S(2)}, u32[]{:S(2)}) collective-permute-start(bf16[144,1728]{1,0:T(8,128)(2,1)} %get-tuple-element.228), channel_id=1, source_target_pairs={{0,2},{1,3},{2,0},{3,1},{4,6},{5,7},{6,4},{7,5},{8,10},{9,11},{10,... | collective-permute-start | bytes 1493000 | tf_op jit(solution)/shard_map/ppermute | solution.py:24
  25.3 14.1 %collective-permute-start.2 = (bf16[144,1728]{1,0:T(8,128)(2,1)}, bf16[144,1728]{1,0:T(8,128)(2,1)}, u32[]{:S(2)}, u32[]{:S(2)}) collective-permute-start(bf16[144,1728]{1,0:T(8,128)(2,1)} %get-tuple-element.230), channel_id=1, source_target_pairs={{0,3},{1,2},{2,1},{3,0},{4,7},{5,6},{6,5},{7,4},{8,11},{9,10},{10,... | collective-permute-start | bytes 1493000 | tf_op jit(solution)/shard_map/ppermute | solution.py:24
  25.6 16.6 %collective-permute-start.7 = (bf16[144,1728]{1,0:T(8,128)(2,1)S(1)}, bf16[144,1728]{1,0:T(8,128)(2,1)}, u32[]{:S(2)}, u32[]{:S(2)}) collective-permute-start(bf16[144,1728]{1,0:T(8,128)(2,1)S(1)} %collective-permute-done.refs_6_.refs_11_), channel_id=1, source_target_pairs={{0,4},{4,0},{8,12},{12,8},{16,20},{20,16},{24,28},{28,24},{1,5},{5... | collective-permute-start | bytes 1493000 | tf_op jit(solution)/shard_map/ppermute | solution.py:24
  27.4 16.5 %collective-permute-start.6 = (bf16[144,1728]{1,0:T(8,128)(2,1)S(1)}, bf16[144,1728]{1,0:T(8,128)(2,1)}, u32[]{:S(2)}, u32[]{:S(2)}) collective-permute-start(bf16[144,1728]{1,0:T(8,128)(2,1)S(1)} %collective-permute-done.refs_6_.refs_11_), channel_id=1, source_target_pairs={{0,8},{4,12},{8,0},{12,4},{16,24},{20,28},{24,16},{28,20},{1,9},{5... | collective-permute-start | bytes 1493000 | tf_op jit(solution)/shard_map/ppermute | solution.py:24
  29.0 58.9 %collective-permute-start.8 = (bf16[256,2304]{1,0:T(8,128)(2,1)S(1)}, bf16[256,2304]{1,0:T(8,128)(2,1)S(1)}, u32[]{:S(2)}, u32[]{:S(2)}) collective-permute-start(bf16[256,2304]{1,0:T(8,128)(2,1)S(1)} %fusion.6.refs_0_), channel_id=1, source_target_pairs={{0,1},{1,0},{2,3},{3,2},{4,5},{5,4},{6,7},{7,6},{8,9},{9,8},{10,11... | collective-permute-start | bytes 3538952 | tf_op jit(solution)/shard_map/ppermute | solution.py:24
  42.2 14.4 %collective-permute-start.4 = (bf16[144,1728]{1,0:T(8,128)(2,1)}, bf16[144,1728]{1,0:T(8,128)(2,1)S(1)}, u32[]{:S(2)}, u32[]{:S(2)}) collective-permute-start(bf16[144,1728]{1,0:T(8,128)(2,1)} %collective-permute-done.2.refs_10_.refs_15_), channel_id=1, source_target_pairs={{0,8},{4,12},{8,0},{12,4},{16,24},{20,28},{24,16},{28,20},{1,9},{5... | collective-permute-start | bytes 1493000 | tf_op jit(solution)/shard_map/ppermute | solution.py:24
  43.9 14.2 %collective-permute-start.3 = (bf16[144,1728]{1,0:T(8,128)(2,1)}, bf16[144,1728]{1,0:T(8,128)(2,1)S(1)}, u32[]{:S(2)}, u32[]{:S(2)}) collective-permute-start(bf16[144,1728]{1,0:T(8,128)(2,1)} %collective-permute-done.2.refs_10_.refs_15_), channel_id=1, source_target_pairs={{0,4},{4,0},{8,12},{12,8},{16,20},{20,16},{24,28},{28,24},{1,5},{5... | collective-permute-start | bytes 1493000 | tf_op jit(solution)/shard_map/ppermute | solution.py:24
  47.1 19.1 %collective-permute-start.14 = (bf16[3,16,5760]{2,1,0:T(8,128)(2,1)S(1)}, bf16[3,16,5760]{2,1,0:T(8,128)(2,1)S(1)}, u32[]{:S(2)}, u32[]{:S(2)}) collective-permute-start(bf16[3,16,5760]{2,1,0:T(8,128)(2,1)S(1)} %fusion.15), channel_id=1, source_target_pairs={{0,1},{1,0},{2,3},{3,2},{4,5},{5,4},{6,7},{7,6},{8,9},{9,8},{10,11... | collective-permute-start | bytes 1658888 | tf_op jit(solution)/shard_map/ppermute | solution.py:24
  49.4 38.5 %collective-permute-start.16 = (bf16[576,1728]{1,0:T(8,128)(2,1)}, bf16[576,1728]{1,0:T(8,128)(2,1)}, u32[]{:S(2)}, u32[]{:S(2)}) collective-permute-start(bf16[576,1728]{1,0:T(8,128)(2,1)} %get-tuple-element.251), channel_id=1, source_target_pairs={{0,1},{1,0},{2,3},{3,2},{4,5},{5,4},{6,7},{7,6},{8,9},{9,8},{10,11... | collective-permute-start | bytes 5971976 | tf_op jit(solution)/shard_map/ppermute | solution.py:24
  58.1 27.2 %collective-permute-start.9 = (bf16[256,2304]{1,0:T(8,128)(2,1)S(1)}, bf16[256,2304]{1,0:T(8,128)(2,1)S(1)}, u32[]{:S(2)}, u32[]{:S(2)}) collective-permute-start(bf16[256,2304]{1,0:T(8,128)(2,1)S(1)} %fusion.6.refs_0_), channel_id=1, source_target_pairs={{0,2},{1,3},{2,0},{3,1},{4,6},{5,7},{6,4},{7,5},{8,10},{9,11},{10,... | collective-permute-start | bytes 3538952 | tf_op jit(solution)/shard_map/ppermute | solution.py:24
  85.4 24.5 %collective-permute-start.17 = (bf16[2,144,1440]{2,1,0:T(8,128)(2,1)}, bf16[2,144,1440]{2,1,0:T(8,128)(2,1)}, u32[]{:S(2)}, u32[]{:S(2)}) collective-permute-start(bf16[2,144,1440]{2,1,0:T(8,128)(2,1)} %get-tuple-element.261), channel_id=1, source_target_pairs={{0,2},{1,3},{2,0},{3,1},{4,6},{5,7},{6,4},{7,5},{8,10},{9,11},{10,... | collective-permute-start | bytes 2488328 | tf_op jit(solution)/shard_map/ppermute | solution.py:24
  87.5 45.4 %collective-permute-start.18 = (bf16[2,144,1440]{2,1,0:T(8,128)(2,1)}, bf16[2,144,1440]{2,1,0:T(8,128)(2,1)S(1)}, u32[]{:S(2)}, u32[]{:S(2)}) collective-permute-start(bf16[2,144,1440]{2,1,0:T(8,128)(2,1)} %get-tuple-element.268), channel_id=1, source_target_pairs={{0,3},{1,2},{2,1},{3,0},{4,7},{5,6},{6,5},{7,4},{8,11},{9,10},{10,... | collective-permute-start | bytes 2488328 | tf_op jit(solution)/shard_map/ppermute | solution.py:24
  109.9 23.0 %collective-permute-start.20 = (bf16[2,144,1440]{2,1,0:T(8,128)(2,1)}, bf16[2,144,1440]{2,1,0:T(8,128)(2,1)S(1)}, u32[]{:S(2)}, u32[]{:S(2)}) collective-permute-start(bf16[2,144,1440]{2,1,0:T(8,128)(2,1)} %collective-permute-done.17.refs_6_), channel_id=1, source_target_pairs={{0,4},{4,0},{8,12},{12,8},{16,20},{20,16},{24,28},{28,24},{1,5},{5... | collective-permute-start | bytes 2488328 | tf_op jit(solution)/shard_map/ppermute | solution.py:24
  111.2 21.8 %collective-permute-start.19 = (bf16[2,144,1440]{2,1,0:T(8,128)(2,1)}, bf16[2,144,1440]{2,1,0:T(8,128)(2,1)S(1)}, u32[]{:S(2)}, u32[]{:S(2)}) collective-permute-start(bf16[2,144,1440]{2,1,0:T(8,128)(2,1)} %collective-permute-done.17.refs_6_), channel_id=1, source_target_pairs={{0,8},{4,12},{8,0},{12,4},{16,24},{20,28},{24,16},{28,20},{1,9},{5... | collective-permute-start | bytes 2488328 | tf_op jit(solution)/shard_map/ppermute | solution.py:24
  112.0 20.9 %collective-permute-start.21 = (bf16[5,8,2304]{2,1,0:T(8,128)(2,1)S(1)}, bf16[5,8,2304]{2,1,0:T(8,128)(2,1)S(1)}, u32[]{:S(2)}, u32[]{:S(2)}) collective-permute-start(bf16[5,8,2304]{2,1,0:T(8,128)(2,1)S(1)} %copy-done.96), channel_id=1, source_target_pairs={{0,2},{1,3},{2,0},{3,1},{4,6},{5,7},{6,4},{7,5},{8,10},{9,11},{10,... | collective-permute-start | bytes 552968 | tf_op jit(solution)/shard_map/ppermute | solution.py:24
  141.5 21.8 %collective-permute-start.26 = (bf16[2,144,1440]{2,1,0:T(8,128)(2,1)}, bf16[2,144,1440]{2,1,0:T(8,128)(2,1)S(1)}, u32[]{:S(2)}, u32[]{:S(2)}) collective-permute-start(bf16[2,144,1440]{2,1,0:T(8,128)(2,1)} %copy-done.105), channel_id=1, source_target_pairs={{0,8},{4,12},{8,0},{12,4},{16,24},{20,28},{24,16},{28,20},{1,9},{5... | collective-permute-start | bytes 2488328 | tf_op jit(solution)/shard_map/ppermute | solution.py:24
  142.5 22.8 %collective-permute-start.25 = (bf16[2,144,1440]{2,1,0:T(8,128)(2,1)}, bf16[2,144,1440]{2,1,0:T(8,128)(2,1)S(1)}, u32[]{:S(2)}, u32[]{:S(2)}) collective-permute-start(bf16[2,144,1440]{2,1,0:T(8,128)(2,1)} %copy-done.105), channel_id=1, source_target_pairs={{0,4},{4,0},{8,12},{12,8},{16,20},{20,16},{24,28},{28,24},{1,5},{5... | collective-permute-start | bytes 2488328 | tf_op jit(solution)/shard_map/ppermute | solution.py:24
  143.9 39.1 %collective-permute-start.30 = (bf16[2,144,1440]{2,1,0:T(8,128)(2,1)}, bf16[2,144,1440]{2,1,0:T(8,128)(2,1)S(1)}, u32[]{:S(2)}, u32[]{:S(2)}) collective-permute-start(bf16[2,144,1440]{2,1,0:T(8,128)(2,1)} %copy-done.107), channel_id=1, source_target_pairs={{0,4},{4,0},{8,12},{12,8},{16,20},{20,16},{24,28},{28,24},{1,5},{5... | collective-permute-start | bytes 2488328 | tf_op jit(solution)/shard_map/ppermute | solution.py:24
  149.7 16.6 %collective-permute-start.29 = (bf16[3,8,5760]{2,1,0:T(8,128)(2,1)S(1)}, bf16[3,8,5760]{2,1,0:T(8,128)(2,1)S(1)}, u32[]{:S(2)}, u32[]{:S(2)}) collective-permute-start(bf16[3,8,5760]{2,1,0:T(8,128)(2,1)S(1)} %collective-permute-done.24), channel_id=1, source_target_pairs={{0,1},{1,0},{2,3},{3,2},{4,5},{5,4},{6,7},{7,6},{8,9},{9,8},{10,11... | collective-permute-start | bytes 829448 | tf_op jit(solution)/shard_map/ppermute | solution.py:24
  149.7 49.3 %collective-permute-start.35 = (bf16[256,2304]{1,0:T(8,128)(2,1)}, bf16[256,2304]{1,0:T(8,128)(2,1)S(1)}, u32[]{:S(2)}, u32[]{:S(2)}) collective-permute-start(bf16[256,2304]{1,0:T(8,128)(2,1)} %multiply_convert_fusion.2.refs_2_), channel_id=1, source_target_pairs={{0,1},{1,0},{2,3},{3,2},{4,5},{5,4},{6,7},{7,6},{8,9},{9,8},{10,11... | collective-permute-start | bytes 3538952 | tf_op jit(solution)/shard_map/ppermute | solution.py:24
  163.3 28.5 %collective-permute-start.28 = (bf16[256,2432]{1,0:T(8,128)(2,1)S(1)}, bf16[256,2432]{1,0:T(8,128)(2,1)S(1)}, u32[]{:S(2)}, u32[]{:S(2)}) collective-permute-start(bf16[256,2432]{1,0:T(8,128)(2,1)S(1)} %add_convert_fusion.2), channel_id=1, source_target_pairs={{0,2},{1,3},{2,0},{3,1},{4,6},{5,7},{6,4},{7,5},{8,10},{9,11},{10,... | collective-permute-start | bytes 3735560 | tf_op jit(solution)/shard_map/ppermute | solution.py:24
  165.2 20.0 %collective-permute-start.31 = (bf16[2,144,1440]{2,1,0:T(8,128)(2,1)S(1)}, bf16[2,144,1440]{2,1,0:T(8,128)(2,1)S(1)}, u32[]{:S(2)}, u32[]{:S(2)}) collective-permute-start(bf16[2,144,1440]{2,1,0:T(8,128)(2,1)S(1)} %collective-permute-done.25.refs_11_), channel_id=1, source_target_pairs={{0,8},{4,12},{8,0},{12,4},{16,24},{20,28},{24,16},{28,20},{1,9},{5... | collective-permute-start | bytes 2488328 | tf_op jit(solution)/shard_map/ppermute | solution.py:24
  166.2 25.6 %collective-permute-start.27 = (bf16[256,2432]{1,0:T(8,128)(2,1)S(1)}, bf16[256,2432]{1,0:T(8,128)(2,1)S(1)}, u32[]{:S(2)}, u32[]{:S(2)}) collective-permute-start(bf16[256,2432]{1,0:T(8,128)(2,1)S(1)} %get-tuple-element.283), channel_id=1, source_target_pairs={{0,1},{1,0},{2,3},{3,2},{4,5},{5,4},{6,7},{7,6},{8,9},{9,8},{10,11... | collective-permute-start | bytes 3735560 | tf_op jit(solution)/shard_map/ppermute | solution.py:24
  183.0 16.0 %collective-permute-start.36 = (bf16[2,576,1440]{2,1,0:T(8,128)(2,1)S(1)}, bf16[2,576,1440]{2,1,0:T(8,128)(2,1)S(1)}, u32[]{:S(2)}, u32[]{:S(2)}) collective-permute-start(bf16[2,576,1440]{2,1,0:T(8,128)(2,1)S(1)} %get-tuple-element.293), channel_id=1, source_target_pairs={{0,1},{1,0},{2,3},{3,2},{4,5},{5,4},{6,7},{7,6},{8,9},{9,8},{10,11... | collective-permute-start | bytes 9953288 | tf_op jit(solution)/shard_map/ppermute | solution.py:24
  195.6 42.1 %collective-permute-start.32 = (bf16[256,2304]{1,0:T(8,128)(2,1)S(1)}, bf16[256,2304]{1,0:T(8,128)(2,1)S(1)}, u32[]{:S(2)}, u32[]{:S(2)}) collective-permute-start(bf16[256,2304]{1,0:T(8,128)(2,1)S(1)} %multiply_convert_fusion.1.refs_0_.refs_2_), channel_id=1, source_target_pairs={{0,2},{1,3},{2,0},{3,1},{4,6},{5,7},{6,4},{7,5},{8,10},{9,11},{10,... | collective-permute-start | bytes 3538952 | tf_op jit(solution)/shard_map/ppermute | solution.py:24
  197.7 51.5 %collective-permute-start.33 = (bf16[256,2304]{1,0:T(8,128)(2,1)}, bf16[256,2304]{1,0:T(8,128)(2,1)S(1)}, u32[]{:S(2)}, u32[]{:S(2)}) collective-permute-start(bf16[256,2304]{1,0:T(8,128)(2,1)} %multiply_convert_fusion.2.refs_2_), channel_id=1, source_target_pairs={{0,2},{1,3},{2,0},{3,1},{4,6},{5,7},{6,4},{7,5},{8,10},{9,11},{10,... | collective-permute-start | bytes 3538952 | tf_op jit(solution)/shard_map/ppermute | solution.py:24
  298.8 29.4 %collective-permute-start.40 = (bf16[256,2432]{1,0:T(8,128)(2,1)}, bf16[256,2432]{1,0:T(8,128)(2,1)S(1)}, u32[]{:S(2)}, u32[]{:S(2)}) collective-permute-start(bf16[256,2432]{1,0:T(8,128)(2,1)} %add_convert_fusion.1), channel_id=1, source_target_pairs={{0,2},{1,3},{2,0},{3,1},{4,6},{5,7},{6,4},{7,5},{8,10},{9,11},{10,... | collective-permute-start | bytes 3735560 | tf_op jit(solution)/shard_map/ppermute | solution.py:24
  300.3 27.9 %collective-permute-start.43 = (bf16[256,2432]{1,0:T(8,128)(2,1)}, bf16[256,2432]{1,0:T(8,128)(2,1)S(1)}, u32[]{:S(2)}, u32[]{:S(2)}) collective-permute-start(bf16[256,2432]{1,0:T(8,128)(2,1)} %get-tuple-element.324), channel_id=1, source_target_pairs={{0,1},{1,0},{2,3},{3,2},{4,5},{5,4},{6,7},{7,6},{8,9},{9,8},{10,11... | collective-permute-start | bytes 3735560 | tf_op jit(solution)/shard_map/ppermute | solution.py:24
  336.3 30.1 %collective-permute-start.45 = (bf16[256,2432]{1,0:T(8,128)(2,1)}, bf16[256,2432]{1,0:T(8,128)(2,1)}, u32[]{:S(2)}, u32[]{:S(2)}) collective-permute-start(bf16[256,2432]{1,0:T(8,128)(2,1)} %concatenate.198.refs_0_), channel_id=1, source_target_pairs={{0,2},{1,3},{2,0},{3,1},{4,6},{5,7},{6,4},{7,5},{8,10},{9,11},{10,... | collective-permute-start | bytes 3735560 | tf_op jit(solution)/shard_map/ppermute | solution.py:24
  366.4 32.8 %collective-permute-start.48 = (bf16[256,2432]{1,0:T(8,128)(2,1)}, bf16[256,2432]{1,0:T(8,128)(2,1)}, u32[]{:S(2)}, u32[]{:S(2)}) collective-permute-start(bf16[256,2432]{1,0:T(8,128)(2,1)} %add_convert_fusion), channel_id=1, source_target_pairs={{0,2},{1,3},{2,0},{3,1},{4,6},{5,7},{6,4},{7,5},{8,10},{9,11},{10,... | collective-permute-start | bytes 3735560 | tf_op jit(solution)/shard_map/ppermute | solution.py:24
  369.1 30.1 %collective-permute-start.49 = (bf16[2,64,1440]{2,1,0:T(8,128)(2,1)}, bf16[2,64,1440]{2,1,0:T(8,128)(2,1)S(1)}, u32[]{:S(2)}, u32[]{:S(2)}) collective-permute-start(bf16[2,64,1440]{2,1,0:T(8,128)(2,1)} %maximum_select_fusion.6), channel_id=1, source_target_pairs={{0,16},{4,20},{8,24},{12,28},{16,0},{20,4},{24,8},{28,12},{1,17},{... | collective-permute-start | bytes 1105928 | tf_op jit(solution)/shard_map/ppermute | solution.py:24
  400.1 15.9 %collective-permute-start.51 = (bf16[256,16]{1,0:T(8,128)(2,1)S(1)}, bf16[256,16]{1,0:T(8,128)(2,1)S(1)}, u32[]{:S(2)}, u32[]{:S(2)}) collective-permute-start(bf16[256,16]{1,0:T(8,128)(2,1)S(1)} %fusion.34), channel_id=1, source_target_pairs={{0,2},{1,3},{2,0},{3,1},{4,6},{5,7},{6,4},{7,5},{8,10},{9,11},{10,... | collective-permute-start | bytes 24584 | tf_op jit(solution)/shard_map/ppermute | solution.py:24
  401.2 14.8 %collective-permute-start.52 = (bf16[256,16]{1,0:T(8,128)(2,1)S(1)}, bf16[256,16]{1,0:T(8,128)(2,1)S(1)}, u32[]{:S(2)}, u32[]{:S(2)}) collective-permute-start(bf16[256,16]{1,0:T(8,128)(2,1)S(1)} %fusion.34), channel_id=1, source_target_pairs={{0,1},{1,0},{2,3},{3,2},{4,5},{5,4},{6,7},{7,6},{8,9},{9,8},{10,11... | collective-permute-start | bytes 24584 | tf_op jit(solution)/shard_map/ppermute | solution.py:24
  401.4 20.0 %collective-permute-start.50 = (bf16[4,64,1440]{2,1,0:T(8,128)(2,1)S(1)}, bf16[4,64,1440]{2,1,0:T(8,128)(2,1)S(1)}, u32[]{:S(2)}, u32[]{:S(2)}) collective-permute-start(bf16[4,64,1440]{2,1,0:T(8,128)(2,1)S(1)} %maximum_select_fusion.3), channel_id=1, source_target_pairs={{0,4},{4,0},{8,12},{12,8},{16,20},{20,16},{24,28},{28,24},{1,5},{5... | collective-permute-start | bytes 2211848 | tf_op jit(solution)/shard_map/ppermute | solution.py:24
  424.4 20.8 %collective-permute-start.57 = (bf16[2,48,1440]{2,1,0:T(8,128)(2,1)S(1)}, bf16[2,48,1440]{2,1,0:T(8,128)(2,1)S(1)}, u32[]{:S(2)}, u32[]{:S(2)}) collective-permute-start(bf16[2,48,1440]{2,1,0:T(8,128)(2,1)S(1)} %get-tuple-element.462), channel_id=1, source_target_pairs={{0,3},{1,2},{2,1},{3,0},{4,7},{5,6},{6,5},{7,4},{8,11},{9,10},{10,... | collective-permute-start | bytes 829448 | tf_op jit(solution)/shard_map/ppermute | solution.py:24
  425.5 19.7 %collective-permute-start.55 = (bf16[2,48,1440]{2,1,0:T(8,128)(2,1)S(1)}, bf16[2,48,1440]{2,1,0:T(8,128)(2,1)S(1)}, u32[]{:S(2)}, u32[]{:S(2)}) collective-permute-start(bf16[2,48,1440]{2,1,0:T(8,128)(2,1)S(1)} %get-tuple-element.463), channel_id=1, source_target_pairs={{0,1},{1,0},{2,3},{3,2},{4,5},{5,4},{6,7},{7,6},{8,9},{9,8},{10,11... | collective-permute-start | bytes 829448 | tf_op jit(solution)/shard_map/ppermute | solution.py:24
  425.6 19.7 %collective-permute-start.56 = (bf16[2,48,1440]{2,1,0:T(8,128)(2,1)S(1)}, bf16[2,48,1440]{2,1,0:T(8,128)(2,1)S(1)}, u32[]{:S(2)}, u32[]{:S(2)}) collective-permute-start(bf16[2,48,1440]{2,1,0:T(8,128)(2,1)S(1)} %get-tuple-element.464), channel_id=1, source_target_pairs={{0,2},{1,3},{2,0},{3,1},{4,6},{5,7},{6,4},{7,5},{8,10},{9,11},{10,... | collective-permute-start | bytes 829448 | tf_op jit(solution)/shard_map/ppermute | solution.py:24
  428.6 16.6 %collective-permute-start.54 = (bf16[1,80,576]{2,1,0:T(8,128)(2,1)S(1)}, bf16[1,80,576]{2,1,0:T(8,128)(2,1)S(1)}, u32[]{:S(2)}, u32[]{:S(2)}) collective-permute-start(bf16[1,80,576]{2,1,0:T(8,128)(2,1)S(1)} %pad_maximum_fusion.8), channel_id=1, source_target_pairs={{0,8},{4,12},{8,0},{12,4},{16,24},{20,28},{24,16},{28,20},{1,9},{5... | collective-permute-start | bytes 276488 | tf_op jit(solution)/shard_map/ppermute | solution.py:24
  446.2 15.1 %collective-permute-start.60 = (bf16[2,80,576]{2,1,0:T(8,128)(2,1)S(1)}, bf16[2,80,576]{2,1,0:T(8,128)(2,1)S(1)}, u32[]{:S(2)}, u32[]{:S(2)}) collective-permute-start(bf16[2,80,576]{2,1,0:T(8,128)(2,1)S(1)} %maximum_select_fusion.8), channel_id=1, source_target_pairs={{0,16},{4,20},{8,24},{12,28},{16,0},{20,4},{24,8},{28,12},{1,17},{... | collective-permute-start | bytes 552968 | tf_op jit(solution)/shard_map/ppermute | solution.py:24
  447.4 13.9 %collective-permute-start.59 = (bf16[48,1024]{1,0:T(8,128)(2,1)S(1)}, bf16[48,1024]{1,0:T(8,128)(2,1)S(1)}, u32[]{:S(2)}, u32[]{:S(2)}) collective-permute-start(bf16[48,1024]{1,0:T(8,128)(2,1)S(1)} %add_convert_fusion.7), channel_id=1, source_target_pairs={{0,2},{1,3},{2,0},{3,1},{4,6},{5,7},{6,4},{7,5},{8,10},{9,11},{10,... | collective-permute-start | bytes 294920 | tf_op jit(solution)/shard_map/ppermute | solution.py:24
  461.3 13.9 %collective-permute-start.61 = (bf16[256,2304]{1,0:T(8,128)(2,1)}, bf16[256,2304]{1,0:T(8,128)(2,1)}, u32[]{:S(2)}, u32[]{:S(2)}) collective-permute-start(bf16[256,2304]{1,0:T(8,128)(2,1)} %get-tuple-element.406), channel_id=1, source_target_pairs={{0,1},{1,0},{2,3},{3,2},{4,5},{5,4},{6,7},{7,6},{8,9},{9,8},{10,11... | collective-permute-start | bytes 3538952 | tf_op jit(solution)/shard_map/ppermute | solution.py:24
  475.2 17.3 %collective-permute-start.62 = (bf16[1,96,576]{2,1,0:T(8,128)(2,1)S(1)}, bf16[1,96,576]{2,1,0:T(8,128)(2,1)S(1)}, u32[]{:S(2)}, u32[]{:S(2)}) collective-permute-start(bf16[1,96,576]{2,1,0:T(8,128)(2,1)S(1)} %pad_maximum_fusion.7), channel_id=1, source_target_pairs={{0,8},{4,12},{8,0},{12,4},{16,24},{20,28},{24,16},{28,20},{1,9},{5... | collective-permute-start | bytes 331784 | tf_op jit(solution)/shard_map/ppermute | solution.py:24
  475.9 16.6 %collective-permute-start.63 = (bf16[4,80,576]{2,1,0:T(8,128)(2,1)S(1)}, bf16[4,80,576]{2,1,0:T(8,128)(2,1)S(1)}, u32[]{:S(2)}, u32[]{:S(2)}) collective-permute-start(bf16[4,80,576]{2,1,0:T(8,128)(2,1)S(1)} %maximum_select_fusion.5), channel_id=1, source_target_pairs={{0,4},{4,0},{8,12},{12,8},{16,20},{20,16},{24,28},{28,24},{1,5},{5... | collective-permute-start | bytes 1105928 | tf_op jit(solution)/shard_map/ppermute | solution.py:24
  479.1 39.9 %collective-permute-start.66 = (bf16[256,2304]{1,0:T(8,128)(2,1)S(1)}, bf16[256,2304]{1,0:T(8,128)(2,1)S(1)}, u32[]{:S(2)}, u32[]{:S(2)}) collective-permute-start(bf16[256,2304]{1,0:T(8,128)(2,1)S(1)} %add_convert_fusion.4), channel_id=1, source_target_pairs={{0,2},{1,3},{2,0},{3,1},{4,6},{5,7},{6,4},{7,5},{8,10},{9,11},{10,... | collective-permute-start | bytes 3538952 | tf_op jit(solution)/shard_map/ppermute | solution.py:24
  495.9 16.5 %collective-permute-start.72 = (bf16[2,80,576]{2,1,0:T(8,128)(2,1)S(1)}, bf16[2,80,576]{2,1,0:T(8,128)(2,1)S(1)}, u32[]{:S(2)}, u32[]{:S(2)}) collective-permute-start(bf16[2,80,576]{2,1,0:T(8,128)(2,1)S(1)} %get-tuple-element.472), channel_id=1, source_target_pairs={{0,2},{1,3},{2,0},{3,1},{4,6},{5,7},{6,4},{7,5},{8,10},{9,11},{10,... | collective-permute-start | bytes 552968 | tf_op jit(solution)/shard_map/ppermute | solution.py:24
  497.1 17.6 %collective-permute-start.73 = (bf16[2,80,576]{2,1,0:T(8,128)(2,1)S(1)}, bf16[2,80,576]{2,1,0:T(8,128)(2,1)S(1)}, u32[]{:S(2)}, u32[]{:S(2)}) collective-permute-start(bf16[2,80,576]{2,1,0:T(8,128)(2,1)S(1)} %get-tuple-element.473), channel_id=1, source_target_pairs={{0,3},{1,2},{2,1},{3,0},{4,7},{5,6},{6,5},{7,4},{8,11},{9,10},{10,... | collective-permute-start | bytes 552968 | tf_op jit(solution)/shard_map/ppermute | solution.py:24
  507.2 18.0 %collective-permute-start.70 = (bf16[256,2304]{1,0:T(8,128)(2,1)S(1)}, bf16[256,2304]{1,0:T(8,128)(2,1)S(1)}, u32[]{:S(2)}, u32[]{:S(2)}) collective-permute-start(bf16[256,2304]{1,0:T(8,128)(2,1)S(1)} %copy-done.104), channel_id=1, source_target_pairs={{0,1},{1,0},{2,3},{3,2},{4,5},{5,4},{6,7},{7,6},{8,9},{9,8},{10,11... | collective-permute-start | bytes 3538952 | tf_op jit(solution)/shard_map/ppermute | solution.py:24
  (140 other events, 1125.1 us)

commit v5 on v4

--- a/solution.py
+++ b/solution.py
@@ -352,7 +352,7 @@
         4 * heads * length * length * HDIM * 4,
         16 * heads * length * HDIM,
         "attend",
-        limit=32,
+        limit=56,
         grid=(heads // each,),
     )(starts, query, key, value)
 
@@ -430,6 +430,7 @@
                     totals[head].T * scale, cos_ref[here, :], -sin_ref[here, :]
                 ).astype(BF16)
         thins = [None] * 3
+        sums = [[], [], []]
         for head in range(heads):
             dk_ref[head] = turn(key_sum[head] * scale, cos_ref[...], -sin_ref[...]).astype(BF16)
             dv_ref[head] = value_sum[head].astype(BF16)
@@ -437,9 +438,11 @@
                 here = slice(number * rank, (number + 1) * rank)
                 term = dot_t(b_ref[head, here, :], ref[head])
                 thins[number] = term if head == 0 else thins[number] + term
-                out_ref[head, here, :] = dot(narrow_ref[here, :], ref[head])
+                sums[number].append(dot(narrow_ref[here, :], ref[head]))
         for number in range(3):
-            thin_ref[number * rank : (number + 1) * rank, :] = thins[number]
+            here = slice(number * rank, (number + 1) * rank)
+            thin_ref[here, :] = thins[number]
+            out_ref[here, :] = jnp.concatenate(sums[number], axis=1)
 
     step = first // heads
     spec = pl.BlockSpec((heads, length, HDIM), lambda h: (step, 0, 0))
@@ -452,12 +455,12 @@
         [jax.ShapeDtypeStruct((heads, length, HDIM), BF16)] * 3
         + [
             jax.ShapeDtypeStruct((thin, length), F32),
-            jax.ShapeDtypeStruct((heads, thin, HDIM), F32),
+            jax.ShapeDtypeStruct((thin, heads * HDIM), F32),
         ],
         [smem(), smem(), spec, spec, spec, spec]
         + [pl.BlockSpec((heads, 1, length), lambda h: (step, 0, 0)), half, half, table, table, thin_spec]
         + [pl.BlockSpec((heads, thin, HDIM), lambda h: (step, 0, 0))],
-        [out] * 3 + [thin_spec, pl.BlockSpec((heads, thin, HDIM), lambda h: (0, 0, 0))],
+        [out] * 3 + [thin_spec, pl.BlockSpec((thin, heads * HDIM), lambda h: (0, 0))],
         [
             pltpu.VMEM((count, 2 * rows, rows), F32),
             pltpu.VMEM((heads, length, HDIM), F32),
@@ -760,6 +763,8 @@
     )
     first_b_four = hop(first_b_two, "rep", 2)
     mlp_leaving = [side(gate_up, rep_place % 4 * quarter, quarter, place ^ j, ff_cols) for j in (2, 3)]
+    mlp_near_out = side(gate_up, 0, k_rows, place ^ 1, ff_cols)
+    mlp_own = side(gate_up, 0, k_rows, place, ff_cols)
     grad_feed = (BRANCH * grad_out).astype(BF16)
     half = HDIM // 2
     frequency = jnp.exp(jnp.arange(half, dtype=F32) * (-2.0 / HDIM) * math.log(THETA))
@@ -775,8 +780,12 @@
     b_wide = jnp.concatenate(
         [jnp.pad(b_first[i], ((0, 0), (i * head_cols, (2 - i) * head_cols))) for i in range(3)]
     )
-    normed_far, first_a_four, first_b_four, mlp_leaving, grad_feed, b_wide, a_first, rest_part, wide_part, tables = fence(
-        normed_far, first_a_four, first_b_four, mlp_leaving, grad_feed, b_wide, a_first, rest_part, wide_part, tables
+    (
+        normed_far, first_a_four, first_b_four, mlp_leaving, mlp_near_out, mlp_own, grad_feed, b_wide, a_first,
+        rest_part, wide_part, tables,
+    ) = fence(
+        normed_far, first_a_four, first_b_four, mlp_leaving, mlp_near_out, mlp_own, grad_feed, b_wide, a_first,
+        rest_part, wide_part, tables,
     )
     cosine, sine, cosine_pair, sine_pair = tables
     first_blocks = (normed, normed_near, normed_far, core(normed_far))
@@ -807,23 +816,24 @@
     b_out, b_down = rest[3], rest[4]
     far_out = close_attention(mixed, place, attention_output_weight, a_out, (2, 3), rows)
     far_sum = (far_out[0].astype(F32) + core(far_out[1]).astype(F32)).astype(BF16)
-    far_sum, mixed_here, grad_feed, wide_far, gate_up = fence(far_sum, mixed, grad_feed, wide_far, gate_up)
-    branch_far = across(far_sum)
-    mlp_near_out = side(gate_up, 0, k_rows, place ^ 1, ff_cols)
-    mlp_own = side(gate_up, 0, k_rows, place, ff_cols)
+    far_sum, mixed_here, grad_feed, wide_far, mlp_near_out = fence(
+        far_sum, mixed, grad_feed, wide_far, mlp_near_out
+    )
+    branch_low, far_rest = across(far_sum[: rows // 2]), far_sum[rows // 2 :]
     feed_near_in = core(grad_feed)
     near_out = close_attention(mixed_here, place, attention_output_weight, a_out, (0, 1), rows)
-    near_out, mlp_b_two, mlp_b_three, mlp_near_out, mlp_own = fence(
-        near_out, mlp_b_two, mlp_b_three, mlp_near_out, mlp_own
+    near_out, mlp_b_two, mlp_b_three, branch_low, far_rest = fence(
+        near_out, mlp_b_two, mlp_b_three, branch_low, far_rest
     )
     mlp_a_four, mlp_b_four = hop(mlp_a_two, "rep", 1), hop(mlp_b_two, "rep", 2)
+    branch_high = across(far_rest)
     near_here = core(near_out[1])
     mlp_near = core(mlp_near_out)
     hidden_cols = own_columns(whole_picked(wide_chip, wide_far, place), ff_cols)
-    near_here, branch_far, hidden_cols, mlp_own, mlp_a_four, mlp_b_four = fence(
-        near_here, branch_far, hidden_cols, mlp_own, mlp_a_four, mlp_b_four
-    )
-    feed_far_in = across(after(grad_feed, branch_far))
+    near_here, branch_high, hidden_cols, mlp_own = fence(near_here, branch_high, hidden_cols, mlp_own)
+    branch_far = jnp.concatenate([branch_low, branch_high])
+    feed_low = across(after(grad_feed[: rows // 2], branch_high))
+    feed_rest = after(grad_feed[rows // 2 :], branch_high)
     a_hidden, b_hidden = hidden_cols[0], hidden_cols[1:]
     branch_own = near_out[0].astype(F32) + near_here.astype(F32) + branch_far.astype(F32)
     narrow_out = branch_own[:, width : width + rank].astype(BF16)
@@ -832,7 +842,10 @@
     normed_second = norm_rows(middle, gain_two).astype(BF16)
     second_far = across(normed_second)
     second_near = core(normed_second)
-    second_near, feed_near_in, mlp_near = fence(second_near, feed_near_in, mlp_near)
+    second_near, feed_near_in, mlp_near, mlp_a_four, mlp_b_four, feed_low = fence(
+        second_near, feed_near_in, mlp_near, mlp_a_four, mlp_b_four, feed_low
+    )
+    feed_high = across(feed_rest)
     mlp_offsets, mlp_pieces = arrange(
         k_rows, mlp_own, mlp_near,
         (
@@ -846,7 +859,8 @@
         down_projection_weight, a_mlp, b_down, a_hidden, b_hidden,
     )
     feed_near, back_near = parts[:2], parts[2:]
-    second_far, feed_far_in, back_near, feed_near = fence(second_far, feed_far_in, back_near, feed_near)
+    second_far, feed_high, back_near, feed_near = fence(second_far, feed_high, back_near, feed_near)
+    feed_far_in = jnp.concatenate([feed_low, feed_high])
     second_blocks = (normed_second, second_near, second_far, core(second_far))
     feed_blocks = (grad_feed, feed_near_in, feed_far_in, core(feed_far_in))
     *parts, sum_far = feed_forward(
@@ -858,7 +872,7 @@
     back_sum, back_near, feed_near, feed_far, sum_near = fence(
         back_sum, back_near, feed_near, feed_far, sum_near
     )
-    back_from_far = across(back_sum)
+    back_low, back_rest = across(back_sum[: rows // 2]), back_sum[rows // 2 :]
 
     bits = reps_bits()
     back_here = core(back_near[1])
@@ -867,11 +881,16 @@
     mark = jnp.full((rank, ff_cols), pick.astype(F32))
     wide_all = jnp.concatenate([sum_near + sum_far, mark]).astype(BF16)[None]
     wide_hop = hop(wide_all, "rep", bits[0])
+    back_low, feed_here, feed_mate, back_here, back_rest, sum_near = fence(
+        back_low, feed_here, feed_mate, back_here, back_rest, sum_near
+    )
+    back_high = across(back_rest)
     feed_here = feed_near[0].astype(F32) + feed_here.astype(F32)
     feed_sum = (feed_far[0].astype(F32) + feed_mate.astype(F32)).astype(BF16)
-    back_from_far, feed_here, feed_sum, back_here, wide_hop = fence(
-        back_from_far, feed_here, feed_sum, back_here, wide_hop
-    )
+    back_high, feed_here, feed_sum, back_here, wide_hop = fence(
+        back_high, feed_here, feed_sum, back_here, wide_hop
+    )
+    back_from_far = jnp.concatenate([back_low, back_high])
     second_own = back_near[0].astype(F32) + back_here.astype(F32) + back_from_far.astype(F32)
     grad_narrow_mlp = second_own[:, width : width + 2 * rank].astype(BF16)
     grad_normed_second = second_own[:, :width] + dot(grad_narrow_mlp, a_mlp)
@@ -890,7 +909,9 @@
         (branch_rows, branch_near_in), second_blocks[:2], (0, 1), place, mixed,
         attention_output_weight, a_out, b_out,
     )
-    branch_far_in, mixed_near = fence(branch_far_in, mixed_near)
+    branch_far_in, mixed_near, wide_hop = fence(branch_far_in, mixed_near, wide_hop)
+    wide_all = both(wide_all, wide_hop, rep_place, bits[-2])
+    wide_hop = hop(wide_all, "rep", bits[-1])
     feed_from_far = across(after(feed_sum, branch_far_in))
     mixed_far, grad_a_far, thin_far = open_attention(
         (branch_far_in, core(branch_far_in)), second_blocks[2:], (2, 3), place, mixed,
@@ -905,28 +926,26 @@
             narrow_first, b_heads, rows, first, heads,
         )
 
-    mixed_far, starts_one = fence(mixed_far, starts)
+    mixed_far, starts_one, wide_all = fence(mixed_far, starts, wide_all)
     heads = query.shape[0]
     third = heads // 3
     part_one = attend_part(0, third, starts_one)
     part_one, feed_from_far, wide_hop, starts_two = fence(part_one, feed_from_far, wide_hop, starts_one)
-    wide_all = both(wide_all, wide_hop, rep_place, bits[-2])
-    wide_hop = hop(wide_all, "rep", bits[-1])
+    wide_all = both(wide_all, wide_hop, rep_place, bits[-1])
+    picks = wide_all[:, -1, :1].astype(F32)
+    adapters = adapter_model_input_maps.shape[1] * group
+    chosen = (picks == jnp.arange(adapters, dtype=jnp.int32).astype(F32)[None, :]).astype(F32)
+    wide_sent = send_sums(wide_all[:, :-rank], chosen, place)
     feed_own = feed_here + feed_from_far.astype(F32)
     narrow_down = feed_own[:, width : width + rank].astype(BF16)
     down_far = across(narrow_down)
     down_near = core(narrow_down)
     starts_two, narrow_down = fence(starts_two, narrow_down)
     part_two = attend_part(third, third, starts_two)
-    part_two, wide_hop, down_far, down_near, starts_three = fence(
-        part_two, wide_hop, down_far, down_near, starts_two
+    part_two, down_far, down_near, starts_three, wide_sent = fence(
+        part_two, down_far, down_near, starts_two, wide_sent
     )
     down_thin = (narrow_down, down_near, down_far, core(down_far))
-    wide_all = both(wide_all, wide_hop, rep_place, bits[-1])
-    picks = wide_all[:, -1, :1].astype(F32)
-    adapters = adapter_model_input_maps.shape[1] * group
-    chosen = (picks == jnp.arange(adapters, dtype=jnp.int32).astype(F32)[None, :]).astype(F32)
-    wide_sent = send_sums(wide_all[:, :-rank], chosen, place)
     grad_b_down = sum(t_dot(left, right) for left, right in zip(down_thin, feed_blocks))
     early_all = jnp.concatenate(
         [
@@ -937,7 +956,7 @@
     early_hop = hop(early_all, "rep", bits[0])
     early_all, starts_three = fence(early_all, starts_three)
     part_three = attend_part(2 * third, heads - 2 * third, starts_three)
-    part_three, early_hop, wide_sent = fence(part_three, early_hop, wide_sent)
+    part_three, early_hop = fence(part_three, early_hop)
     parts = (part_one, part_two, part_three)
     first_grads = [part[number] for number in range(3) for part in parts]
     thin = (part_one[3] + part_two[3] + part_three[3]).astype(BF16)
@@ -945,38 +964,35 @@
     early_all = both(early_all, early_hop, rep_place, bits[0])
     for bit in bits[1:-2]:
         early_all = both(early_all, hop(early_all, "rep", bit), rep_place, bit)
+    grad_b_first = jnp.concatenate([part[4] for part in parts], axis=1)
+    thin = (thin.astype(F32) + thin_hop.astype(F32)).astype(BF16)
+    thin, early_all, grad_b_first = fence(thin, early_all, grad_b_first)
+    thin_hop = across(thin)
     early_hop = hop(early_all, "rep", bits[-2])
-    thin = (thin.astype(F32) + thin_hop.astype(F32)).astype(BF16)
-    thin, first_grads, early_all = fence(thin, first_grads, early_all)
-    thin_hop = across(thin)
+    grad_narrow = (thin.astype(F32) + thin_hop.astype(F32)).astype(BF16)
+    late_all = jnp.concatenate(
+        [own_columns(thin_product(grad_narrow, place, first_blocks), head_cols), grad_b_first]
+    ).astype(BF16)[None]
+    late_all, first_grads = fence(late_all, first_grads)
+    late_hop = hop(late_all, "rep", bits[0])
     back_rows_far = project_back(first_grads, place, first_offsets, first_pieces, (2, 3), rows)
-    back_rows_far, thin_hop, early_hop = fence(back_rows_far, thin_hop, early_hop)
+    back_rows_far, late_hop, early_hop = fence(back_rows_far, late_hop, early_hop)
     back_mate = core(back_rows_far[1])
-    grad_narrow = (thin.astype(F32) + thin_hop.astype(F32)).astype(BF16)
-    grad_b_first = jnp.concatenate([part[4] for part in parts]).transpose(1, 0, 2)
-    late_all = jnp.concatenate(
-        [
-            own_columns(thin_product(grad_narrow, place, first_blocks), head_cols),
-            grad_b_first.reshape(3 * rank, head_cols),
-        ]
-    ).astype(BF16)[None]
-    late_all, grad_narrow, back_mate, early_all, early_hop = fence(
-        late_all, grad_narrow, back_mate, early_all, early_hop
-    )
-    late_hop = hop(late_all, "rep", bits[0])
-    back_sum = (back_rows_far[0].astype(F32) + back_mate.astype(F32)).astype(BF16)
-    early_all = both(early_all, early_hop, rep_place, bits[-2])
-    early_hop = hop(early_all, "rep", bits[-1])
-    back_sum, grads_here, early_all = fence(back_sum, first_grads, early_all)
-    back_far_in = across(back_sum)
-    back_rows_near = project_back(grads_here, place, first_offsets, first_pieces, (0, 1), rows)
-    late_hop, back_rows_near, early_hop = fence(late_hop, back_rows_near, early_hop)
-    back_rows_here = core(back_rows_near[1])
     late_all = both(late_all, late_hop, rep_place, bits[0])
     for bit in bits[1:-2]:
         late_all = both(late_all, hop(late_all, "rep", bit), rep_place, bit)
     late_hop = hop(late_all, "rep", bits[-2])
+    early_all = both(early_all, early_hop, rep_place, bits[-2])
+    early_hop = hop(early_all, "rep", bits[-1])
+    back_sum = (back_rows_far[0].astype(F32) + back_mate.astype(F32)).astype(BF16)
+    back_sum, first_grads, early_all, late_all = fence(back_sum, first_grads, early_all, late_all)
+    back_low, back_high = across(back_sum[: rows // 2]), across(back_sum[rows // 2 :])
+    back_rows_near = project_back(first_grads, place, first_offsets, first_pieces, (0, 1), rows)
+    back_rows_near, late_hop, early_hop, back_low = fence(back_rows_near, late_hop, early_hop, back_low)
+    back_rows_here = core(back_rows_near[1])
+    late_all = both(late_all, late_hop, rep_place, bits[-2])
     late_all, early_hop, early_all = fence(late_all, early_hop, early_all)
+    late_hop = hop(late_all, "rep", bits[-1])
     early_sent = send_sums(both(early_all, early_hop, rep_place, bits[-1]), chosen, place)
 
     def whole_maps(stacked, low, high, n):
@@ -986,11 +1002,11 @@
 
     feed = feed_here[:, :width] + feed_from_far[:, :width].astype(F32) + dot(narrow_down, b_down)
     output = (middle + BRANCH * feed).astype(BF16)
-    late_hop, output = fence(late_hop, output)
-    late_all = both(late_all, late_hop, rep_place, bits[-2])
-    late_hop = hop(late_all, "rep", bits[-1])
     hidden_maps = whole_maps(jnp.stack(wide_sent), 0, 3 * rank, ff_cols)
-    late_hop, hidden_maps, back_far_in = fence(late_hop, hidden_maps, back_far_in)
+    late_hop, hidden_maps, output, back_high, back_rows_here = fence(
+        late_hop, hidden_maps, output, back_high, back_rows_here
+    )
+    back_far_in = jnp.concatenate([back_low, back_high])
     late_sent = send_sums(both(late_all, late_hop, rep_place, bits[-1]), chosen, place)
     narrow_own = lax.dynamic_slice_in_dim(grad_narrow, place * rows, rows, 1)
     grad_normed = (
@@ -998,8 +1014,8 @@
         + t_dot(narrow_own, a_first)
     )
     input_grad = grad_middle + norm_back(residual_in, gain_one, grad_normed)
+    late_sent, input_grad, early_sent = fence(late_sent, input_grad, early_sent)
     early_got = jnp.stack(early_sent)
-    late_sent, input_grad, early_got = fence(late_sent, input_grad, early_got)
     late_got = jnp.stack(late_sent)
     grad_a_model = jnp.concatenate(
         [

time: 548 us -> 527 us (0.962)
  local copies, waits for them, and re-layouts: 78.2 us -> 66.5 us
  waiting for transfers between devices: 149 us -> 142 us
  other arithmetic: 42.7 us -> 37.2 us
    unnamed x227 -> x236, local copies, waits for them, and re-layouts: 37.8 us -> 29.4 us
    ppermute x74 -> x78, waiting for transfers between devices: 149 us -> 142 us  [hop(): return lax.ppermute(values, axis, [(i, i ^ bit) for i in range(size)])]
    ppermute x74 -> x78, starting transfers between devices: 57.2 us -> 60.1 us  [hop(): return lax.ppermute(values, axis, [(i, i ^ bit) for i in range(size)])]
  transfers between devices with their start and end apart: 74 -> 78, of which waited for: 30 -> 32; matrix products, arithmetic and copies ran while one was open for 14% -> 12% of each run, Pallas kernels for 30% -> 32%
where the time goes in v5:
time: 527 us; the launch traced here: 520 us
  Pallas kernels  202 us (38%)
  waiting for transfers between devices  142 us (27%)
  local copies, waits for them, and re-layouts  66.5 us (13%)
  starting transfers between devices  60.1 us (11%)
  other arithmetic  37.2 us (7%)
  matrix products  8.21 us (2%)
    ppermute x78, waiting for transfers between devices, hop(): return lax.ppermute(values, axis, [(i, i ^ bit) for i in range(size)])  142 us
    pallas_call x2, Pallas kernels, feed_forward(): call(kernel, [out] * (2 * count) + [jax.ShapeDtypeStruct((3 * rank, size)...  71.5 us
    ppermute x78, starting transfers between devices, hop(): return lax.ppermute(values, axis, [(i, i ^ bit) for i in range(size)])  60.1 us
    pallas_call x3, Pallas kernels, attend_back(): call(kernel, [jax.ShapeDtypeStruct((heads, length, HDIM), BF16)] * 3 + [j...  38.3 us
    unnamed x236, local copies, waits for them, and re-layouts  29.4 us
    pallas_call x2, Pallas kernels, project_back(): call(kernel, [jax.ShapeDtypeStruct((rows, width), BF16)] * count, [smem()...  24.8 us
    pallas_call x1, Pallas kernels, project(): call(kernel, [by_heads] * 3 + [jax.ShapeDtypeStruct((thin, rows * count),...  21 us
    pallas_call x1, Pallas kernels, attend(): call(kernel, [jax.ShapeDtypeStruct(query.shape, BF16), jax.ShapeDtypeStru...  16.5 us
  transfers between devices with their start and end apart: 78, of which 32 were waited for; matrix products, arithmetic and copies ran while one was open for 12% of the time, Pallas kernels for 32%

profile of v5, /device:TPU:0, one launch (start us, length us, event | category | flops | bytes accessed | tf_op | source)
XLA Modules:
  0.0 519.8 jit_solution(14189958953040399132)
XLA Ops:
  1.4 2.0 fusion.48
  5.3 3.6 sides_far.1
  8.9 2.6 collective-permute-start
  13.0 1.9 fusion.30
  21.4 1.8 pad_maximum_fusion.5
  29.0 7.0 %sides_near.1 = (bf16[576,1728]{1,0:T(8,128)(2,1)}, bf16[576,1728]{1,0:T(8,128)(2,1)}) custom-call(s32[2]{0:T(128)} %get-tuple-element.579.where_ref, bf16[3,576,2304]{2,1,0:T(8,128)(2,1)} %w_ref.4), custom_call_target="tpu_custom_call" | custom-call | bytes 11943936 | tf_op jit(solution)/shard_map/sides_near/pallas_call | solution.py:140
  36.1 3.3 collective-permute-done.2.refs_10_.refs_15_
  49.6 7.2 %collective-permute-done.4.refs_12_.refs_17_ = bf16[144,1728]{1,0:T(8,128)(2,1)S(1)} collective-permute-done((bf16[144,1728]{1,0:T(8,128)(2,1)}, bf16[144,1728]{1,0:T(8,128)(2,1)S(1)}, u32[]{:S(2)}, u32[]{:S(2)}) %collective-permute-start.4) | collective-permute-done | bytes 497696 | tf_op jit(solution)/shard_map/ppermute | solution.py:24
  61.7 10.1 %constant_dynamic-slice_fusion.7 = (bf16[2,576,1440]{2,1,0:T(8,128)(2,1)}, bf16[2,576,1440]{2,1,0:T(8,128)(2,1)}) fusion(bf16[2,576,5760]{2,1,0:T(8,128)(2,1)} %param.22, s32[]{:T(128)S(6)} %select_n.350, s32[]{:T(128)S(6)} %select_n.349), kind=kLoop, calls=%fused_computation.182 | loop fusion | bytes 13271048 | tf_op jit(solution)/shard_map/dynamic_slice | solution.py:118
  71.9 3.6 constant_dynamic-slice_fusion.9
  78.8 10.1 %collective-permute-done.11.refs_13_.refs_18_ = bf16[144,1728]{1,0:T(8,128)(2,1)S(1)} collective-permute-done((bf16[144,1728]{1,0:T(8,128)(2,1)S(1)}, bf16[144,1728]{1,0:T(8,128)(2,1)S(1)}, u32[]{:S(2)}, u32[]{:S(2)}) %collective-permute-start.11) | collective-permute-done | bytes 497696 | tf_op jit(solution)/shard_map/ppermute | solution.py:24
  93.3 21.0 %project.1 = (bf16[9,1024,64]{2,1,0:T(8,128)(2,1)}, bf16[9,1024,64]{2,1,0:T(8,128)(2,1)}, bf16[9,1024,64]{2,1,0:T(8,128)(2,1)}, bf16[48,1024]{1,0:T(8,128)(2,1)}) custom-call(s32[1]{0:T(128)} %bitcast.place_ref, s32[10]{0:T(128)} %stack.110.offsets_ref, bf16[256,2304]{1,0:T(8,128)(2,1)} %copy-done.8, bf16[256,2304]{1,0:T(8,128)(2,1)} %copy-done.19, ...), custom_call_target="tpu_custom_call" | custom-call | flops 8153726976 | bytes 19759104 | tf_op jit(solution)/shard_map/project/pallas_call | solution.py:252
  117.2 16.5 %attend.1 = (bf16[9,1024,64]{2,1,0:T(8,128)(2,1)}, f32[9,1,1024]{2,1,0:T(1,128)}) custom-call(s32[2]{0:T(128)} %bitcast.175, bf16[9,1024,64]{2,1,0:T(8,128)(2,1)} %get-tuple-element.276.q_ref, bf16[9,1024,64]{2,1,0:T(8,128)(2,1)} %get-tuple-element.277.k_ref, bf16[9,1024,64]{2,1,0:T(8,128)(2,1)} %get-tuple-element.278.v_ref), custom_call_target="tpu_custom_call" | custom-call | flops 9663676416 | bytes 9437184 | tf_op jit(solution)/shard_map/attend/pallas_call | solution.py:346
  141.5 2.2 close_attention.2
  147.2 5.7 %collective-permute-done.24 = bf16[3,8,5760]{2,1,0:T(8,128)(2,1)S(1)} collective-permute-done((bf16[3,8,5760]{2,1,0:T(8,128)(2,1)S(1)}, bf16[3,8,5760]{2,1,0:T(8,128)(2,1)S(1)}, u32[]{:S(2)}, u32[]{:S(2)}) %collective-permute-start.24) | collective-permute-done | bytes 276512 | tf_op jit(solution)/shard_map/ppermute | solution.py:24
  154.4 2.2 close_attention.3
  156.7 9.5 %collective-permute-done.26.refs_12_ = bf16[2,144,1440]{2,1,0:T(8,128)(2,1)S(1)} collective-permute-done((bf16[2,144,1440]{2,1,0:T(8,128)(2,1)S(1)}, bf16[2,144,1440]{2,1,0:T(8,128)(2,1)S(1)}, u32[]{:S(2)}, u32[]{:S(2)}) %collective-permute-start.26) | collective-permute-done | bytes 829472 | tf_op jit(solution)/shard_map/ppermute | solution.py:24
  166.1 2.0 collective-permute-done.25.refs_11_
  170.8 13.8 %collective-permute-done.29 = bf16[128,2432]{1,0:T(8,128)(2,1)S(1)} collective-permute-done((bf16[128,2432]{1,0:T(8,128)(2,1)S(1)}, bf16[128,2432]{1,0:T(8,128)(2,1)S(1)}, u32[]{:S(2)}, u32[]{:S(2)}) %collective-permute-start.29) | collective-permute-done | bytes 622624 | tf_op jit(solution)/shard_map/ppermute | solution.py:24
  192.8 12.8 %collective-permute-done.37.refs_13_ = bf16[2,144,1440]{2,1,0:T(8,128)(2,1)S(1)} collective-permute-done((bf16[2,144,1440]{2,1,0:T(8,128)(2,1)S(1)}, bf16[2,144,1440]{2,1,0:T(8,128)(2,1)S(1)}, u32[]{:S(2)}, u32[]{:S(2)}) %collective-permute-start.37) | collective-permute-done | bytes 829472 | tf_op jit(solution)/shard_map/ppermute | solution.py:24
  207.2 1.8 copy-done.106
  209.3 35.5 %feed_forward.2 = (bf16[256,2432]{1,0:T(8,128)(2,1)}, bf16[256,2432]{1,0:T(8,128)(2,1)}, bf16[256,2432]{1,0:T(8,128)(2,1)}, bf16[256,2432]{1,0:T(8,128)(2,1)}, f32[48,1440]{1,0:T(8,128)}) custom-call(s32[10]{0:T(128)} %stack.110.offsets_ref, bf16[256,2304]{1,0:T(8,128)(2,1)} %copy-done.6, bf16[256,2304]{1,0:T(8,128)(2,1)} %copy-done.27, ...), custom_call_target="tpu_custom_call" | custom-call | flops 20384317440 | bytes 29343744 | tf_op jit(solution)/shard_map/feed_forward/pallas_call | solution.py:621
  245.6 2.3 collective-permute-done.40.refs_3_
  250.6 35.9 %feed_forward.3 = (bf16[256,2432]{1,0:T(8,128)(2,1)}, bf16[256,2432]{1,0:T(8,128)(2,1)}, bf16[256,2432]{1,0:T(8,128)(2,1)}, bf16[256,2432]{1,0:T(8,128)(2,1)}, f32[48,1440]{1,0:T(8,128)}) custom-call(s32[10]{0:T(128)} %stack.110.offsets_ref, bf16[256,2304]{1,0:T(8,128)(2,1)} %copy-done.23, bf16[256,2304]{1,0:T(8,128)(2,1)} %copy-done.25, ...), custom_call_target="tpu_custom_call" | custom-call | flops 20384317440 | bytes 29343744 | tf_op jit(solution)/shard_map/feed_forward/pallas_call | solution.py:621
  287.9 2.1 collective-permute-done.41
  290.0 2.0 add_convert_fusion.1
  294.4 14.8 %collective-permute-done.42 = bf16[128,2432]{1,0:T(8,128)(2,1)S(1)} collective-permute-done((bf16[128,2432]{1,0:T(8,128)(2,1)S(1)}, bf16[128,2432]{1,0:T(8,128)(2,1)S(1)}, u32[]{:S(2)}, u32[]{:S(2)}) %collective-permute-start.42) | collective-permute-done | bytes 622624 | tf_op jit(solution)/shard_map/ppermute | solution.py:24
  312.8 11.9 %collective-permute-done.46 = bf16[128,2432]{1,0:T(8,128)(2,1)S(1)} collective-permute-done((bf16[128,2432]{1,0:T(8,128)(2,1)S(1)}, bf16[128,2432]{1,0:T(8,128)(2,1)S(1)}, u32[]{:S(2)}, u32[]{:S(2)}) %collective-permute-start.46) | collective-permute-done | bytes 622624 | tf_op jit(solution)/shard_map/ppermute | solution.py:24
  326.9 2.5 multiply_convert_fusion
  329.3 3.1 concatenate.206.refs_0_
  333.0 2.6 collective-permute-start.50
  341.2 6.1 %open_attention.2 = (bf16[9,512,64]{2,1,0:T(8,128)(2,1)S(1)}, f32[16,576]{1,0:T(8,128)S(1)}, f32[48,2304]{1,0:T(8,128)S(1)}) custom-call(s32[1]{0:T(128)} %bitcast.place_ref, bf16[256,2432]{1,0:T(8,128)(2,1)S(1)} %copy-done.5, bf16[256,2432]{1,0:T(8,128)(2,1)} %collective-permute-done.49.refs_1_, bf16[256,2304]{1,0:T(8,128)(2,1)S(1)} %copy-done.7, ...), custom_call_target="tpu_custom_call" | custom-call | flops 1358954496 | bytes 8552448 | tf_op jit(solution)/shard_map/open_attention/pallas_call | solution.py:548
  348.3 5.3 %collective-permute-done.50 = bf16[2,64,1440]{2,1,0:T(8,128)(2,1)S(1)} collective-permute-done((bf16[2,64,1440]{2,1,0:T(8,128)(2,1)S(1)}, bf16[2,64,1440]{2,1,0:T(8,128)(2,1)S(1)}, u32[]{:S(2)}, u32[]{:S(2)}) %collective-permute-start.50) | collective-permute-done | bytes 368672 | tf_op jit(solution)/shard_map/ppermute | solution.py:24
  354.3 8.2 %collective-permute-done.48.refs_0_ = bf16[256,2432]{1,0:T(8,128)(2,1)} collective-permute-done((bf16[256,2432]{1,0:T(8,128)(2,1)}, bf16[256,2432]{1,0:T(8,128)(2,1)}, u32[]{:S(2)}, u32[]{:S(2)}) %collective-permute-start.48) | collective-permute-done | bytes 1245216 | tf_op jit(solution)/shard_map/ppermute | solution.py:24
  370.4 6.6 %open_attention.3 = (bf16[9,512,64]{2,1,0:T(8,128)(2,1)S(1)}, f32[16,576]{1,0:T(8,128)S(1)}, f32[48,2304]{1,0:T(8,128)S(1)}) custom-call(s32[1]{0:T(128)} %bitcast.place_ref, bf16[256,2432]{1,0:T(8,128)(2,1)} %collective-permute-done.48.refs_0_, bf16[256,2432]{1,0:T(8,128)(2,1)} %collective-permute-done.51.refs_1_, bf16[256,2304]{1,0:T(8,128)(2,1)S(1)} %copy-done.24, ...), custom_call_target="tpu_custom_call" | custom-call | flops 1358954496 | bytes 8552448 | tf_op jit(solution)/shard_map/open_attention/pallas_call | solution.py:548
  378.8 12.9 %attend_back.3 = (bf16[3,1024,64]{2,1,0:T(8,128)(2,1)S(1)}, bf16[3,1024,64]{2,1,0:T(8,128)(2,1)S(1)}, bf16[3,1024,64]{2,1,0:T(8,128)(2,1)S(1)}, f32[48,1024]{1,0:T(8,128)S(1)}, f32[48,192]{1,0:T(8,128)S(1)}) custom-call(s32[2]{0:T(128)S(1)} %bitcast.176, s32[1]{0:T(128)} %bitcast.place_ref, bf16[9,1024,64]{2,1,0:T(8,128)(2,1)S(1)} %copy-done.34, ...), custom_call_target="tpu_custom_call" | custom-call | flops 8053063680 | bytes 6291456 | tf_op jit(solution)/shard_map/attend_back/pallas_call | solution.py:453
  399.2 12.7 %attend_back.4 = (bf16[3,1024,64]{2,1,0:T(8,128)(2,1)S(1)}, bf16[3,1024,64]{2,1,0:T(8,128)(2,1)S(1)}, bf16[3,1024,64]{2,1,0:T(8,128)(2,1)S(1)}, f32[48,1024]{1,0:T(8,128)S(1)}, f32[48,192]{1,0:T(8,128)S(1)}) custom-call(s32[2]{0:T(128)S(1)} %bitcast.177, s32[1]{0:T(128)} %bitcast.place_ref, bf16[9,1024,64]{2,1,0:T(8,128)(2,1)S(1)} %copy-done.34, ...), custom_call_target="tpu_custom_call" | custom-call | flops 8053063680 | bytes 6291456 | tf_op jit(solution)/shard_map/attend_back/pallas_call | solution.py:453
  416.4 12.7 %attend_back.5 = (bf16[3,1024,64]{2,1,0:T(8,128)(2,1)S(1)}, bf16[3,1024,64]{2,1,0:T(8,128)(2,1)S(1)}, bf16[3,1024,64]{2,1,0:T(8,128)(2,1)S(1)}, f32[48,1024]{1,0:T(8,128)S(1)}, f32[48,192]{1,0:T(8,128)S(1)}) custom-call(s32[2]{0:T(128)S(1)} %bitcast.178, s32[1]{0:T(128)} %bitcast.place_ref, bf16[9,1024,64]{2,1,0:T(8,128)(2,1)S(1)} %copy-done.34, ...), custom_call_target="tpu_custom_call" | custom-call | flops 8053063680 | bytes 6291456 | tf_op jit(solution)/shard_map/attend_back/pallas_call | solution.py:453
  432.3 2.6 collective-permute-start.64
  435.6 2.2 thin_product.1
  438.6 12.4 %project_back.2 = (bf16[256,2304]{1,0:T(8,128)(2,1)}, bf16[256,2304]{1,0:T(8,128)(2,1)}) custom-call(s32[1]{0:T(128)} %bitcast.place_ref, s32[10]{0:T(128)} %stack.110.offsets_ref, bf16[3,1024,64]{2,1,0:T(8,128)(2,1)} %copy-done.10, bf16[3,1024,64]{2,1,0:T(8,128)(2,1)} %copy-done.13, bf16[3,1024,64]{2,1,0:T(8,128)(2,1)} %copy-done.16, ...), custom_call_target="tpu_custom_call" | custom-call | flops 4076863488 | bytes 12091392 | tf_op jit(solution)/shard_map/project_back/pallas_call | solution.py:658
  451.8 3.6 add_convert_fusion.3
  462.1 3.4 collective-permute-start.66
  467.0 12.4 %project_back.3 = (bf16[256,2304]{1,0:T(8,128)(2,1)}, bf16[256,2304]{1,0:T(8,128)(2,1)}) custom-call(s32[1]{0:T(128)} %bitcast.place_ref, s32[10]{0:T(128)} %stack.110.offsets_ref, bf16[3,1024,64]{2,1,0:T(8,128)(2,1)} %copy-done.10, bf16[3,1024,64]{2,1,0:T(8,128)(2,1)} %copy-done.13, bf16[3,1024,64]{2,1,0:T(8,128)(2,1)} %copy-done.16, ...), custom_call_target="tpu_custom_call" | custom-call | flops 4076863488 | bytes 12091392 | tf_op jit(solution)/shard_map/project_back/pallas_call | solution.py:658
  484.7 11.9 %collective-permute-done.70 = bf16[128,2304]{1,0:T(8,128)(2,1)S(1)} collective-permute-done((bf16[128,2304]{1,0:T(8,128)(2,1)S(1)}, bf16[128,2304]{1,0:T(8,128)(2,1)S(1)}, u32[]{:S(2)}, u32[]{:S(2)}) %collective-permute-start.70) | collective-permute-done | bytes 589856 | tf_op jit(solution)/shard_map/ppermute | solution.py:24
  501.5 2.1 fusion.11
  504.2 2.0 fusion.10
  508.2 6.5 %collective-permute-done.73 = bf16[2,96,576]{2,1,0:T(8,128)(2,1)S(1)} collective-permute-done((bf16[2,96,576]{2,1,0:T(8,128)(2,1)S(1)}, bf16[2,96,576]{2,1,0:T(8,128)(2,1)S(1)}, u32[]{:S(2)}, u32[]{:S(2)}) %collective-permute-start.73) | collective-permute-done | bytes 221216 | tf_op jit(solution)/shard_map/ppermute | solution.py:24
  (493 shorter events, 139.1 us)
Async XLA Ops:
  4.2 19.1 %collective-permute-start.1 = (bf16[6,16,2304]{2,1,0:T(8,128)(2,1)}, bf16[6,16,2304]{2,1,0:T(8,128)(2,1)}, u32[]{:S(2)}, u32[]{:S(2)}) collective-permute-start(bf16[6,16,2304]{2,1,0:T(8,128)(2,1)} %fusion.20), channel_id=1, source_target_pairs={{0,1},{1,0},{2,3},{3,2},{4,5},{5,4},{6,7},{7,6},{8,9},{9,8},{10,11... | collective-permute-start | bytes 1327112 | tf_op jit(solution)/shard_map/ppermute | solution.py:24
  8.9 15.7 %collective-permute-start = (bf16[144,1728]{1,0:T(8,128)(2,1)}, bf16[144,1728]{1,0:T(8,128)(2,1)S(1)}, u32[]{:S(2)}, u32[]{:S(2)}) collective-permute-start(bf16[144,1728]{1,0:T(8,128)(2,1)} %get-tuple-element.240), channel_id=1, source_target_pairs={{0,2},{1,3},{2,0},{3,1},{4,6},{5,7},{6,4},{7,5},{8,10},{9,11},{10,... | collective-permute-start | bytes 1493000 | tf_op jit(solution)/shard_map/ppermute | solution.py:24
  25.6 16.7 %collective-permute-start.7 = (bf16[144,1728]{1,0:T(8,128)(2,1)S(1)}, bf16[144,1728]{1,0:T(8,128)(2,1)}, u32[]{:S(2)}, u32[]{:S(2)}) collective-permute-start(bf16[144,1728]{1,0:T(8,128)(2,1)S(1)} %collective-permute-done.refs_6_.refs_11_), channel_id=1, source_target_pairs={{0,4},{4,0},{8,12},{12,8},{16,20},{20,16},{24,28},{28,24},{1,5},{5... | collective-permute-start | bytes 1493000 | tf_op jit(solution)/shard_map/ppermute | solution.py:24
  27.4 16.6 %collective-permute-start.6 = (bf16[144,1728]{1,0:T(8,128)(2,1)S(1)}, bf16[144,1728]{1,0:T(8,128)(2,1)}, u32[]{:S(2)}, u32[]{:S(2)}) collective-permute-start(bf16[144,1728]{1,0:T(8,128)(2,1)S(1)} %collective-permute-done.refs_6_.refs_11_), channel_id=1, source_target_pairs={{0,8},{4,12},{8,0},{12,4},{16,24},{20,28},{24,16},{28,20},{1,9},{5... | collective-permute-start | bytes 1493000 | tf_op jit(solution)/shard_map/ppermute | solution.py:24
  29.0 63.3 %collective-permute-start.8 = (bf16[256,2304]{1,0:T(8,128)(2,1)S(1)}, bf16[256,2304]{1,0:T(8,128)(2,1)S(1)}, u32[]{:S(2)}, u32[]{:S(2)}) collective-permute-start(bf16[256,2304]{1,0:T(8,128)(2,1)S(1)} %fusion.7.refs_0_), channel_id=1, source_target_pairs={{0,1},{1,0},{2,3},{3,2},{4,5},{5,4},{6,7},{7,6},{8,9},{9,8},{10,11... | collective-permute-start | bytes 3538952 | tf_op jit(solution)/shard_map/ppermute | solution.py:24
  47.1 29.2 %collective-permute-start.14 = (bf16[3,16,5760]{2,1,0:T(8,128)(2,1)S(1)}, bf16[3,16,5760]{2,1,0:T(8,128)(2,1)S(1)}, u32[]{:S(2)}, u32[]{:S(2)}) collective-permute-start(bf16[3,16,5760]{2,1,0:T(8,128)(2,1)S(1)} %fusion.16), channel_id=1, source_target_pairs={{0,1},{1,0},{2,3},{3,2},{4,5},{5,4},{6,7},{7,6},{8,9},{9,8},{10,11... | collective-permute-start | bytes 1658888 | tf_op jit(solution)/shard_map/ppermute | solution.py:24
  49.4 42.9 %collective-permute-start.16 = (bf16[576,1728]{1,0:T(8,128)(2,1)}, bf16[576,1728]{1,0:T(8,128)(2,1)}, u32[]{:S(2)}, u32[]{:S(2)}) collective-permute-start(bf16[576,1728]{1,0:T(8,128)(2,1)} %get-tuple-element.263), channel_id=1, source_target_pairs={{0,1},{1,0},{2,3},{3,2},{4,5},{5,4},{6,7},{7,6},{8,9},{9,8},{10,11... | collective-permute-start | bytes 5971976 | tf_op jit(solution)/shard_map/ppermute | solution.py:24
  56.7 22.1 %collective-permute-start.10 = (bf16[144,1728]{1,0:T(8,128)(2,1)}, bf16[144,1728]{1,0:T(8,128)(2,1)S(1)}, u32[]{:S(2)}, u32[]{:S(2)}) collective-permute-start(bf16[144,1728]{1,0:T(8,128)(2,1)} %collective-permute-done.6.refs_7_.refs_12_), channel_id=1, source_target_pairs={{0,4},{4,0},{8,12},{12,8},{16,20},{20,16},{24,28},{28,24},{1,5},{5... | collective-permute-start | bytes 1493000 | tf_op jit(solution)/shard_map/ppermute | solution.py:24
  58.1 30.8 %collective-permute-start.9 = (bf16[256,2304]{1,0:T(8,128)(2,1)S(1)}, bf16[256,2304]{1,0:T(8,128)(2,1)S(1)}, u32[]{:S(2)}, u32[]{:S(2)}) collective-permute-start(bf16[256,2304]{1,0:T(8,128)(2,1)S(1)} %fusion.7.refs_0_), channel_id=1, source_target_pairs={{0,2},{1,3},{2,0},{3,1},{4,6},{5,7},{6,4},{7,5},{8,10},{9,11},{10,... | collective-permute-start | bytes 3538952 | tf_op jit(solution)/shard_map/ppermute | solution.py:24
  89.7 24.6 %collective-permute-start.17 = (bf16[2,144,1440]{2,1,0:T(8,128)(2,1)}, bf16[2,144,1440]{2,1,0:T(8,128)(2,1)}, u32[]{:S(2)}, u32[]{:S(2)}) collective-permute-start(bf16[2,144,1440]{2,1,0:T(8,128)(2,1)} %get-tuple-element.273), channel_id=1, source_target_pairs={{0,2},{1,3},{2,0},{3,1},{4,6},{5,7},{6,4},{7,5},{8,10},{9,11},{10,... | collective-permute-start | bytes 2488328 | tf_op jit(solution)/shard_map/ppermute | solution.py:24
  90.9 42.8 %collective-permute-start.18 = (bf16[2,144,1440]{2,1,0:T(8,128)(2,1)}, bf16[2,144,1440]{2,1,0:T(8,128)(2,1)S(1)}, u32[]{:S(2)}, u32[]{:S(2)}) collective-permute-start(bf16[2,144,1440]{2,1,0:T(8,128)(2,1)} %get-tuple-element.280), channel_id=1, source_target_pairs={{0,3},{1,2},{2,1},{3,0},{4,7},{5,6},{6,5},{7,4},{8,11},{9,10},{10,... | collective-permute-start | bytes 2488328 | tf_op jit(solution)/shard_map/ppermute | solution.py:24
  114.3 22.1 %collective-permute-start.20 = (bf16[2,144,1440]{2,1,0:T(8,128)(2,1)}, bf16[2,144,1440]{2,1,0:T(8,128)(2,1)S(1)}, u32[]{:S(2)}, u32[]{:S(2)}) collective-permute-start(bf16[2,144,1440]{2,1,0:T(8,128)(2,1)} %collective-permute-done.17.refs_6_), channel_id=1, source_target_pairs={{0,4},{4,0},{8,12},{12,8},{16,20},{20,16},{24,28},{28,24},{1,5},{5... | collective-permute-start | bytes 2488328 | tf_op jit(solution)/shard_map/ppermute | solution.py:24
  115.6 21.9 %collective-permute-start.19 = (bf16[2,144,1440]{2,1,0:T(8,128)(2,1)}, bf16[2,144,1440]{2,1,0:T(8,128)(2,1)}, u32[]{:S(2)}, u32[]{:S(2)}) collective-permute-start(bf16[2,144,1440]{2,1,0:T(8,128)(2,1)} %collective-permute-done.17.refs_6_), channel_id=1, source_target_pairs={{0,8},{4,12},{8,0},{12,4},{16,24},{20,28},{24,16},{28,20},{1,9},{5... | collective-permute-start | bytes 2488328 | tf_op jit(solution)/shard_map/ppermute | solution.py:24
  116.5 18.4 %collective-permute-start.21 = (bf16[5,8,2304]{2,1,0:T(8,128)(2,1)S(1)}, bf16[5,8,2304]{2,1,0:T(8,128)(2,1)S(1)}, u32[]{:S(2)}, u32[]{:S(2)}) collective-permute-start(bf16[5,8,2304]{2,1,0:T(8,128)(2,1)S(1)} %copy-done.96), channel_id=1, source_target_pairs={{0,2},{1,3},{2,0},{3,1},{4,6},{5,7},{6,4},{7,5},{8,10},{9,11},{10,... | collective-permute-start | bytes 552968 | tf_op jit(solution)/shard_map/ppermute | solution.py:24
  144.5 21.6 %collective-permute-start.26 = (bf16[2,144,1440]{2,1,0:T(8,128)(2,1)S(1)}, bf16[2,144,1440]{2,1,0:T(8,128)(2,1)S(1)}, u32[]{:S(2)}, u32[]{:S(2)}) collective-permute-start(bf16[2,144,1440]{2,1,0:T(8,128)(2,1)S(1)} %collective-permute-done.18.refs_10_), channel_id=1, source_target_pairs={{0,8},{4,12},{8,0},{12,4},{16,24},{20,28},{24,16},{28,20},{1,9},{5... | collective-permute-start | bytes 2488328 | tf_op jit(solution)/shard_map/ppermute | solution.py:24
  145.6 22.5 %collective-permute-start.25 = (bf16[2,144,1440]{2,1,0:T(8,128)(2,1)S(1)}, bf16[2,144,1440]{2,1,0:T(8,128)(2,1)S(1)}, u32[]{:S(2)}, u32[]{:S(2)}) collective-permute-start(bf16[2,144,1440]{2,1,0:T(8,128)(2,1)S(1)} %collective-permute-done.18.refs_10_), channel_id=1, source_target_pairs={{0,4},{4,0},{8,12},{12,8},{16,20},{20,16},{24,28},{28,24},{1,5},{5... | collective-permute-start | bytes 2488328 | tf_op jit(solution)/shard_map/ppermute | solution.py:24
  152.9 15.6 %collective-permute-start.27 = (bf16[128,2432]{1,0:T(8,128)(2,1)S(1)}, bf16[128,2432]{1,0:T(8,128)(2,1)S(1)}, u32[]{:S(2)}, u32[]{:S(2)}) collective-permute-start(bf16[128,2432]{1,0:T(8,128)(2,1)S(1)} %get-tuple-element.507), channel_id=1, source_target_pairs={{0,2},{1,3},{2,0},{3,1},{4,6},{5,7},{6,4},{7,5},{8,10},{9,11},{10,... | collective-permute-start | bytes 1867784 | tf_op jit(solution)/shard_map/ppermute | solution.py:24
  153.5 16.0 %collective-permute-start.30 = (bf16[3,8,5760]{2,1,0:T(8,128)(2,1)S(1)}, bf16[3,8,5760]{2,1,0:T(8,128)(2,1)S(1)}, u32[]{:S(2)}, u32[]{:S(2)}) collective-permute-start(bf16[3,8,5760]{2,1,0:T(8,128)(2,1)S(1)} %collective-permute-done.24), channel_id=1, source_target_pairs={{0,1},{1,0},{2,3},{3,2},{4,5},{5,4},{6,7},{7,6},{8,9},{9,8},{10,11... | collective-permute-start | bytes 829448 | tf_op jit(solution)/shard_map/ppermute | solution.py:24
  153.6 35.2 %collective-permute-start.36 = (bf16[2,144,1440]{2,1,0:T(8,128)(2,1)}, bf16[2,144,1440]{2,1,0:T(8,128)(2,1)S(1)}, u32[]{:S(2)}, u32[]{:S(2)}) collective-permute-start(bf16[2,144,1440]{2,1,0:T(8,128)(2,1)} %collective-permute-done.19.refs_7_), channel_id=1, source_target_pairs={{0,4},{4,0},{8,12},{12,8},{16,20},{20,16},{24,28},{28,24},{1,5},{5... | collective-permute-start | bytes 2488328 | tf_op jit(solution)/shard_map/ppermute | solution.py:24
  166.1 26.1 %collective-permute-start.34 = (bf16[256,2304]{1,0:T(8,128)(2,1)S(1)}, bf16[256,2304]{1,0:T(8,128)(2,1)S(1)}, u32[]{:S(2)}, u32[]{:S(2)}) collective-permute-start(bf16[256,2304]{1,0:T(8,128)(2,1)S(1)} %copy-done.48), channel_id=1, source_target_pairs={{0,1},{1,0},{2,3},{3,2},{4,5},{5,4},{6,7},{7,6},{8,9},{9,8},{10,11... | collective-permute-start | bytes 3538952 | tf_op jit(solution)/shard_map/ppermute | solution.py:24
  168.2 39.0 %collective-permute-start.35 = (bf16[2,576,1440]{2,1,0:T(8,128)(2,1)S(1)}, bf16[2,576,1440]{2,1,0:T(8,128)(2,1)S(1)}, u32[]{:S(2)}, u32[]{:S(2)}) collective-permute-start(bf16[2,576,1440]{2,1,0:T(8,128)(2,1)S(1)} %copy-done.51), channel_id=1, source_target_pairs={{0,1},{1,0},{2,3},{3,2},{4,5},{5,4},{6,7},{7,6},{8,9},{9,8},{10,11... | collective-permute-start | bytes 9953288 | tf_op jit(solution)/shard_map/ppermute | solution.py:24
  168.5 16.1 %collective-permute-start.29 = (bf16[128,2432]{1,0:T(8,128)(2,1)S(1)}, bf16[128,2432]{1,0:T(8,128)(2,1)S(1)}, u32[]{:S(2)}, u32[]{:S(2)}) collective-permute-start(bf16[128,2432]{1,0:T(8,128)(2,1)S(1)} %get-tuple-element.297), channel_id=1, source_target_pairs={{0,2},{1,3},{2,0},{3,1},{4,6},{5,7},{6,4},{7,5},{8,10},{9,11},{10,... | collective-permute-start | bytes 1867784 | tf_op jit(solution)/shard_map/ppermute | solution.py:24
  169.5 16.0 %collective-permute-start.28 = (bf16[256,2432]{1,0:T(8,128)(2,1)S(1)}, bf16[256,2432]{1,0:T(8,128)(2,1)S(1)}, u32[]{:S(2)}, u32[]{:S(2)}) collective-permute-start(bf16[256,2432]{1,0:T(8,128)(2,1)S(1)} %get-tuple-element.296), channel_id=1, source_target_pairs={{0,1},{1,0},{2,3},{3,2},{4,5},{5,4},{6,7},{7,6},{8,9},{9,8},{10,11... | collective-permute-start | bytes 3735560 | tf_op jit(solution)/shard_map/ppermute | solution.py:24
  184.6 20.9 %collective-permute-start.37 = (bf16[2,144,1440]{2,1,0:T(8,128)(2,1)S(1)}, bf16[2,144,1440]{2,1,0:T(8,128)(2,1)S(1)}, u32[]{:S(2)}, u32[]{:S(2)}) collective-permute-start(bf16[2,144,1440]{2,1,0:T(8,128)(2,1)S(1)} %collective-permute-done.25.refs_11_), channel_id=1, source_target_pairs={{0,8},{4,12},{8,0},{12,4},{16,24},{20,28},{24,16},{28,20},{1,9},{5... | collective-permute-start | bytes 2488328 | tf_op jit(solution)/shard_map/ppermute | solution.py:24
  188.6 18.6 %collective-permute-start.33 = (bf16[256,2304]{1,0:T(8,128)(2,1)S(1)}, bf16[256,2304]{1,0:T(8,128)(2,1)S(1)}, u32[]{:S(2)}, u32[]{:S(2)}) collective-permute-start(bf16[256,2304]{1,0:T(8,128)(2,1)S(1)} %multiply_convert_fusion.1.refs_0_.refs_2_), channel_id=1, source_target_pairs={{0,1},{1,0},{2,3},{3,2},{4,5},{5,4},{6,7},{7,6},{8,9},{9,8},{10,11... | collective-permute-start | bytes 3538952 | tf_op jit(solution)/shard_map/ppermute | solution.py:24
  188.7 18.4 %collective-permute-start.38 = (bf16[128,2304]{1,0:T(8,128)(2,1)S(1)}, bf16[128,2304]{1,0:T(8,128)(2,1)S(1)}, u32[]{:S(2)}, u32[]{:S(2)}) collective-permute-start(bf16[128,2304]{1,0:T(8,128)(2,1)S(1)} %get-tuple-element.308), channel_id=1, source_target_pairs={{0,2},{1,3},{2,0},{3,1},{4,6},{5,7},{6,4},{7,5},{8,10},{9,11},{10,... | collective-permute-start | bytes 1769480 | tf_op jit(solution)/shard_map/ppermute | solution.py:24
  192.3 52.7 %collective-permute-start.31 = (bf16[256,2304]{1,0:T(8,128)(2,1)S(1)}, bf16[256,2304]{1,0:T(8,128)(2,1)S(1)}, u32[]{:S(2)}, u32[]{:S(2)}) collective-permute-start(bf16[256,2304]{1,0:T(8,128)(2,1)S(1)} %multiply_convert_fusion.1.refs_0_.refs_2_), channel_id=1, source_target_pairs={{0,2},{1,3},{2,0},{3,1},{4,6},{5,7},{6,4},{7,5},{8,10},{9,11},{10,... | collective-permute-start | bytes 3538952 | tf_op jit(solution)/shard_map/ppermute | solution.py:24
  205.5 39.4 %collective-permute-start.32 = (bf16[128,2304]{1,0:T(8,128)(2,1)S(1)}, bf16[128,2304]{1,0:T(8,128)(2,1)S(1)}, u32[]{:S(2)}, u32[]{:S(2)}) collective-permute-start(bf16[128,2304]{1,0:T(8,128)(2,1)S(1)} %get-tuple-element.304), channel_id=1, source_target_pairs={{0,2},{1,3},{2,0},{3,1},{4,6},{5,7},{6,4},{7,5},{8,10},{9,11},{10,... | collective-permute-start | bytes 1769480 | tf_op jit(solution)/shard_map/ppermute | solution.py:24
  292.0 17.2 %collective-permute-start.43 = (bf16[256,2432]{1,0:T(8,128)(2,1)S(1)}, bf16[256,2432]{1,0:T(8,128)(2,1)S(1)}, u32[]{:S(2)}, u32[]{:S(2)}) collective-permute-start(bf16[256,2432]{1,0:T(8,128)(2,1)S(1)} %copy-done.108), channel_id=1, source_target_pairs={{0,1},{1,0},{2,3},{3,2},{4,5},{5,4},{6,7},{7,6},{8,9},{9,8},{10,11... | collective-permute-start | bytes 3735560 | tf_op jit(solution)/shard_map/ppermute | solution.py:24
  292.2 17.0 %collective-permute-start.44 = (bf16[256,2432]{1,0:T(8,128)(2,1)S(1)}, bf16[256,2432]{1,0:T(8,128)(2,1)S(1)}, u32[]{:S(2)}, u32[]{:S(2)}) collective-permute-start(bf16[256,2432]{1,0:T(8,128)(2,1)S(1)} %copy-done.109), channel_id=1, source_target_pairs={{0,1},{1,0},{2,3},{3,2},{4,5},{5,4},{6,7},{7,6},{8,9},{9,8},{10,11... | collective-permute-start | bytes 3735560 | tf_op jit(solution)/shard_map/ppermute | solution.py:24
  292.6 16.6 %collective-permute-start.45 = (bf16[256,2432]{1,0:T(8,128)(2,1)S(1)}, bf16[256,2432]{1,0:T(8,128)(2,1)S(1)}, u32[]{:S(2)}, u32[]{:S(2)}) collective-permute-start(bf16[256,2432]{1,0:T(8,128)(2,1)S(1)} %copy-done.107), channel_id=1, source_target_pairs={{0,1},{1,0},{2,3},{3,2},{4,5},{5,4},{6,7},{7,6},{8,9},{9,8},{10,11... | collective-permute-start | bytes 3735560 | tf_op jit(solution)/shard_map/ppermute | solution.py:24
  292.8 16.4 %collective-permute-start.42 = (bf16[128,2432]{1,0:T(8,128)(2,1)S(1)}, bf16[128,2432]{1,0:T(8,128)(2,1)S(1)}, u32[]{:S(2)}, u32[]{:S(2)}) collective-permute-start(bf16[128,2432]{1,0:T(8,128)(2,1)S(1)} %get-tuple-element.505), channel_id=1, source_target_pairs={{0,2},{1,3},{2,0},{3,1},{4,6},{5,7},{6,4},{7,5},{8,10},{9,11},{10,... | collective-permute-start | bytes 1867784 | tf_op jit(solution)/shard_map/ppermute | solution.py:24
  293.4 19.4 %collective-permute-start.47 = (bf16[1,64,1440]{2,1,0:T(8,128)(2,1)S(1)}, bf16[1,64,1440]{2,1,0:T(8,128)(2,1)S(1)}, u32[]{:S(2)}, u32[]{:S(2)}) collective-permute-start(bf16[1,64,1440]{2,1,0:T(8,128)(2,1)S(1)} %pad_bitcast_fusion), channel_id=1, source_target_pairs={{0,8},{4,12},{8,0},{12,4},{16,24},{20,28},{24,16},{28,20},{1,9},{5... | collective-permute-start | bytes 552968 | tf_op jit(solution)/shard_map/ppermute | solution.py:24
  309.2 15.6 %collective-permute-start.46 = (bf16[128,2432]{1,0:T(8,128)(2,1)S(1)}, bf16[128,2432]{1,0:T(8,128)(2,1)S(1)}, u32[]{:S(2)}, u32[]{:S(2)}) collective-permute-start(bf16[128,2432]{1,0:T(8,128)(2,1)S(1)} %get-tuple-element.340), channel_id=1, source_target_pairs={{0,2},{1,3},{2,0},{3,1},{4,6},{5,7},{6,4},{7,5},{8,10},{9,11},{10,... | collective-permute-start | bytes 1867784 | tf_op jit(solution)/shard_map/ppermute | solution.py:24
  332.4 30.1 %collective-permute-start.48 = (bf16[256,2432]{1,0:T(8,128)(2,1)}, bf16[256,2432]{1,0:T(8,128)(2,1)}, u32[]{:S(2)}, u32[]{:S(2)}) collective-permute-start(bf16[256,2432]{1,0:T(8,128)(2,1)} %concatenate.206.refs_0_), channel_id=1, source_target_pairs={{0,2},{1,3},{2,0},{3,1},{4,6},{5,7},{6,4},{7,5},{8,10},{9,11},{10,... | collective-permute-start | bytes 3735560 | tf_op jit(solution)/shard_map/ppermute | solution.py:24
  333.0 20.6 %collective-permute-start.50 = (bf16[2,64,1440]{2,1,0:T(8,128)(2,1)S(1)}, bf16[2,64,1440]{2,1,0:T(8,128)(2,1)S(1)}, u32[]{:S(2)}, u32[]{:S(2)}) collective-permute-start(bf16[2,64,1440]{2,1,0:T(8,128)(2,1)S(1)} %maximum_select_fusion.6), channel_id=1, source_target_pairs={{0,16},{4,20},{8,24},{12,28},{16,0},{20,4},{24,8},{28,12},{1,17},{... | collective-permute-start | bytes 1105928 | tf_op jit(solution)/shard_map/ppermute | solution.py:24
  362.6 30.1 %collective-permute-start.52 = (bf16[256,2432]{1,0:T(8,128)(2,1)}, bf16[256,2432]{1,0:T(8,128)(2,1)}, u32[]{:S(2)}, u32[]{:S(2)}) collective-permute-start(bf16[256,2432]{1,0:T(8,128)(2,1)} %add_convert_fusion), channel_id=1, source_target_pairs={{0,2},{1,3},{2,0},{3,1},{4,6},{5,7},{6,4},{7,5},{8,10},{9,11},{10,... | collective-permute-start | bytes 3735560 | tf_op jit(solution)/shard_map/ppermute | solution.py:24
  365.8 26.0 %collective-permute-start.53 = (bf16[4,64,1440]{2,1,0:T(8,128)(2,1)S(1)}, bf16[4,64,1440]{2,1,0:T(8,128)(2,1)S(1)}, u32[]{:S(2)}, u32[]{:S(2)}) collective-permute-start(bf16[4,64,1440]{2,1,0:T(8,128)(2,1)S(1)} %maximum_select_fusion.3), channel_id=1, source_target_pairs={{0,4},{4,0},{8,12},{12,8},{16,20},{20,16},{24,28},{28,24},{1,5},{5... | collective-permute-start | bytes 2211848 | tf_op jit(solution)/shard_map/ppermute | solution.py:24
  393.6 18.4 %collective-permute-start.54 = (bf16[256,16]{1,0:T(8,128)(2,1)S(1)}, bf16[256,16]{1,0:T(8,128)(2,1)S(1)}, u32[]{:S(2)}, u32[]{:S(2)}) collective-permute-start(bf16[256,16]{1,0:T(8,128)(2,1)S(1)} %fusion.35), channel_id=1, source_target_pairs={{0,2},{1,3},{2,0},{3,1},{4,6},{5,7},{6,4},{7,5},{8,10},{9,11},{10,... | collective-permute-start | bytes 24584 | tf_op jit(solution)/shard_map/ppermute | solution.py:24
  394.5 17.5 %collective-permute-start.55 = (bf16[256,16]{1,0:T(8,128)(2,1)S(1)}, bf16[256,16]{1,0:T(8,128)(2,1)S(1)}, u32[]{:S(2)}, u32[]{:S(2)}) collective-permute-start(bf16[256,16]{1,0:T(8,128)(2,1)S(1)} %fusion.35), channel_id=1, source_target_pairs={{0,1},{1,0},{2,3},{3,2},{4,5},{5,4},{6,7},{7,6},{8,9},{9,8},{10,11... | collective-permute-start | bytes 24584 | tf_op jit(solution)/shard_map/ppermute | solution.py:24
  432.3 18.7 %collective-permute-start.64 = (bf16[2,80,576]{2,1,0:T(8,128)(2,1)S(1)}, bf16[2,80,576]{2,1,0:T(8,128)(2,1)S(1)}, u32[]{:S(2)}, u32[]{:S(2)}) collective-permute-start(bf16[2,80,576]{2,1,0:T(8,128)(2,1)S(1)} %maximum_select_fusion.8), channel_id=1, source_target_pairs={{0,16},{4,20},{8,24},{12,28},{16,0},{20,4},{24,8},{28,12},{1,17},{... | collective-permute-start | bytes 552968 | tf_op jit(solution)/shard_map/ppermute | solution.py:24
  459.7 19.7 %collective-permute-start.68 = (bf16[128,2304]{1,0:T(8,128)(2,1)}, bf16[128,2304]{1,0:T(8,128)(2,1)}, u32[]{:S(2)}, u32[]{:S(2)}) collective-permute-start(bf16[128,2304]{1,0:T(8,128)(2,1)} %get-tuple-element.509), channel_id=1, source_target_pairs={{0,2},{1,3},{2,0},{3,1},{4,6},{5,7},{6,4},{7,5},{8,10},{9,11},{10,... | collective-permute-start | bytes 1769480 | tf_op jit(solution)/shard_map/ppermute | solution.py:24
  462.1 17.3 %collective-permute-start.66 = (bf16[2,96,576]{2,1,0:T(8,128)(2,1)S(1)}, bf16[2,96,576]{2,1,0:T(8,128)(2,1)S(1)}, u32[]{:S(2)}, u32[]{:S(2)}) collective-permute-start(bf16[2,96,576]{2,1,0:T(8,128)(2,1)S(1)} %maximum_select_fusion.7), channel_id=1, source_target_pairs={{0,16},{4,20},{8,24},{12,28},{16,0},{20,4},{24,8},{28,12},{1,17},{... | collective-permute-start | bytes 663560 | tf_op jit(solution)/shard_map/ppermute | solution.py:24
  479.4 17.7 %collective-permute-start.71 = (bf16[256,2304]{1,0:T(8,128)(2,1)}, bf16[256,2304]{1,0:T(8,128)(2,1)S(1)}, u32[]{:S(2)}, u32[]{:S(2)}) collective-permute-start(bf16[256,2304]{1,0:T(8,128)(2,1)} %get-tuple-element.455), channel_id=1, source_target_pairs={{0,1},{1,0},{2,3},{3,2},{4,5},{5,4},{6,7},{7,6},{8,9},{9,8},{10,11... | collective-permute-start | bytes 3538952 | tf_op jit(solution)/shard_map/ppermute | solution.py:24
  480.4 16.2 %collective-permute-start.70 = (bf16[128,2304]{1,0:T(8,128)(2,1)S(1)}, bf16[128,2304]{1,0:T(8,128)(2,1)S(1)}, u32[]{:S(2)}, u32[]{:S(2)}) collective-permute-start(bf16[128,2304]{1,0:T(8,128)(2,1)S(1)} %copy-done.82), channel_id=1, source_target_pairs={{0,2},{1,3},{2,0},{3,1},{4,6},{5,7},{6,4},{7,5},{8,10},{9,11},{10,... | collective-permute-start | bytes 1769480 | tf_op jit(solution)/shard_map/ppermute | solution.py:24
  481.0 16.1 %collective-permute-start.69 = (bf16[4,96,576]{2,1,0:T(8,128)(2,1)S(1)}, bf16[4,96,576]{2,1,0:T(8,128)(2,1)S(1)}, u32[]{:S(2)}, u32[]{:S(2)}) collective-permute-start(bf16[4,96,576]{2,1,0:T(8,128)(2,1)S(1)} %maximum_select_fusion.4), channel_id=1, source_target_pairs={{0,4},{4,0},{8,12},{12,8},{16,20},{20,16},{24,28},{28,24},{1,5},{5... | collective-permute-start | bytes 1327112 | tf_op jit(solution)/shard_map/ppermute | solution.py:24
  483.4 20.2 %collective-permute-start.77 = (bf16[2,80,576]{2,1,0:T(8,128)(2,1)S(1)}, bf16[2,80,576]{2,1,0:T(8,128)(2,1)S(1)}, u32[]{:S(2)}, u32[]{:S(2)}) collective-permute-start(bf16[2,80,576]{2,1,0:T(8,128)(2,1)S(1)} %get-tuple-element.494), channel_id=1, source_target_pairs={{0,3},{1,2},{2,1},{3,0},{4,7},{5,6},{6,5},{7,4},{8,11},{9,10},{10,... | collective-permute-start | bytes 552968 | tf_op jit(solution)/shard_map/ppermute | solution.py:24
  483.5 24.0 %collective-permute-start.75 = (bf16[2,80,576]{2,1,0:T(8,128)(2,1)S(1)}, bf16[2,80,576]{2,1,0:T(8,128)(2,1)S(1)}, u32[]{:S(2)}, u32[]{:S(2)}) collective-permute-start(bf16[2,80,576]{2,1,0:T(8,128)(2,1)S(1)} %get-tuple-element.495), channel_id=1, source_target_pairs={{0,1},{1,0},{2,3},{3,2},{4,5},{5,4},{6,7},{7,6},{8,9},{9,8},{10,11... | collective-permute-start | bytes 552968 | tf_op jit(solution)/shard_map/ppermute | solution.py:24
  (147 other events, 1153.0 us)

commit v6 on v5

--- a/solution.py
+++ b/solution.py
@@ -82,13 +82,16 @@
     return jnp.where((rep_place // bit) % 2 == 0, low, high)
 
 
-def send_sums(everyone, chosen, place):
+def send_sums(everyone, chosen, place, rank):
     group = lax.axis_size("shard")
+    everyone = everyone.reshape(everyone.shape[0], -1, rank, everyone.shape[2])
     per = chosen.shape[1] // group
     sent = []
     for j in range(group):
         marks = lax.dynamic_slice_in_dim(chosen, (place ^ j) * per, per, 1)
-        sums = jnp.sum(marks[:, :, None, None] * everyone[:, None].astype(F32), axis=0).astype(BF16)
+        sums = jnp.sum(
+            marks[:, None, :, None, None] * everyone[:, :, None].astype(F32), axis=0
+        ).astype(BF16)
         sent.append(hop(sums, "shard", j) if j else sums)
     return sent
 
@@ -763,8 +766,6 @@
     )
     first_b_four = hop(first_b_two, "rep", 2)
     mlp_leaving = [side(gate_up, rep_place % 4 * quarter, quarter, place ^ j, ff_cols) for j in (2, 3)]
-    mlp_near_out = side(gate_up, 0, k_rows, place ^ 1, ff_cols)
-    mlp_own = side(gate_up, 0, k_rows, place, ff_cols)
     grad_feed = (BRANCH * grad_out).astype(BF16)
     half = HDIM // 2
     frequency = jnp.exp(jnp.arange(half, dtype=F32) * (-2.0 / HDIM) * math.log(THETA))
@@ -781,11 +782,11 @@
         [jnp.pad(b_first[i], ((0, 0), (i * head_cols, (2 - i) * head_cols))) for i in range(3)]
     )
     (
-        normed_far, first_a_four, first_b_four, mlp_leaving, mlp_near_out, mlp_own, grad_feed, b_wide, a_first,
-        rest_part, wide_part, tables,
+        normed_far, first_a_four, first_b_four, mlp_leaving, grad_feed, b_wide, a_first, rest_part, wide_part,
+        tables,
     ) = fence(
-        normed_far, first_a_four, first_b_four, mlp_leaving, mlp_near_out, mlp_own, grad_feed, b_wide, a_first,
-        rest_part, wide_part, tables,
+        normed_far, first_a_four, first_b_four, mlp_leaving, grad_feed, b_wide, a_first, rest_part, wide_part,
+        tables,
     )
     cosine, sine, cosine_pair, sine_pair = tables
     first_blocks = (normed, normed_near, normed_far, core(normed_far))
@@ -816,14 +817,15 @@
     b_out, b_down = rest[3], rest[4]
     far_out = close_attention(mixed, place, attention_output_weight, a_out, (2, 3), rows)
     far_sum = (far_out[0].astype(F32) + core(far_out[1]).astype(F32)).astype(BF16)
-    far_sum, mixed_here, grad_feed, wide_far, mlp_near_out = fence(
-        far_sum, mixed, grad_feed, wide_far, mlp_near_out
-    )
+    far_sum, mixed_here, grad_feed, wide_far = fence(far_sum, mixed, grad_feed, wide_far)
     branch_low, far_rest = across(far_sum[: rows // 2]), far_sum[rows // 2 :]
     feed_near_in = core(grad_feed)
     near_out = close_attention(mixed_here, place, attention_output_weight, a_out, (0, 1), rows)
-    near_out, mlp_b_two, mlp_b_three, branch_low, far_rest = fence(
-        near_out, mlp_b_two, mlp_b_three, branch_low, far_rest
+    near_out, gate_up = fence(near_out, gate_up)
+    mlp_near_out = side(gate_up, 0, k_rows, place ^ 1, ff_cols)
+    mlp_own = side(gate_up, 0, k_rows, place, ff_cols)
+    near_out, mlp_b_two, mlp_b_three, branch_low, far_rest, mlp_near_out, mlp_own = fence(
+        near_out, mlp_b_two, mlp_b_three, branch_low, far_rest, mlp_near_out, mlp_own
     )
     mlp_a_four, mlp_b_four = hop(mlp_a_two, "rep", 1), hop(mlp_b_two, "rep", 2)
     branch_high = across(far_rest)
@@ -909,9 +911,10 @@
         (branch_rows, branch_near_in), second_blocks[:2], (0, 1), place, mixed,
         attention_output_weight, a_out, b_out,
     )
-    branch_far_in, mixed_near, wide_hop = fence(branch_far_in, mixed_near, wide_hop)
+    mixed_near, wide_hop = fence(mixed_near, wide_hop)
     wide_all = both(wide_all, wide_hop, rep_place, bits[-2])
     wide_hop = hop(wide_all, "rep", bits[-1])
+    branch_far_in, mixed_near, wide_all = fence(branch_far_in, mixed_near, wide_all)
     feed_from_far = across(after(feed_sum, branch_far_in))
     mixed_far, grad_a_far, thin_far = open_attention(
         (branch_far_in, core(branch_far_in)), second_blocks[2:], (2, 3), place, mixed,
@@ -935,7 +938,7 @@
     picks = wide_all[:, -1, :1].astype(F32)
     adapters = adapter_model_input_maps.shape[1] * group
     chosen = (picks == jnp.arange(adapters, dtype=jnp.int32).astype(F32)[None, :]).astype(F32)
-    wide_sent = send_sums(wide_all[:, :-rank], chosen, place)
+    wide_sent = send_sums(wide_all[:, :-rank], chosen, place, rank)
     feed_own = feed_here + feed_from_far.astype(F32)
     narrow_down = feed_own[:, width : width + rank].astype(BF16)
     down_far = across(narrow_down)
@@ -993,21 +996,21 @@
     late_all = both(late_all, late_hop, rep_place, bits[-2])
     late_all, early_hop, early_all = fence(late_all, early_hop, early_all)
     late_hop = hop(late_all, "rep", bits[-1])
-    early_sent = send_sums(both(early_all, early_hop, rep_place, bits[-1]), chosen, place)
-
-    def whole_maps(stacked, low, high, n):
-        part = stacked[:, :, low:high].reshape(group, stacked.shape[1], -1, rank, n)
+    early_sent = send_sums(both(early_all, early_hop, rep_place, bits[-1]), chosen, place, rank)
+
+    def whole_maps(stacked, low, high):
+        part = stacked[:, low // rank : high // rank]
         pieces = [lax.dynamic_index_in_dim(part, place ^ i, 0, keepdims=False) for i in range(group)]
-        return jnp.concatenate(pieces, axis=-1).transpose(1, 0, 2, 3).astype(F32)
+        return jnp.concatenate(pieces, axis=-1).astype(F32)
 
     feed = feed_here[:, :width] + feed_from_far[:, :width].astype(F32) + dot(narrow_down, b_down)
     output = (middle + BRANCH * feed).astype(BF16)
-    hidden_maps = whole_maps(jnp.stack(wide_sent), 0, 3 * rank, ff_cols)
+    hidden_maps = whole_maps(jnp.stack(wide_sent), 0, 3 * rank)
     late_hop, hidden_maps, output, back_high, back_rows_here = fence(
         late_hop, hidden_maps, output, back_high, back_rows_here
     )
     back_far_in = jnp.concatenate([back_low, back_high])
-    late_sent = send_sums(both(late_all, late_hop, rep_place, bits[-1]), chosen, place)
+    late_sent = send_sums(both(late_all, late_hop, rep_place, bits[-1]), chosen, place, rank)
     narrow_own = lax.dynamic_slice_in_dim(grad_narrow, place * rows, rows, 1)
     grad_normed = (
         back_rows_near[0].astype(F32) + back_rows_here.astype(F32) + back_far_in.astype(F32)
@@ -1019,16 +1022,16 @@
     late_got = jnp.stack(late_sent)
     grad_a_model = jnp.concatenate(
         [
-            whole_maps(late_got, 0, 3 * rank, head_cols),
-            whole_maps(early_got, 0, rank, head_cols),
-            whole_maps(early_got, 2 * rank, 4 * rank, head_cols),
+            whole_maps(late_got, 0, 3 * rank),
+            whole_maps(early_got, 0, rank),
+            whole_maps(early_got, 2 * rank, 4 * rank),
         ]
     )
     grad_b_model = jnp.concatenate(
         [
-            whole_maps(late_got, 3 * rank, 6 * rank, head_cols),
-            whole_maps(early_got, rank, 2 * rank, head_cols),
-            whole_maps(early_got, 4 * rank, 5 * rank, head_cols),
+            whole_maps(late_got, 3 * rank, 6 * rank),
+            whole_maps(early_got, rank, 2 * rank),
+            whole_maps(early_got, 4 * rank, 5 * rank),
         ]
     )
     return (

time: 527 us -> 525 us (level)
  waiting for transfers between devices: 142 us -> 134 us
  other arithmetic: 37.2 us -> 42.7 us
    ppermute x78, waiting for transfers between devices: 142 us -> 134 us  [hop(): return lax.ppermute(values, axis, [(i, i ^ bit) for i in range(size)])]
    unnamed x236 -> x229, local copies, waits for them, and re-layouts: 29.4 us -> 25.6 us
  transfers between devices with their start and end apart: 78 -> 78, of which waited for: 32 -> 31; matrix products, arithmetic and copies ran while one was open for 12% -> 13% of each run, Pallas kernels for 32% -> 31%
where the time goes in v6:
time: 525 us; the launch traced here: 517 us
  Pallas kernels  199 us (38%)
  waiting for transfers between devices  134 us (26%)
  starting transfers between devices  65.1 us (12%)
  local copies, waits for them, and re-layouts  65 us (12%)
  other arithmetic  42.7 us (8%)
  matrix products  7.92 us (2%)
    ppermute x78, waiting for transfers between devices, hop(): return lax.ppermute(values, axis, [(i, i ^ bit) for i in range(size)])  134 us
    pallas_call x2, Pallas kernels, feed_forward(): call(kernel, [out] * (2 * count) + [jax.ShapeDtypeStruct((3 * rank, size)...  71.4 us
    ppermute x78, starting transfers between devices, hop(): return lax.ppermute(values, axis, [(i, i ^ bit) for i in range(size)])  65.1 us
    pallas_call x3, Pallas kernels, attend_back(): call(kernel, [jax.ShapeDtypeStruct((heads, length, HDIM), BF16)] * 3 + [j...  35.8 us
    unnamed x229, local copies, waits for them, and re-layouts  25.6 us
    pallas_call x2, Pallas kernels, project_back(): call(kernel, [jax.ShapeDtypeStruct((rows, width), BF16)] * count, [smem()...  24.7 us
    pallas_call x1, Pallas kernels, project(): call(kernel, [by_heads] * 3 + [jax.ShapeDtypeStruct((thin, rows * count),...  21 us
    pallas_call x1, Pallas kernels, attend(): call(kernel, [jax.ShapeDtypeStruct(query.shape, BF16), jax.ShapeDtypeStru...  15.8 us
  transfers between devices with their start and end apart: 78, of which 31 were waited for; matrix products, arithmetic and copies ran while one was open for 13% of the time, Pallas kernels for 31%

profile of v6, /device:TPU:0, one launch (start us, length us, event | category | flops | bytes accessed | tf_op | source)
XLA Modules:
  0.0 517.0 jit_solution(2165704468202056408)
XLA Ops:
  1.4 2.0 fusion.48
  5.2 3.6 sides_far.1
  8.9 2.6 collective-permute-start
  29.0 7.0 %sides_near.1 = (bf16[576,1728]{1,0:T(8,128)(2,1)}, bf16[576,1728]{1,0:T(8,128)(2,1)}) custom-call(s32[2]{0:T(128)} %get-tuple-element.575.where_ref, bf16[3,576,2304]{2,1,0:T(8,128)(2,1)} %w_ref.4), custom_call_target="tpu_custom_call" | custom-call | bytes 11943936 | tf_op jit(solution)/shard_map/sides_near/pallas_call | solution.py:143
  36.1 3.3 collective-permute-done.2.refs_10_.refs_15_
  49.6 7.0 %collective-permute-done.4.refs_12_.refs_17_ = bf16[144,1728]{1,0:T(8,128)(2,1)S(1)} collective-permute-done((bf16[144,1728]{1,0:T(8,128)(2,1)}, bf16[144,1728]{1,0:T(8,128)(2,1)S(1)}, u32[]{:S(2)}, u32[]{:S(2)}) %collective-permute-start.4) | collective-permute-done | bytes 497696 | tf_op jit(solution)/shard_map/ppermute | solution.py:24
  61.8 3.6 constant_dynamic-slice_fusion.9
  70.1 8.7 %collective-permute-done.11.refs_13_.refs_18_ = bf16[144,1728]{1,0:T(8,128)(2,1)S(1)} collective-permute-done((bf16[144,1728]{1,0:T(8,128)(2,1)S(1)}, bf16[144,1728]{1,0:T(8,128)(2,1)S(1)}, u32[]{:S(2)}, u32[]{:S(2)}) %collective-permute-start.11) | collective-permute-done | bytes 497696 | tf_op jit(solution)/shard_map/ppermute | solution.py:24
  78.9 6.5 %collective-permute-done.9.refs_2_ = bf16[256,2304]{1,0:T(8,128)(2,1)S(1)} collective-permute-done((bf16[256,2304]{1,0:T(8,128)(2,1)S(1)}, bf16[256,2304]{1,0:T(8,128)(2,1)S(1)}, u32[]{:S(2)}, u32[]{:S(2)}) %collective-permute-start.9) | collective-permute-done | bytes 1179680 | tf_op jit(solution)/shard_map/ppermute | solution.py:24
  88.9 21.0 %project.1 = (bf16[9,1024,64]{2,1,0:T(8,128)(2,1)}, bf16[9,1024,64]{2,1,0:T(8,128)(2,1)}, bf16[9,1024,64]{2,1,0:T(8,128)(2,1)}, bf16[48,1024]{1,0:T(8,128)(2,1)}) custom-call(s32[1]{0:T(128)} %bitcast.place_ref, s32[10]{0:T(128)} %stack.110.offsets_ref, bf16[256,2304]{1,0:T(8,128)(2,1)} %copy-done.9, bf16[256,2304]{1,0:T(8,128)(2,1)} %copy-done.20, ...), custom_call_target="tpu_custom_call" | custom-call | flops 8153726976 | bytes 19759104 | tf_op jit(solution)/shard_map/project/pallas_call | solution.py:255
  113.6 15.8 %attend.1 = (bf16[9,1024,64]{2,1,0:T(8,128)(2,1)}, f32[9,1,1024]{2,1,0:T(1,128)}) custom-call(s32[2]{0:T(128)} %bitcast.170, bf16[9,1024,64]{2,1,0:T(8,128)(2,1)} %get-tuple-element.280.q_ref, bf16[9,1024,64]{2,1,0:T(8,128)(2,1)} %get-tuple-element.281.k_ref, bf16[9,1024,64]{2,1,0:T(8,128)(2,1)} %get-tuple-element.282.v_ref), custom_call_target="tpu_custom_call" | custom-call | flops 9663676416 | bytes 9437184 | tf_op jit(solution)/shard_map/attend/pallas_call | solution.py:349
  137.1 2.2 close_attention.2
  143.8 4.6 collective-permute-done.24
  153.9 2.2 close_attention.3
  156.1 9.0 %constant_dynamic-slice_fusion.4 = (bf16[2,576,1440]{2,1,0:T(8,128)(2,1)}, bf16[2,576,1440]{2,1,0:T(8,128)(2,1)S(1)}) fusion(bf16[2,576,5760]{2,1,0:T(8,128)(2,1)} %param.22, s32[]{:T(128)S(6)} %select_n.365, s32[]{:T(128)S(6)} %select_n.364), kind=kLoop, calls=%fused_computation.177 | loop fusion | bytes 13271048 | tf_op jit(solution)/shard_map/dynamic_slice | solution.py:121
  169.7 12.0 %collective-permute-done.29 = bf16[128,2432]{1,0:T(8,128)(2,1)S(1)} collective-permute-done((bf16[128,2432]{1,0:T(8,128)(2,1)S(1)}, bf16[128,2432]{1,0:T(8,128)(2,1)S(1)}, u32[]{:S(2)}, u32[]{:S(2)}) %collective-permute-start.29) | collective-permute-done | bytes 622624 | tf_op jit(solution)/shard_map/ppermute | solution.py:24
  191.6 11.7 %collective-permute-done.38 = bf16[128,2304]{1,0:T(8,128)(2,1)S(1)} collective-permute-done((bf16[128,2304]{1,0:T(8,128)(2,1)S(1)}, bf16[128,2304]{1,0:T(8,128)(2,1)S(1)}, u32[]{:S(2)}, u32[]{:S(2)}) %collective-permute-start.38) | collective-permute-done | bytes 589856 | tf_op jit(solution)/shard_map/ppermute | solution.py:24
  205.6 35.9 %feed_forward.2 = (bf16[256,2432]{1,0:T(8,128)(2,1)}, bf16[256,2432]{1,0:T(8,128)(2,1)}, bf16[256,2432]{1,0:T(8,128)(2,1)}, bf16[256,2432]{1,0:T(8,128)(2,1)}, f32[48,1440]{1,0:T(8,128)}) custom-call(s32[10]{0:T(128)} %stack.110.offsets_ref, bf16[256,2304]{1,0:T(8,128)(2,1)} %copy-done.7, bf16[256,2304]{1,0:T(8,128)(2,1)} %copy-done.28, ...), custom_call_target="tpu_custom_call" | custom-call | flops 20384317440 | bytes 29343744 | tf_op jit(solution)/shard_map/feed_forward/pallas_call | solution.py:624
  242.2 2.3 collective-permute-done.40.refs_3_
  247.3 35.5 %feed_forward.3 = (bf16[256,2432]{1,0:T(8,128)(2,1)}, bf16[256,2432]{1,0:T(8,128)(2,1)}, bf16[256,2432]{1,0:T(8,128)(2,1)}, bf16[256,2432]{1,0:T(8,128)(2,1)}, f32[48,1440]{1,0:T(8,128)}) custom-call(s32[10]{0:T(128)} %stack.110.offsets_ref, bf16[256,2304]{1,0:T(8,128)(2,1)} %copy-done.24, bf16[256,2304]{1,0:T(8,128)(2,1)} %copy-done.26, ...), custom_call_target="tpu_custom_call" | custom-call | flops 20384317440 | bytes 29343744 | tf_op jit(solution)/shard_map/feed_forward/pallas_call | solution.py:624
  284.0 2.1 collective-permute-done.41
  286.1 2.0 add_convert_fusion.1
  290.8 14.5 %collective-permute-done.42 = bf16[128,2432]{1,0:T(8,128)(2,1)S(1)} collective-permute-done((bf16[128,2432]{1,0:T(8,128)(2,1)S(1)}, bf16[128,2432]{1,0:T(8,128)(2,1)S(1)}, u32[]{:S(2)}, u32[]{:S(2)}) %collective-permute-start.42) | collective-permute-done | bytes 622624 | tf_op jit(solution)/shard_map/ppermute | solution.py:24
  308.9 11.9 %collective-permute-done.46 = bf16[128,2432]{1,0:T(8,128)(2,1)S(1)} collective-permute-done((bf16[128,2432]{1,0:T(8,128)(2,1)S(1)}, bf16[128,2432]{1,0:T(8,128)(2,1)S(1)}, u32[]{:S(2)}, u32[]{:S(2)}) %collective-permute-start.46) | collective-permute-done | bytes 622624 | tf_op jit(solution)/shard_map/ppermute | solution.py:24
  323.0 2.5 multiply_convert_fusion
  325.5 3.5 concatenate.265.refs_0_
  330.3 2.6 collective-permute-start.50
  338.5 6.1 %open_attention.2 = (bf16[9,512,64]{2,1,0:T(8,128)(2,1)S(1)}, f32[16,576]{1,0:T(8,128)S(1)}, f32[48,2304]{1,0:T(8,128)S(1)}) custom-call(s32[1]{0:T(128)} %bitcast.place_ref, bf16[256,2432]{1,0:T(8,128)(2,1)S(1)} %copy-done.6, bf16[256,2432]{1,0:T(8,128)(2,1)} %collective-permute-done.49.refs_1_, bf16[256,2304]{1,0:T(8,128)(2,1)S(1)} %copy-done.8, ...), custom_call_target="tpu_custom_call" | custom-call | flops 1358954496 | bytes 8552448 | tf_op jit(solution)/shard_map/open_attention/pallas_call | solution.py:551
  345.6 5.6 %collective-permute-done.50 = bf16[2,64,1440]{2,1,0:T(8,128)(2,1)} collective-permute-done((bf16[2,64,1440]{2,1,0:T(8,128)(2,1)}, bf16[2,64,1440]{2,1,0:T(8,128)(2,1)}, u32[]{:S(2)}, u32[]{:S(2)}) %collective-permute-start.50) | collective-permute-done | bytes 368672 | tf_op jit(solution)/shard_map/ppermute | solution.py:24
  351.2 2.6 maximum_select_fusion.3
  353.7 5.4 %collective-permute-done.48.refs_0_ = bf16[256,2432]{1,0:T(8,128)(2,1)} collective-permute-done((bf16[256,2432]{1,0:T(8,128)(2,1)}, bf16[256,2432]{1,0:T(8,128)(2,1)}, u32[]{:S(2)}, u32[]{:S(2)}) %collective-permute-start.48) | collective-permute-done | bytes 1245216 | tf_op jit(solution)/shard_map/ppermute | solution.py:24
  366.7 6.6 %open_attention.3 = (bf16[9,512,64]{2,1,0:T(8,128)(2,1)S(1)}, f32[16,576]{1,0:T(8,128)S(1)}, f32[48,2304]{1,0:T(8,128)S(1)}) custom-call(s32[1]{0:T(128)} %bitcast.place_ref, bf16[256,2432]{1,0:T(8,128)(2,1)} %collective-permute-done.48.refs_0_, bf16[256,2432]{1,0:T(8,128)(2,1)} %collective-permute-done.51.refs_1_, bf16[256,2304]{1,0:T(8,128)(2,1)S(1)} %copy-done.25, ...), custom_call_target="tpu_custom_call" | custom-call | flops 1358954496 | bytes 8552448 | tf_op jit(solution)/shard_map/open_attention/pallas_call | solution.py:551
  375.1 11.9 %attend_back.3 = (bf16[3,1024,64]{2,1,0:T(8,128)(2,1)S(1)}, bf16[3,1024,64]{2,1,0:T(8,128)(2,1)S(1)}, bf16[3,1024,64]{2,1,0:T(8,128)(2,1)S(1)}, f32[48,1024]{1,0:T(8,128)S(1)}, f32[48,192]{1,0:T(8,128)S(1)}) custom-call(s32[2]{0:T(128)S(1)} %bitcast.171, s32[1]{0:T(128)} %bitcast.place_ref, bf16[9,1024,64]{2,1,0:T(8,128)(2,1)S(1)} %copy-done.35, ...), custom_call_target="tpu_custom_call" | custom-call | flops 8053063680 | bytes 6291456 | tf_op jit(solution)/shard_map/attend_back/pallas_call | solution.py:456
  387.0 2.3 collective-permute-done.52
  395.3 12.1 %attend_back.4 = (bf16[3,1024,64]{2,1,0:T(8,128)(2,1)S(1)}, bf16[3,1024,64]{2,1,0:T(8,128)(2,1)S(1)}, bf16[3,1024,64]{2,1,0:T(8,128)(2,1)S(1)}, f32[48,1024]{1,0:T(8,128)S(1)}, f32[48,192]{1,0:T(8,128)S(1)}) custom-call(s32[2]{0:T(128)S(1)} %bitcast.172, s32[1]{0:T(128)} %bitcast.place_ref, bf16[9,1024,64]{2,1,0:T(8,128)(2,1)S(1)} %copy-done.35, ...), custom_call_target="tpu_custom_call" | custom-call | flops 8053063680 | bytes 6291456 | tf_op jit(solution)/shard_map/attend_back/pallas_call | solution.py:456
  413.2 11.9 %attend_back.5 = (bf16[3,1024,64]{2,1,0:T(8,128)(2,1)S(1)}, bf16[3,1024,64]{2,1,0:T(8,128)(2,1)S(1)}, bf16[3,1024,64]{2,1,0:T(8,128)(2,1)S(1)}, f32[48,1024]{1,0:T(8,128)S(1)}, f32[48,192]{1,0:T(8,128)S(1)}) custom-call(s32[2]{0:T(128)S(1)} %bitcast.173, s32[1]{0:T(128)} %bitcast.place_ref, bf16[9,1024,64]{2,1,0:T(8,128)(2,1)S(1)} %copy-done.35, ...), custom_call_target="tpu_custom_call" | custom-call | flops 8053063680 | bytes 6291456 | tf_op jit(solution)/shard_map/attend_back/pallas_call | solution.py:456
  428.2 3.4 collective-permute-start.64
  431.7 2.2 thin_product.1
  434.9 12.4 %project_back.2 = (bf16[256,2304]{1,0:T(8,128)(2,1)}, bf16[256,2304]{1,0:T(8,128)(2,1)}) custom-call(s32[1]{0:T(128)} %bitcast.place_ref, s32[10]{0:T(128)} %stack.110.offsets_ref, bf16[3,1024,64]{2,1,0:T(8,128)(2,1)} %copy-done.11, bf16[3,1024,64]{2,1,0:T(8,128)(2,1)} %copy-done.14, bf16[3,1024,64]{2,1,0:T(8,128)(2,1)} %copy-done.17, ...), custom_call_target="tpu_custom_call" | custom-call | flops 4076863488 | bytes 12091392 | tf_op jit(solution)/shard_map/project_back/pallas_call | solution.py:661
  448.3 2.2 collective-permute-done.65
  454.5 3.4 collective-permute-start.66
  458.7 12.4 %project_back.3 = (bf16[256,2304]{1,0:T(8,128)(2,1)}, bf16[256,2304]{1,0:T(8,128)(2,1)}) custom-call(s32[1]{0:T(128)} %bitcast.place_ref, s32[10]{0:T(128)} %stack.110.offsets_ref, bf16[3,1024,64]{2,1,0:T(8,128)(2,1)} %copy-done.11, bf16[3,1024,64]{2,1,0:T(8,128)(2,1)} %copy-done.14, bf16[3,1024,64]{2,1,0:T(8,128)(2,1)} %copy-done.17, ...), custom_call_target="tpu_custom_call" | custom-call | flops 4076863488 | bytes 12091392 | tf_op jit(solution)/shard_map/project_back/pallas_call | solution.py:661
  471.8 2.9 add_convert_fusion.3
  482.2 11.2 %collective-permute-done.70 = bf16[128,2304]{1,0:T(8,128)(2,1)S(1)} collective-permute-done((bf16[128,2304]{1,0:T(8,128)(2,1)S(1)}, bf16[128,2304]{1,0:T(8,128)(2,1)S(1)}, u32[]{:S(2)}, u32[]{:S(2)}) %collective-permute-start.70) | collective-permute-done | bytes 589856 | tf_op jit(solution)/shard_map/ppermute | solution.py:24
  498.1 2.5 fusion.11
  501.3 2.0 fusion.10
  504.5 2.0 collective-permute-done.74
  506.5 5.7 %collective-permute-done.73 = bf16[6,2,16,576]{3,2,1,0:T(8,128)(2,1)S(1)} collective-permute-done((bf16[6,2,16,576]{3,2,1,0:T(8,128)(2,1)S(1)}, bf16[6,2,16,576]{3,2,1,0:T(8,128)(2,1)S(1)}, u32[]{:S(2)}, u32[]{:S(2)}) %collective-permute-start.73) | collective-permute-done | bytes 221216 | tf_op jit(solution)/shard_map/ppermute | solution.py:24
  (487 shorter events, 151.4 us)
Async XLA Ops:
  4.2 19.2 %collective-permute-start.1 = (bf16[6,16,2304]{2,1,0:T(8,128)(2,1)}, bf16[6,16,2304]{2,1,0:T(8,128)(2,1)}, u32[]{:S(2)}, u32[]{:S(2)}) collective-permute-start(bf16[6,16,2304]{2,1,0:T(8,128)(2,1)} %fusion.20), channel_id=1, source_target_pairs={{0,1},{1,0},{2,3},{3,2},{4,5},{5,4},{6,7},{7,6},{8,9},{9,8},{10,11... | collective-permute-start | bytes 1327112 | tf_op jit(solution)/shard_map/ppermute | solution.py:24
  8.9 15.8 %collective-permute-start = (bf16[144,1728]{1,0:T(8,128)(2,1)}, bf16[144,1728]{1,0:T(8,128)(2,1)S(1)}, u32[]{:S(2)}, u32[]{:S(2)}) collective-permute-start(bf16[144,1728]{1,0:T(8,128)(2,1)} %get-tuple-element.244), channel_id=1, source_target_pairs={{0,2},{1,3},{2,0},{3,1},{4,6},{5,7},{6,4},{7,5},{8,10},{9,11},{10,... | collective-permute-start | bytes 1493000 | tf_op jit(solution)/shard_map/ppermute | solution.py:24
  25.6 16.6 %collective-permute-start.7 = (bf16[144,1728]{1,0:T(8,128)(2,1)S(1)}, bf16[144,1728]{1,0:T(8,128)(2,1)}, u32[]{:S(2)}, u32[]{:S(2)}) collective-permute-start(bf16[144,1728]{1,0:T(8,128)(2,1)S(1)} %collective-permute-done.refs_6_.refs_11_), channel_id=1, source_target_pairs={{0,4},{4,0},{8,12},{12,8},{16,20},{20,16},{24,28},{28,24},{1,5},{5... | collective-permute-start | bytes 1493000 | tf_op jit(solution)/shard_map/ppermute | solution.py:24
  27.4 16.5 %collective-permute-start.6 = (bf16[144,1728]{1,0:T(8,128)(2,1)S(1)}, bf16[144,1728]{1,0:T(8,128)(2,1)}, u32[]{:S(2)}, u32[]{:S(2)}) collective-permute-start(bf16[144,1728]{1,0:T(8,128)(2,1)S(1)} %collective-permute-done.refs_6_.refs_11_), channel_id=1, source_target_pairs={{0,8},{4,12},{8,0},{12,4},{16,24},{20,28},{24,16},{28,20},{1,9},{5... | collective-permute-start | bytes 1493000 | tf_op jit(solution)/shard_map/ppermute | solution.py:24
  29.0 58.9 %collective-permute-start.8 = (bf16[256,2304]{1,0:T(8,128)(2,1)S(1)}, bf16[256,2304]{1,0:T(8,128)(2,1)S(1)}, u32[]{:S(2)}, u32[]{:S(2)}) collective-permute-start(bf16[256,2304]{1,0:T(8,128)(2,1)S(1)} %fusion.7.refs_0_), channel_id=1, source_target_pairs={{0,1},{1,0},{2,3},{3,2},{4,5},{5,4},{6,7},{7,6},{8,9},{9,8},{10,11... | collective-permute-start | bytes 3538952 | tf_op jit(solution)/shard_map/ppermute | solution.py:24
  47.2 19.1 %collective-permute-start.14 = (bf16[3,16,5760]{2,1,0:T(8,128)(2,1)S(1)}, bf16[3,16,5760]{2,1,0:T(8,128)(2,1)S(1)}, u32[]{:S(2)}, u32[]{:S(2)}) collective-permute-start(bf16[3,16,5760]{2,1,0:T(8,128)(2,1)S(1)} %fusion.16), channel_id=1, source_target_pairs={{0,1},{1,0},{2,3},{3,2},{4,5},{5,4},{6,7},{7,6},{8,9},{9,8},{10,11... | collective-permute-start | bytes 1658888 | tf_op jit(solution)/shard_map/ppermute | solution.py:24
  49.4 38.5 %collective-permute-start.16 = (bf16[576,1728]{1,0:T(8,128)(2,1)}, bf16[576,1728]{1,0:T(8,128)(2,1)}, u32[]{:S(2)}, u32[]{:S(2)}) collective-permute-start(bf16[576,1728]{1,0:T(8,128)(2,1)} %get-tuple-element.267), channel_id=1, source_target_pairs={{0,1},{1,0},{2,3},{3,2},{4,5},{5,4},{6,7},{7,6},{8,9},{9,8},{10,11... | collective-permute-start | bytes 5971976 | tf_op jit(solution)/shard_map/ppermute | solution.py:24
  58.1 27.2 %collective-permute-start.9 = (bf16[256,2304]{1,0:T(8,128)(2,1)S(1)}, bf16[256,2304]{1,0:T(8,128)(2,1)S(1)}, u32[]{:S(2)}, u32[]{:S(2)}) collective-permute-start(bf16[256,2304]{1,0:T(8,128)(2,1)S(1)} %fusion.7.refs_0_), channel_id=1, source_target_pairs={{0,2},{1,3},{2,0},{3,1},{4,6},{5,7},{6,4},{7,5},{8,10},{9,11},{10,... | collective-permute-start | bytes 3538952 | tf_op jit(solution)/shard_map/ppermute | solution.py:24
  85.4 24.5 %collective-permute-start.17 = (bf16[2,144,1440]{2,1,0:T(8,128)(2,1)}, bf16[2,144,1440]{2,1,0:T(8,128)(2,1)}, u32[]{:S(2)}, u32[]{:S(2)}) collective-permute-start(bf16[2,144,1440]{2,1,0:T(8,128)(2,1)} %get-tuple-element.277), channel_id=1, source_target_pairs={{0,2},{1,3},{2,0},{3,1},{4,6},{5,7},{6,4},{7,5},{8,10},{9,11},{10,... | collective-permute-start | bytes 2488328 | tf_op jit(solution)/shard_map/ppermute | solution.py:24
  87.6 41.8 %collective-permute-start.18 = (bf16[2,144,1440]{2,1,0:T(8,128)(2,1)}, bf16[2,144,1440]{2,1,0:T(8,128)(2,1)}, u32[]{:S(2)}, u32[]{:S(2)}) collective-permute-start(bf16[2,144,1440]{2,1,0:T(8,128)(2,1)} %get-tuple-element.284), channel_id=1, source_target_pairs={{0,3},{1,2},{2,1},{3,0},{4,7},{5,6},{6,5},{7,4},{8,11},{9,10},{10,... | collective-permute-start | bytes 2488328 | tf_op jit(solution)/shard_map/ppermute | solution.py:24
  109.9 22.2 %collective-permute-start.20 = (bf16[2,144,1440]{2,1,0:T(8,128)(2,1)}, bf16[2,144,1440]{2,1,0:T(8,128)(2,1)S(1)}, u32[]{:S(2)}, u32[]{:S(2)}) collective-permute-start(bf16[2,144,1440]{2,1,0:T(8,128)(2,1)} %collective-permute-done.17.refs_6_), channel_id=1, source_target_pairs={{0,4},{4,0},{8,12},{12,8},{16,20},{20,16},{24,28},{28,24},{1,5},{5... | collective-permute-start | bytes 2488328 | tf_op jit(solution)/shard_map/ppermute | solution.py:24
  111.2 21.8 %collective-permute-start.19 = (bf16[2,144,1440]{2,1,0:T(8,128)(2,1)}, bf16[2,144,1440]{2,1,0:T(8,128)(2,1)S(1)}, u32[]{:S(2)}, u32[]{:S(2)}) collective-permute-start(bf16[2,144,1440]{2,1,0:T(8,128)(2,1)} %collective-permute-done.17.refs_6_), channel_id=1, source_target_pairs={{0,8},{4,12},{8,0},{12,4},{16,24},{20,28},{24,16},{28,20},{1,9},{5... | collective-permute-start | bytes 2488328 | tf_op jit(solution)/shard_map/ppermute | solution.py:24
  112.1 18.5 %collective-permute-start.21 = (bf16[5,8,2304]{2,1,0:T(8,128)(2,1)S(1)}, bf16[5,8,2304]{2,1,0:T(8,128)(2,1)S(1)}, u32[]{:S(2)}, u32[]{:S(2)}) collective-permute-start(bf16[5,8,2304]{2,1,0:T(8,128)(2,1)S(1)} %copy-done.99), channel_id=1, source_target_pairs={{0,2},{1,3},{2,0},{3,1},{4,6},{5,7},{6,4},{7,5},{8,10},{9,11},{10,... | collective-permute-start | bytes 552968 | tf_op jit(solution)/shard_map/ppermute | solution.py:24
  141.0 24.1 %collective-permute-start.26 = (bf16[2,144,1440]{2,1,0:T(8,128)(2,1)}, bf16[2,144,1440]{2,1,0:T(8,128)(2,1)}, u32[]{:S(2)}, u32[]{:S(2)}) collective-permute-start(bf16[2,144,1440]{2,1,0:T(8,128)(2,1)} %collective-permute-done.18.refs_10_), channel_id=1, source_target_pairs={{0,8},{4,12},{8,0},{12,4},{16,24},{20,28},{24,16},{28,20},{1,9},{5... | collective-permute-start | bytes 2488328 | tf_op jit(solution)/shard_map/ppermute | solution.py:24
  142.6 23.1 %collective-permute-start.25 = (bf16[2,144,1440]{2,1,0:T(8,128)(2,1)}, bf16[2,144,1440]{2,1,0:T(8,128)(2,1)}, u32[]{:S(2)}, u32[]{:S(2)}) collective-permute-start(bf16[2,144,1440]{2,1,0:T(8,128)(2,1)} %collective-permute-done.18.refs_10_), channel_id=1, source_target_pairs={{0,4},{4,0},{8,12},{12,8},{16,20},{20,16},{24,28},{28,24},{1,5},{5... | collective-permute-start | bytes 2488328 | tf_op jit(solution)/shard_map/ppermute | solution.py:24
  149.5 16.1 %collective-permute-start.27 = (bf16[128,2432]{1,0:T(8,128)(2,1)}, bf16[128,2432]{1,0:T(8,128)(2,1)}, u32[]{:S(2)}, u32[]{:S(2)}) collective-permute-start(bf16[128,2432]{1,0:T(8,128)(2,1)} %get-tuple-element.503), channel_id=1, source_target_pairs={{0,2},{1,3},{2,0},{3,1},{4,6},{5,7},{6,4},{7,5},{8,10},{9,11},{10,... | collective-permute-start | bytes 1867784 | tf_op jit(solution)/shard_map/ppermute | solution.py:24
  151.0 36.2 %collective-permute-start.36 = (bf16[2,144,1440]{2,1,0:T(8,128)(2,1)}, bf16[2,144,1440]{2,1,0:T(8,128)(2,1)}, u32[]{:S(2)}, u32[]{:S(2)}) collective-permute-start(bf16[2,144,1440]{2,1,0:T(8,128)(2,1)} %copy-done.112), channel_id=1, source_target_pairs={{0,4},{4,0},{8,12},{12,8},{16,20},{20,16},{24,28},{28,24},{1,5},{5... | collective-permute-start | bytes 2488328 | tf_op jit(solution)/shard_map/ppermute | solution.py:24
  152.2 14.7 %collective-permute-start.30 = (bf16[3,8,5760]{2,1,0:T(8,128)(2,1)S(1)}, bf16[3,8,5760]{2,1,0:T(8,128)(2,1)S(1)}, u32[]{:S(2)}, u32[]{:S(2)}) collective-permute-start(bf16[3,8,5760]{2,1,0:T(8,128)(2,1)S(1)} %collective-permute-done.24), channel_id=1, source_target_pairs={{0,1},{1,0},{2,3},{3,2},{4,5},{5,4},{6,7},{7,6},{8,9},{9,8},{10,11... | collective-permute-start | bytes 829448 | tf_op jit(solution)/shard_map/ppermute | solution.py:24
  165.1 24.5 %collective-permute-start.34 = (bf16[256,2304]{1,0:T(8,128)(2,1)S(1)}, bf16[256,2304]{1,0:T(8,128)(2,1)S(1)}, u32[]{:S(2)}, u32[]{:S(2)}) collective-permute-start(bf16[256,2304]{1,0:T(8,128)(2,1)S(1)} %copy-done.49), channel_id=1, source_target_pairs={{0,1},{1,0},{2,3},{3,2},{4,5},{5,4},{6,7},{7,6},{8,9},{9,8},{10,11... | collective-permute-start | bytes 3538952 | tf_op jit(solution)/shard_map/ppermute | solution.py:24
  165.6 16.0 %collective-permute-start.29 = (bf16[128,2432]{1,0:T(8,128)(2,1)S(1)}, bf16[128,2432]{1,0:T(8,128)(2,1)S(1)}, u32[]{:S(2)}, u32[]{:S(2)}) collective-permute-start(bf16[128,2432]{1,0:T(8,128)(2,1)S(1)} %copy-done.80), channel_id=1, source_target_pairs={{0,2},{1,3},{2,0},{3,1},{4,6},{5,7},{6,4},{7,5},{8,10},{9,11},{10,... | collective-permute-start | bytes 1867784 | tf_op jit(solution)/shard_map/ppermute | solution.py:24
  166.9 14.8 %collective-permute-start.28 = (bf16[256,2432]{1,0:T(8,128)(2,1)S(1)}, bf16[256,2432]{1,0:T(8,128)(2,1)S(1)}, u32[]{:S(2)}, u32[]{:S(2)}) collective-permute-start(bf16[256,2432]{1,0:T(8,128)(2,1)S(1)} %get-tuple-element.302), channel_id=1, source_target_pairs={{0,1},{1,0},{2,3},{3,2},{4,5},{5,4},{6,7},{7,6},{8,9},{9,8},{10,11... | collective-permute-start | bytes 3735560 | tf_op jit(solution)/shard_map/ppermute | solution.py:24
  168.1 23.1 %collective-permute-start.37 = (bf16[2,144,1440]{2,1,0:T(8,128)(2,1)}, bf16[2,144,1440]{2,1,0:T(8,128)(2,1)S(1)}, u32[]{:S(2)}, u32[]{:S(2)}) collective-permute-start(bf16[2,144,1440]{2,1,0:T(8,128)(2,1)} %collective-permute-done.25.refs_11_), channel_id=1, source_target_pairs={{0,8},{4,12},{8,0},{12,4},{16,24},{20,28},{24,16},{28,20},{1,9},{5... | collective-permute-start | bytes 2488328 | tf_op jit(solution)/shard_map/ppermute | solution.py:24
  181.7 21.7 %collective-permute-start.35 = (bf16[2,576,1440]{2,1,0:T(8,128)(2,1)S(1)}, bf16[2,576,1440]{2,1,0:T(8,128)(2,1)S(1)}, u32[]{:S(2)}, u32[]{:S(2)}) collective-permute-start(bf16[2,576,1440]{2,1,0:T(8,128)(2,1)S(1)} %get-tuple-element.311), channel_id=1, source_target_pairs={{0,1},{1,0},{2,3},{3,2},{4,5},{5,4},{6,7},{7,6},{8,9},{9,8},{10,11... | collective-permute-start | bytes 9953288 | tf_op jit(solution)/shard_map/ppermute | solution.py:24
  185.7 17.6 %collective-permute-start.33 = (bf16[256,2304]{1,0:T(8,128)(2,1)S(1)}, bf16[256,2304]{1,0:T(8,128)(2,1)S(1)}, u32[]{:S(2)}, u32[]{:S(2)}) collective-permute-start(bf16[256,2304]{1,0:T(8,128)(2,1)S(1)} %multiply_convert_fusion.1.refs_0_.refs_2_), channel_id=1, source_target_pairs={{0,1},{1,0},{2,3},{3,2},{4,5},{5,4},{6,7},{7,6},{8,9},{9,8},{10,11... | collective-permute-start | bytes 3538952 | tf_op jit(solution)/shard_map/ppermute | solution.py:24
  187.2 16.2 %collective-permute-start.38 = (bf16[128,2304]{1,0:T(8,128)(2,1)S(1)}, bf16[128,2304]{1,0:T(8,128)(2,1)S(1)}, u32[]{:S(2)}, u32[]{:S(2)}) collective-permute-start(bf16[128,2304]{1,0:T(8,128)(2,1)S(1)} %get-tuple-element.314), channel_id=1, source_target_pairs={{0,2},{1,3},{2,0},{3,1},{4,6},{5,7},{6,4},{7,5},{8,10},{9,11},{10,... | collective-permute-start | bytes 1769480 | tf_op jit(solution)/shard_map/ppermute | solution.py:24
  189.6 52.0 %collective-permute-start.31 = (bf16[256,2304]{1,0:T(8,128)(2,1)S(1)}, bf16[256,2304]{1,0:T(8,128)(2,1)S(1)}, u32[]{:S(2)}, u32[]{:S(2)}) collective-permute-start(bf16[256,2304]{1,0:T(8,128)(2,1)S(1)} %multiply_convert_fusion.1.refs_0_.refs_2_), channel_id=1, source_target_pairs={{0,2},{1,3},{2,0},{3,1},{4,6},{5,7},{6,4},{7,5},{8,10},{9,11},{10,... | collective-permute-start | bytes 3538952 | tf_op jit(solution)/shard_map/ppermute | solution.py:24
  191.2 50.4 %collective-permute-start.32 = (bf16[128,2304]{1,0:T(8,128)(2,1)}, bf16[128,2304]{1,0:T(8,128)(2,1)S(1)}, u32[]{:S(2)}, u32[]{:S(2)}) collective-permute-start(bf16[128,2304]{1,0:T(8,128)(2,1)} %get-tuple-element.310), channel_id=1, source_target_pairs={{0,2},{1,3},{2,0},{3,1},{4,6},{5,7},{6,4},{7,5},{8,10},{9,11},{10,... | collective-permute-start | bytes 1769480 | tf_op jit(solution)/shard_map/ppermute | solution.py:24
  288.1 17.2 %collective-permute-start.43 = (bf16[256,2432]{1,0:T(8,128)(2,1)S(1)}, bf16[256,2432]{1,0:T(8,128)(2,1)S(1)}, u32[]{:S(2)}, u32[]{:S(2)}) collective-permute-start(bf16[256,2432]{1,0:T(8,128)(2,1)S(1)} %copy-done.109), channel_id=1, source_target_pairs={{0,1},{1,0},{2,3},{3,2},{4,5},{5,4},{6,7},{7,6},{8,9},{9,8},{10,11... | collective-permute-start | bytes 3735560 | tf_op jit(solution)/shard_map/ppermute | solution.py:24
  288.3 17.0 %collective-permute-start.44 = (bf16[256,2432]{1,0:T(8,128)(2,1)S(1)}, bf16[256,2432]{1,0:T(8,128)(2,1)S(1)}, u32[]{:S(2)}, u32[]{:S(2)}) collective-permute-start(bf16[256,2432]{1,0:T(8,128)(2,1)S(1)} %copy-done.110), channel_id=1, source_target_pairs={{0,1},{1,0},{2,3},{3,2},{4,5},{5,4},{6,7},{7,6},{8,9},{9,8},{10,11... | collective-permute-start | bytes 3735560 | tf_op jit(solution)/shard_map/ppermute | solution.py:24
  288.7 16.6 %collective-permute-start.45 = (bf16[256,2432]{1,0:T(8,128)(2,1)S(1)}, bf16[256,2432]{1,0:T(8,128)(2,1)S(1)}, u32[]{:S(2)}, u32[]{:S(2)}) collective-permute-start(bf16[256,2432]{1,0:T(8,128)(2,1)S(1)} %copy-done.108), channel_id=1, source_target_pairs={{0,1},{1,0},{2,3},{3,2},{4,5},{5,4},{6,7},{7,6},{8,9},{9,8},{10,11... | collective-permute-start | bytes 3735560 | tf_op jit(solution)/shard_map/ppermute | solution.py:24
  288.9 16.4 %collective-permute-start.42 = (bf16[128,2432]{1,0:T(8,128)(2,1)S(1)}, bf16[128,2432]{1,0:T(8,128)(2,1)S(1)}, u32[]{:S(2)}, u32[]{:S(2)}) collective-permute-start(bf16[128,2432]{1,0:T(8,128)(2,1)S(1)} %get-tuple-element.501), channel_id=1, source_target_pairs={{0,2},{1,3},{2,0},{3,1},{4,6},{5,7},{6,4},{7,5},{8,10},{9,11},{10,... | collective-permute-start | bytes 1867784 | tf_op jit(solution)/shard_map/ppermute | solution.py:24
  289.5 19.4 %collective-permute-start.47 = (bf16[1,64,1440]{2,1,0:T(8,128)(2,1)S(1)}, bf16[1,64,1440]{2,1,0:T(8,128)(2,1)S(1)}, u32[]{:S(2)}, u32[]{:S(2)}) collective-permute-start(bf16[1,64,1440]{2,1,0:T(8,128)(2,1)S(1)} %pad_bitcast_fusion), channel_id=1, source_target_pairs={{0,8},{4,12},{8,0},{12,4},{16,24},{20,28},{24,16},{28,20},{1,9},{5... | collective-permute-start | bytes 552968 | tf_op jit(solution)/shard_map/ppermute | solution.py:24
  305.3 15.5 %collective-permute-start.46 = (bf16[128,2432]{1,0:T(8,128)(2,1)S(1)}, bf16[128,2432]{1,0:T(8,128)(2,1)S(1)}, u32[]{:S(2)}, u32[]{:S(2)}) collective-permute-start(bf16[128,2432]{1,0:T(8,128)(2,1)S(1)} %get-tuple-element.346), channel_id=1, source_target_pairs={{0,2},{1,3},{2,0},{3,1},{4,6},{5,7},{6,4},{7,5},{8,10},{9,11},{10,... | collective-permute-start | bytes 1867784 | tf_op jit(solution)/shard_map/ppermute | solution.py:24
  329.0 30.1 %collective-permute-start.48 = (bf16[256,2432]{1,0:T(8,128)(2,1)}, bf16[256,2432]{1,0:T(8,128)(2,1)}, u32[]{:S(2)}, u32[]{:S(2)}) collective-permute-start(bf16[256,2432]{1,0:T(8,128)(2,1)} %concatenate.265.refs_0_), channel_id=1, source_target_pairs={{0,2},{1,3},{2,0},{3,1},{4,6},{5,7},{6,4},{7,5},{8,10},{9,11},{10,... | collective-permute-start | bytes 3735560 | tf_op jit(solution)/shard_map/ppermute | solution.py:24
  330.3 20.8 %collective-permute-start.50 = (bf16[2,64,1440]{2,1,0:T(8,128)(2,1)}, bf16[2,64,1440]{2,1,0:T(8,128)(2,1)}, u32[]{:S(2)}, u32[]{:S(2)}) collective-permute-start(bf16[2,64,1440]{2,1,0:T(8,128)(2,1)} %maximum_select_fusion.6), channel_id=1, source_target_pairs={{0,16},{4,20},{8,24},{12,28},{16,0},{20,4},{24,8},{28,12},{1,17},{... | collective-permute-start | bytes 1105928 | tf_op jit(solution)/shard_map/ppermute | solution.py:24
  359.1 30.1 %collective-permute-start.52 = (bf16[256,2432]{1,0:T(8,128)(2,1)}, bf16[256,2432]{1,0:T(8,128)(2,1)}, u32[]{:S(2)}, u32[]{:S(2)}) collective-permute-start(bf16[256,2432]{1,0:T(8,128)(2,1)} %add_convert_fusion), channel_id=1, source_target_pairs={{0,2},{1,3},{2,0},{3,1},{4,6},{5,7},{6,4},{7,5},{8,10},{9,11},{10,... | collective-permute-start | bytes 3735560 | tf_op jit(solution)/shard_map/ppermute | solution.py:24
  360.8 26.2 %collective-permute-start.53 = (bf16[4,64,1440]{2,1,0:T(8,128)(2,1)}, bf16[4,64,1440]{2,1,0:T(8,128)(2,1)S(1)}, u32[]{:S(2)}, u32[]{:S(2)}) collective-permute-start(bf16[4,64,1440]{2,1,0:T(8,128)(2,1)} %maximum_select_fusion.3), channel_id=1, source_target_pairs={{0,4},{4,0},{8,12},{12,8},{16,20},{20,16},{24,28},{28,24},{1,5},{5... | collective-permute-start | bytes 2211848 | tf_op jit(solution)/shard_map/ppermute | solution.py:24
  390.1 17.5 %collective-permute-start.54 = (bf16[256,16]{1,0:T(8,128)(2,1)S(1)}, bf16[256,16]{1,0:T(8,128)(2,1)S(1)}, u32[]{:S(2)}, u32[]{:S(2)}) collective-permute-start(bf16[256,16]{1,0:T(8,128)(2,1)S(1)} %fusion.35), channel_id=1, source_target_pairs={{0,2},{1,3},{2,0},{3,1},{4,6},{5,7},{6,4},{7,5},{8,10},{9,11},{10,... | collective-permute-start | bytes 24584 | tf_op jit(solution)/shard_map/ppermute | solution.py:24
  390.6 17.0 %collective-permute-start.55 = (bf16[256,16]{1,0:T(8,128)(2,1)S(1)}, bf16[256,16]{1,0:T(8,128)(2,1)S(1)}, u32[]{:S(2)}, u32[]{:S(2)}) collective-permute-start(bf16[256,16]{1,0:T(8,128)(2,1)S(1)} %fusion.35), channel_id=1, source_target_pairs={{0,1},{1,0},{2,3},{3,2},{4,5},{5,4},{6,7},{7,6},{8,9},{9,8},{10,11... | collective-permute-start | bytes 24584 | tf_op jit(solution)/shard_map/ppermute | solution.py:24
  393.1 14.5 %collective-permute-start.58 = (bf16[3,2,16,1440]{3,2,1,0:T(8,128)(2,1)S(1)}, bf16[3,2,16,1440]{3,2,1,0:T(8,128)(2,1)S(1)}, u32[]{:S(2)}, u32[]{:S(2)}) collective-permute-start(bf16[3,2,16,1440]{3,2,1,0:T(8,128)(2,1)S(1)} %get-tuple-element.482), channel_id=1, source_target_pairs={{0,3},{1,2},{2,1},{3,0},{4,7},{5,6},{6,5},{7,4},{8,11},{9,10},{10,... | collective-permute-start | bytes 829448 | tf_op jit(solution)/shard_map/ppermute | solution.py:24
  428.2 19.1 %collective-permute-start.64 = (bf16[2,80,576]{2,1,0:T(8,128)(2,1)S(1)}, bf16[2,80,576]{2,1,0:T(8,128)(2,1)S(1)}, u32[]{:S(2)}, u32[]{:S(2)}) collective-permute-start(bf16[2,80,576]{2,1,0:T(8,128)(2,1)S(1)} %maximum_select_fusion.8), channel_id=1, source_target_pairs={{0,16},{4,20},{8,24},{12,28},{16,0},{20,4},{24,8},{28,12},{1,17},{... | collective-permute-start | bytes 552968 | tf_op jit(solution)/shard_map/ppermute | solution.py:24
  453.1 18.1 %collective-permute-start.68 = (bf16[128,2304]{1,0:T(8,128)(2,1)}, bf16[128,2304]{1,0:T(8,128)(2,1)}, u32[]{:S(2)}, u32[]{:S(2)}) collective-permute-start(bf16[128,2304]{1,0:T(8,128)(2,1)} %get-tuple-element.505), channel_id=1, source_target_pairs={{0,2},{1,3},{2,0},{3,1},{4,6},{5,7},{6,4},{7,5},{8,10},{9,11},{10,... | collective-permute-start | bytes 1769480 | tf_op jit(solution)/shard_map/ppermute | solution.py:24
  454.5 16.6 %collective-permute-start.66 = (bf16[2,96,576]{2,1,0:T(8,128)(2,1)}, bf16[2,96,576]{2,1,0:T(8,128)(2,1)S(1)}, u32[]{:S(2)}, u32[]{:S(2)}) collective-permute-start(bf16[2,96,576]{2,1,0:T(8,128)(2,1)} %maximum_select_fusion.7), channel_id=1, source_target_pairs={{0,16},{4,20},{8,24},{12,28},{16,0},{20,4},{24,8},{28,12},{1,17},{... | collective-permute-start | bytes 663560 | tf_op jit(solution)/shard_map/ppermute | solution.py:24
  471.8 22.1 %collective-permute-start.71 = (bf16[256,2304]{1,0:T(8,128)(2,1)}, bf16[256,2304]{1,0:T(8,128)(2,1)}, u32[]{:S(2)}, u32[]{:S(2)}) collective-permute-start(bf16[256,2304]{1,0:T(8,128)(2,1)} %get-tuple-element.463), channel_id=1, source_target_pairs={{0,1},{1,0},{2,3},{3,2},{4,5},{5,4},{6,7},{7,6},{8,9},{9,8},{10,11... | collective-permute-start | bytes 3538952 | tf_op jit(solution)/shard_map/ppermute | solution.py:24
  477.3 16.1 %collective-permute-start.70 = (bf16[128,2304]{1,0:T(8,128)(2,1)S(1)}, bf16[128,2304]{1,0:T(8,128)(2,1)S(1)}, u32[]{:S(2)}, u32[]{:S(2)}) collective-permute-start(bf16[128,2304]{1,0:T(8,128)(2,1)S(1)} %copy-done.84), channel_id=1, source_target_pairs={{0,2},{1,3},{2,0},{3,1},{4,6},{5,7},{6,4},{7,5},{8,10},{9,11},{10,... | collective-permute-start | bytes 1769480 | tf_op jit(solution)/shard_map/ppermute | solution.py:24
  477.9 16.0 %collective-permute-start.69 = (bf16[4,96,576]{2,1,0:T(8,128)(2,1)S(1)}, bf16[4,96,576]{2,1,0:T(8,128)(2,1)S(1)}, u32[]{:S(2)}, u32[]{:S(2)}) collective-permute-start(bf16[4,96,576]{2,1,0:T(8,128)(2,1)S(1)} %maximum_select_fusion.4), channel_id=1, source_target_pairs={{0,4},{4,0},{8,12},{12,8},{16,20},{20,16},{24,28},{28,24},{1,5},{5... | collective-permute-start | bytes 1327112 | tf_op jit(solution)/shard_map/ppermute | solution.py:24
  480.4 20.2 %collective-permute-start.77 = (bf16[5,2,16,576]{3,2,1,0:T(8,128)(2,1)S(1)}, bf16[5,2,16,576]{3,2,1,0:T(8,128)(2,1)S(1)}, u32[]{:S(2)}, u32[]{:S(2)}) collective-permute-start(bf16[5,2,16,576]{3,2,1,0:T(8,128)(2,1)S(1)} %get-tuple-element.490), channel_id=1, source_target_pairs={{0,3},{1,2},{2,1},{3,0},{4,7},{5,6},{6,5},{7,4},{8,11},{9,10},{10,... | collective-permute-start | bytes 552968 | tf_op jit(solution)/shard_map/ppermute | solution.py:24
  481.6 22.9 %collective-permute-start.75 = (bf16[5,2,16,576]{3,2,1,0:T(8,128)(2,1)S(1)}, bf16[5,2,16,576]{3,2,1,0:T(8,128)(2,1)S(1)}, u32[]{:S(2)}, u32[]{:S(2)}) collective-permute-start(bf16[5,2,16,576]{3,2,1,0:T(8,128)(2,1)S(1)} %get-tuple-element.491), channel_id=1, source_target_pairs={{0,1},{1,0},{2,3},{3,2},{4,5},{5,4},{6,7},{7,6},{8,9},{9,8},{10,11... | collective-permute-start | bytes 552968 | tf_op jit(solution)/shard_map/ppermute | solution.py:24
  (145 other events, 1132.0 us)

commit v7 on v6

--- a/solution.py
+++ b/solution.py
@@ -380,9 +380,9 @@
         for head in range(heads):
             key_turned[head] = k_ref[head].astype(F32).T.astype(BF16)
 
-        def pair(head, query, keys, mask, new):
+        def pair(head, query, keys, mask, new, many=1):
             q, g, logs, inner = query
-            here = slice(keys * rows, (keys + 1) * rows)
+            here = slice(keys * rows, (keys + many) * rows)
             raw = dot_t(k_ref[head, here, :], q)
             if mask is not None:
                 raw = raw + mask
@@ -415,9 +415,11 @@
                 queries.append((q_ref[head, here, :], g, log_ref[head, :, here], inner))
             last = block == count - 1
             totals = [pair(head, queries[head], block, bias[block, :rows, :], last) for head in range(heads)]
-            for keys in range(block):
+            for keys in range(0, block, 4):
                 for head in range(heads):
-                    totals[head] = totals[head] + pair(head, queries[head], keys, None, last)
+                    totals[head] = totals[head] + pair(
+                        head, queries[head], keys, None, last, min(4, block - keys)
+                    )
             if not last:
                 for head in range(heads):
                     query_sum[head] = totals[head]

time: 525 us -> 523 us (level)
  transfers between devices with their start and end apart: 78 -> 78, of which waited for: 31 -> 32; matrix products, arithmetic and copies ran while one was open for 13% -> 13% of each run, Pallas kernels for 31% -> 31%
where the time goes in v7:
time: 523 us; the launch traced here: 516 us
  Pallas kernels  198 us (38%)
  waiting for transfers between devices  136 us (26%)
  local copies, waits for them, and re-layouts  65 us (12%)
  starting transfers between devices  62.7 us (12%)
  other arithmetic  42.7 us (8%)
  matrix products  7.93 us (2%)
    ppermute x78, waiting for transfers between devices, hop(): return lax.ppermute(values, axis, [(i, i ^ bit) for i in range(size)])  136 us
    pallas_call x2, Pallas kernels, feed_forward(): call(kernel, [out] * (2 * count) + [jax.ShapeDtypeStruct((3 * rank, size)...  71.4 us
    ppermute x78, starting transfers between devices, hop(): return lax.ppermute(values, axis, [(i, i ^ bit) for i in range(size)])  62.7 us
    pallas_call x3, Pallas kernels, attend_back(): call(kernel, [jax.ShapeDtypeStruct((heads, length, HDIM), BF16)] * 3 + [j...  34.8 us
    unnamed x229, local copies, waits for them, and re-layouts  25.6 us
    pallas_call x2, Pallas kernels, project_back(): call(kernel, [jax.ShapeDtypeStruct((rows, width), BF16)] * count, [smem()...  24.7 us
    pallas_call x1, Pallas kernels, project(): call(kernel, [by_heads] * 3 + [jax.ShapeDtypeStruct((thin, rows * count),...  21 us
    pallas_call x1, Pallas kernels, attend(): call(kernel, [jax.ShapeDtypeStruct(query.shape, BF16), jax.ShapeDtypeStru...  16.5 us
  transfers between devices with their start and end apart: 78, of which 32 were waited for; matrix products, arithmetic and copies ran while one was open for 13% of the time, Pallas kernels for 31%

profile of v7, /device:TPU:0, one launch (start us, length us, event | category | flops | bytes accessed | tf_op | source)
XLA Modules:
  0.0 515.8 jit_solution(13130970708083187465)
XLA Ops:
  1.4 2.0 fusion.48
  5.2 3.6 sides_far.1
  8.9 2.6 collective-permute-start
  13.0 1.9 fusion.30
  29.0 7.0 %sides_near.1 = (bf16[576,1728]{1,0:T(8,128)(2,1)}, bf16[576,1728]{1,0:T(8,128)(2,1)}) custom-call(s32[2]{0:T(128)} %get-tuple-element.575.where_ref, bf16[3,576,2304]{2,1,0:T(8,128)(2,1)} %w_ref.4), custom_call_target="tpu_custom_call" | custom-call | bytes 11943936 | tf_op jit(solution)/shard_map/sides_near/pallas_call | solution.py:143
  36.1 3.3 collective-permute-done.2.refs_10_.refs_15_
  49.6 7.0 %collective-permute-done.4.refs_12_.refs_17_ = bf16[144,1728]{1,0:T(8,128)(2,1)S(1)} collective-permute-done((bf16[144,1728]{1,0:T(8,128)(2,1)}, bf16[144,1728]{1,0:T(8,128)(2,1)S(1)}, u32[]{:S(2)}, u32[]{:S(2)}) %collective-permute-start.4) | collective-permute-done | bytes 497696 | tf_op jit(solution)/shard_map/ppermute | solution.py:24
  61.8 3.6 constant_dynamic-slice_fusion.9
  70.1 8.7 %collective-permute-done.11.refs_13_.refs_18_ = bf16[144,1728]{1,0:T(8,128)(2,1)S(1)} collective-permute-done((bf16[144,1728]{1,0:T(8,128)(2,1)S(1)}, bf16[144,1728]{1,0:T(8,128)(2,1)S(1)}, u32[]{:S(2)}, u32[]{:S(2)}) %collective-permute-start.11) | collective-permute-done | bytes 497696 | tf_op jit(solution)/shard_map/ppermute | solution.py:24
  78.9 6.5 %collective-permute-done.9.refs_2_ = bf16[256,2304]{1,0:T(8,128)(2,1)S(1)} collective-permute-done((bf16[256,2304]{1,0:T(8,128)(2,1)S(1)}, bf16[256,2304]{1,0:T(8,128)(2,1)S(1)}, u32[]{:S(2)}, u32[]{:S(2)}) %collective-permute-start.9) | collective-permute-done | bytes 1179680 | tf_op jit(solution)/shard_map/ppermute | solution.py:24
  88.9 21.0 %project.1 = (bf16[9,1024,64]{2,1,0:T(8,128)(2,1)}, bf16[9,1024,64]{2,1,0:T(8,128)(2,1)}, bf16[9,1024,64]{2,1,0:T(8,128)(2,1)}, bf16[48,1024]{1,0:T(8,128)(2,1)}) custom-call(s32[1]{0:T(128)} %bitcast.place_ref, s32[10]{0:T(128)} %stack.110.offsets_ref, bf16[256,2304]{1,0:T(8,128)(2,1)} %copy-done.9, bf16[256,2304]{1,0:T(8,128)(2,1)} %copy-done.20, ...), custom_call_target="tpu_custom_call" | custom-call | flops 8153726976 | bytes 19759104 | tf_op jit(solution)/shard_map/project/pallas_call | solution.py:255
  113.6 16.5 %attend.1 = (bf16[9,1024,64]{2,1,0:T(8,128)(2,1)}, f32[9,1,1024]{2,1,0:T(1,128)}) custom-call(s32[2]{0:T(128)} %bitcast.170, bf16[9,1024,64]{2,1,0:T(8,128)(2,1)} %get-tuple-element.280.q_ref, bf16[9,1024,64]{2,1,0:T(8,128)(2,1)} %get-tuple-element.281.k_ref, bf16[9,1024,64]{2,1,0:T(8,128)(2,1)} %get-tuple-element.282.v_ref), custom_call_target="tpu_custom_call" | custom-call | flops 9663676416 | bytes 9437184 | tf_op jit(solution)/shard_map/attend/pallas_call | solution.py:349
  137.1 2.2 close_attention.2
  143.8 4.6 collective-permute-done.24
  153.9 2.2 close_attention.3
  156.1 9.0 %constant_dynamic-slice_fusion.4 = (bf16[2,576,1440]{2,1,0:T(8,128)(2,1)}, bf16[2,576,1440]{2,1,0:T(8,128)(2,1)S(1)}) fusion(bf16[2,576,5760]{2,1,0:T(8,128)(2,1)} %param.22, s32[]{:T(128)S(6)} %select_n.365, s32[]{:T(128)S(6)} %select_n.364), kind=kLoop, calls=%fused_computation.177 | loop fusion | bytes 13271048 | tf_op jit(solution)/shard_map/dynamic_slice | solution.py:121
  169.7 12.0 %collective-permute-done.29 = bf16[128,2432]{1,0:T(8,128)(2,1)S(1)} collective-permute-done((bf16[128,2432]{1,0:T(8,128)(2,1)S(1)}, bf16[128,2432]{1,0:T(8,128)(2,1)S(1)}, u32[]{:S(2)}, u32[]{:S(2)}) %collective-permute-start.29) | collective-permute-done | bytes 622624 | tf_op jit(solution)/shard_map/ppermute | solution.py:24
  191.6 11.7 %collective-permute-done.38 = bf16[128,2304]{1,0:T(8,128)(2,1)S(1)} collective-permute-done((bf16[128,2304]{1,0:T(8,128)(2,1)S(1)}, bf16[128,2304]{1,0:T(8,128)(2,1)S(1)}, u32[]{:S(2)}, u32[]{:S(2)}) %collective-permute-start.38) | collective-permute-done | bytes 589856 | tf_op jit(solution)/shard_map/ppermute | solution.py:24
  205.6 35.9 %feed_forward.2 = (bf16[256,2432]{1,0:T(8,128)(2,1)}, bf16[256,2432]{1,0:T(8,128)(2,1)}, bf16[256,2432]{1,0:T(8,128)(2,1)}, bf16[256,2432]{1,0:T(8,128)(2,1)}, f32[48,1440]{1,0:T(8,128)}) custom-call(s32[10]{0:T(128)} %stack.110.offsets_ref, bf16[256,2304]{1,0:T(8,128)(2,1)} %copy-done.7, bf16[256,2304]{1,0:T(8,128)(2,1)} %copy-done.28, ...), custom_call_target="tpu_custom_call" | custom-call | flops 20384317440 | bytes 29343744 | tf_op jit(solution)/shard_map/feed_forward/pallas_call | solution.py:626
  242.2 2.3 collective-permute-done.40.refs_3_
  247.3 35.5 %feed_forward.3 = (bf16[256,2432]{1,0:T(8,128)(2,1)}, bf16[256,2432]{1,0:T(8,128)(2,1)}, bf16[256,2432]{1,0:T(8,128)(2,1)}, bf16[256,2432]{1,0:T(8,128)(2,1)}, f32[48,1440]{1,0:T(8,128)}) custom-call(s32[10]{0:T(128)} %stack.110.offsets_ref, bf16[256,2304]{1,0:T(8,128)(2,1)} %copy-done.24, bf16[256,2304]{1,0:T(8,128)(2,1)} %copy-done.26, ...), custom_call_target="tpu_custom_call" | custom-call | flops 20384317440 | bytes 29343744 | tf_op jit(solution)/shard_map/feed_forward/pallas_call | solution.py:626
  284.0 2.1 collective-permute-done.41
  286.1 2.0 add_convert_fusion.1
  290.8 14.5 %collective-permute-done.42 = bf16[128,2432]{1,0:T(8,128)(2,1)S(1)} collective-permute-done((bf16[128,2432]{1,0:T(8,128)(2,1)S(1)}, bf16[128,2432]{1,0:T(8,128)(2,1)S(1)}, u32[]{:S(2)}, u32[]{:S(2)}) %collective-permute-start.42) | collective-permute-done | bytes 622624 | tf_op jit(solution)/shard_map/ppermute | solution.py:24
  308.9 11.9 %collective-permute-done.46 = bf16[128,2432]{1,0:T(8,128)(2,1)S(1)} collective-permute-done((bf16[128,2432]{1,0:T(8,128)(2,1)S(1)}, bf16[128,2432]{1,0:T(8,128)(2,1)S(1)}, u32[]{:S(2)}, u32[]{:S(2)}) %collective-permute-start.46) | collective-permute-done | bytes 622624 | tf_op jit(solution)/shard_map/ppermute | solution.py:24
  323.0 2.5 multiply_convert_fusion
  325.5 3.5 concatenate.265.refs_0_
  330.3 2.6 collective-permute-start.50
  338.5 6.1 %open_attention.2 = (bf16[9,512,64]{2,1,0:T(8,128)(2,1)S(1)}, f32[16,576]{1,0:T(8,128)S(1)}, f32[48,2304]{1,0:T(8,128)S(1)}) custom-call(s32[1]{0:T(128)} %bitcast.place_ref, bf16[256,2432]{1,0:T(8,128)(2,1)S(1)} %copy-done.6, bf16[256,2432]{1,0:T(8,128)(2,1)} %collective-permute-done.49.refs_1_, bf16[256,2304]{1,0:T(8,128)(2,1)S(1)} %copy-done.8, ...), custom_call_target="tpu_custom_call" | custom-call | flops 1358954496 | bytes 8552448 | tf_op jit(solution)/shard_map/open_attention/pallas_call | solution.py:553
  345.6 5.6 %collective-permute-done.50 = bf16[2,64,1440]{2,1,0:T(8,128)(2,1)} collective-permute-done((bf16[2,64,1440]{2,1,0:T(8,128)(2,1)}, bf16[2,64,1440]{2,1,0:T(8,128)(2,1)}, u32[]{:S(2)}, u32[]{:S(2)}) %collective-permute-start.50) | collective-permute-done | bytes 368672 | tf_op jit(solution)/shard_map/ppermute | solution.py:24
  351.2 2.6 maximum_select_fusion.3
  353.7 5.4 %collective-permute-done.48.refs_0_ = bf16[256,2432]{1,0:T(8,128)(2,1)} collective-permute-done((bf16[256,2432]{1,0:T(8,128)(2,1)}, bf16[256,2432]{1,0:T(8,128)(2,1)}, u32[]{:S(2)}, u32[]{:S(2)}) %collective-permute-start.48) | collective-permute-done | bytes 1245216 | tf_op jit(solution)/shard_map/ppermute | solution.py:24
  366.7 6.6 %open_attention.3 = (bf16[9,512,64]{2,1,0:T(8,128)(2,1)S(1)}, f32[16,576]{1,0:T(8,128)S(1)}, f32[48,2304]{1,0:T(8,128)S(1)}) custom-call(s32[1]{0:T(128)} %bitcast.place_ref, bf16[256,2432]{1,0:T(8,128)(2,1)} %collective-permute-done.48.refs_0_, bf16[256,2432]{1,0:T(8,128)(2,1)} %collective-permute-done.51.refs_1_, bf16[256,2304]{1,0:T(8,128)(2,1)S(1)} %copy-done.25, ...), custom_call_target="tpu_custom_call" | custom-call | flops 1358954496 | bytes 8552448 | tf_op jit(solution)/shard_map/open_attention/pallas_call | solution.py:553
  375.1 11.5 %attend_back.3 = (bf16[3,1024,64]{2,1,0:T(8,128)(2,1)S(1)}, bf16[3,1024,64]{2,1,0:T(8,128)(2,1)S(1)}, bf16[3,1024,64]{2,1,0:T(8,128)(2,1)S(1)}, f32[48,1024]{1,0:T(8,128)S(1)}, f32[48,192]{1,0:T(8,128)S(1)}) custom-call(s32[2]{0:T(128)S(1)} %bitcast.171, s32[1]{0:T(128)} %bitcast.place_ref, bf16[9,1024,64]{2,1,0:T(8,128)(2,1)S(1)} %copy-done.35, ...), custom_call_target="tpu_custom_call" | custom-call | flops 8053063680 | bytes 6291456 | tf_op jit(solution)/shard_map/attend_back/pallas_call | solution.py:458
  386.6 2.6 collective-permute-done.52
  395.3 11.7 %attend_back.4 = (bf16[3,1024,64]{2,1,0:T(8,128)(2,1)S(1)}, bf16[3,1024,64]{2,1,0:T(8,128)(2,1)S(1)}, bf16[3,1024,64]{2,1,0:T(8,128)(2,1)S(1)}, f32[48,1024]{1,0:T(8,128)S(1)}, f32[48,192]{1,0:T(8,128)S(1)}) custom-call(s32[2]{0:T(128)S(1)} %bitcast.172, s32[1]{0:T(128)} %bitcast.place_ref, bf16[9,1024,64]{2,1,0:T(8,128)(2,1)S(1)} %copy-done.35, ...), custom_call_target="tpu_custom_call" | custom-call | flops 8053063680 | bytes 6291456 | tf_op jit(solution)/shard_map/attend_back/pallas_call | solution.py:458
  413.2 11.5 %attend_back.5 = (bf16[3,1024,64]{2,1,0:T(8,128)(2,1)S(1)}, bf16[3,1024,64]{2,1,0:T(8,128)(2,1)S(1)}, bf16[3,1024,64]{2,1,0:T(8,128)(2,1)S(1)}, f32[48,1024]{1,0:T(8,128)S(1)}, f32[48,192]{1,0:T(8,128)S(1)}) custom-call(s32[2]{0:T(128)S(1)} %bitcast.173, s32[1]{0:T(128)} %bitcast.place_ref, bf16[9,1024,64]{2,1,0:T(8,128)(2,1)S(1)} %copy-done.35, ...), custom_call_target="tpu_custom_call" | custom-call | flops 8053063680 | bytes 6291456 | tf_op jit(solution)/shard_map/attend_back/pallas_call | solution.py:458
  431.2 2.2 thin_product.1
  434.4 12.4 %project_back.2 = (bf16[256,2304]{1,0:T(8,128)(2,1)}, bf16[256,2304]{1,0:T(8,128)(2,1)}) custom-call(s32[1]{0:T(128)} %bitcast.place_ref, s32[10]{0:T(128)} %stack.110.offsets_ref, bf16[3,1024,64]{2,1,0:T(8,128)(2,1)} %copy-done.11, bf16[3,1024,64]{2,1,0:T(8,128)(2,1)} %copy-done.14, bf16[3,1024,64]{2,1,0:T(8,128)(2,1)} %copy-done.17, ...), custom_call_target="tpu_custom_call" | custom-call | flops 4076863488 | bytes 12091392 | tf_op jit(solution)/shard_map/project_back/pallas_call | solution.py:663
  447.7 2.2 collective-permute-done.65
  454.1 2.6 collective-permute-start.66
  457.5 12.4 %project_back.3 = (bf16[256,2304]{1,0:T(8,128)(2,1)}, bf16[256,2304]{1,0:T(8,128)(2,1)}) custom-call(s32[1]{0:T(128)} %bitcast.place_ref, s32[10]{0:T(128)} %stack.110.offsets_ref, bf16[3,1024,64]{2,1,0:T(8,128)(2,1)} %copy-done.11, bf16[3,1024,64]{2,1,0:T(8,128)(2,1)} %copy-done.14, bf16[3,1024,64]{2,1,0:T(8,128)(2,1)} %copy-done.17, ...), custom_call_target="tpu_custom_call" | custom-call | flops 4076863488 | bytes 12091392 | tf_op jit(solution)/shard_map/project_back/pallas_call | solution.py:663
  470.6 2.9 add_convert_fusion.3
  481.0 11.2 %collective-permute-done.70 = bf16[128,2304]{1,0:T(8,128)(2,1)S(1)} collective-permute-done((bf16[128,2304]{1,0:T(8,128)(2,1)S(1)}, bf16[128,2304]{1,0:T(8,128)(2,1)S(1)}, u32[]{:S(2)}, u32[]{:S(2)}) %collective-permute-start.70) | collective-permute-done | bytes 589856 | tf_op jit(solution)/shard_map/ppermute | solution.py:24
  496.9 2.5 fusion.11
  500.1 2.0 fusion.10
  503.3 2.0 collective-permute-done.74
  505.3 5.7 %collective-permute-done.73 = bf16[6,2,16,576]{3,2,1,0:T(8,128)(2,1)S(1)} collective-permute-done((bf16[6,2,16,576]{3,2,1,0:T(8,128)(2,1)S(1)}, bf16[6,2,16,576]{3,2,1,0:T(8,128)(2,1)S(1)}, u32[]{:S(2)}, u32[]{:S(2)}) %collective-permute-start.73) | collective-permute-done | bytes 221216 | tf_op jit(solution)/shard_map/ppermute | solution.py:24
  (487 shorter events, 152.6 us)
Async XLA Ops:
  4.2 19.2 %collective-permute-start.1 = (bf16[6,16,2304]{2,1,0:T(8,128)(2,1)}, bf16[6,16,2304]{2,1,0:T(8,128)(2,1)}, u32[]{:S(2)}, u32[]{:S(2)}) collective-permute-start(bf16[6,16,2304]{2,1,0:T(8,128)(2,1)} %fusion.20), channel_id=1, source_target_pairs={{0,1},{1,0},{2,3},{3,2},{4,5},{5,4},{6,7},{7,6},{8,9},{9,8},{10,11... | collective-permute-start | bytes 1327112 | tf_op jit(solution)/shard_map/ppermute | solution.py:24
  8.9 15.8 %collective-permute-start = (bf16[144,1728]{1,0:T(8,128)(2,1)}, bf16[144,1728]{1,0:T(8,128)(2,1)S(1)}, u32[]{:S(2)}, u32[]{:S(2)}) collective-permute-start(bf16[144,1728]{1,0:T(8,128)(2,1)} %get-tuple-element.244), channel_id=1, source_target_pairs={{0,2},{1,3},{2,0},{3,1},{4,6},{5,7},{6,4},{7,5},{8,10},{9,11},{10,... | collective-permute-start | bytes 1493000 | tf_op jit(solution)/shard_map/ppermute | solution.py:24
  25.6 16.6 %collective-permute-start.7 = (bf16[144,1728]{1,0:T(8,128)(2,1)S(1)}, bf16[144,1728]{1,0:T(8,128)(2,1)}, u32[]{:S(2)}, u32[]{:S(2)}) collective-permute-start(bf16[144,1728]{1,0:T(8,128)(2,1)S(1)} %collective-permute-done.refs_6_.refs_11_), channel_id=1, source_target_pairs={{0,4},{4,0},{8,12},{12,8},{16,20},{20,16},{24,28},{28,24},{1,5},{5... | collective-permute-start | bytes 1493000 | tf_op jit(solution)/shard_map/ppermute | solution.py:24
  27.4 16.5 %collective-permute-start.6 = (bf16[144,1728]{1,0:T(8,128)(2,1)S(1)}, bf16[144,1728]{1,0:T(8,128)(2,1)}, u32[]{:S(2)}, u32[]{:S(2)}) collective-permute-start(bf16[144,1728]{1,0:T(8,128)(2,1)S(1)} %collective-permute-done.refs_6_.refs_11_), channel_id=1, source_target_pairs={{0,8},{4,12},{8,0},{12,4},{16,24},{20,28},{24,16},{28,20},{1,9},{5... | collective-permute-start | bytes 1493000 | tf_op jit(solution)/shard_map/ppermute | solution.py:24
  29.0 58.9 %collective-permute-start.8 = (bf16[256,2304]{1,0:T(8,128)(2,1)S(1)}, bf16[256,2304]{1,0:T(8,128)(2,1)S(1)}, u32[]{:S(2)}, u32[]{:S(2)}) collective-permute-start(bf16[256,2304]{1,0:T(8,128)(2,1)S(1)} %fusion.7.refs_0_), channel_id=1, source_target_pairs={{0,1},{1,0},{2,3},{3,2},{4,5},{5,4},{6,7},{7,6},{8,9},{9,8},{10,11... | collective-permute-start | bytes 3538952 | tf_op jit(solution)/shard_map/ppermute | solution.py:24
  42.2 14.4 %collective-permute-start.4 = (bf16[144,1728]{1,0:T(8,128)(2,1)}, bf16[144,1728]{1,0:T(8,128)(2,1)S(1)}, u32[]{:S(2)}, u32[]{:S(2)}) collective-permute-start(bf16[144,1728]{1,0:T(8,128)(2,1)} %collective-permute-done.2.refs_10_.refs_15_), channel_id=1, source_target_pairs={{0,8},{4,12},{8,0},{12,4},{16,24},{20,28},{24,16},{28,20},{1,9},{5... | collective-permute-start | bytes 1493000 | tf_op jit(solution)/shard_map/ppermute | solution.py:24
  47.2 19.1 %collective-permute-start.14 = (bf16[3,16,5760]{2,1,0:T(8,128)(2,1)S(1)}, bf16[3,16,5760]{2,1,0:T(8,128)(2,1)S(1)}, u32[]{:S(2)}, u32[]{:S(2)}) collective-permute-start(bf16[3,16,5760]{2,1,0:T(8,128)(2,1)S(1)} %fusion.16), channel_id=1, source_target_pairs={{0,1},{1,0},{2,3},{3,2},{4,5},{5,4},{6,7},{7,6},{8,9},{9,8},{10,11... | collective-permute-start | bytes 1658888 | tf_op jit(solution)/shard_map/ppermute | solution.py:24
  49.4 38.5 %collective-permute-start.16 = (bf16[576,1728]{1,0:T(8,128)(2,1)}, bf16[576,1728]{1,0:T(8,128)(2,1)}, u32[]{:S(2)}, u32[]{:S(2)}) collective-permute-start(bf16[576,1728]{1,0:T(8,128)(2,1)} %get-tuple-element.267), channel_id=1, source_target_pairs={{0,1},{1,0},{2,3},{3,2},{4,5},{5,4},{6,7},{7,6},{8,9},{9,8},{10,11... | collective-permute-start | bytes 5971976 | tf_op jit(solution)/shard_map/ppermute | solution.py:24
  58.1 27.2 %collective-permute-start.9 = (bf16[256,2304]{1,0:T(8,128)(2,1)S(1)}, bf16[256,2304]{1,0:T(8,128)(2,1)S(1)}, u32[]{:S(2)}, u32[]{:S(2)}) collective-permute-start(bf16[256,2304]{1,0:T(8,128)(2,1)S(1)} %fusion.7.refs_0_), channel_id=1, source_target_pairs={{0,2},{1,3},{2,0},{3,1},{4,6},{5,7},{6,4},{7,5},{8,10},{9,11},{10,... | collective-permute-start | bytes 3538952 | tf_op jit(solution)/shard_map/ppermute | solution.py:24
  85.4 24.5 %collective-permute-start.17 = (bf16[2,144,1440]{2,1,0:T(8,128)(2,1)}, bf16[2,144,1440]{2,1,0:T(8,128)(2,1)}, u32[]{:S(2)}, u32[]{:S(2)}) collective-permute-start(bf16[2,144,1440]{2,1,0:T(8,128)(2,1)} %get-tuple-element.277), channel_id=1, source_target_pairs={{0,2},{1,3},{2,0},{3,1},{4,6},{5,7},{6,4},{7,5},{8,10},{9,11},{10,... | collective-permute-start | bytes 2488328 | tf_op jit(solution)/shard_map/ppermute | solution.py:24
  87.6 42.4 %collective-permute-start.18 = (bf16[2,144,1440]{2,1,0:T(8,128)(2,1)}, bf16[2,144,1440]{2,1,0:T(8,128)(2,1)}, u32[]{:S(2)}, u32[]{:S(2)}) collective-permute-start(bf16[2,144,1440]{2,1,0:T(8,128)(2,1)} %get-tuple-element.284), channel_id=1, source_target_pairs={{0,3},{1,2},{2,1},{3,0},{4,7},{5,6},{6,5},{7,4},{8,11},{9,10},{10,... | collective-permute-start | bytes 2488328 | tf_op jit(solution)/shard_map/ppermute | solution.py:24
  109.9 22.2 %collective-permute-start.20 = (bf16[2,144,1440]{2,1,0:T(8,128)(2,1)}, bf16[2,144,1440]{2,1,0:T(8,128)(2,1)S(1)}, u32[]{:S(2)}, u32[]{:S(2)}) collective-permute-start(bf16[2,144,1440]{2,1,0:T(8,128)(2,1)} %collective-permute-done.17.refs_6_), channel_id=1, source_target_pairs={{0,4},{4,0},{8,12},{12,8},{16,20},{20,16},{24,28},{28,24},{1,5},{5... | collective-permute-start | bytes 2488328 | tf_op jit(solution)/shard_map/ppermute | solution.py:24
  111.2 21.8 %collective-permute-start.19 = (bf16[2,144,1440]{2,1,0:T(8,128)(2,1)}, bf16[2,144,1440]{2,1,0:T(8,128)(2,1)S(1)}, u32[]{:S(2)}, u32[]{:S(2)}) collective-permute-start(bf16[2,144,1440]{2,1,0:T(8,128)(2,1)} %collective-permute-done.17.refs_6_), channel_id=1, source_target_pairs={{0,8},{4,12},{8,0},{12,4},{16,24},{20,28},{24,16},{28,20},{1,9},{5... | collective-permute-start | bytes 2488328 | tf_op jit(solution)/shard_map/ppermute | solution.py:24
  112.1 18.5 %collective-permute-start.21 = (bf16[5,8,2304]{2,1,0:T(8,128)(2,1)S(1)}, bf16[5,8,2304]{2,1,0:T(8,128)(2,1)S(1)}, u32[]{:S(2)}, u32[]{:S(2)}) collective-permute-start(bf16[5,8,2304]{2,1,0:T(8,128)(2,1)S(1)} %copy-done.99), channel_id=1, source_target_pairs={{0,2},{1,3},{2,0},{3,1},{4,6},{5,7},{6,4},{7,5},{8,10},{9,11},{10,... | collective-permute-start | bytes 552968 | tf_op jit(solution)/shard_map/ppermute | solution.py:24
  141.0 24.1 %collective-permute-start.26 = (bf16[2,144,1440]{2,1,0:T(8,128)(2,1)}, bf16[2,144,1440]{2,1,0:T(8,128)(2,1)}, u32[]{:S(2)}, u32[]{:S(2)}) collective-permute-start(bf16[2,144,1440]{2,1,0:T(8,128)(2,1)} %collective-permute-done.18.refs_10_), channel_id=1, source_target_pairs={{0,8},{4,12},{8,0},{12,4},{16,24},{20,28},{24,16},{28,20},{1,9},{5... | collective-permute-start | bytes 2488328 | tf_op jit(solution)/shard_map/ppermute | solution.py:24
  142.6 23.1 %collective-permute-start.25 = (bf16[2,144,1440]{2,1,0:T(8,128)(2,1)}, bf16[2,144,1440]{2,1,0:T(8,128)(2,1)}, u32[]{:S(2)}, u32[]{:S(2)}) collective-permute-start(bf16[2,144,1440]{2,1,0:T(8,128)(2,1)} %collective-permute-done.18.refs_10_), channel_id=1, source_target_pairs={{0,4},{4,0},{8,12},{12,8},{16,20},{20,16},{24,28},{28,24},{1,5},{5... | collective-permute-start | bytes 2488328 | tf_op jit(solution)/shard_map/ppermute | solution.py:24
  149.5 16.1 %collective-permute-start.27 = (bf16[128,2432]{1,0:T(8,128)(2,1)}, bf16[128,2432]{1,0:T(8,128)(2,1)}, u32[]{:S(2)}, u32[]{:S(2)}) collective-permute-start(bf16[128,2432]{1,0:T(8,128)(2,1)} %get-tuple-element.503), channel_id=1, source_target_pairs={{0,2},{1,3},{2,0},{3,1},{4,6},{5,7},{6,4},{7,5},{8,10},{9,11},{10,... | collective-permute-start | bytes 1867784 | tf_op jit(solution)/shard_map/ppermute | solution.py:24
  151.0 36.2 %collective-permute-start.36 = (bf16[2,144,1440]{2,1,0:T(8,128)(2,1)}, bf16[2,144,1440]{2,1,0:T(8,128)(2,1)}, u32[]{:S(2)}, u32[]{:S(2)}) collective-permute-start(bf16[2,144,1440]{2,1,0:T(8,128)(2,1)} %copy-done.112), channel_id=1, source_target_pairs={{0,4},{4,0},{8,12},{12,8},{16,20},{20,16},{24,28},{28,24},{1,5},{5... | collective-permute-start | bytes 2488328 | tf_op jit(solution)/shard_map/ppermute | solution.py:24
  152.2 14.7 %collective-permute-start.30 = (bf16[3,8,5760]{2,1,0:T(8,128)(2,1)S(1)}, bf16[3,8,5760]{2,1,0:T(8,128)(2,1)S(1)}, u32[]{:S(2)}, u32[]{:S(2)}) collective-permute-start(bf16[3,8,5760]{2,1,0:T(8,128)(2,1)S(1)} %collective-permute-done.24), channel_id=1, source_target_pairs={{0,1},{1,0},{2,3},{3,2},{4,5},{5,4},{6,7},{7,6},{8,9},{9,8},{10,11... | collective-permute-start | bytes 829448 | tf_op jit(solution)/shard_map/ppermute | solution.py:24
  165.1 24.5 %collective-permute-start.34 = (bf16[256,2304]{1,0:T(8,128)(2,1)S(1)}, bf16[256,2304]{1,0:T(8,128)(2,1)S(1)}, u32[]{:S(2)}, u32[]{:S(2)}) collective-permute-start(bf16[256,2304]{1,0:T(8,128)(2,1)S(1)} %copy-done.49), channel_id=1, source_target_pairs={{0,1},{1,0},{2,3},{3,2},{4,5},{5,4},{6,7},{7,6},{8,9},{9,8},{10,11... | collective-permute-start | bytes 3538952 | tf_op jit(solution)/shard_map/ppermute | solution.py:24
  165.6 16.0 %collective-permute-start.29 = (bf16[128,2432]{1,0:T(8,128)(2,1)S(1)}, bf16[128,2432]{1,0:T(8,128)(2,1)S(1)}, u32[]{:S(2)}, u32[]{:S(2)}) collective-permute-start(bf16[128,2432]{1,0:T(8,128)(2,1)S(1)} %copy-done.80), channel_id=1, source_target_pairs={{0,2},{1,3},{2,0},{3,1},{4,6},{5,7},{6,4},{7,5},{8,10},{9,11},{10,... | collective-permute-start | bytes 1867784 | tf_op jit(solution)/shard_map/ppermute | solution.py:24
  166.9 14.8 %collective-permute-start.28 = (bf16[256,2432]{1,0:T(8,128)(2,1)S(1)}, bf16[256,2432]{1,0:T(8,128)(2,1)S(1)}, u32[]{:S(2)}, u32[]{:S(2)}) collective-permute-start(bf16[256,2432]{1,0:T(8,128)(2,1)S(1)} %get-tuple-element.302), channel_id=1, source_target_pairs={{0,1},{1,0},{2,3},{3,2},{4,5},{5,4},{6,7},{7,6},{8,9},{9,8},{10,11... | collective-permute-start | bytes 3735560 | tf_op jit(solution)/shard_map/ppermute | solution.py:24
  168.1 23.1 %collective-permute-start.37 = (bf16[2,144,1440]{2,1,0:T(8,128)(2,1)}, bf16[2,144,1440]{2,1,0:T(8,128)(2,1)S(1)}, u32[]{:S(2)}, u32[]{:S(2)}) collective-permute-start(bf16[2,144,1440]{2,1,0:T(8,128)(2,1)} %collective-permute-done.25.refs_11_), channel_id=1, source_target_pairs={{0,8},{4,12},{8,0},{12,4},{16,24},{20,28},{24,16},{28,20},{1,9},{5... | collective-permute-start | bytes 2488328 | tf_op jit(solution)/shard_map/ppermute | solution.py:24
  181.7 21.7 %collective-permute-start.35 = (bf16[2,576,1440]{2,1,0:T(8,128)(2,1)S(1)}, bf16[2,576,1440]{2,1,0:T(8,128)(2,1)S(1)}, u32[]{:S(2)}, u32[]{:S(2)}) collective-permute-start(bf16[2,576,1440]{2,1,0:T(8,128)(2,1)S(1)} %get-tuple-element.311), channel_id=1, source_target_pairs={{0,1},{1,0},{2,3},{3,2},{4,5},{5,4},{6,7},{7,6},{8,9},{9,8},{10,11... | collective-permute-start | bytes 9953288 | tf_op jit(solution)/shard_map/ppermute | solution.py:24
  185.7 17.6 %collective-permute-start.33 = (bf16[256,2304]{1,0:T(8,128)(2,1)S(1)}, bf16[256,2304]{1,0:T(8,128)(2,1)S(1)}, u32[]{:S(2)}, u32[]{:S(2)}) collective-permute-start(bf16[256,2304]{1,0:T(8,128)(2,1)S(1)} %multiply_convert_fusion.1.refs_0_.refs_2_), channel_id=1, source_target_pairs={{0,1},{1,0},{2,3},{3,2},{4,5},{5,4},{6,7},{7,6},{8,9},{9,8},{10,11... | collective-permute-start | bytes 3538952 | tf_op jit(solution)/shard_map/ppermute | solution.py:24
  187.2 16.2 %collective-permute-start.38 = (bf16[128,2304]{1,0:T(8,128)(2,1)S(1)}, bf16[128,2304]{1,0:T(8,128)(2,1)S(1)}, u32[]{:S(2)}, u32[]{:S(2)}) collective-permute-start(bf16[128,2304]{1,0:T(8,128)(2,1)S(1)} %get-tuple-element.314), channel_id=1, source_target_pairs={{0,2},{1,3},{2,0},{3,1},{4,6},{5,7},{6,4},{7,5},{8,10},{9,11},{10,... | collective-permute-start | bytes 1769480 | tf_op jit(solution)/shard_map/ppermute | solution.py:24
  189.6 52.0 %collective-permute-start.31 = (bf16[256,2304]{1,0:T(8,128)(2,1)S(1)}, bf16[256,2304]{1,0:T(8,128)(2,1)S(1)}, u32[]{:S(2)}, u32[]{:S(2)}) collective-permute-start(bf16[256,2304]{1,0:T(8,128)(2,1)S(1)} %multiply_convert_fusion.1.refs_0_.refs_2_), channel_id=1, source_target_pairs={{0,2},{1,3},{2,0},{3,1},{4,6},{5,7},{6,4},{7,5},{8,10},{9,11},{10,... | collective-permute-start | bytes 3538952 | tf_op jit(solution)/shard_map/ppermute | solution.py:24
  191.2 50.4 %collective-permute-start.32 = (bf16[128,2304]{1,0:T(8,128)(2,1)}, bf16[128,2304]{1,0:T(8,128)(2,1)S(1)}, u32[]{:S(2)}, u32[]{:S(2)}) collective-permute-start(bf16[128,2304]{1,0:T(8,128)(2,1)} %get-tuple-element.310), channel_id=1, source_target_pairs={{0,2},{1,3},{2,0},{3,1},{4,6},{5,7},{6,4},{7,5},{8,10},{9,11},{10,... | collective-permute-start | bytes 1769480 | tf_op jit(solution)/shard_map/ppermute | solution.py:24
  288.1 17.2 %collective-permute-start.43 = (bf16[256,2432]{1,0:T(8,128)(2,1)S(1)}, bf16[256,2432]{1,0:T(8,128)(2,1)S(1)}, u32[]{:S(2)}, u32[]{:S(2)}) collective-permute-start(bf16[256,2432]{1,0:T(8,128)(2,1)S(1)} %copy-done.109), channel_id=1, source_target_pairs={{0,1},{1,0},{2,3},{3,2},{4,5},{5,4},{6,7},{7,6},{8,9},{9,8},{10,11... | collective-permute-start | bytes 3735560 | tf_op jit(solution)/shard_map/ppermute | solution.py:24
  288.3 17.0 %collective-permute-start.44 = (bf16[256,2432]{1,0:T(8,128)(2,1)S(1)}, bf16[256,2432]{1,0:T(8,128)(2,1)S(1)}, u32[]{:S(2)}, u32[]{:S(2)}) collective-permute-start(bf16[256,2432]{1,0:T(8,128)(2,1)S(1)} %copy-done.110), channel_id=1, source_target_pairs={{0,1},{1,0},{2,3},{3,2},{4,5},{5,4},{6,7},{7,6},{8,9},{9,8},{10,11... | collective-permute-start | bytes 3735560 | tf_op jit(solution)/shard_map/ppermute | solution.py:24
  288.7 16.6 %collective-permute-start.45 = (bf16[256,2432]{1,0:T(8,128)(2,1)S(1)}, bf16[256,2432]{1,0:T(8,128)(2,1)S(1)}, u32[]{:S(2)}, u32[]{:S(2)}) collective-permute-start(bf16[256,2432]{1,0:T(8,128)(2,1)S(1)} %copy-done.108), channel_id=1, source_target_pairs={{0,1},{1,0},{2,3},{3,2},{4,5},{5,4},{6,7},{7,6},{8,9},{9,8},{10,11... | collective-permute-start | bytes 3735560 | tf_op jit(solution)/shard_map/ppermute | solution.py:24
  288.9 16.4 %collective-permute-start.42 = (bf16[128,2432]{1,0:T(8,128)(2,1)S(1)}, bf16[128,2432]{1,0:T(8,128)(2,1)S(1)}, u32[]{:S(2)}, u32[]{:S(2)}) collective-permute-start(bf16[128,2432]{1,0:T(8,128)(2,1)S(1)} %get-tuple-element.501), channel_id=1, source_target_pairs={{0,2},{1,3},{2,0},{3,1},{4,6},{5,7},{6,4},{7,5},{8,10},{9,11},{10,... | collective-permute-start | bytes 1867784 | tf_op jit(solution)/shard_map/ppermute | solution.py:24
  289.5 19.4 %collective-permute-start.47 = (bf16[1,64,1440]{2,1,0:T(8,128)(2,1)S(1)}, bf16[1,64,1440]{2,1,0:T(8,128)(2,1)S(1)}, u32[]{:S(2)}, u32[]{:S(2)}) collective-permute-start(bf16[1,64,1440]{2,1,0:T(8,128)(2,1)S(1)} %pad_bitcast_fusion), channel_id=1, source_target_pairs={{0,8},{4,12},{8,0},{12,4},{16,24},{20,28},{24,16},{28,20},{1,9},{5... | collective-permute-start | bytes 552968 | tf_op jit(solution)/shard_map/ppermute | solution.py:24
  305.3 15.5 %collective-permute-start.46 = (bf16[128,2432]{1,0:T(8,128)(2,1)S(1)}, bf16[128,2432]{1,0:T(8,128)(2,1)S(1)}, u32[]{:S(2)}, u32[]{:S(2)}) collective-permute-start(bf16[128,2432]{1,0:T(8,128)(2,1)S(1)} %get-tuple-element.346), channel_id=1, source_target_pairs={{0,2},{1,3},{2,0},{3,1},{4,6},{5,7},{6,4},{7,5},{8,10},{9,11},{10,... | collective-permute-start | bytes 1867784 | tf_op jit(solution)/shard_map/ppermute | solution.py:24
  329.0 30.1 %collective-permute-start.48 = (bf16[256,2432]{1,0:T(8,128)(2,1)}, bf16[256,2432]{1,0:T(8,128)(2,1)}, u32[]{:S(2)}, u32[]{:S(2)}) collective-permute-start(bf16[256,2432]{1,0:T(8,128)(2,1)} %concatenate.265.refs_0_), channel_id=1, source_target_pairs={{0,2},{1,3},{2,0},{3,1},{4,6},{5,7},{6,4},{7,5},{8,10},{9,11},{10,... | collective-permute-start | bytes 3735560 | tf_op jit(solution)/shard_map/ppermute | solution.py:24
  330.3 20.8 %collective-permute-start.50 = (bf16[2,64,1440]{2,1,0:T(8,128)(2,1)}, bf16[2,64,1440]{2,1,0:T(8,128)(2,1)}, u32[]{:S(2)}, u32[]{:S(2)}) collective-permute-start(bf16[2,64,1440]{2,1,0:T(8,128)(2,1)} %maximum_select_fusion.6), channel_id=1, source_target_pairs={{0,16},{4,20},{8,24},{12,28},{16,0},{20,4},{24,8},{28,12},{1,17},{... | collective-permute-start | bytes 1105928 | tf_op jit(solution)/shard_map/ppermute | solution.py:24
  359.1 30.1 %collective-permute-start.52 = (bf16[256,2432]{1,0:T(8,128)(2,1)}, bf16[256,2432]{1,0:T(8,128)(2,1)}, u32[]{:S(2)}, u32[]{:S(2)}) collective-permute-start(bf16[256,2432]{1,0:T(8,128)(2,1)} %add_convert_fusion), channel_id=1, source_target_pairs={{0,2},{1,3},{2,0},{3,1},{4,6},{5,7},{6,4},{7,5},{8,10},{9,11},{10,... | collective-permute-start | bytes 3735560 | tf_op jit(solution)/shard_map/ppermute | solution.py:24
  360.8 25.8 %collective-permute-start.53 = (bf16[4,64,1440]{2,1,0:T(8,128)(2,1)}, bf16[4,64,1440]{2,1,0:T(8,128)(2,1)S(1)}, u32[]{:S(2)}, u32[]{:S(2)}) collective-permute-start(bf16[4,64,1440]{2,1,0:T(8,128)(2,1)} %maximum_select_fusion.3), channel_id=1, source_target_pairs={{0,4},{4,0},{8,12},{12,8},{16,20},{20,16},{24,28},{28,24},{1,5},{5... | collective-permute-start | bytes 2211848 | tf_op jit(solution)/shard_map/ppermute | solution.py:24
  390.1 17.1 %collective-permute-start.54 = (bf16[256,16]{1,0:T(8,128)(2,1)S(1)}, bf16[256,16]{1,0:T(8,128)(2,1)S(1)}, u32[]{:S(2)}, u32[]{:S(2)}) collective-permute-start(bf16[256,16]{1,0:T(8,128)(2,1)S(1)} %fusion.35), channel_id=1, source_target_pairs={{0,2},{1,3},{2,0},{3,1},{4,6},{5,7},{6,4},{7,5},{8,10},{9,11},{10,... | collective-permute-start | bytes 24584 | tf_op jit(solution)/shard_map/ppermute | solution.py:24
  390.6 16.6 %collective-permute-start.55 = (bf16[256,16]{1,0:T(8,128)(2,1)S(1)}, bf16[256,16]{1,0:T(8,128)(2,1)S(1)}, u32[]{:S(2)}, u32[]{:S(2)}) collective-permute-start(bf16[256,16]{1,0:T(8,128)(2,1)S(1)} %fusion.35), channel_id=1, source_target_pairs={{0,1},{1,0},{2,3},{3,2},{4,5},{5,4},{6,7},{7,6},{8,9},{9,8},{10,11... | collective-permute-start | bytes 24584 | tf_op jit(solution)/shard_map/ppermute | solution.py:24
  427.8 18.9 %collective-permute-start.64 = (bf16[2,80,576]{2,1,0:T(8,128)(2,1)S(1)}, bf16[2,80,576]{2,1,0:T(8,128)(2,1)S(1)}, u32[]{:S(2)}, u32[]{:S(2)}) collective-permute-start(bf16[2,80,576]{2,1,0:T(8,128)(2,1)S(1)} %maximum_select_fusion.8), channel_id=1, source_target_pairs={{0,16},{4,20},{8,24},{12,28},{16,0},{20,4},{24,8},{28,12},{1,17},{... | collective-permute-start | bytes 552968 | tf_op jit(solution)/shard_map/ppermute | solution.py:24
  452.5 17.4 %collective-permute-start.68 = (bf16[128,2304]{1,0:T(8,128)(2,1)}, bf16[128,2304]{1,0:T(8,128)(2,1)}, u32[]{:S(2)}, u32[]{:S(2)}) collective-permute-start(bf16[128,2304]{1,0:T(8,128)(2,1)} %get-tuple-element.505), channel_id=1, source_target_pairs={{0,2},{1,3},{2,0},{3,1},{4,6},{5,7},{6,4},{7,5},{8,10},{9,11},{10,... | collective-permute-start | bytes 1769480 | tf_op jit(solution)/shard_map/ppermute | solution.py:24
  454.1 15.8 %collective-permute-start.66 = (bf16[2,96,576]{2,1,0:T(8,128)(2,1)}, bf16[2,96,576]{2,1,0:T(8,128)(2,1)S(1)}, u32[]{:S(2)}, u32[]{:S(2)}) collective-permute-start(bf16[2,96,576]{2,1,0:T(8,128)(2,1)} %maximum_select_fusion.7), channel_id=1, source_target_pairs={{0,16},{4,20},{8,24},{12,28},{16,0},{20,4},{24,8},{28,12},{1,17},{... | collective-permute-start | bytes 663560 | tf_op jit(solution)/shard_map/ppermute | solution.py:24
  470.6 22.0 %collective-permute-start.71 = (bf16[256,2304]{1,0:T(8,128)(2,1)}, bf16[256,2304]{1,0:T(8,128)(2,1)}, u32[]{:S(2)}, u32[]{:S(2)}) collective-permute-start(bf16[256,2304]{1,0:T(8,128)(2,1)} %get-tuple-element.463), channel_id=1, source_target_pairs={{0,1},{1,0},{2,3},{3,2},{4,5},{5,4},{6,7},{7,6},{8,9},{9,8},{10,11... | collective-permute-start | bytes 3538952 | tf_op jit(solution)/shard_map/ppermute | solution.py:24
  476.1 16.1 %collective-permute-start.70 = (bf16[128,2304]{1,0:T(8,128)(2,1)S(1)}, bf16[128,2304]{1,0:T(8,128)(2,1)S(1)}, u32[]{:S(2)}, u32[]{:S(2)}) collective-permute-start(bf16[128,2304]{1,0:T(8,128)(2,1)S(1)} %copy-done.84), channel_id=1, source_target_pairs={{0,2},{1,3},{2,0},{3,1},{4,6},{5,7},{6,4},{7,5},{8,10},{9,11},{10,... | collective-permute-start | bytes 1769480 | tf_op jit(solution)/shard_map/ppermute | solution.py:24
  476.6 16.0 %collective-permute-start.69 = (bf16[4,96,576]{2,1,0:T(8,128)(2,1)S(1)}, bf16[4,96,576]{2,1,0:T(8,128)(2,1)S(1)}, u32[]{:S(2)}, u32[]{:S(2)}) collective-permute-start(bf16[4,96,576]{2,1,0:T(8,128)(2,1)S(1)} %maximum_select_fusion.4), channel_id=1, source_target_pairs={{0,4},{4,0},{8,12},{12,8},{16,20},{20,16},{24,28},{28,24},{1,5},{5... | collective-permute-start | bytes 1327112 | tf_op jit(solution)/shard_map/ppermute | solution.py:24
  479.2 20.2 %collective-permute-start.77 = (bf16[5,2,16,576]{3,2,1,0:T(8,128)(2,1)S(1)}, bf16[5,2,16,576]{3,2,1,0:T(8,128)(2,1)S(1)}, u32[]{:S(2)}, u32[]{:S(2)}) collective-permute-start(bf16[5,2,16,576]{3,2,1,0:T(8,128)(2,1)S(1)} %get-tuple-element.490), channel_id=1, source_target_pairs={{0,3},{1,2},{2,1},{3,0},{4,7},{5,6},{6,5},{7,4},{8,11},{9,10},{10,... | collective-permute-start | bytes 552968 | tf_op jit(solution)/shard_map/ppermute | solution.py:24
  480.4 22.9 %collective-permute-start.75 = (bf16[5,2,16,576]{3,2,1,0:T(8,128)(2,1)S(1)}, bf16[5,2,16,576]{3,2,1,0:T(8,128)(2,1)S(1)}, u32[]{:S(2)}, u32[]{:S(2)}) collective-permute-start(bf16[5,2,16,576]{3,2,1,0:T(8,128)(2,1)S(1)} %get-tuple-element.491), channel_id=1, source_target_pairs={{0,1},{1,0},{2,3},{3,2},{4,5},{5,4},{6,7},{7,6},{8,9},{9,8},{10,11... | collective-permute-start | bytes 552968 | tf_op jit(solution)/shard_map/ppermute | solution.py:24
  (145 other events, 1131.9 us)

commit v8 on v7

--- a/solution.py
+++ b/solution.py
@@ -384,7 +384,10 @@
             q, g, logs, inner = query
             here = slice(keys * rows, (keys + many) * rows)
             raw = dot_t(k_ref[head, here, :], q)
-            if mask is not None:
+            if many > 1:
+                edge = (many - 1) * rows
+                raw = jnp.concatenate([raw[:edge], raw[edge:] + mask], axis=0)
+            else:
                 raw = raw + mask
             probs = jnp.exp2(raw * factor - logs)
             grad_probs = dot_t(v_ref[head, here, :], g)
@@ -414,12 +417,9 @@
                 inner = (dot_t(ones, high) + dot_t(ones, low))[:1]
                 queries.append((q_ref[head, here, :], g, log_ref[head, :, here], inner))
             last = block == count - 1
-            totals = [pair(head, queries[head], block, bias[block, :rows, :], last) for head in range(heads)]
-            for keys in range(0, block, 4):
-                for head in range(heads):
-                    totals[head] = totals[head] + pair(
-                        head, queries[head], keys, None, last, min(4, block - keys)
-                    )
+            totals = [
+                pair(head, queries[head], 0, bias[block, :rows, :], last, block + 1) for head in range(heads)
+            ]
             if not last:
                 for head in range(heads):
                     query_sum[head] = totals[head]

time: 523 us -> 523 us (level)
  no operation moved by 1% of the time
where the time goes in v8:
time: 523 us; the launch traced here: 515 us
  Pallas kernels  196 us (37%)
  waiting for transfers between devices  136 us (26%)
  local copies, waits for them, and re-layouts  65 us (12%)
  starting transfers between devices  63.6 us (12%)
  other arithmetic  42.7 us (8%)
  matrix products  7.92 us (2%)
    ppermute x78, waiting for transfers between devices, hop(): return lax.ppermute(values, axis, [(i, i ^ bit) for i in range(size)])  136 us
    pallas_call x2, Pallas kernels, feed_forward(): call(kernel, [out] * (2 * count) + [jax.ShapeDtypeStruct((3 * rank, size)...  71.4 us
    ppermute x78, starting transfers between devices, hop(): return lax.ppermute(values, axis, [(i, i ^ bit) for i in range(size)])  63.6 us
    pallas_call x3, Pallas kernels, attend_back(): call(kernel, [jax.ShapeDtypeStruct((heads, length, HDIM), BF16)] * 3 + [j...  32.9 us
    unnamed x229, local copies, waits for them, and re-layouts  25.6 us
    pallas_call x2, Pallas kernels, project_back(): call(kernel, [jax.ShapeDtypeStruct((rows, width), BF16)] * count, [smem()...  24.7 us
    pallas_call x1, Pallas kernels, project(): call(kernel, [by_heads] * 3 + [jax.ShapeDtypeStruct((thin, rows * count),...  21 us
    pallas_call x1, Pallas kernels, attend(): call(kernel, [jax.ShapeDtypeStruct(query.shape, BF16), jax.ShapeDtypeStru...  16.5 us
  transfers between devices with their start and end apart: 78, of which 32 were waited for; matrix products, arithmetic and copies ran while one was open for 13% of the time, Pallas kernels for 31%

profile of v8, /device:TPU:0, one launch (start us, length us, event | category | flops | bytes accessed | tf_op | source)
XLA Modules:
  0.0 515.1 jit_solution(5903824226276767272)
XLA Ops:
  5.2 3.6 sides_far.1
  8.9 2.6 collective-permute-start
  29.0 7.0 %sides_near.1 = (bf16[576,1728]{1,0:T(8,128)(2,1)}, bf16[576,1728]{1,0:T(8,128)(2,1)}) custom-call(s32[2]{0:T(128)} %get-tuple-element.575.where_ref, bf16[3,576,2304]{2,1,0:T(8,128)(2,1)} %w_ref.4), custom_call_target="tpu_custom_call" | custom-call | bytes 11943936 | tf_op jit(solution)/shard_map/sides_near/pallas_call | solution.py:143
  36.1 3.3 collective-permute-done.2.refs_10_.refs_15_
  49.6 7.0 %collective-permute-done.4.refs_12_.refs_17_ = bf16[144,1728]{1,0:T(8,128)(2,1)S(1)} collective-permute-done((bf16[144,1728]{1,0:T(8,128)(2,1)}, bf16[144,1728]{1,0:T(8,128)(2,1)S(1)}, u32[]{:S(2)}, u32[]{:S(2)}) %collective-permute-start.4) | collective-permute-done | bytes 497696 | tf_op jit(solution)/shard_map/ppermute | solution.py:24
  61.8 3.6 constant_dynamic-slice_fusion.9
  70.1 8.7 %collective-permute-done.11.refs_13_.refs_18_ = bf16[144,1728]{1,0:T(8,128)(2,1)S(1)} collective-permute-done((bf16[144,1728]{1,0:T(8,128)(2,1)S(1)}, bf16[144,1728]{1,0:T(8,128)(2,1)S(1)}, u32[]{:S(2)}, u32[]{:S(2)}) %collective-permute-start.11) | collective-permute-done | bytes 497696 | tf_op jit(solution)/shard_map/ppermute | solution.py:24
  78.9 6.5 %collective-permute-done.9.refs_2_ = bf16[256,2304]{1,0:T(8,128)(2,1)S(1)} collective-permute-done((bf16[256,2304]{1,0:T(8,128)(2,1)S(1)}, bf16[256,2304]{1,0:T(8,128)(2,1)S(1)}, u32[]{:S(2)}, u32[]{:S(2)}) %collective-permute-start.9) | collective-permute-done | bytes 1179680 | tf_op jit(solution)/shard_map/ppermute | solution.py:24
  88.9 21.0 %project.1 = (bf16[9,1024,64]{2,1,0:T(8,128)(2,1)}, bf16[9,1024,64]{2,1,0:T(8,128)(2,1)}, bf16[9,1024,64]{2,1,0:T(8,128)(2,1)}, bf16[48,1024]{1,0:T(8,128)(2,1)}) custom-call(s32[1]{0:T(128)} %bitcast.place_ref, s32[10]{0:T(128)} %stack.110.offsets_ref, bf16[256,2304]{1,0:T(8,128)(2,1)} %copy-done.9, bf16[256,2304]{1,0:T(8,128)(2,1)} %copy-done.20, ...), custom_call_target="tpu_custom_call" | custom-call | flops 8153726976 | bytes 19759104 | tf_op jit(solution)/shard_map/project/pallas_call | solution.py:255
  113.6 16.5 %attend.1 = (bf16[9,1024,64]{2,1,0:T(8,128)(2,1)}, f32[9,1,1024]{2,1,0:T(1,128)}) custom-call(s32[2]{0:T(128)} %bitcast.170, bf16[9,1024,64]{2,1,0:T(8,128)(2,1)} %get-tuple-element.280.q_ref, bf16[9,1024,64]{2,1,0:T(8,128)(2,1)} %get-tuple-element.281.k_ref, bf16[9,1024,64]{2,1,0:T(8,128)(2,1)} %get-tuple-element.282.v_ref), custom_call_target="tpu_custom_call" | custom-call | flops 9663676416 | bytes 9437184 | tf_op jit(solution)/shard_map/attend/pallas_call | solution.py:349
  137.1 2.2 close_attention.2
  143.8 4.6 collective-permute-done.24
  153.9 2.2 close_attention.3
  156.1 9.0 %constant_dynamic-slice_fusion.4 = (bf16[2,576,1440]{2,1,0:T(8,128)(2,1)}, bf16[2,576,1440]{2,1,0:T(8,128)(2,1)S(1)}) fusion(bf16[2,576,5760]{2,1,0:T(8,128)(2,1)} %param.22, s32[]{:T(128)S(6)} %select_n.365, s32[]{:T(128)S(6)} %select_n.364), kind=kLoop, calls=%fused_computation.177 | loop fusion | bytes 13271048 | tf_op jit(solution)/shard_map/dynamic_slice | solution.py:121
  169.7 12.0 %collective-permute-done.29 = bf16[128,2432]{1,0:T(8,128)(2,1)S(1)} collective-permute-done((bf16[128,2432]{1,0:T(8,128)(2,1)S(1)}, bf16[128,2432]{1,0:T(8,128)(2,1)S(1)}, u32[]{:S(2)}, u32[]{:S(2)}) %collective-permute-start.29) | collective-permute-done | bytes 622624 | tf_op jit(solution)/shard_map/ppermute | solution.py:24
  191.6 11.7 %collective-permute-done.38 = bf16[128,2304]{1,0:T(8,128)(2,1)S(1)} collective-permute-done((bf16[128,2304]{1,0:T(8,128)(2,1)S(1)}, bf16[128,2304]{1,0:T(8,128)(2,1)S(1)}, u32[]{:S(2)}, u32[]{:S(2)}) %collective-permute-start.38) | collective-permute-done | bytes 589856 | tf_op jit(solution)/shard_map/ppermute | solution.py:24
  205.6 35.9 %feed_forward.2 = (bf16[256,2432]{1,0:T(8,128)(2,1)}, bf16[256,2432]{1,0:T(8,128)(2,1)}, bf16[256,2432]{1,0:T(8,128)(2,1)}, bf16[256,2432]{1,0:T(8,128)(2,1)}, f32[48,1440]{1,0:T(8,128)}) custom-call(s32[10]{0:T(128)} %stack.110.offsets_ref, bf16[256,2304]{1,0:T(8,128)(2,1)} %copy-done.7, bf16[256,2304]{1,0:T(8,128)(2,1)} %copy-done.28, ...), custom_call_target="tpu_custom_call" | custom-call | flops 20384317440 | bytes 29343744 | tf_op jit(solution)/shard_map/feed_forward/pallas_call | solution.py:626
  242.2 2.3 collective-permute-done.40.refs_3_
  247.3 35.5 %feed_forward.3 = (bf16[256,2432]{1,0:T(8,128)(2,1)}, bf16[256,2432]{1,0:T(8,128)(2,1)}, bf16[256,2432]{1,0:T(8,128)(2,1)}, bf16[256,2432]{1,0:T(8,128)(2,1)}, f32[48,1440]{1,0:T(8,128)}) custom-call(s32[10]{0:T(128)} %stack.110.offsets_ref, bf16[256,2304]{1,0:T(8,128)(2,1)} %copy-done.24, bf16[256,2304]{1,0:T(8,128)(2,1)} %copy-done.26, ...), custom_call_target="tpu_custom_call" | custom-call | flops 20384317440 | bytes 29343744 | tf_op jit(solution)/shard_map/feed_forward/pallas_call | solution.py:626
  284.0 2.1 collective-permute-done.41
  286.1 2.0 add_convert_fusion.1
  290.8 14.5 %collective-permute-done.42 = bf16[128,2432]{1,0:T(8,128)(2,1)S(1)} collective-permute-done((bf16[128,2432]{1,0:T(8,128)(2,1)S(1)}, bf16[128,2432]{1,0:T(8,128)(2,1)S(1)}, u32[]{:S(2)}, u32[]{:S(2)}) %collective-permute-start.42) | collective-permute-done | bytes 622624 | tf_op jit(solution)/shard_map/ppermute | solution.py:24
  308.9 11.9 %collective-permute-done.46 = bf16[128,2432]{1,0:T(8,128)(2,1)S(1)} collective-permute-done((bf16[128,2432]{1,0:T(8,128)(2,1)S(1)}, bf16[128,2432]{1,0:T(8,128)(2,1)S(1)}, u32[]{:S(2)}, u32[]{:S(2)}) %collective-permute-start.46) | collective-permute-done | bytes 622624 | tf_op jit(solution)/shard_map/ppermute | solution.py:24
  323.0 2.5 multiply_convert_fusion
  325.5 3.5 concatenate.265.refs_0_
  330.3 2.6 collective-permute-start.50
  338.5 6.1 %open_attention.2 = (bf16[9,512,64]{2,1,0:T(8,128)(2,1)S(1)}, f32[16,576]{1,0:T(8,128)S(1)}, f32[48,2304]{1,0:T(8,128)S(1)}) custom-call(s32[1]{0:T(128)} %bitcast.place_ref, bf16[256,2432]{1,0:T(8,128)(2,1)S(1)} %copy-done.6, bf16[256,2432]{1,0:T(8,128)(2,1)} %collective-permute-done.49.refs_1_, bf16[256,2304]{1,0:T(8,128)(2,1)S(1)} %copy-done.8, ...), custom_call_target="tpu_custom_call" | custom-call | flops 1358954496 | bytes 8552448 | tf_op jit(solution)/shard_map/open_attention/pallas_call | solution.py:553
  345.6 5.6 %collective-permute-done.50 = bf16[2,64,1440]{2,1,0:T(8,128)(2,1)} collective-permute-done((bf16[2,64,1440]{2,1,0:T(8,128)(2,1)}, bf16[2,64,1440]{2,1,0:T(8,128)(2,1)}, u32[]{:S(2)}, u32[]{:S(2)}) %collective-permute-start.50) | collective-permute-done | bytes 368672 | tf_op jit(solution)/shard_map/ppermute | solution.py:24
  351.2 2.6 maximum_select_fusion.3
  353.7 5.4 %collective-permute-done.48.refs_0_ = bf16[256,2432]{1,0:T(8,128)(2,1)} collective-permute-done((bf16[256,2432]{1,0:T(8,128)(2,1)}, bf16[256,2432]{1,0:T(8,128)(2,1)}, u32[]{:S(2)}, u32[]{:S(2)}) %collective-permute-start.48) | collective-permute-done | bytes 1245216 | tf_op jit(solution)/shard_map/ppermute | solution.py:24
  366.7 6.6 %open_attention.3 = (bf16[9,512,64]{2,1,0:T(8,128)(2,1)S(1)}, f32[16,576]{1,0:T(8,128)S(1)}, f32[48,2304]{1,0:T(8,128)S(1)}) custom-call(s32[1]{0:T(128)} %bitcast.place_ref, bf16[256,2432]{1,0:T(8,128)(2,1)} %collective-permute-done.48.refs_0_, bf16[256,2432]{1,0:T(8,128)(2,1)} %collective-permute-done.51.refs_1_, bf16[256,2304]{1,0:T(8,128)(2,1)S(1)} %copy-done.25, ...), custom_call_target="tpu_custom_call" | custom-call | flops 1358954496 | bytes 8552448 | tf_op jit(solution)/shard_map/open_attention/pallas_call | solution.py:553
  375.1 10.9 %attend_back.3 = (bf16[3,1024,64]{2,1,0:T(8,128)(2,1)S(1)}, bf16[3,1024,64]{2,1,0:T(8,128)(2,1)S(1)}, bf16[3,1024,64]{2,1,0:T(8,128)(2,1)S(1)}, f32[48,1024]{1,0:T(8,128)S(1)}, f32[48,192]{1,0:T(8,128)S(1)}) custom-call(s32[2]{0:T(128)S(1)} %bitcast.171, s32[1]{0:T(128)} %bitcast.place_ref, bf16[9,1024,64]{2,1,0:T(8,128)(2,1)S(1)} %copy-done.35, ...), custom_call_target="tpu_custom_call" | custom-call | flops 8053063680 | bytes 6291456 | tf_op jit(solution)/shard_map/attend_back/pallas_call | solution.py:458
  386.0 3.2 collective-permute-done.52
  395.3 11.1 %attend_back.4 = (bf16[3,1024,64]{2,1,0:T(8,128)(2,1)S(1)}, bf16[3,1024,64]{2,1,0:T(8,128)(2,1)S(1)}, bf16[3,1024,64]{2,1,0:T(8,128)(2,1)S(1)}, f32[48,1024]{1,0:T(8,128)S(1)}, f32[48,192]{1,0:T(8,128)S(1)}) custom-call(s32[2]{0:T(128)S(1)} %bitcast.172, s32[1]{0:T(128)} %bitcast.place_ref, bf16[9,1024,64]{2,1,0:T(8,128)(2,1)S(1)} %copy-done.35, ...), custom_call_target="tpu_custom_call" | custom-call | flops 8053063680 | bytes 6291456 | tf_op jit(solution)/shard_map/attend_back/pallas_call | solution.py:458
  406.7 2.1 collective-permute-done.57
  413.2 10.9 %attend_back.5 = (bf16[3,1024,64]{2,1,0:T(8,128)(2,1)S(1)}, bf16[3,1024,64]{2,1,0:T(8,128)(2,1)S(1)}, bf16[3,1024,64]{2,1,0:T(8,128)(2,1)S(1)}, f32[48,1024]{1,0:T(8,128)S(1)}, f32[48,192]{1,0:T(8,128)S(1)}) custom-call(s32[2]{0:T(128)S(1)} %bitcast.173, s32[1]{0:T(128)} %bitcast.place_ref, bf16[9,1024,64]{2,1,0:T(8,128)(2,1)S(1)} %copy-done.35, ...), custom_call_target="tpu_custom_call" | custom-call | flops 8053063680 | bytes 6291456 | tf_op jit(solution)/shard_map/attend_back/pallas_call | solution.py:458
  427.2 2.6 collective-permute-start.64
  430.5 2.2 thin_product.1
  433.1 12.4 %project_back.2 = (bf16[256,2304]{1,0:T(8,128)(2,1)}, bf16[256,2304]{1,0:T(8,128)(2,1)}) custom-call(s32[1]{0:T(128)} %bitcast.place_ref, s32[10]{0:T(128)} %stack.110.offsets_ref, bf16[3,1024,64]{2,1,0:T(8,128)(2,1)} %copy-done.11, bf16[3,1024,64]{2,1,0:T(8,128)(2,1)} %copy-done.14, bf16[3,1024,64]{2,1,0:T(8,128)(2,1)} %copy-done.17, ...), custom_call_target="tpu_custom_call" | custom-call | flops 4076863488 | bytes 12091392 | tf_op jit(solution)/shard_map/project_back/pallas_call | solution.py:663
  446.5 2.2 collective-permute-done.65
  452.7 3.4 collective-permute-start.66
  456.9 12.4 %project_back.3 = (bf16[256,2304]{1,0:T(8,128)(2,1)}, bf16[256,2304]{1,0:T(8,128)(2,1)}) custom-call(s32[1]{0:T(128)} %bitcast.place_ref, s32[10]{0:T(128)} %stack.110.offsets_ref, bf16[3,1024,64]{2,1,0:T(8,128)(2,1)} %copy-done.11, bf16[3,1024,64]{2,1,0:T(8,128)(2,1)} %copy-done.14, bf16[3,1024,64]{2,1,0:T(8,128)(2,1)} %copy-done.17, ...), custom_call_target="tpu_custom_call" | custom-call | flops 4076863488 | bytes 12091392 | tf_op jit(solution)/shard_map/project_back/pallas_call | solution.py:663
  470.0 2.9 add_convert_fusion.3
  480.4 11.2 %collective-permute-done.70 = bf16[128,2304]{1,0:T(8,128)(2,1)S(1)} collective-permute-done((bf16[128,2304]{1,0:T(8,128)(2,1)S(1)}, bf16[128,2304]{1,0:T(8,128)(2,1)S(1)}, u32[]{:S(2)}, u32[]{:S(2)}) %collective-permute-start.70) | collective-permute-done | bytes 589856 | tf_op jit(solution)/shard_map/ppermute | solution.py:24
  496.3 2.5 fusion.11
  499.4 2.0 fusion.10
  502.6 2.0 collective-permute-done.74
  504.7 5.7 %collective-permute-done.73 = bf16[6,2,16,576]{3,2,1,0:T(8,128)(2,1)S(1)} collective-permute-done((bf16[6,2,16,576]{3,2,1,0:T(8,128)(2,1)S(1)}, bf16[6,2,16,576]{3,2,1,0:T(8,128)(2,1)S(1)}, u32[]{:S(2)}, u32[]{:S(2)}) %collective-permute-start.73) | collective-permute-done | bytes 221216 | tf_op jit(solution)/shard_map/ppermute | solution.py:24
  (487 shorter events, 151.7 us)
Async XLA Ops:
  4.2 19.2 %collective-permute-start.1 = (bf16[6,16,2304]{2,1,0:T(8,128)(2,1)}, bf16[6,16,2304]{2,1,0:T(8,128)(2,1)}, u32[]{:S(2)}, u32[]{:S(2)}) collective-permute-start(bf16[6,16,2304]{2,1,0:T(8,128)(2,1)} %fusion.20), channel_id=1, source_target_pairs={{0,1},{1,0},{2,3},{3,2},{4,5},{5,4},{6,7},{7,6},{8,9},{9,8},{10,11... | collective-permute-start | bytes 1327112 | tf_op jit(solution)/shard_map/ppermute | solution.py:24
  8.9 15.8 %collective-permute-start = (bf16[144,1728]{1,0:T(8,128)(2,1)}, bf16[144,1728]{1,0:T(8,128)(2,1)S(1)}, u32[]{:S(2)}, u32[]{:S(2)}) collective-permute-start(bf16[144,1728]{1,0:T(8,128)(2,1)} %get-tuple-element.244), channel_id=1, source_target_pairs={{0,2},{1,3},{2,0},{3,1},{4,6},{5,7},{6,4},{7,5},{8,10},{9,11},{10,... | collective-permute-start | bytes 1493000 | tf_op jit(solution)/shard_map/ppermute | solution.py:24
  25.6 16.6 %collective-permute-start.7 = (bf16[144,1728]{1,0:T(8,128)(2,1)S(1)}, bf16[144,1728]{1,0:T(8,128)(2,1)}, u32[]{:S(2)}, u32[]{:S(2)}) collective-permute-start(bf16[144,1728]{1,0:T(8,128)(2,1)S(1)} %collective-permute-done.refs_6_.refs_11_), channel_id=1, source_target_pairs={{0,4},{4,0},{8,12},{12,8},{16,20},{20,16},{24,28},{28,24},{1,5},{5... | collective-permute-start | bytes 1493000 | tf_op jit(solution)/shard_map/ppermute | solution.py:24
  27.4 16.5 %collective-permute-start.6 = (bf16[144,1728]{1,0:T(8,128)(2,1)S(1)}, bf16[144,1728]{1,0:T(8,128)(2,1)}, u32[]{:S(2)}, u32[]{:S(2)}) collective-permute-start(bf16[144,1728]{1,0:T(8,128)(2,1)S(1)} %collective-permute-done.refs_6_.refs_11_), channel_id=1, source_target_pairs={{0,8},{4,12},{8,0},{12,4},{16,24},{20,28},{24,16},{28,20},{1,9},{5... | collective-permute-start | bytes 1493000 | tf_op jit(solution)/shard_map/ppermute | solution.py:24
  29.0 58.9 %collective-permute-start.8 = (bf16[256,2304]{1,0:T(8,128)(2,1)S(1)}, bf16[256,2304]{1,0:T(8,128)(2,1)S(1)}, u32[]{:S(2)}, u32[]{:S(2)}) collective-permute-start(bf16[256,2304]{1,0:T(8,128)(2,1)S(1)} %fusion.7.refs_0_), channel_id=1, source_target_pairs={{0,1},{1,0},{2,3},{3,2},{4,5},{5,4},{6,7},{7,6},{8,9},{9,8},{10,11... | collective-permute-start | bytes 3538952 | tf_op jit(solution)/shard_map/ppermute | solution.py:24
  42.2 14.4 %collective-permute-start.4 = (bf16[144,1728]{1,0:T(8,128)(2,1)}, bf16[144,1728]{1,0:T(8,128)(2,1)S(1)}, u32[]{:S(2)}, u32[]{:S(2)}) collective-permute-start(bf16[144,1728]{1,0:T(8,128)(2,1)} %collective-permute-done.2.refs_10_.refs_15_), channel_id=1, source_target_pairs={{0,8},{4,12},{8,0},{12,4},{16,24},{20,28},{24,16},{28,20},{1,9},{5... | collective-permute-start | bytes 1493000 | tf_op jit(solution)/shard_map/ppermute | solution.py:24
  47.2 19.1 %collective-permute-start.14 = (bf16[3,16,5760]{2,1,0:T(8,128)(2,1)S(1)}, bf16[3,16,5760]{2,1,0:T(8,128)(2,1)S(1)}, u32[]{:S(2)}, u32[]{:S(2)}) collective-permute-start(bf16[3,16,5760]{2,1,0:T(8,128)(2,1)S(1)} %fusion.16), channel_id=1, source_target_pairs={{0,1},{1,0},{2,3},{3,2},{4,5},{5,4},{6,7},{7,6},{8,9},{9,8},{10,11... | collective-permute-start | bytes 1658888 | tf_op jit(solution)/shard_map/ppermute | solution.py:24
  49.4 38.5 %collective-permute-start.16 = (bf16[576,1728]{1,0:T(8,128)(2,1)}, bf16[576,1728]{1,0:T(8,128)(2,1)}, u32[]{:S(2)}, u32[]{:S(2)}) collective-permute-start(bf16[576,1728]{1,0:T(8,128)(2,1)} %get-tuple-element.267), channel_id=1, source_target_pairs={{0,1},{1,0},{2,3},{3,2},{4,5},{5,4},{6,7},{7,6},{8,9},{9,8},{10,11... | collective-permute-start | bytes 5971976 | tf_op jit(solution)/shard_map/ppermute | solution.py:24
  58.1 27.2 %collective-permute-start.9 = (bf16[256,2304]{1,0:T(8,128)(2,1)S(1)}, bf16[256,2304]{1,0:T(8,128)(2,1)S(1)}, u32[]{:S(2)}, u32[]{:S(2)}) collective-permute-start(bf16[256,2304]{1,0:T(8,128)(2,1)S(1)} %fusion.7.refs_0_), channel_id=1, source_target_pairs={{0,2},{1,3},{2,0},{3,1},{4,6},{5,7},{6,4},{7,5},{8,10},{9,11},{10,... | collective-permute-start | bytes 3538952 | tf_op jit(solution)/shard_map/ppermute | solution.py:24
  85.4 24.5 %collective-permute-start.17 = (bf16[2,144,1440]{2,1,0:T(8,128)(2,1)}, bf16[2,144,1440]{2,1,0:T(8,128)(2,1)}, u32[]{:S(2)}, u32[]{:S(2)}) collective-permute-start(bf16[2,144,1440]{2,1,0:T(8,128)(2,1)} %get-tuple-element.277), channel_id=1, source_target_pairs={{0,2},{1,3},{2,0},{3,1},{4,6},{5,7},{6,4},{7,5},{8,10},{9,11},{10,... | collective-permute-start | bytes 2488328 | tf_op jit(solution)/shard_map/ppermute | solution.py:24
  87.6 42.4 %collective-permute-start.18 = (bf16[2,144,1440]{2,1,0:T(8,128)(2,1)}, bf16[2,144,1440]{2,1,0:T(8,128)(2,1)}, u32[]{:S(2)}, u32[]{:S(2)}) collective-permute-start(bf16[2,144,1440]{2,1,0:T(8,128)(2,1)} %get-tuple-element.284), channel_id=1, source_target_pairs={{0,3},{1,2},{2,1},{3,0},{4,7},{5,6},{6,5},{7,4},{8,11},{9,10},{10,... | collective-permute-start | bytes 2488328 | tf_op jit(solution)/shard_map/ppermute | solution.py:24
  109.9 22.2 %collective-permute-start.20 = (bf16[2,144,1440]{2,1,0:T(8,128)(2,1)}, bf16[2,144,1440]{2,1,0:T(8,128)(2,1)S(1)}, u32[]{:S(2)}, u32[]{:S(2)}) collective-permute-start(bf16[2,144,1440]{2,1,0:T(8,128)(2,1)} %collective-permute-done.17.refs_6_), channel_id=1, source_target_pairs={{0,4},{4,0},{8,12},{12,8},{16,20},{20,16},{24,28},{28,24},{1,5},{5... | collective-permute-start | bytes 2488328 | tf_op jit(solution)/shard_map/ppermute | solution.py:24
  111.2 21.8 %collective-permute-start.19 = (bf16[2,144,1440]{2,1,0:T(8,128)(2,1)}, bf16[2,144,1440]{2,1,0:T(8,128)(2,1)S(1)}, u32[]{:S(2)}, u32[]{:S(2)}) collective-permute-start(bf16[2,144,1440]{2,1,0:T(8,128)(2,1)} %collective-permute-done.17.refs_6_), channel_id=1, source_target_pairs={{0,8},{4,12},{8,0},{12,4},{16,24},{20,28},{24,16},{28,20},{1,9},{5... | collective-permute-start | bytes 2488328 | tf_op jit(solution)/shard_map/ppermute | solution.py:24
  112.1 18.5 %collective-permute-start.21 = (bf16[5,8,2304]{2,1,0:T(8,128)(2,1)S(1)}, bf16[5,8,2304]{2,1,0:T(8,128)(2,1)S(1)}, u32[]{:S(2)}, u32[]{:S(2)}) collective-permute-start(bf16[5,8,2304]{2,1,0:T(8,128)(2,1)S(1)} %copy-done.99), channel_id=1, source_target_pairs={{0,2},{1,3},{2,0},{3,1},{4,6},{5,7},{6,4},{7,5},{8,10},{9,11},{10,... | collective-permute-start | bytes 552968 | tf_op jit(solution)/shard_map/ppermute | solution.py:24
  141.0 24.1 %collective-permute-start.26 = (bf16[2,144,1440]{2,1,0:T(8,128)(2,1)}, bf16[2,144,1440]{2,1,0:T(8,128)(2,1)}, u32[]{:S(2)}, u32[]{:S(2)}) collective-permute-start(bf16[2,144,1440]{2,1,0:T(8,128)(2,1)} %collective-permute-done.18.refs_10_), channel_id=1, source_target_pairs={{0,8},{4,12},{8,0},{12,4},{16,24},{20,28},{24,16},{28,20},{1,9},{5... | collective-permute-start | bytes 2488328 | tf_op jit(solution)/shard_map/ppermute | solution.py:24
  142.6 23.1 %collective-permute-start.25 = (bf16[2,144,1440]{2,1,0:T(8,128)(2,1)}, bf16[2,144,1440]{2,1,0:T(8,128)(2,1)}, u32[]{:S(2)}, u32[]{:S(2)}) collective-permute-start(bf16[2,144,1440]{2,1,0:T(8,128)(2,1)} %collective-permute-done.18.refs_10_), channel_id=1, source_target_pairs={{0,4},{4,0},{8,12},{12,8},{16,20},{20,16},{24,28},{28,24},{1,5},{5... | collective-permute-start | bytes 2488328 | tf_op jit(solution)/shard_map/ppermute | solution.py:24
  149.5 16.1 %collective-permute-start.27 = (bf16[128,2432]{1,0:T(8,128)(2,1)}, bf16[128,2432]{1,0:T(8,128)(2,1)}, u32[]{:S(2)}, u32[]{:S(2)}) collective-permute-start(bf16[128,2432]{1,0:T(8,128)(2,1)} %get-tuple-element.503), channel_id=1, source_target_pairs={{0,2},{1,3},{2,0},{3,1},{4,6},{5,7},{6,4},{7,5},{8,10},{9,11},{10,... | collective-permute-start | bytes 1867784 | tf_op jit(solution)/shard_map/ppermute | solution.py:24
  151.0 36.2 %collective-permute-start.36 = (bf16[2,144,1440]{2,1,0:T(8,128)(2,1)}, bf16[2,144,1440]{2,1,0:T(8,128)(2,1)}, u32[]{:S(2)}, u32[]{:S(2)}) collective-permute-start(bf16[2,144,1440]{2,1,0:T(8,128)(2,1)} %copy-done.112), channel_id=1, source_target_pairs={{0,4},{4,0},{8,12},{12,8},{16,20},{20,16},{24,28},{28,24},{1,5},{5... | collective-permute-start | bytes 2488328 | tf_op jit(solution)/shard_map/ppermute | solution.py:24
  152.2 14.7 %collective-permute-start.30 = (bf16[3,8,5760]{2,1,0:T(8,128)(2,1)S(1)}, bf16[3,8,5760]{2,1,0:T(8,128)(2,1)S(1)}, u32[]{:S(2)}, u32[]{:S(2)}) collective-permute-start(bf16[3,8,5760]{2,1,0:T(8,128)(2,1)S(1)} %collective-permute-done.24), channel_id=1, source_target_pairs={{0,1},{1,0},{2,3},{3,2},{4,5},{5,4},{6,7},{7,6},{8,9},{9,8},{10,11... | collective-permute-start | bytes 829448 | tf_op jit(solution)/shard_map/ppermute | solution.py:24
  165.1 24.5 %collective-permute-start.34 = (bf16[256,2304]{1,0:T(8,128)(2,1)S(1)}, bf16[256,2304]{1,0:T(8,128)(2,1)S(1)}, u32[]{:S(2)}, u32[]{:S(2)}) collective-permute-start(bf16[256,2304]{1,0:T(8,128)(2,1)S(1)} %copy-done.49), channel_id=1, source_target_pairs={{0,1},{1,0},{2,3},{3,2},{4,5},{5,4},{6,7},{7,6},{8,9},{9,8},{10,11... | collective-permute-start | bytes 3538952 | tf_op jit(solution)/shard_map/ppermute | solution.py:24
  165.6 16.0 %collective-permute-start.29 = (bf16[128,2432]{1,0:T(8,128)(2,1)S(1)}, bf16[128,2432]{1,0:T(8,128)(2,1)S(1)}, u32[]{:S(2)}, u32[]{:S(2)}) collective-permute-start(bf16[128,2432]{1,0:T(8,128)(2,1)S(1)} %copy-done.80), channel_id=1, source_target_pairs={{0,2},{1,3},{2,0},{3,1},{4,6},{5,7},{6,4},{7,5},{8,10},{9,11},{10,... | collective-permute-start | bytes 1867784 | tf_op jit(solution)/shard_map/ppermute | solution.py:24
  166.9 14.8 %collective-permute-start.28 = (bf16[256,2432]{1,0:T(8,128)(2,1)S(1)}, bf16[256,2432]{1,0:T(8,128)(2,1)S(1)}, u32[]{:S(2)}, u32[]{:S(2)}) collective-permute-start(bf16[256,2432]{1,0:T(8,128)(2,1)S(1)} %get-tuple-element.302), channel_id=1, source_target_pairs={{0,1},{1,0},{2,3},{3,2},{4,5},{5,4},{6,7},{7,6},{8,9},{9,8},{10,11... | collective-permute-start | bytes 3735560 | tf_op jit(solution)/shard_map/ppermute | solution.py:24
  168.1 23.1 %collective-permute-start.37 = (bf16[2,144,1440]{2,1,0:T(8,128)(2,1)}, bf16[2,144,1440]{2,1,0:T(8,128)(2,1)S(1)}, u32[]{:S(2)}, u32[]{:S(2)}) collective-permute-start(bf16[2,144,1440]{2,1,0:T(8,128)(2,1)} %collective-permute-done.25.refs_11_), channel_id=1, source_target_pairs={{0,8},{4,12},{8,0},{12,4},{16,24},{20,28},{24,16},{28,20},{1,9},{5... | collective-permute-start | bytes 2488328 | tf_op jit(solution)/shard_map/ppermute | solution.py:24
  181.7 21.7 %collective-permute-start.35 = (bf16[2,576,1440]{2,1,0:T(8,128)(2,1)S(1)}, bf16[2,576,1440]{2,1,0:T(8,128)(2,1)S(1)}, u32[]{:S(2)}, u32[]{:S(2)}) collective-permute-start(bf16[2,576,1440]{2,1,0:T(8,128)(2,1)S(1)} %get-tuple-element.311), channel_id=1, source_target_pairs={{0,1},{1,0},{2,3},{3,2},{4,5},{5,4},{6,7},{7,6},{8,9},{9,8},{10,11... | collective-permute-start | bytes 9953288 | tf_op jit(solution)/shard_map/ppermute | solution.py:24
  185.7 17.6 %collective-permute-start.33 = (bf16[256,2304]{1,0:T(8,128)(2,1)S(1)}, bf16[256,2304]{1,0:T(8,128)(2,1)S(1)}, u32[]{:S(2)}, u32[]{:S(2)}) collective-permute-start(bf16[256,2304]{1,0:T(8,128)(2,1)S(1)} %multiply_convert_fusion.1.refs_0_.refs_2_), channel_id=1, source_target_pairs={{0,1},{1,0},{2,3},{3,2},{4,5},{5,4},{6,7},{7,6},{8,9},{9,8},{10,11... | collective-permute-start | bytes 3538952 | tf_op jit(solution)/shard_map/ppermute | solution.py:24
  187.2 16.2 %collective-permute-start.38 = (bf16[128,2304]{1,0:T(8,128)(2,1)S(1)}, bf16[128,2304]{1,0:T(8,128)(2,1)S(1)}, u32[]{:S(2)}, u32[]{:S(2)}) collective-permute-start(bf16[128,2304]{1,0:T(8,128)(2,1)S(1)} %get-tuple-element.314), channel_id=1, source_target_pairs={{0,2},{1,3},{2,0},{3,1},{4,6},{5,7},{6,4},{7,5},{8,10},{9,11},{10,... | collective-permute-start | bytes 1769480 | tf_op jit(solution)/shard_map/ppermute | solution.py:24
  189.6 52.0 %collective-permute-start.31 = (bf16[256,2304]{1,0:T(8,128)(2,1)S(1)}, bf16[256,2304]{1,0:T(8,128)(2,1)S(1)}, u32[]{:S(2)}, u32[]{:S(2)}) collective-permute-start(bf16[256,2304]{1,0:T(8,128)(2,1)S(1)} %multiply_convert_fusion.1.refs_0_.refs_2_), channel_id=1, source_target_pairs={{0,2},{1,3},{2,0},{3,1},{4,6},{5,7},{6,4},{7,5},{8,10},{9,11},{10,... | collective-permute-start | bytes 3538952 | tf_op jit(solution)/shard_map/ppermute | solution.py:24
  191.2 50.4 %collective-permute-start.32 = (bf16[128,2304]{1,0:T(8,128)(2,1)}, bf16[128,2304]{1,0:T(8,128)(2,1)S(1)}, u32[]{:S(2)}, u32[]{:S(2)}) collective-permute-start(bf16[128,2304]{1,0:T(8,128)(2,1)} %get-tuple-element.310), channel_id=1, source_target_pairs={{0,2},{1,3},{2,0},{3,1},{4,6},{5,7},{6,4},{7,5},{8,10},{9,11},{10,... | collective-permute-start | bytes 1769480 | tf_op jit(solution)/shard_map/ppermute | solution.py:24
  288.1 17.2 %collective-permute-start.43 = (bf16[256,2432]{1,0:T(8,128)(2,1)S(1)}, bf16[256,2432]{1,0:T(8,128)(2,1)S(1)}, u32[]{:S(2)}, u32[]{:S(2)}) collective-permute-start(bf16[256,2432]{1,0:T(8,128)(2,1)S(1)} %copy-done.109), channel_id=1, source_target_pairs={{0,1},{1,0},{2,3},{3,2},{4,5},{5,4},{6,7},{7,6},{8,9},{9,8},{10,11... | collective-permute-start | bytes 3735560 | tf_op jit(solution)/shard_map/ppermute | solution.py:24
  288.3 17.0 %collective-permute-start.44 = (bf16[256,2432]{1,0:T(8,128)(2,1)S(1)}, bf16[256,2432]{1,0:T(8,128)(2,1)S(1)}, u32[]{:S(2)}, u32[]{:S(2)}) collective-permute-start(bf16[256,2432]{1,0:T(8,128)(2,1)S(1)} %copy-done.110), channel_id=1, source_target_pairs={{0,1},{1,0},{2,3},{3,2},{4,5},{5,4},{6,7},{7,6},{8,9},{9,8},{10,11... | collective-permute-start | bytes 3735560 | tf_op jit(solution)/shard_map/ppermute | solution.py:24
  288.7 16.6 %collective-permute-start.45 = (bf16[256,2432]{1,0:T(8,128)(2,1)S(1)}, bf16[256,2432]{1,0:T(8,128)(2,1)S(1)}, u32[]{:S(2)}, u32[]{:S(2)}) collective-permute-start(bf16[256,2432]{1,0:T(8,128)(2,1)S(1)} %copy-done.108), channel_id=1, source_target_pairs={{0,1},{1,0},{2,3},{3,2},{4,5},{5,4},{6,7},{7,6},{8,9},{9,8},{10,11... | collective-permute-start | bytes 3735560 | tf_op jit(solution)/shard_map/ppermute | solution.py:24
  288.9 16.4 %collective-permute-start.42 = (bf16[128,2432]{1,0:T(8,128)(2,1)S(1)}, bf16[128,2432]{1,0:T(8,128)(2,1)S(1)}, u32[]{:S(2)}, u32[]{:S(2)}) collective-permute-start(bf16[128,2432]{1,0:T(8,128)(2,1)S(1)} %get-tuple-element.501), channel_id=1, source_target_pairs={{0,2},{1,3},{2,0},{3,1},{4,6},{5,7},{6,4},{7,5},{8,10},{9,11},{10,... | collective-permute-start | bytes 1867784 | tf_op jit(solution)/shard_map/ppermute | solution.py:24
  289.5 19.4 %collective-permute-start.47 = (bf16[1,64,1440]{2,1,0:T(8,128)(2,1)S(1)}, bf16[1,64,1440]{2,1,0:T(8,128)(2,1)S(1)}, u32[]{:S(2)}, u32[]{:S(2)}) collective-permute-start(bf16[1,64,1440]{2,1,0:T(8,128)(2,1)S(1)} %pad_bitcast_fusion), channel_id=1, source_target_pairs={{0,8},{4,12},{8,0},{12,4},{16,24},{20,28},{24,16},{28,20},{1,9},{5... | collective-permute-start | bytes 552968 | tf_op jit(solution)/shard_map/ppermute | solution.py:24
  305.3 15.5 %collective-permute-start.46 = (bf16[128,2432]{1,0:T(8,128)(2,1)S(1)}, bf16[128,2432]{1,0:T(8,128)(2,1)S(1)}, u32[]{:S(2)}, u32[]{:S(2)}) collective-permute-start(bf16[128,2432]{1,0:T(8,128)(2,1)S(1)} %get-tuple-element.346), channel_id=1, source_target_pairs={{0,2},{1,3},{2,0},{3,1},{4,6},{5,7},{6,4},{7,5},{8,10},{9,11},{10,... | collective-permute-start | bytes 1867784 | tf_op jit(solution)/shard_map/ppermute | solution.py:24
  329.0 30.1 %collective-permute-start.48 = (bf16[256,2432]{1,0:T(8,128)(2,1)}, bf16[256,2432]{1,0:T(8,128)(2,1)}, u32[]{:S(2)}, u32[]{:S(2)}) collective-permute-start(bf16[256,2432]{1,0:T(8,128)(2,1)} %concatenate.265.refs_0_), channel_id=1, source_target_pairs={{0,2},{1,3},{2,0},{3,1},{4,6},{5,7},{6,4},{7,5},{8,10},{9,11},{10,... | collective-permute-start | bytes 3735560 | tf_op jit(solution)/shard_map/ppermute | solution.py:24
  330.3 20.8 %collective-permute-start.50 = (bf16[2,64,1440]{2,1,0:T(8,128)(2,1)}, bf16[2,64,1440]{2,1,0:T(8,128)(2,1)}, u32[]{:S(2)}, u32[]{:S(2)}) collective-permute-start(bf16[2,64,1440]{2,1,0:T(8,128)(2,1)} %maximum_select_fusion.6), channel_id=1, source_target_pairs={{0,16},{4,20},{8,24},{12,28},{16,0},{20,4},{24,8},{28,12},{1,17},{... | collective-permute-start | bytes 1105928 | tf_op jit(solution)/shard_map/ppermute | solution.py:24
  359.1 30.1 %collective-permute-start.52 = (bf16[256,2432]{1,0:T(8,128)(2,1)}, bf16[256,2432]{1,0:T(8,128)(2,1)}, u32[]{:S(2)}, u32[]{:S(2)}) collective-permute-start(bf16[256,2432]{1,0:T(8,128)(2,1)} %add_convert_fusion), channel_id=1, source_target_pairs={{0,2},{1,3},{2,0},{3,1},{4,6},{5,7},{6,4},{7,5},{8,10},{9,11},{10,... | collective-permute-start | bytes 3735560 | tf_op jit(solution)/shard_map/ppermute | solution.py:24
  360.8 25.2 %collective-permute-start.53 = (bf16[4,64,1440]{2,1,0:T(8,128)(2,1)}, bf16[4,64,1440]{2,1,0:T(8,128)(2,1)S(1)}, u32[]{:S(2)}, u32[]{:S(2)}) collective-permute-start(bf16[4,64,1440]{2,1,0:T(8,128)(2,1)} %maximum_select_fusion.3), channel_id=1, source_target_pairs={{0,4},{4,0},{8,12},{12,8},{16,20},{20,16},{24,28},{28,24},{1,5},{5... | collective-permute-start | bytes 2211848 | tf_op jit(solution)/shard_map/ppermute | solution.py:24
  390.1 16.5 %collective-permute-start.54 = (bf16[256,16]{1,0:T(8,128)(2,1)S(1)}, bf16[256,16]{1,0:T(8,128)(2,1)S(1)}, u32[]{:S(2)}, u32[]{:S(2)}) collective-permute-start(bf16[256,16]{1,0:T(8,128)(2,1)S(1)} %fusion.35), channel_id=1, source_target_pairs={{0,2},{1,3},{2,0},{3,1},{4,6},{5,7},{6,4},{7,5},{8,10},{9,11},{10,... | collective-permute-start | bytes 24584 | tf_op jit(solution)/shard_map/ppermute | solution.py:24
  390.6 16.0 %collective-permute-start.55 = (bf16[256,16]{1,0:T(8,128)(2,1)S(1)}, bf16[256,16]{1,0:T(8,128)(2,1)S(1)}, u32[]{:S(2)}, u32[]{:S(2)}) collective-permute-start(bf16[256,16]{1,0:T(8,128)(2,1)S(1)} %fusion.35), channel_id=1, source_target_pairs={{0,1},{1,0},{2,3},{3,2},{4,5},{5,4},{6,7},{7,6},{8,9},{9,8},{10,11... | collective-permute-start | bytes 24584 | tf_op jit(solution)/shard_map/ppermute | solution.py:24
  427.2 18.3 %collective-permute-start.64 = (bf16[2,80,576]{2,1,0:T(8,128)(2,1)S(1)}, bf16[2,80,576]{2,1,0:T(8,128)(2,1)S(1)}, u32[]{:S(2)}, u32[]{:S(2)}) collective-permute-start(bf16[2,80,576]{2,1,0:T(8,128)(2,1)S(1)} %maximum_select_fusion.8), channel_id=1, source_target_pairs={{0,16},{4,20},{8,24},{12,28},{16,0},{20,4},{24,8},{28,12},{1,17},{... | collective-permute-start | bytes 552968 | tf_op jit(solution)/shard_map/ppermute | solution.py:24
  451.3 18.1 %collective-permute-start.68 = (bf16[128,2304]{1,0:T(8,128)(2,1)}, bf16[128,2304]{1,0:T(8,128)(2,1)}, u32[]{:S(2)}, u32[]{:S(2)}) collective-permute-start(bf16[128,2304]{1,0:T(8,128)(2,1)} %get-tuple-element.505), channel_id=1, source_target_pairs={{0,2},{1,3},{2,0},{3,1},{4,6},{5,7},{6,4},{7,5},{8,10},{9,11},{10,... | collective-permute-start | bytes 1769480 | tf_op jit(solution)/shard_map/ppermute | solution.py:24
  452.7 16.5 %collective-permute-start.66 = (bf16[2,96,576]{2,1,0:T(8,128)(2,1)}, bf16[2,96,576]{2,1,0:T(8,128)(2,1)S(1)}, u32[]{:S(2)}, u32[]{:S(2)}) collective-permute-start(bf16[2,96,576]{2,1,0:T(8,128)(2,1)} %maximum_select_fusion.7), channel_id=1, source_target_pairs={{0,16},{4,20},{8,24},{12,28},{16,0},{20,4},{24,8},{28,12},{1,17},{... | collective-permute-start | bytes 663560 | tf_op jit(solution)/shard_map/ppermute | solution.py:24
  470.0 22.0 %collective-permute-start.71 = (bf16[256,2304]{1,0:T(8,128)(2,1)}, bf16[256,2304]{1,0:T(8,128)(2,1)}, u32[]{:S(2)}, u32[]{:S(2)}) collective-permute-start(bf16[256,2304]{1,0:T(8,128)(2,1)} %get-tuple-element.463), channel_id=1, source_target_pairs={{0,1},{1,0},{2,3},{3,2},{4,5},{5,4},{6,7},{7,6},{8,9},{9,8},{10,11... | collective-permute-start | bytes 3538952 | tf_op jit(solution)/shard_map/ppermute | solution.py:24
  475.4 16.1 %collective-permute-start.70 = (bf16[128,2304]{1,0:T(8,128)(2,1)S(1)}, bf16[128,2304]{1,0:T(8,128)(2,1)S(1)}, u32[]{:S(2)}, u32[]{:S(2)}) collective-permute-start(bf16[128,2304]{1,0:T(8,128)(2,1)S(1)} %copy-done.84), channel_id=1, source_target_pairs={{0,2},{1,3},{2,0},{3,1},{4,6},{5,7},{6,4},{7,5},{8,10},{9,11},{10,... | collective-permute-start | bytes 1769480 | tf_op jit(solution)/shard_map/ppermute | solution.py:24
  476.0 16.0 %collective-permute-start.69 = (bf16[4,96,576]{2,1,0:T(8,128)(2,1)S(1)}, bf16[4,96,576]{2,1,0:T(8,128)(2,1)S(1)}, u32[]{:S(2)}, u32[]{:S(2)}) collective-permute-start(bf16[4,96,576]{2,1,0:T(8,128)(2,1)S(1)} %maximum_select_fusion.4), channel_id=1, source_target_pairs={{0,4},{4,0},{8,12},{12,8},{16,20},{20,16},{24,28},{28,24},{1,5},{5... | collective-permute-start | bytes 1327112 | tf_op jit(solution)/shard_map/ppermute | solution.py:24
  478.6 20.2 %collective-permute-start.77 = (bf16[5,2,16,576]{3,2,1,0:T(8,128)(2,1)S(1)}, bf16[5,2,16,576]{3,2,1,0:T(8,128)(2,1)S(1)}, u32[]{:S(2)}, u32[]{:S(2)}) collective-permute-start(bf16[5,2,16,576]{3,2,1,0:T(8,128)(2,1)S(1)} %get-tuple-element.490), channel_id=1, source_target_pairs={{0,3},{1,2},{2,1},{3,0},{4,7},{5,6},{6,5},{7,4},{8,11},{9,10},{10,... | collective-permute-start | bytes 552968 | tf_op jit(solution)/shard_map/ppermute | solution.py:24
  479.7 22.9 %collective-permute-start.75 = (bf16[5,2,16,576]{3,2,1,0:T(8,128)(2,1)S(1)}, bf16[5,2,16,576]{3,2,1,0:T(8,128)(2,1)S(1)}, u32[]{:S(2)}, u32[]{:S(2)}) collective-permute-start(bf16[5,2,16,576]{3,2,1,0:T(8,128)(2,1)S(1)} %get-tuple-element.491), channel_id=1, source_target_pairs={{0,1},{1,0},{2,3},{3,2},{4,5},{5,4},{6,7},{7,6},{8,9},{9,8},{10,11... | collective-permute-start | bytes 552968 | tf_op jit(solution)/shard_map/ppermute | solution.py:24
  (145 other events, 1136.4 us)
